TPU v7x, 32 devices: a whole 2x2x4 slice. The times are simulated.
32 devices in a mesh: rep: 4 (over z), fsdp: 8 (over y, x, core).
Axes of the slice: x: 2, y: 2, z: 4, core: 2. Of those that a mesh axis runs over, the one named last changes fastest.
Arguments:
- inputs: bfloat16 [64, 512, 768], P(('rep', 'fsdp')), may hold values from -6 to 6
- seg_ids: int32 [64, 512], P(('rep', 'fsdp')), may hold values from 0 to 7, never falling along the last dimension, each value on 1 to 128 neighbouring positions
- example_map: int32 [64, 8], P(('rep', 'fsdp')), may hold values from 0 to 7
- labels: int32 [64, 8], P(('rep', 'fsdp')), may hold values from 0 to 13
- out_cotangent: bfloat16 [64, 512, 768], P(('rep', 'fsdp')), may hold values from -0.079589844 to 0.079589844
- params: float32 [7204864], P('fsdp'), as said below
- moment_one: float32 [7204864], P('fsdp'), may hold values from -4 to 4
- moment_two: float32 [7204864], P('fsdp'), may hold values from 0.01 to 10
Outputs:
- layer_out: bfloat16 [64, 512, 768], P(('rep', 'fsdp'))
- logits: float32 [64, 8, 14], P(('rep', 'fsdp'))
- input_grad: bfloat16 [64, 512, 768], P(('rep', 'fsdp'))
- adam_step: float32 [7204864], P('fsdp')
- new_moment_one: float32 [7204864], P('fsdp')
- new_moment_two: float32 [7204864], P('fsdp')
Inputs may be any that keep to these rules, and one draw needn't show every extreme that they name: params holds the parameters in the layout of weights_bf; its last 882 entries are zero.
All inputs are finite; a program needn't handle non-finite values.
Results may differ from a plain program's by a relative error of at most 0.014.
Values may be sent and summed in bfloat16 or wider, within the bound.
No kernel may reach another device: no remote copies, remote signals or barrier semaphores. Data moves between devices by JAX's collectives and lax.ppermute only.
A program may use at most 256 MiB of HBM per device.

v0:
```python
import functools
import math

import jax
import jax.numpy as jnp
from jax import lax
from jax.experimental import pallas as pl
from jax.experimental.pallas import tpu as pltpu
from jax.sharding import PartitionSpec as P

D = 768
HEADS = 12
PAIRS = HEADS // 2
FF = 3072
LEN = 512
STU = 128
CLASSES = 14
SEGS = 8
EXR = 8
LANE = 128
CHUNK = 160

NORM_EPS = 1e-12
MASKED = -1e30
BETA_ONE = 0.9
BETA_TWO = 0.999
ADAM_EPS = 1e-08
CORRECT_ONE = 0.9999734386
CORRECT_TWO = 0.0952078529

F32 = jnp.float32
BF = jnp.bfloat16
HIGH = lax.Precision.HIGHEST
SDS = jax.ShapeDtypeStruct

QB = 128
WINDOWS = tuple((max(0, i - 1) * QB, min(LEN // QB, i + 2) * QB) for i in range(LEN // QB))
OFFSETS = tuple(sum(hi - lo for lo, hi in WINDOWS[:i]) for i in range(len(WINDOWS)))
WIDE = sum(hi - lo for lo, hi in WINDOWS)

TABLE = {}
_row = 0
for _name, _size in (
    ("w_qkv", D * 3 * D),
    ("b_qv", 2 * D),
    ("w_out", D * D),
    ("b_out", D),
    ("gain_one", D),
    ("shift_one", D),
    ("w_in", D * FF),
    ("b_in", FF),
    ("w_back", FF * D),
    ("b_back", D),
    ("gain_two", D),
    ("shift_two", D),
    ("w_stu", D * STU),
    ("b_stu", STU),
    ("pool_query", STU),
    ("w_mid", STU * STU),
    ("b_mid", STU),
    ("w_cls", STU * CLASSES),
    ("b_cls", LANE),
):
    TABLE[_name] = _row
    _row += _size // LANE
USED = _row
SPLIT = TABLE["w_out"]

NN = (((1,), (0,)), ((), ()))
NT = (((1,), (1,)), ((), ()))
TN = (((0,), (0,)), ((), ()))


def dot(a, b, dims=NN, precision=None):
    return lax.dot_general(a, b, dims, precision=precision, preferred_element_type=F32)


def whole(*shape):
    return pl.BlockSpec(shape, lambda *_: (0,) * len(shape))


def params_of(mib=60):
    return pltpu.CompilerParams(vmem_limit_bytes=mib << 20, dimension_semantics=None)


def at(i, n):
    return pl.ds(pl.multiple_of(i * n, n), n)


def unpack_kernel(shard_rows, count, g_ref, wqkv, bq, wout, win, wback, wstu, wmid, vec, small, wcls, flat):
    d = pl.program_id(0)
    padded = g_ref.shape[1]

    def widen(m, _):
        flat[pl.ds(d * shard_rows + m * CHUNK, CHUNK), :] = g_ref[0, at(m, CHUNK), :].astype(F32)
        return 0

    lax.fori_loop(0, padded // CHUNK, widen, 0)

    @pl.when(d == count - 1)
    def _():
        def matrix(out, name, rows):
            tall, broad = out.shape
            cols = broad // LANE

            def some(k, _):
                for j in range(cols):
                    out[at(k, rows), j * LANE : (j + 1) * LANE] = flat[
                        pl.ds(TABLE[name] + k * (rows * cols) + j, rows, stride=cols), :
                    ].astype(BF)
                return 0

            lax.fori_loop(0, tall // rows, some, 0)

        matrix(wqkv, "w_qkv", 32)
        matrix(wout, "w_out", 64)
        matrix(win, "w_in", 32)
        matrix(wback, "w_back", 64)

        def line(out, row, name, blocks, skip=0):
            first = TABLE[name] + skip
            for j in range(blocks):
                out[row : row + 1, j * LANE : (j + 1) * LANE] = flat[first + j : first + j + 1, :]

        wstu[...] = flat[TABLE["w_stu"] : TABLE["w_stu"] + D, :].astype(BF)
        wmid[...] = flat[TABLE["w_mid"] : TABLE["w_mid"] + STU, :]
        wcls[...] = flat[TABLE["w_cls"] : TABLE["w_cls"] + 16, :]
        nb = D // LANE
        line(vec, 0, "b_out", nb)
        line(vec, 1, "gain_one", nb)
        line(vec, 2, "shift_one", nb)
        line(vec, 3, "b_back", nb)
        line(vec, 4, "gain_two", nb)
        line(vec, 5, "shift_two", nb)
        for q in range(4):
            line(vec, 8 + q, "b_in", nb, q * nb)
        line(small, 0, "b_stu", 1)
        line(small, 1, "pool_query", 1)
        line(small, 2, "b_mid", 1)
        lane = lax.broadcasted_iota(jnp.int32, (1, LANE), 1)
        small[3:4, :] = jnp.where(lane < CLASSES, flat[TABLE["b_cls"] : TABLE["b_cls"] + 1, :], 0.0)
        wide = lax.broadcasted_iota(jnp.int32, (1, 3 * D), 1)
        bq[0:1, :] = jnp.zeros((1, 3 * D), F32)
        bq[1:2, :] = jnp.where(wide < D, 0.125, 1.0).astype(F32)
        for j in range(nb):
            first = TABLE["b_qv"]
            bq[0:1, j * LANE : (j + 1) * LANE] = flat[first + j : first + j + 1, :]
            bq[0:1, 2 * D + j * LANE : 2 * D + (j + 1) * LANE] = flat[first + nb + j : first + nb + j + 1, :]


def unpack(gathered, shard_rows):
    count, padded, _ = gathered.shape
    outs = (
        SDS((D, 3 * D), BF),
        SDS((8, 3 * D), F32),
        SDS((D, D), BF),
        SDS((D, FF), BF),
        SDS((FF, D), BF),
        SDS((D, STU), BF),
        SDS((STU, STU), F32),
        SDS((16, D), F32),
        SDS((8, LANE), F32),
        SDS((16, LANE), F32),
    )
    return pl.pallas_call(
        functools.partial(unpack_kernel, shard_rows, count),
        grid=(count,),
        in_specs=[pl.BlockSpec((1, padded, LANE), lambda d: (d, 0, 0))],
        out_specs=[whole(*o.shape) for o in outs],
        out_shape=outs,
        scratch_shapes=[pltpu.VMEM(((count - 1) * shard_rows + padded + 16, LANE), F32)],
        compiler_params=params_of(),
        name="unpack",
    )(gathered)


def half_masks():
    lane = lax.broadcasted_iota(jnp.int32, (1, LANE), 1)
    return ((lane < 64).astype(F32).astype(BF), (lane >= 64).astype(F32).astype(BF))


def attend_kernel(x_ref, segc_ref, segr_ref, w_ref, bq_ref, qkv_ref, p_ref, att_ref, bias):
    def project(t, _):
        cols = at(t, 256)
        r = dot(x_ref[0], w_ref[:, cols])
        qkv_ref[0, :, cols] = ((r + bq_ref[0:1, cols]) * bq_ref[1:2, cols]).astype(BF)
        return 0

    lax.fori_loop(0, 3 * D // 256, project, 0)

    for i, (lo, hi) in enumerate(WINDOWS):
        bias[:, OFFSETS[i] : OFFSETS[i] + hi - lo] = jnp.where(
            segc_ref[0, i * QB : (i + 1) * QB, :] == segr_ref[0, :, lo:hi], 0.0, MASKED
        )

    masks = half_masks()

    def pair(p, _):
        q2 = qkv_ref[0, :, at(p, LANE)]
        k2 = qkv_ref[0, :, at(p + PAIRS, LANE)]
        v2 = qkv_ref[0, :, at(p + 2 * PAIRS, LANE)]
        for i, (lo, hi) in enumerate(WINDOWS):
            out = jnp.zeros((QB, LANE), F32)
            for h in range(2):
                s = dot(q2[i * QB : (i + 1) * QB] * masks[h], k2[lo:hi], NT)
                s = s + bias[:, OFFSETS[i] : OFFSETS[i] + hi - lo]
                e = jnp.exp(s - jnp.max(s, axis=-1, keepdims=True))
                a = (e * (1.0 / jnp.sum(e, axis=-1, keepdims=True))).astype(BF)
                p_ref[0, 2 * p + h, :, OFFSETS[i] : OFFSETS[i] + hi - lo] = a
                out = out + dot(a, v2[lo:hi] * masks[h])
            att_ref[0, i * QB : (i + 1) * QB, at(p, LANE)] = out.astype(BF)
        return 0

    lax.fori_loop(0, PAIRS, pair, 0)


def row_spec(*shape):
    return pl.BlockSpec((1, *shape), lambda r: (r,) + (0,) * len(shape))


def attend(x, segc, segr, wqkv, bq):
    rows = x.shape[0]
    return pl.pallas_call(
        attend_kernel,
        grid=(rows,),
        in_specs=[row_spec(LEN, D), row_spec(LEN, 1), row_spec(1, LEN), whole(D, 3 * D), whole(8, 3 * D)],
        out_specs=[row_spec(LEN, 3 * D), row_spec(HEADS, QB, WIDE), row_spec(LEN, D)],
        out_shape=[SDS((rows, LEN, 3 * D), BF), SDS((rows, HEADS, QB, WIDE), BF), SDS((rows, LEN, D), BF)],
        scratch_shapes=[pltpu.VMEM((QB, WIDE), F32)],
        compiler_params=params_of(),
        name="attend",
    )(x, segc, segr, wqkv, bq)


TB = 64


def fold(v):
    return jnp.sum(v.reshape(v.shape[0] // 8, 8, v.shape[1]), axis=0)


def middle_kernel(
    x_ref,
    att_ref,
    segc_ref,
    hot_ref,
    cot_ref,
    wout,
    win,
    wback,
    wstu,
    wmid,
    vec,
    small,
    wcls,
    out_ref,
    logit_ref,
    nbf_ref,
    act_ref,
    dffn_ref,
    dinner_ref,
    dstu_ref,
    dh1_ref,
    dbr_ref,
    datt_ref,
    vg_ref,
    sg_ref,
    gmid_ref,
    gcls_ref,
    hid,
    n1,
    nrm,
    n2,
    q1,
    q2,
    gp,
    acc,
    accb,
):
    r = pl.program_id(0)

    @pl.when(r == 0)
    def _():
        acc[...] = jnp.zeros_like(acc)
        accb[...] = jnp.zeros_like(accb)
        sg_ref[...] = jnp.zeros_like(sg_ref)
        gmid_ref[...] = jnp.zeros_like(gmid_ref)
        gcls_ref[...] = jnp.zeros_like(gcls_ref)

    def first(t, _):
        cols = at(t, 256)
        hid[:, cols] = x_ref[0, :, cols].astype(F32) + (dot(att_ref[0], wout[:, cols]) + vec[0:1, cols])
        return 0

    lax.fori_loop(0, D // 256, first, 0)

    def norm_one(b, _):
        rows = at(b, TB)
        h = hid[rows, :]
        c = h - jnp.mean(h, axis=-1, keepdims=True)
        q = lax.rsqrt(jnp.mean(c * c, axis=-1, keepdims=True) + NORM_EPS)
        n = c * q
        n1[rows, :] = n
        q1[rows, :] = jnp.broadcast_to(q, (TB, LANE))
        y = n * vec[1:2, :] + vec[2:3, :]
        nrm[rows, :] = y
        nbf_ref[0, rows, :] = y.astype(BF)
        return 0

    lax.fori_loop(0, LEN // TB, norm_one, 0)

    def inner(t, _):
        cols = at(t, 256)
        bias = vec[pl.ds(8 + t // 3, 1), at(t % 3, 256)]
        u = dot(nbf_ref[0], win[:, cols]) + bias
        cdf = 0.5 * (1.0 + lax.erf(u * (0.5**0.5)))
        act_ref[0, :, cols] = (u * cdf).astype(BF)
        gp[:, cols] = cdf + u * (jnp.exp(-0.5 * u * u) * (1.0 / math.sqrt(2.0 * math.pi)))
        return 0

    lax.fori_loop(0, FF // 256, inner, 0)

    def second(t, _):
        cols = at(t, 256)
        hid[:, cols] = nrm[:, cols] + (dot(act_ref[0], wback[:, cols]) + vec[3:4, cols])
        return 0

    lax.fori_loop(0, D // 256, second, 0)

    def norm_two(b, _):
        rows = at(b, TB)
        h = hid[rows, :]
        c = h - jnp.mean(h, axis=-1, keepdims=True)
        q = lax.rsqrt(jnp.mean(c * c, axis=-1, keepdims=True) + NORM_EPS)
        n = c * q
        n2[rows, :] = n
        q2[rows, :] = jnp.broadcast_to(q, (TB, LANE))
        out_ref[0, rows, :] = (n * vec[4:5, :] + vec[5:6, :]).astype(BF)
        return 0

    lax.fori_loop(0, LEN // TB, norm_two, 0)

    lane = lax.broadcasted_iota(jnp.int32, (1, LANE), 1)
    left = lane < 64
    stu = dot(out_ref[0], wstu[...]) + small[0:1, :]
    pq = small[1:2, :] * 0.125
    sp = stu * pq
    s0 = jnp.sum(jnp.where(left, sp, 0.0), axis=-1, keepdims=True)
    s1 = jnp.sum(jnp.where(left, 0.0, sp), axis=-1, keepdims=True)
    member = (segc_ref[0] == (lane & 7)) & (lane < 16)
    e = jnp.where(member, jnp.where(lane < 8, s0, s1), MASKED)
    e = jnp.where(member, jnp.exp(e - jnp.max(e, axis=0, keepdims=True)), 0.0)
    total = jnp.sum(e, axis=0, keepdims=True)
    w = e * (1.0 / jnp.where(total == 0.0, 1.0, total))
    pooled16 = dot(w, stu, TN, HIGH)
    pooled = jnp.where(left, pooled16[0:8], pooled16[8:16])
    mid = jnp.tanh(dot(pooled, wmid[...], NN, HIGH) + small[2:3, :])
    logits = dot(mid, wcls[...], NN, HIGH) + small[3:4, :]
    logit_ref[0] = logits[:, :CLASSES]
    real = lane < CLASSES
    z = jnp.where(real, logits, MASKED)
    z = jnp.where(real, jnp.exp(z - jnp.max(z, axis=-1, keepdims=True)), 0.0)
    dl = z * (1.0 / jnp.sum(z, axis=-1, keepdims=True)) - hot_ref[0]
    gcls_ref[...] += dot(mid, dl, TN, HIGH)
    dpre = dot(dl, wcls[...], NT, HIGH) * (1.0 - mid * mid)
    gmid_ref[...] += dot(pooled, dpre, TN, HIGH)
    dpool = dot(dpre, wmid[...], NT, HIGH)
    zero = jnp.zeros((LANE - 16, LANE), F32)
    dp16 = jnp.concatenate([jnp.where(left, dpool, 0.0), jnp.where(left, 0.0, dpool), zero], axis=0)
    ones8 = jnp.ones((8, 1), F32)
    qp16 = jnp.concatenate([ones8 * jnp.where(left, pq, 0.0), ones8 * jnp.where(left, 0.0, pq), zero], axis=0)
    dpw = dot(stu, dp16, NT, HIGH)
    t16 = w * (dpw - jnp.sum(w * dpw, axis=0, keepdims=True))
    dstu = dot(w, dp16, NN, HIGH) + dot(t16, qp16, NN, HIGH)
    gq = dot(t16, stu, TN, HIGH)
    gq = jnp.sum(jnp.where(left, gq[0:8], gq[8:16]), axis=0, keepdims=True) * 0.125
    dstu_ref[0] = dstu.astype(BF)
    sg_ref[0:1, :] += jnp.sum(dstu, axis=0, keepdims=True)
    sg_ref[1:2, :] += gq
    sg_ref[2:3, :] += jnp.sum(dpre, axis=0, keepdims=True)
    sg_ref[3:4, :] += jnp.sum(dl, axis=0, keepdims=True)

    def spread(t, _):
        cols = at(t, 256)
        hid[:, cols] = cot_ref[0, :, cols].astype(F32) + dot(dstu_ref[0], wstu[cols, :], NT)
        return 0

    lax.fori_loop(0, D // 256, spread, 0)

    def back_two(b, _):
        rows = at(b, TB)
        g = hid[rows, :]
        n = n2[rows, :]
        acc[4] += fold(g * n)
        acc[5] += fold(g)
        ev = g * vec[4:5, :]
        d = q2[rows, 0:1] * (
            ev - jnp.mean(ev, axis=-1, keepdims=True) - n * jnp.mean(ev * n, axis=-1, keepdims=True)
        )
        acc[3] += fold(d)
        hid[rows, :] = d
        dffn_ref[0, rows, :] = d.astype(BF)
        return 0

    lax.fori_loop(0, LEN // TB, back_two, 0)

    def outer(t, _):
        cols = at(t, 256)
        d = dot(dffn_ref[0], wback[cols, :], NT) * gp[:, cols]
        accb[:, cols] += fold(d)
        dinner_ref[0, :, cols] = d.astype(BF)
        return 0

    lax.fori_loop(0, FF // 256, outer, 0)

    def third(t, _):
        cols = at(t, 256)
        hid[:, cols] += dot(dinner_ref[0], win[cols, :], NT)
        return 0

    lax.fori_loop(0, D // 256, third, 0)

    def back_one(b, _):
        rows = at(b, TB)
        g = hid[rows, :]
        n = n1[rows, :]
        acc[1] += fold(g * n)
        acc[2] += fold(g)
        ev = g * vec[1:2, :]
        d = q1[rows, 0:1] * (
            ev - jnp.mean(ev, axis=-1, keepdims=True) - n * jnp.mean(ev * n, axis=-1, keepdims=True)
        )
        acc[0] += fold(d)
        dh1_ref[0, rows, :] = d
        dbr_ref[0, rows, :] = d.astype(BF)
        return 0

    lax.fori_loop(0, LEN // TB, back_one, 0)

    def fourth(t, _):
        cols = at(t, 256)
        datt_ref[0, :, cols] = dot(dbr_ref[0], wout[cols, :], NT).astype(BF)
        return 0

    lax.fori_loop(0, D // 256, fourth, 0)

    @pl.when(r == pl.num_programs(0) - 1)
    def _():
        vg_ref[...] = jnp.zeros_like(vg_ref)
        for i in range(6):
            vg_ref[i : i + 1, :] = jnp.sum(acc[i], axis=0, keepdims=True)
        for i in range(4):
            vg_ref[8 + i : 9 + i, :] = jnp.sum(accb[:, i * D : (i + 1) * D], axis=0, keepdims=True)


def once(*shape):
    return pl.BlockSpec(shape, lambda *_: (0,) * len(shape), pipeline_mode=pl.Buffered(1))


def middle(x, att, segc, hot, cot, wout, win, wback, wstu, wmid, vec, small, wcls):
    rows = x.shape[0]
    tok = lambda n, dt: SDS((rows, LEN, n), dt)
    return pl.pallas_call(
        middle_kernel,
        grid=(rows,),
        in_specs=[
            row_spec(LEN, D),
            row_spec(LEN, D),
            row_spec(LEN, 1),
            row_spec(SEGS, LANE),
            row_spec(LEN, D),
            once(D, D),
            once(D, FF),
            once(FF, D),
            once(D, STU),
            once(STU, STU),
            once(16, D),
            once(8, LANE),
            once(STU, LANE),
        ],
        out_specs=[
            row_spec(LEN, D),
            row_spec(SEGS, CLASSES),
            row_spec(LEN, D),
            row_spec(LEN, FF),
            row_spec(LEN, D),
            row_spec(LEN, FF),
            row_spec(LEN, STU),
            row_spec(LEN, D),
            row_spec(LEN, D),
            row_spec(LEN, D),
            whole(16, D),
            whole(8, LANE),
            whole(STU, STU),
            whole(STU, LANE),
        ],
        out_shape=[
            tok(D, BF),
            SDS((rows, SEGS, CLASSES), F32),
            tok(D, BF),
            tok(FF, BF),
            tok(D, BF),
            tok(FF, BF),
            tok(STU, BF),
            tok(D, F32),
            tok(D, BF),
            tok(D, BF),
            SDS((16, D), F32),
            SDS((8, LANE), F32),
            SDS((STU, STU), F32),
            SDS((STU, LANE), F32),
        ],
        scratch_shapes=[
            pltpu.VMEM((LEN, D), F32),
            pltpu.VMEM((LEN, D), F32),
            pltpu.VMEM((LEN, D), F32),
            pltpu.VMEM((LEN, D), F32),
            pltpu.VMEM((LEN, LANE), F32),
            pltpu.VMEM((LEN, LANE), F32),
            pltpu.VMEM((LEN, FF), F32),
            pltpu.VMEM((6, 8, D), F32),
            pltpu.VMEM((8, FF), F32),
        ],
        compiler_params=params_of(),
        name="middle",
    )(x, att, segc, hot, cot, wout, win, wback, wstu, wmid, vec, small, wcls)


def retreat_kernel(qkv_ref, p_ref, datt_ref, dh1_ref, w_ref, dproj_ref, dx_ref, bg_ref, dk, dv):
    @pl.when(pl.program_id(0) == 0)
    def _():
        bg_ref[...] = jnp.zeros_like(bg_ref)

    masks = half_masks()

    def pair(p, _):
        q2 = qkv_ref[0, :, at(p, LANE)]
        k2 = qkv_ref[0, :, at(p + PAIRS, LANE)]
        v2 = qkv_ref[0, :, at(p + 2 * PAIRS, LANE)]
        d2 = datt_ref[0, :, at(p, LANE)]
        dk[...] = jnp.zeros_like(dk)
        dv[...] = jnp.zeros_like(dv)
        bq = jnp.zeros((1, LANE), F32)
        for i, (lo, hi) in enumerate(WINDOWS):
            dq = jnp.zeros((QB, LANE), F32)
            for h in range(2):
                a = p_ref[0, 2 * p + h, :, OFFSETS[i] : OFFSETS[i] + hi - lo]
                da = d2[i * QB : (i + 1) * QB] * masks[h]
                qh = q2[i * QB : (i + 1) * QB] * masks[h]
                wide = a.astype(F32)
                dp = dot(da, v2[lo:hi], NT)
                t = wide * dp
                ds = (t - wide * jnp.sum(t, axis=-1, keepdims=True)).astype(BF)
                dq = dq + dot(ds, k2[lo:hi] * masks[h])
                dk[lo:hi, :] += dot(ds, qh, TN)
                dv[lo:hi, :] += dot(a, da, TN)
            dq = dq * 0.125
            bq = bq + jnp.sum(dq, axis=0, keepdims=True)
            dproj_ref[0, i * QB : (i + 1) * QB, at(p, LANE)] = dq.astype(BF)
        dproj_ref[0, :, at(p + PAIRS, LANE)] = dk[...].astype(BF)
        dproj_ref[0, :, at(p + 2 * PAIRS, LANE)] = dv[...].astype(BF)
        bg_ref[0:1, at(p, LANE)] += bq
        bg_ref[1:2, at(p, LANE)] += jnp.sum(dv[...], axis=0, keepdims=True)
        return 0

    lax.fori_loop(0, PAIRS, pair, 0)

    def back(t, _):
        cols = at(t, 256)
        dx_ref[0, :, cols] = (dh1_ref[0, :, cols] + dot(dproj_ref[0], w_ref[cols, :], NT)).astype(BF)
        return 0

    lax.fori_loop(0, D // 256, back, 0)


def retreat(qkv, probs, datt, dh1, wqkv):
    rows = qkv.shape[0]
    return pl.pallas_call(
        retreat_kernel,
        grid=(rows,),
        in_specs=[
            row_spec(LEN, 3 * D),
            row_spec(HEADS, QB, WIDE),
            row_spec(LEN, D),
            row_spec(LEN, D),
            once(D, 3 * D),
        ],
        out_specs=[row_spec(LEN, 3 * D), row_spec(LEN, D), whole(8, D)],
        out_shape=[SDS((rows, LEN, 3 * D), BF), SDS((rows, LEN, D), BF), SDS((8, D), F32)],
        scratch_shapes=[pltpu.VMEM((LEN, LANE), F32), pltpu.VMEM((LEN, LANE), F32)],
        compiler_params=params_of(),
        name="retreat",
    )(qkv, probs, datt, dh1, wqkv)


def store_product(flat, first, lhs_ref, rhs_ref, turned, step=256):
    tokens, tall = lhs_ref.shape
    broad = rhs_ref.shape[1]
    cols = broad // LANE
    block = min(tall, turned.shape[0])

    def rows_of(m, _):
        for b in range(block // 256):
            turned[b * 256 : (b + 1) * 256, :] = lhs_ref[:, pl.ds(pl.multiple_of(m * block + b * 256, 256), 256)].T

        def cols_of(t, _):
            r = dot(turned[0:block, :], rhs_ref[:, at(t, step)])
            for j in range(step // LANE):
                place = first + m * (block * cols) + t * (step // LANE) + j
                flat[pl.ds(place, block, stride=cols), :] = r[:, j * LANE : (j + 1) * LANE]
            return 0

        lax.fori_loop(0, broad // step, cols_of, 0)
        return 0

    lax.fori_loop(0, tall // block, rows_of, 0)


def send_shards(flat, base, stop, shard_rows, out_ref, stage, sems):
    count, padded, _ = out_ref.shape
    plan = []
    for d in range(count):
        lo, hi = max(base, d * shard_rows), min(stop, (d + 1) * shard_rows)
        if hi <= lo:
            continue
        first = (lo - d * shard_rows) // 16 * 16
        last = min(padded, -(-(hi - d * shard_rows) // 16) * 16)
        plan.append((d, first, last))
    for n, (d, first, last) in enumerate(plan):
        slot = n % 2
        if n >= 2:
            e, f, g = plan[n - 2]
            pltpu.make_async_copy(stage.at[slot, pl.ds(f, g - f)], out_ref.at[e, pl.ds(f, g - f)], sems.at[slot]).wait()
        size = math.gcd(last - first, CHUNK)

        def narrow(m, _, d=d, first=first, size=size, slot=slot):
            src = d * shard_rows - base + first + m * size + 16
            stage[slot, pl.ds(pl.multiple_of(first + m * size, 16), size), :] = flat[pl.ds(src, size), :].astype(BF)
            return 0

        lax.fori_loop(0, (last - first) // size, narrow, 0)
        pltpu.make_async_copy(
            stage.at[slot, pl.ds(first, last - first)], out_ref.at[d, pl.ds(first, last - first)], sems.at[slot]
        ).start()
    for n in range(max(0, len(plan) - 2), len(plan)):
        e, f, g = plan[n]
        slot = n % 2
        pltpu.make_async_copy(stage.at[slot, pl.ds(f, g - f)], out_ref.at[e, pl.ds(f, g - f)], sems.at[slot]).wait()


def put_line(flat, first, src_ref, row):
    for j in range(src_ref.shape[1] // LANE):
        flat[first + j : first + j + 1, :] = src_ref[row : row + 1, j * LANE : (j + 1) * LANE]


def late_kernel(
    shard_rows, att, dbr, nbf, dinner, act, dffn, outb, dstu, vg, sg, gmid, gcls, out_ref, edge_ref, flat, turned, stage, sems
):
    first = lambda name: TABLE[name] - SPLIT + 16
    store_product(flat, first("w_out"), att, dbr, turned)
    store_product(flat, first("w_in"), nbf, dinner, turned)
    store_product(flat, first("w_back"), act, dffn, turned)
    for b in range(D // 256):
        turned[b * 256 : (b + 1) * 256, :] = outb[:, b * 256 : (b + 1) * 256].T
    flat[first("w_stu") : first("w_stu") + D, :] = dot(turned[...], dstu[...])
    for row, name in enumerate(("b_out", "gain_one", "shift_one", "b_back", "gain_two", "shift_two")):
        put_line(flat, first(name), vg, row)
    for q in range(4):
        put_line(flat, first("b_in") + q * (D // LANE), vg, 8 + q)
    put_line(flat, first("b_stu"), sg, 0)
    put_line(flat, first("pool_query"), sg, 1)
    put_line(flat, first("b_mid"), sg, 2)
    put_line(flat, first("b_cls"), sg, 3)
    flat[first("w_mid") : first("w_mid") + STU, :] = gmid[...]
    flat[first("w_cls") : first("w_cls") + CLASSES, :] = gcls[0:CLASSES, :]
    tail = USED - SPLIT + 16
    flat[tail:, :] = jnp.zeros((flat.shape[0] - tail, LANE), F32)
    flat[0:16, :] = jnp.zeros((16, LANE), F32)
    edge_ref[...] = flat[16:32, :]
    send_shards(flat, SPLIT, out_ref.shape[0] * shard_rows, shard_rows, out_ref, stage, sems)


def early_kernel(shard_rows, x, dproj, bg, edge, _, out_ref, flat, turned, stage, sems):
    store_product(flat, 16, x, dproj, turned)
    put_line(flat, 16 + TABLE["b_qv"], bg, 0)
    put_line(flat, 16 + TABLE["b_qv"] + D // LANE, bg, 1)
    flat[16 + SPLIT : 32 + SPLIT, :] = edge[...]
    send_shards(flat, 0, SPLIT, shard_rows, out_ref, stage, sems)


VM = pl.BlockSpec(memory_space=pltpu.VMEM)
ANY = pl.BlockSpec(memory_space=pl.ANY)


def late_grads(shard_rows, count, padded, *arrays):
    rows = count * shard_rows - SPLIT
    return pl.pallas_call(
        functools.partial(late_kernel, shard_rows),
        in_specs=[VM] * len(arrays),
        out_specs=[ANY, VM],
        out_shape=[SDS((count, padded, LANE), BF), SDS((16, LANE), F32)],
        scratch_shapes=[
            pltpu.VMEM((16 + rows + 48, LANE), F32),
            pltpu.VMEM((D, arrays[0].shape[0]), BF),
            pltpu.VMEM((2, padded, LANE), BF),
            pltpu.SemaphoreType.DMA((2,)),
        ],
        compiler_params=params_of(),
        name="late_grads",
    )(*arrays)


def early_grads(shard_rows, x, dproj, bg, edge, partial):
    count, padded, _ = partial.shape
    return pl.pallas_call(
        functools.partial(early_kernel, shard_rows),
        in_specs=[VM] * 4 + [ANY],
        out_specs=ANY,
        out_shape=SDS(partial.shape, BF),
        scratch_shapes=[
            pltpu.VMEM((16 + SPLIT + 48, LANE), F32),
            pltpu.VMEM((D, x.shape[0]), BF),
            pltpu.VMEM((2, padded, LANE), BF),
            pltpu.SemaphoreType.DMA((2,)),
        ],
        input_output_aliases={4: 0},
        compiler_params=params_of(),
        name="early_grads",
    )(x, dproj, bg, edge, partial)


def adam_update(first_part, second_part, grad_part):
    first_new = BETA_ONE * first_part + (1.0 - BETA_ONE) * grad_part
    second_new = BETA_TWO * second_part + (1.0 - BETA_TWO) * grad_part * grad_part
    step_dir = first_new / CORRECT_ONE / (jnp.sqrt(second_new / CORRECT_TWO) + ADAM_EPS)
    return (step_dir, first_new, second_new)


def shards(inputs, seg_ids, example_map, labels, out_cotangent, params, moment_one, moment_two):
    rows = inputs.shape[0]
    count = lax.axis_size("fsdp")
    shard_rows = params.shape[0] // LANE
    padded = -(-shard_rows // CHUNK) * CHUNK
    mine = jnp.pad(params.reshape(shard_rows, LANE).astype(BF), ((0, padded - shard_rows), (0, 0)))
    gathered = lax.all_gather(mine, "fsdp", axis=0, tiled=False)
    pick = example_map[:, :, None] == jnp.arange(EXR)[None, None, :]
    seg_label = jnp.sum(jnp.where(pick, labels[:, None, :], 0), axis=-1)
    hot = (seg_label[:, :, None] == jnp.arange(LANE)[None, None, :]).astype(F32)
    segc, segr = seg_ids[:, :, None], seg_ids[:, None, :]

    wqkv, bq, wout, win, wback, wstu, wmid, vec, small, wcls = unpack(gathered, shard_rows)
    wcls = jnp.pad(wcls[:CLASSES].reshape(STU, CLASSES), ((0, 0), (0, LANE - CLASSES)))
    qkv, probs, att = attend(inputs, segc, segr, wqkv, bq)
    out, logits, nbf, act, dffn, dinner, dstu, dh1, dbr, datt, vg, sg, gmid, gcls = middle(
        inputs, att, segc, hot, out_cotangent, wout, win, wback, wstu, wmid, vec, small, wcls
    )
    gcls = jnp.pad(gcls[:, :CLASSES].reshape(CLASSES, LANE), ((0, 2), (0, 0)))
    flat2 = lambda v: v.reshape(rows * LEN, v.shape[-1])
    partial, edge = late_grads(
        shard_rows,
        count,
        padded,
        flat2(att),
        flat2(dbr),
        flat2(nbf),
        flat2(dinner),
        flat2(act),
        flat2(dffn),
        flat2(out),
        flat2(dstu),
        vg,
        sg,
        gmid,
        gcls,
    )
    dproj, dx, bg = retreat(qkv, probs, datt, dh1, wqkv)
    grads = early_grads(shard_rows, flat2(inputs), flat2(dproj), bg, edge, partial)
    owned = lax.psum_scatter(grads, "fsdp", scatter_dimension=0, tiled=False)
    owned = lax.psum(owned, "rep")
    grad = owned[:shard_rows].astype(F32).reshape(-1)
    step_dir, first_new, second_new = adam_update(moment_one, moment_two, grad)
    return (out, logits, dx, step_dir, first_new, second_new)


def solution(mesh):
    rows = P(("rep", "fsdp"), None, None)
    flat_rows = P(("rep", "fsdp"), None)
    in_specs = (rows, flat_rows, flat_rows, flat_rows, rows, P("fsdp"), P("fsdp"), P("fsdp"))
    out_specs = (rows, rows, rows, P("fsdp"), P("fsdp"), P("fsdp"))
    return jax.shard_map(shards, mesh=mesh, in_specs=in_specs, out_specs=out_specs, check_vma=False)
```

profile of v0, /device:TPU:0, one launch (start us, length us, event | category | flops | bytes accessed | tf_op | source)
XLA Modules:
  0.0 491.2 jit_solution(6718889549191726132)
XLA Ops:
  7.2 0.0 all-gather.3.cloned.1.call-start
  7.2 2.2 convert_bitcast_fusion
  9.4 0.0 copy-start
  9.4 0.0 copy-start.1
  9.4 0.0 copy-start.2
  9.4 1.3 pad.12
  10.8 0.0 all-gather.3.cloned.1.call-update
  10.8 0.0 reduce-scatter.2.cloned.1.call-start
  10.9 0.0 copy-done
  10.9 0.6 broadcast_in_dim.24.segr_ref
  11.5 1.0 copy.17.segc_ref
  12.5 0.0 copy-done.1
  12.5 0.0 copy-done.2
  12.5 0.2 select_reduce_fusion
  12.7 0.7 fusion.2.hot_ref
  13.4 80.2 %all-gather.3.cloned.1.call-done = bf16[56320,128]{1,0:T(8,128)(2,1)} async-done(((bf16[7040,128]{1,0:T(8,128)(2,1)}), bf16[56320,128]{1,0:T(8,128)(2,1)}) %all-gather.3.cloned.1.call-update) | async-done | bytes 14417936 | tf_op jit(solution)/shard_map/all_gather | solution.py:745
  93.6 17.9 %unpack.1 = (bf16[768,2304]{1,0:T(8,128)(2,1)}, f32[8,2304]{1,0:T(8,128)}, bf16[768,768]{1,0:T(8,128)(2,1)}, bf16[768,3072]{1,0:T(8,128)(2,1)}, bf16[3072,768]{1...) custom-call(bf16[8,7040,128]{2,1,0:T(8,128)(2,1)} %bitcast.26), custom_call_target="tpu_custom_call" | custom-call | tf_op jit(solution)/shard_map/unpack/pallas_call | solution.py:165
  111.5 0.8 reshape.59
  112.3 0.6 pad.13.wcls
  112.9 32.9 %attend.1 = (bf16[2,512,2304]{2,1,0:T(8,128)(2,1)}, bf16[2,12,128,1280]{3,2,1,0:T(8,128)(2,1)}, bf16[2,512,768]{2,1,0:T(8,128)(2,1)}) custom-call(bf16[2,512,768]{2,1,0:T(8,128)(2,1)} %x_ref.3, s32[2,512,1]{2,1,0:T(8,128)} %copy.17.segc_ref, s32[2,1,512]{2,1,0:T(1,128)} %broadcast_in_dim.24.segr_ref, bf16[768,2304]{1,0:T(8,128)(2,1)} %get-tuple-element.38.w_ref, ...), custom_call_target="tpu_custom_call" | custom-call | tf_op jit(solution)/shard_map/attend/pallas_call | solution.py:223
  145.8 69.7 %middle.1 = (bf16[2,512,768]{2,1,0:T(8,128)(2,1)}, f32[2,8,14]{2,1,0:T(8,128)}, bf16[2,512,768]{2,1,0:T(8,128)(2,1)}, bf16[2,512,3072]{2,1,0:T(8,128)(2,1)}, bf1...) custom-call(bf16[2,512,768]{2,1,0:T(8,128)(2,1)} %x_ref.3, ...), custom_call_target="tpu_custom_call" | custom-call | tf_op jit(solution)/shard_map/middle/pallas_call | solution.py:463
  215.5 1.0 reshape.70
  216.5 0.6 pad.14.gcls
  217.1 36.1 %retreat.1 = (bf16[2,512,2304]{2,1,0:T(8,128)(2,1)}, bf16[2,512,768]{2,1,0:T(8,128)(2,1)}, f32[8,768]{1,0:T(8,128)}) custom-call(bf16[2,512,2304]{2,1,0:T(8,128)(2,1)} %get-tuple-element.51.qkv_ref, bf16[2,12,128,1280]{3,2,1,0:T(8,128)(2,1)} %get-tuple-element.52.p_ref, bf16[2,512,768]{2,1,0:T(8,128)(2,1)} %get-tuple-element.53.datt_ref, ...), custom_call_target="tpu_custom_call" | custom-call | tf_op jit(solution)/shard_map/retreat/pallas_call | solution.py:578
  253.2 32.3 %late_grads.1 = (bf16[8,7040,128]{2,1,0:T(8,128)(2,1)}, f32[16,128]{1,0:T(8,128)}) custom-call(bf16[1024,768]{1,0:T(8,128)(2,1)} %bitcast.28, bf16[1024,768]{1,0:T(8,128)(2,1)} %bitcast.36, bf16[1024,768]{1,0:T(8,128)(2,1)} %bitcast.34, bf16[1024,3072]{1,0:T(8,128)(2,1)} %bitcast.30, bf16[1024,3072]{1,0:T(8,128)(2,1)} %bitcast.29, ...), custom_call_target="tpu_custom_call" | custom-call | tf_op jit(solution)/shard_map/late_grads/pallas_call | solution.py:697
  285.5 10.7 %early_grads.1 = bf16[8,7040,128]{2,1,0:T(8,128)(2,1)} custom-call(bf16[1024,768]{1,0:T(8,128)(2,1)} %bitcast.27, bf16[1024,2304]{1,0:T(8,128)(2,1)} %bitcast.31, f32[8,768]{1,0:T(8,128)} %get-tuple-element.57.bg, f32[16,128]{1,0:T(8,128)} %get-tuple-element.68.edge, bf16[8,7040,128]{2,1,0:T(8,128)(2,1)} %get-tuple-element.69._), custom_call_target="tpu_custom_call", output_to_operand_aliasing={{}: (4, {})} | custom-call | tf_op jit(solution)/shard_map/early_grads/pallas_call | solution.py:715
  296.2 0.0 reduce-scatter.2.cloned.1.call-update
  296.2 0.0 all-reduce.5.cloned.1.call-start
  296.3 102.2 %reduce-scatter.2.cloned.1.call-done = bf16[1,7040,128]{2,1,0:T(8,128)(2,1)} async-done(((bf16[8,7040,128]{2,1,0:T(8,128)(2,1)}), bf16[1,7040,128]{2,1,0:T(8,128)(2,1)}) %reduce-scatter.2.cloned.1.call-update) | async-done | bytes 1802256 | tf_op jit(solution)/shard_map/reduce_scatter | solution.py:778
  398.5 0.0 all-reduce.5.cloned.1.call-update
  398.5 79.1 %all-reduce.5.cloned.1.call-done = bf16[7040,128]{1,0:T(8,128)(2,1)} async-done(((bf16[7040,128]{1,0:T(8,128)(2,1)}), bf16[7040,128]{1,0:T(8,128)(2,1)}) %all-reduce.5.cloned.1.call-update) | async-done | bytes 1802256 | tf_op jit(solution)/shard_map/psum | solution.py:779
  477.6 7.0 %add_divide_fusion = (f32[900608]{0:T(1024)}, f32[900608]{0:T(1024)}, f32[900608]{0:T(1024)}) fusion(bf16[7040,128]{1,0:T(8,128)(2,1)} %all-reduce.5.cloned.1.call-done, f32[900608]{0:T(1024)} %param.14, f32[900608]{0:T(1024)} %param.15), kind=kLoop, calls=%fused_computation.5 | loop fusion | flops 10807296 | bytes 19813376 | tf_op jit(solution)/shard_map/div | solution.py:735
Async XLA Ops:
  7.2 86.4 %all-gather.3.cloned.1.call-start = ((), (), s32[]{:S(2)}) async-start(), calls=%async_computation.3 | async-start | bytes 16220160 | tf_op jit(solution)/shard_map/all_gather | solution.py:745
  9.4 1.5 copy-start
  9.4 3.1 copy-start.1
  9.4 3.1 copy-start.2
  10.8 387.7 %reduce-scatter.2.cloned.1.call-start = ((), (), s32[]{:S(2)}) async-start(), calls=%async_computation.1 | async-start | bytes 16220160 | tf_op jit(solution)/shard_map/reduce_scatter | solution.py:778
  296.2 181.4 %all-reduce.5.cloned.1.call-start = ((), (), s32[]{:S(2)}) async-start(), calls=%async_computation.2 | async-start | bytes 3604480 | tf_op jit(solution)/shard_map/psum | solution.py:779
Sparse Core Ops, SparseCore 0:
  10.9 82.5 all-gather.2
  296.3 102.1 reduce-scatter.1
  401.0 76.5 all-reduce.4
where the time goes:
time: 492 us; the launch traced here: 491 us
  waiting for transfers between devices  262 us (53%)
  Pallas kernels  200 us (41%)
  between operations  13.8 us (3%)
  other arithmetic  10.1 us (2%)
  local copies, waits for them, and re-layouts  6.02 us (1%)
    reduce_scatter x1, waiting for transfers between devices, shards(): owned = lax.psum_scatter(grads, 'fsdp', scatter_dimension=0, tiled=False)  102 us
    all_gather x1, waiting for transfers between devices, shards(): gathered = lax.all_gather(mine, 'fsdp', axis=0, tiled=False)  80.2 us
    psum x1, waiting for transfers between devices, shards(): owned = lax.psum(owned, 'rep')  79.1 us
    pallas_call x1, Pallas kernels, middle(): pl.pallas_call(middle_kernel, grid=(rows,), in_specs=[row_spec(LEN, D), r...  69.7 us
    pallas_call x1, Pallas kernels, retreat(): pl.pallas_call(retreat_kernel, grid=(rows,), in_specs=[row_spec(LEN, 3 *...  36.1 us
    pallas_call x1, Pallas kernels, attend(): pl.pallas_call(attend_kernel, grid=(rows,), in_specs=[row_spec(LEN, D), r...  32.9 us
    pallas_call x1, Pallas kernels, late_grads(): pl.pallas_call(functools.partial(late_kernel, shard_rows), in_specs=[VM]...  32.3 us
    pallas_call x1, Pallas kernels, unpack(): pl.pallas_call(functools.partial(unpack_kernel, shard_rows, count), grid=...  17.9 us
  transfers between devices with their start and end apart: 3, of which 3 were waited for; matrix products, arithmetic and copies ran while one was open for 1% of the time, Pallas kernels for 0%

commit v1 on v0

--- a/solution.py
+++ b/solution.py
@@ -66,6 +66,9 @@
 USED = _row
 SPLIT = TABLE["w_out"]
 
+VM = pl.BlockSpec(memory_space=pltpu.VMEM)
+ANY = pl.BlockSpec(memory_space=pl.ANY)
+
 NN = (((1,), (0,)), ((), ()))
 NT = (((1,), (1,)), ((), ()))
 TN = (((0,), (0,)), ((), ()))
@@ -87,7 +90,68 @@
     return pl.ds(pl.multiple_of(i * n, n), n)
 
 
-def unpack_kernel(shard_rows, count, g_ref, wqkv, bq, wout, win, wback, wstu, wmid, vec, small, wcls, flat):
+def put_matrix(out, flat, first, rows):
+    tall, broad = out.shape
+    cols = broad // LANE
+
+    def some(k, _):
+        for j in range(cols):
+            out[at(k, rows), j * LANE : (j + 1) * LANE] = flat[
+                pl.ds(first + k * (rows * cols) + j, rows, stride=cols), :
+            ].astype(BF)
+        return 0
+
+    lax.fori_loop(0, tall // rows, some, 0)
+
+
+def put_row(out, row, flat, first, blocks, start=0):
+    for j in range(blocks):
+        out[row : row + 1, start + j * LANE : start + (j + 1) * LANE] = flat[first + j : first + j + 1, :]
+
+
+def put_first(flat, wqkv, bq):
+    put_matrix(wqkv, flat, TABLE["w_qkv"], 32)
+    wide = lax.broadcasted_iota(jnp.int32, (1, 3 * D), 1)
+    bq[0:1, :] = jnp.zeros((1, 3 * D), F32)
+    bq[1:2, :] = jnp.where(wide < D, 0.125, 1.0).astype(F32)
+    put_row(bq, 0, flat, TABLE["b_qv"], D // LANE)
+    put_row(bq, 0, flat, TABLE["b_qv"] + D // LANE, D // LANE, 2 * D)
+
+
+def put_rest(flat, wout, win, wback, wstu, wmid, vec, small, wcls):
+    put_matrix(wout, flat, TABLE["w_out"], 64)
+    put_matrix(win, flat, TABLE["w_in"], 32)
+    put_matrix(wback, flat, TABLE["w_back"], 64)
+    wstu[...] = flat[TABLE["w_stu"] : TABLE["w_stu"] + D, :].astype(BF)
+    wmid[...] = flat[TABLE["w_mid"] : TABLE["w_mid"] + STU, :]
+    wcls[...] = flat[TABLE["w_cls"] : TABLE["w_cls"] + 16, :]
+    nb = D // LANE
+    for row, name in enumerate(("b_out", "gain_one", "shift_one", "b_back", "gain_two", "shift_two")):
+        put_row(vec, row, flat, TABLE[name], nb)
+    for q in range(4):
+        put_row(vec, 8 + q, flat, TABLE["b_in"] + q * nb, nb)
+    put_row(small, 0, flat, TABLE["b_stu"], 1)
+    put_row(small, 1, flat, TABLE["pool_query"], 1)
+    put_row(small, 2, flat, TABLE["b_mid"], 1)
+    lane = lax.broadcasted_iota(jnp.int32, (1, LANE), 1)
+    small[3:4, :] = jnp.where(lane < CLASSES, flat[TABLE["b_cls"] : TABLE["b_cls"] + 1, :], 0.0)
+
+
+FIRST = (SDS((D, 3 * D), BF), SDS((8, 3 * D), F32))
+REST = (
+    SDS((D, D), BF),
+    SDS((D, FF), BF),
+    SDS((FF, D), BF),
+    SDS((D, STU), BF),
+    SDS((STU, STU), F32),
+    SDS((16, D), F32),
+    SDS((8, LANE), F32),
+    SDS((16, LANE), F32),
+)
+
+
+def unpack_kernel(shard_rows, count, g_ref, wqkv, bq, *rest):
+    *outs, flat = rest
     d = pl.program_id(0)
     padded = g_ref.shape[1]
 
@@ -99,69 +163,13 @@
 
     @pl.when(d == count - 1)
     def _():
-        def matrix(out, name, rows):
-            tall, broad = out.shape
-            cols = broad // LANE
-
-            def some(k, _):
-                for j in range(cols):
-                    out[at(k, rows), j * LANE : (j + 1) * LANE] = flat[
-                        pl.ds(TABLE[name] + k * (rows * cols) + j, rows, stride=cols), :
-                    ].astype(BF)
-                return 0
-
-            lax.fori_loop(0, tall // rows, some, 0)
-
-        matrix(wqkv, "w_qkv", 32)
-        matrix(wout, "w_out", 64)
-        matrix(win, "w_in", 32)
-        matrix(wback, "w_back", 64)
-
-        def line(out, row, name, blocks, skip=0):
-            first = TABLE[name] + skip
-            for j in range(blocks):
-                out[row : row + 1, j * LANE : (j + 1) * LANE] = flat[first + j : first + j + 1, :]
-
-        wstu[...] = flat[TABLE["w_stu"] : TABLE["w_stu"] + D, :].astype(BF)
-        wmid[...] = flat[TABLE["w_mid"] : TABLE["w_mid"] + STU, :]
-        wcls[...] = flat[TABLE["w_cls"] : TABLE["w_cls"] + 16, :]
-        nb = D // LANE
-        line(vec, 0, "b_out", nb)
-        line(vec, 1, "gain_one", nb)
-        line(vec, 2, "shift_one", nb)
-        line(vec, 3, "b_back", nb)
-        line(vec, 4, "gain_two", nb)
-        line(vec, 5, "shift_two", nb)
-        for q in range(4):
-            line(vec, 8 + q, "b_in", nb, q * nb)
-        line(small, 0, "b_stu", 1)
-        line(small, 1, "pool_query", 1)
-        line(small, 2, "b_mid", 1)
-        lane = lax.broadcasted_iota(jnp.int32, (1, LANE), 1)
-        small[3:4, :] = jnp.where(lane < CLASSES, flat[TABLE["b_cls"] : TABLE["b_cls"] + 1, :], 0.0)
-        wide = lax.broadcasted_iota(jnp.int32, (1, 3 * D), 1)
-        bq[0:1, :] = jnp.zeros((1, 3 * D), F32)
-        bq[1:2, :] = jnp.where(wide < D, 0.125, 1.0).astype(F32)
-        for j in range(nb):
-            first = TABLE["b_qv"]
-            bq[0:1, j * LANE : (j + 1) * LANE] = flat[first + j : first + j + 1, :]
-            bq[0:1, 2 * D + j * LANE : 2 * D + (j + 1) * LANE] = flat[first + nb + j : first + nb + j + 1, :]
+        put_first(flat, wqkv, bq)
+        put_rest(flat, *outs)
 
 
 def unpack(gathered, shard_rows):
     count, padded, _ = gathered.shape
-    outs = (
-        SDS((D, 3 * D), BF),
-        SDS((8, 3 * D), F32),
-        SDS((D, D), BF),
-        SDS((D, FF), BF),
-        SDS((FF, D), BF),
-        SDS((D, STU), BF),
-        SDS((STU, STU), F32),
-        SDS((16, D), F32),
-        SDS((8, LANE), F32),
-        SDS((16, LANE), F32),
-    )
+    outs = FIRST + REST
     return pl.pallas_call(
         functools.partial(unpack_kernel, shard_rows, count),
         grid=(count,),
@@ -172,6 +180,134 @@
         compiler_params=params_of(),
         name="unpack",
     )(gathered)
+
+
+def swap(v, bit):
+    return lax.ppermute(v, "fsdp", [(d, d ^ bit) for d in range(8)])
+
+
+def widen_half(flat, place, src, half, shard_rows):
+    n = src.shape[0]
+    real = min(n, shard_rows - half * n)
+
+    def widen(m, _):
+        flat[pl.ds(place + half * n + m * CHUNK, CHUNK), :] = src[at(m, CHUNK), :].astype(F32)
+        return 0
+
+    lax.fori_loop(0, real // CHUNK, widen, 0)
+    done = real // CHUNK * CHUNK
+    if done < real:
+        flat[pl.ds(place + half * n + done, real - done), :] = src[done : done + CHUNK, :].astype(F32)[: real - done]
+
+
+def unpack_first_kernel(shard_rows, me_ref, *rest):
+    pieces, (wqkv, bq, flat, buf, sems) = rest[:12], rest[12:]
+    chip, core = me_ref[0] >> 1, me_ref[0] & 1
+    picks = []
+    for side in range(2):
+        for half in range(2):
+            slot = side * 2 + half
+            a, b, c = (pieces[side * 6 + kind * 2 + half] for kind in range(3))
+            through = 1 + half
+            for when, src in (
+                (chip == 0, a),
+                (chip == through, b),
+                ((chip != 0) & (chip != through), c),
+            ):
+
+                @pl.when(when)
+                def _(src=src, slot=slot):
+                    pltpu.make_async_copy(src, buf.at[slot], sems.at[slot]).start()
+
+            picks.append((side, half, slot))
+    for side, half, slot in picks:
+        pltpu.make_async_copy(pieces[0], buf.at[slot], sems.at[slot]).wait()
+        place = (core ^ side) * shard_rows
+        widen_half(flat, place, buf.at[slot], half, shard_rows)
+    put_first(flat, wqkv, bq)
+
+
+SM = pl.BlockSpec(memory_space=pltpu.SMEM)
+
+
+def unpack_first(me, shard_rows, *pieces):
+    n = pieces[0].shape[0]
+    return pl.pallas_call(
+        functools.partial(unpack_first_kernel, shard_rows),
+        in_specs=[SM] + [ANY] * len(pieces),
+        out_specs=[VM] * 2,
+        out_shape=FIRST,
+        scratch_shapes=[
+            pltpu.VMEM((2 * shard_rows + 16, LANE), F32),
+            pltpu.VMEM((4, n, LANE), BF),
+            pltpu.SemaphoreType.DMA((4,)),
+        ],
+        compiler_params=params_of(),
+        cost_estimate=pl.CostEstimate(flops=0, bytes_accessed=20 << 20, transcendentals=0),
+        name="unpack_first",
+    )(me, *pieces)
+
+
+def unpack_rest_kernel(shard_rows, owner_ref, *rest):
+    pieces, (*outs, flat, buf, sems) = rest[:16], rest[16:]
+    plan = [(src, n % 2, owner_ref[n % 8] ^ (n // 8)) for n, src in enumerate(pieces)]
+
+    def copy(n):
+        return pltpu.make_async_copy(plan[n][0], buf.at[n % 4], sems.at[n % 4])
+
+    for n in range(3):
+        copy(n).start()
+    for n in range(len(plan)):
+        if n + 3 < len(plan):
+            copy(n + 3).start()
+        copy(n).wait()
+        _, half, owner = plan[n]
+        widen_half(flat, owner * shard_rows, buf.at[n % 4], half, shard_rows)
+    put_rest(flat, *outs)
+
+
+def unpack_rest(owners, shard_rows, *pieces):
+    n = pieces[0].shape[0]
+    return pl.pallas_call(
+        functools.partial(unpack_rest_kernel, shard_rows),
+        in_specs=[SM] + [ANY] * len(pieces),
+        out_specs=[VM] * len(REST),
+        out_shape=REST,
+        scratch_shapes=[
+            pltpu.VMEM((8 * shard_rows + 16, LANE), F32),
+            pltpu.VMEM((4, n, LANE), BF),
+            pltpu.SemaphoreType.DMA((4,)),
+        ],
+        compiler_params=params_of(),
+        cost_estimate=pl.CostEstimate(flops=0, bytes_accessed=60 << 20, transcendentals=0),
+        name="unpack_rest",
+    )(owners, *pieces)
+
+
+def exchange_weights(params, shard_rows, padded):
+    me = lax.axis_index("fsdp")
+    x, y = (me >> 1) & 1, me >> 2
+    half = padded // 2
+    mine = params.reshape(shard_rows, LANE)
+    own_b = jnp.pad(mine[half:].astype(BF), ((0, padded - shard_rows), (0, 0)))
+    own = lax.optimization_barrier((mine[:half].astype(BF), own_b))
+    near = (swap(own[0], 2), swap(own[1], 4))
+    far = (swap(jnp.where(x == 1, near[0], own[0]), 4), swap(jnp.where(y == 1, near[1], own[1]), 2))
+    last = (swap(jnp.where(x == 1, own[0], near[0]), 4), swap(jnp.where(y == 1, own[1], near[1]), 2))
+    early = own + near + far
+    early_c = tuple(swap(v, 1) for v in early)
+    first = unpack_first(me.reshape(1), shard_rows, *early, *early_c)
+
+    def finish(after):
+        late, _ = lax.optimization_barrier((last, after))
+        late_c = tuple(swap(v, 1) for v in late)
+        bits = jnp.array([0, 0, 2, 4, 4, 2, 6, 6], jnp.int32)
+        turned = jnp.array([0, 0, 2, 4, 6, 6, 4, 2], jnp.int32)
+        swapped = jnp.array([0, 0, 0, 0, 1, 0, 1, 0], jnp.int32) * x + jnp.array([0, 0, 0, 0, 0, 1, 0, 1], jnp.int32) * y
+        owners = me ^ jnp.where(swapped == 1, turned, bits)
+        return unpack_rest(owners, shard_rows, *early, *late, *early_c, *late_c)
+
+    return first, finish
 
 
 def half_masks():
@@ -218,18 +354,26 @@
     return pl.BlockSpec((1, *shape), lambda r: (r,) + (0,) * len(shape))
 
 
-def attend(x, segc, segr, wqkv, bq):
+def attend(row, x, segc, segr, wqkv, bq, done):
     rows = x.shape[0]
+    only = lambda *shape: pl.BlockSpec((1, *shape), lambda _: (row,) + (0,) * len(shape))
+    outs = [SDS((rows, LEN, 3 * D), BF), SDS((rows, HEADS, QB, WIDE), BF), SDS((rows, LEN, D), BF)]
+
+    def kernel(*refs):
+        attend_kernel(*refs[:5], *refs[5 + len(done) :])
+
     return pl.pallas_call(
-        attend_kernel,
-        grid=(rows,),
-        in_specs=[row_spec(LEN, D), row_spec(LEN, 1), row_spec(1, LEN), whole(D, 3 * D), whole(8, 3 * D)],
-        out_specs=[row_spec(LEN, 3 * D), row_spec(HEADS, QB, WIDE), row_spec(LEN, D)],
-        out_shape=[SDS((rows, LEN, 3 * D), BF), SDS((rows, HEADS, QB, WIDE), BF), SDS((rows, LEN, D), BF)],
+        kernel,
+        grid=(1,),
+        in_specs=[only(LEN, D), only(LEN, 1), only(1, LEN), VM, VM] + [ANY] * len(done),
+        out_specs=[only(LEN, 3 * D), only(HEADS, QB, WIDE), only(LEN, D)],
+        out_shape=outs,
         scratch_shapes=[pltpu.VMEM((QB, WIDE), F32)],
+        input_output_aliases={5 + i: i for i in range(len(done))},
         compiler_params=params_of(),
+        cost_estimate=pl.CostEstimate(flops=6 * 10**9, bytes_accessed=12 << 20, transcendentals=4 * 10**6),
         name="attend",
-    )(x, segc, segr, wqkv, bq)
+    )(x, segc, segr, wqkv, bq, *done)
 
 
 TB = 64
@@ -688,10 +832,6 @@
     send_shards(flat, 0, SPLIT, shard_rows, out_ref, stage, sems)
 
 
-VM = pl.BlockSpec(memory_space=pltpu.VMEM)
-ANY = pl.BlockSpec(memory_space=pl.ANY)
-
-
 def late_grads(shard_rows, count, padded, *arrays):
     rows = count * shard_rows - SPLIT
     return pl.pallas_call(
@@ -741,16 +881,26 @@
     count = lax.axis_size("fsdp")
     shard_rows = params.shape[0] // LANE
     padded = -(-shard_rows // CHUNK) * CHUNK
-    mine = jnp.pad(params.reshape(shard_rows, LANE).astype(BF), ((0, padded - shard_rows), (0, 0)))
-    gathered = lax.all_gather(mine, "fsdp", axis=0, tiled=False)
     pick = example_map[:, :, None] == jnp.arange(EXR)[None, None, :]
     seg_label = jnp.sum(jnp.where(pick, labels[:, None, :], 0), axis=-1)
     hot = (seg_label[:, :, None] == jnp.arange(LANE)[None, None, :]).astype(F32)
     segc, segr = seg_ids[:, :, None], seg_ids[:, None, :]
 
-    wqkv, bq, wout, win, wback, wstu, wmid, vec, small, wcls = unpack(gathered, shard_rows)
+    if count == 8:
+        first, finish = exchange_weights(params, shard_rows, padded)
+    else:
+        mine = jnp.pad(params.reshape(shard_rows, LANE).astype(BF), ((0, padded - shard_rows), (0, 0)))
+        both = unpack(lax.all_gather(mine, "fsdp", axis=0, tiled=False), shard_rows)
+        first, finish = both[:2], lambda after: both[2:]
+    wqkv, bq = first
+    done = ()
+    for row in range(rows):
+        done = attend(row, inputs, segc, segr, wqkv, bq, done)
+        if row == 0:
+            rest = finish(done[2])
+    qkv, probs, att = done
+    wout, win, wback, wstu, wmid, vec, small, wcls = rest
     wcls = jnp.pad(wcls[:CLASSES].reshape(STU, CLASSES), ((0, 0), (0, LANE - CLASSES)))
-    qkv, probs, att = attend(inputs, segc, segr, wqkv, bq)
     out, logits, nbf, act, dffn, dinner, dstu, dh1, dbr, datt, vg, sg, gmid, gcls = middle(
         inputs, att, segc, hot, out_cotangent, wout, win, wback, wstu, wmid, vec, small, wcls
     )

time: 492 us -> 472 us (0.959)
  waiting for transfers between devices: 262 us -> 219 us
  starting transfers between devices: 0.12 us -> 11 us
    all_gather x1 -> x0, waiting for transfers between devices: 80.2 us -> none  [shards(): gathered = lax.all_gather(mine, 'fsdp', axis=0, tiled=False)]
    ppermute x0 -> x14, waiting for transfers between devices: none -> 37.7 us  [swap(): return lax.ppermute(v, 'fsdp', [(d, d ^ bit) for d in range(8)])]
    ppermute x0 -> x14, starting transfers between devices: none -> 10.9 us  [swap(): return lax.ppermute(v, 'fsdp', [(d, d ^ bit) for d in range(8)])]
    pallas_call x2 -> x4, Pallas kernels: 50.8 us -> 55.8 us  [the longest x2 36.2 us: attend(): pl.pallas_call(kernel, grid=(1,), in_specs=[only(LEN, D), only(LEN, 1), o...]
  transfers between devices with their start and end apart: 3 -> 16, of which waited for: 3 -> 5; matrix products, arithmetic and copies ran while one was open for 1% -> 1% of each run, Pallas kernels for 0% -> 9%
where the time goes in v1:
time: 472 us
  waiting for transfers between devices  219 us (46%)
  Pallas kernels  204 us (43%)
  between operations  14.2 us (3%)
  other arithmetic  14.1 us (3%)
  starting transfers between devices  11 us (2%)
  local copies, waits for them, and re-layouts  8.73 us (2%)
    reduce_scatter x1, waiting for transfers between devices, shards(): owned = lax.psum_scatter(grads, 'fsdp', scatter_dimension=0, tiled=False)  103 us
    psum x1, waiting for transfers between devices, shards(): owned = lax.psum(owned, 'rep')  79.1 us
    pallas_call x1, Pallas kernels, middle(): pl.pallas_call(middle_kernel, grid=(rows,), in_specs=[row_spec(LEN, D), r...  69.7 us
    ppermute x14, waiting for transfers between devices, swap(): return lax.ppermute(v, 'fsdp', [(d, d ^ bit) for d in range(8)])  37.7 us
    pallas_call x2, Pallas kernels, attend(): pl.pallas_call(kernel, grid=(1,), in_specs=[only(LEN, D), only(LEN, 1), o...  36.2 us
    pallas_call x1, Pallas kernels, retreat(): pl.pallas_call(retreat_kernel, grid=(rows,), in_specs=[row_spec(LEN, 3 *...  36.1 us
    pallas_call x1, Pallas kernels, late_grads(): pl.pallas_call(functools.partial(late_kernel, shard_rows), in_specs=[VM]...  32.2 us
    pallas_call x1, Pallas kernels, unpack_rest(): pl.pallas_call(functools.partial(unpack_rest_kernel, shard_rows), in_spec...  14.8 us
  transfers between devices with their start and end apart: 16, of which 5 were waited for; matrix products, arithmetic and copies ran while one was open for 1% of the time, Pallas kernels for 9%

profile of v1, /device:TPU:0, one launch (start us, length us, event | category | flops | bytes accessed | tf_op | source)
XLA Modules:
  0.0 472.0 jit_solution(13295297119923745026)
XLA Ops:
  7.2 0.0 reduce-scatter.2.cloned.1.call-start
  7.2 2.2 convert.5
  9.4 0.1 slice_bitcast_fusion.1
  9.5 0.1 slice_bitcast_fusion.2.rest_0_
  9.6 0.1 pad.12.rest_1_
  9.6 3.0 collective-permute-start.1
  12.7 1.5 collective-permute-start
  14.2 18.5 %collective-permute-done.1.rest_3_ = bf16[3520,128]{1,0:T(8,128)(2,1)S(1)} collective-permute-done((bf16[3520,128]{1,0:T(8,128)(2,1)S(1)}, bf16[3520,128]{1,0:T(8,128)(2,1)S(1)}, u32[]{:S(2)}, u32[]{:S(2)}) %collective-permute-start.1) | collective-permute-done | bytes 901152 | tf_op jit(solution)/shard_map/ppermute | solution.py:186
  32.7 1.2 broadcast_select_fusion
  33.9 1.7 collective-permute-start.3
  35.6 2.2 broadcast_select_fusion.2
  37.8 1.5 collective-permute-start.2
  39.3 0.5 collective-permute-start.6
  39.9 0.1 collective-permute-start.7
  39.9 15.4 %collective-permute-done.3.rest_5_ = bf16[3520,128]{1,0:T(8,128)(2,1)} collective-permute-done((bf16[3520,128]{1,0:T(8,128)(2,1)S(1)}, bf16[3520,128]{1,0:T(8,128)(2,1)}, u32[]{:S(2)}, u32[]{:S(2)}) %collective-permute-start.3) | collective-permute-done | bytes 901152 | tf_op jit(solution)/shard_map/ppermute | solution.py:186
  55.3 3.8 collective-permute-done.2.rest_4_
  59.2 1.0 copy-done.3
  60.1 1.5 collective-permute-start.11
  61.6 0.5 collective-permute-start.10
  62.1 0.6 broadcast_in_dim.24.refs_2_
  62.7 1.1 copy.26.refs_1_.segc_ref
  63.8 0.9 copy-done.4
  64.7 4.8 %unpack_first.1 = (bf16[768,2304]{1,0:T(8,128)(2,1)}, f32[8,2304]{1,0:T(8,128)}) custom-call(s32[1]{0:T(128)} %bitcast.1.me_ref, bf16[3520,128]{1,0:T(8,128)(2,1)} %copy-done, bf16[3520,128]{1,0:T(8,128)(2,1)} %copy-done.1, bf16[3520,128]{1,0:T(8,128)(2,1)} %collective-permute-done.rest_2_, bf16[3520,128]{1,0:T(8,128)(2,1)} %copy-done.2, ...), custom_call_target="tpu_custom_call" | custom-call | bytes 20971520 | tf_op jit(solution)/shard_map/unpack_first/pallas_call | solution.py:235
  69.5 0.0 copy-start.12
  69.6 18.1 %attend.2 = (bf16[2,512,2304]{2,1,0:T(8,128)(2,1)}, bf16[2,12,128,1280]{3,2,1,0:T(8,128)(2,1)}, bf16[2,512,768]{2,1,0:T(8,128)(2,1)}) custom-call(bf16[2,512,768]{2,1,0:T(8,128)(2,1)} %x_ref.1, s32[2,512,1]{2,1,0:T(8,128)} %copy.26.refs_1_.segc_ref, s32[2,1,512]{2,1,0:T(1,128)} %broadcast_in_dim.24.refs_2_, ...), custom_call_target="tpu_custom_call" | custom-call | flops 6000000000 | bytes 12582912 | tf_op jit(solution)/shard_map/attend/pallas_call | solution.py:365
  87.7 0.1 collective-permute-start.12
  87.8 0.5 collective-permute-start.13
  88.3 0.5 fusion.3.owner_ref
  88.8 0.2 select_reduce_fusion
  89.0 0.7 fusion.2.hot_ref
  89.7 18.1 %attend.3 = (bf16[2,512,2304]{2,1,0:T(8,128)(2,1)}, bf16[2,12,128,1280]{3,2,1,0:T(8,128)(2,1)}, bf16[2,512,768]{2,1,0:T(8,128)(2,1)}) custom-call(bf16[2,512,768]{2,1,0:T(8,128)(2,1)} %x_ref.1, s32[2,512,1]{2,1,0:T(8,128)} %copy.26.refs_1_.segc_ref, ...), custom_call_target="tpu_custom_call", output_to_operand_aliasing={{0}: (5, {}), {1}: (6, {}), {2}: (7, {})} | custom-call | flops 6000000000 | bytes 12582912 | tf_op jit(solution)/shard_map/attend/pallas_call | solution.py:365
  107.8 0.9 copy-done.6
  108.8 1.0 copy-done.7
  109.7 14.8 %unpack_rest.1 = (bf16[768,768]{1,0:T(8,128)(2,1)}, bf16[768,3072]{1,0:T(8,128)(2,1)}, bf16[3072,768]{1,0:T(8,128)(2,1)}, bf16[768,128]{1,0:T(8,128)(2,1)}, f32[...) custom-call(s32[8]{0:T(128)} %fusion.3.owner_ref, bf16[3520,128]{1,0:T(8,128)(2,1)} %copy-done, ...), custom_call_target="tpu_custom_call" | custom-call | bytes 62914560 | tf_op jit(solution)/shard_map/unpack_rest/pallas_call | solution.py:271
  124.6 0.8 reshape.82
  125.4 0.6 pad.13.wcls
  126.1 69.7 %middle.1 = (bf16[2,512,768]{2,1,0:T(8,128)(2,1)}, f32[2,8,14]{2,1,0:T(8,128)}, bf16[2,512,768]{2,1,0:T(8,128)(2,1)}, bf16[2,512,3072]{2,1,0:T(8,128)(2,1)}, bf1...) custom-call(bf16[2,512,768]{2,1,0:T(8,128)(2,1)} %x_ref.1, ...), custom_call_target="tpu_custom_call" | custom-call | tf_op jit(solution)/shard_map/middle/pallas_call | solution.py:607
  195.7 1.0 reshape.93
  196.7 0.6 pad.14.gcls
  197.3 36.1 %retreat.1 = (bf16[2,512,2304]{2,1,0:T(8,128)(2,1)}, bf16[2,512,768]{2,1,0:T(8,128)(2,1)}, f32[8,768]{1,0:T(8,128)}) custom-call(bf16[2,512,2304]{2,1,0:T(8,128)(2,1)} %get-tuple-element.65.qkv_ref, bf16[2,12,128,1280]{3,2,1,0:T(8,128)(2,1)} %get-tuple-element.66.p_ref, bf16[2,512,768]{2,1,0:T(8,128)(2,1)} %get-tuple-element.67.datt_ref, ...), custom_call_target="tpu_custom_call" | custom-call | tf_op jit(solution)/shard_map/retreat/pallas_call | solution.py:722
  233.4 32.2 %late_grads.1 = (bf16[8,7040,128]{2,1,0:T(8,128)(2,1)}, f32[16,128]{1,0:T(8,128)}) custom-call(bf16[1024,768]{1,0:T(8,128)(2,1)} %bitcast.29, bf16[1024,768]{1,0:T(8,128)(2,1)} %bitcast.37, bf16[1024,768]{1,0:T(8,128)(2,1)} %bitcast.35, bf16[1024,3072]{1,0:T(8,128)(2,1)} %bitcast.31, bf16[1024,3072]{1,0:T(8,128)(2,1)} %bitcast.30, ...), custom_call_target="tpu_custom_call" | custom-call | tf_op jit(solution)/shard_map/late_grads/pallas_call | solution.py:837
  265.6 10.7 %early_grads.1 = bf16[8,7040,128]{2,1,0:T(8,128)(2,1)} custom-call(bf16[1024,768]{1,0:T(8,128)(2,1)} %bitcast.28, bf16[1024,2304]{1,0:T(8,128)(2,1)} %bitcast.32, f32[8,768]{1,0:T(8,128)} %get-tuple-element.71.bg, f32[16,128]{1,0:T(8,128)} %get-tuple-element.82.edge, bf16[8,7040,128]{2,1,0:T(8,128)(2,1)} %get-tuple-element.83._), custom_call_target="tpu_custom_call", output_to_operand_aliasing={{}: (4, {})} | custom-call | tf_op jit(solution)/shard_map/early_grads/pallas_call | solution.py:855
  276.3 0.0 reduce-scatter.2.cloned.1.call-update
  276.3 0.0 all-reduce.5.cloned.1.call-start
  276.4 102.6 %reduce-scatter.2.cloned.1.call-done = bf16[1,7040,128]{2,1,0:T(8,128)(2,1)} async-done(((bf16[8,7040,128]{2,1,0:T(8,128)(2,1)}), bf16[1,7040,128]{2,1,0:T(8,128)(2,1)}) %reduce-scatter.2.cloned.1.call-update) | async-done | bytes 1802256 | tf_op jit(solution)/shard_map/reduce_scatter | solution.py:928
  378.9 0.0 all-reduce.5.cloned.1.call-update
  379.0 79.1 %all-reduce.5.cloned.1.call-done = bf16[7040,128]{1,0:T(8,128)(2,1)} async-done(((bf16[7040,128]{1,0:T(8,128)(2,1)}), bf16[7040,128]{1,0:T(8,128)(2,1)}) %all-reduce.5.cloned.1.call-update) | async-done | bytes 1802256 | tf_op jit(solution)/shard_map/psum | solution.py:929
  458.1 7.0 %add_divide_fusion = (f32[900608]{0:T(1024)}, f32[900608]{0:T(1024)}, f32[900608]{0:T(1024)}) fusion(bf16[7040,128]{1,0:T(8,128)(2,1)} %all-reduce.5.cloned.1.call-done, f32[900608]{0:T(1024)} %param.18, f32[900608]{0:T(1024)} %param.19), kind=kLoop, calls=%fused_computation.5 | loop fusion | flops 10807296 | bytes 19813376 | tf_op jit(solution)/shard_map/div | solution.py:875
  (40 shorter events, 0.1 us)
Async XLA Ops:
  7.2 371.8 %reduce-scatter.2.cloned.1.call-start = ((), (), s32[]{:S(2)}) async-start(), calls=%async_computation.1 | async-start | bytes 16220160 | tf_op jit(solution)/shard_map/reduce_scatter | solution.py:928
  9.5 28.3 %copy-start = (bf16[3520,128]{1,0:T(8,128)(2,1)}, bf16[3520,128]{1,0:T(8,128)(2,1)S(1)}, u32[]{:S(2)}) copy-start(bf16[3520,128]{1,0:T(8,128)(2,1)S(1)} %slice_bitcast_fusion.2.rest_0_) | copy-start | bytes 2703364
  9.6 29.7 %copy-start.1 = (bf16[3520,128]{1,0:T(8,128)(2,1)}, bf16[3520,128]{1,0:T(8,128)(2,1)S(1)}, u32[]{:S(2)}) copy-start(bf16[3520,128]{1,0:T(8,128)(2,1)S(1)} %pad.12.rest_1_) | copy-start | bytes 2703364
  9.6 23.0 %collective-permute-start.1 = (bf16[3520,128]{1,0:T(8,128)(2,1)S(1)}, bf16[3520,128]{1,0:T(8,128)(2,1)S(1)}, u32[]{:S(2)}, u32[]{:S(2)}) collective-permute-start(bf16[3520,128]{1,0:T(8,128)(2,1)S(1)} %pad.12.rest_1_), channel_id=1, source_target_pairs={{0,4},{1,5},{2,6},{3,7},{4,0},{5,1},{6,2},{7,3},{8,12},{9,13},{10,... | collective-permute-start | bytes 2703368 | tf_op jit(solution)/shard_map/ppermute | solution.py:186
  12.7 27.2 %collective-permute-start.4 = (bf16[3520,128]{1,0:T(8,128)(2,1)S(1)}, bf16[3520,128]{1,0:T(8,128)(2,1)}, u32[]{:S(2)}, u32[]{:S(2)}) collective-permute-start(bf16[3520,128]{1,0:T(8,128)(2,1)S(1)} %slice_bitcast_fusion.2.rest_0_), channel_id=1, source_target_pairs={{0,1},{1,0},{2,3},{3,2},{4,5},{5,4},{6,7},{7,6},{8,9},{9,8},{10,11... | collective-permute-start | bytes 2703368 | tf_op jit(solution)/shard_map/ppermute | solution.py:186
  12.7 22.9 %collective-permute-start = (bf16[3520,128]{1,0:T(8,128)(2,1)S(1)}, bf16[3520,128]{1,0:T(8,128)(2,1)}, u32[]{:S(2)}, u32[]{:S(2)}) collective-permute-start(bf16[3520,128]{1,0:T(8,128)(2,1)S(1)} %slice_bitcast_fusion.2.rest_0_), channel_id=1, source_target_pairs={{0,2},{1,3},{2,0},{3,1},{4,6},{5,7},{6,4},{7,5},{8,10},{9,11},{10,... | collective-permute-start | bytes 2703368 | tf_op jit(solution)/shard_map/ppermute | solution.py:186
  14.2 48.0 %copy-start.8 = (s32[2,512]{1,0:T(2,128)S(1)}, s32[2,512]{1,0:T(2,128)}, u32[]{:S(2)}) copy-start(s32[2,512]{1,0:T(2,128)} %param.13) | copy-start | bytes 12292
  32.7 7.2 %copy-start.2 = (bf16[3520,128]{1,0:T(8,128)(2,1)}, bf16[3520,128]{1,0:T(8,128)(2,1)S(1)}, u32[]{:S(2)}) copy-start(bf16[3520,128]{1,0:T(8,128)(2,1)S(1)} %collective-permute-done.1.rest_3_) | copy-start | bytes 2703364
  33.9 21.4 %collective-permute-start.3 = (bf16[3520,128]{1,0:T(8,128)(2,1)S(1)}, bf16[3520,128]{1,0:T(8,128)(2,1)}, u32[]{:S(2)}, u32[]{:S(2)}) collective-permute-start(bf16[3520,128]{1,0:T(8,128)(2,1)S(1)} %get-tuple-element.88), channel_id=1, source_target_pairs={{0,2},{1,3},{2,0},{3,1},{4,6},{5,7},{6,4},{7,5},{8,10},{9,11},{10,... | collective-permute-start | bytes 2703368 | tf_op jit(solution)/shard_map/ppermute | solution.py:186
  37.8 21.3 %collective-permute-start.2 = (bf16[3520,128]{1,0:T(8,128)(2,1)S(1)}, bf16[3520,128]{1,0:T(8,128)(2,1)}, u32[]{:S(2)}, u32[]{:S(2)}) collective-permute-start(bf16[3520,128]{1,0:T(8,128)(2,1)S(1)} %get-tuple-element.90), channel_id=1, source_target_pairs={{0,4},{1,5},{2,6},{3,7},{4,0},{5,1},{6,2},{7,3},{8,12},{9,13},{10,... | collective-permute-start | bytes 2703368 | tf_op jit(solution)/shard_map/ppermute | solution.py:186
  39.3 19.8 %collective-permute-start.5 = (bf16[3520,128]{1,0:T(8,128)(2,1)S(1)}, bf16[3520,128]{1,0:T(8,128)(2,1)S(1)}, u32[]{:S(2)}, u32[]{:S(2)}) collective-permute-start(bf16[3520,128]{1,0:T(8,128)(2,1)S(1)} %pad.12.rest_1_), channel_id=1, source_target_pairs={{0,1},{1,0},{2,3},{3,2},{4,5},{5,4},{6,7},{7,6},{8,9},{9,8},{10,11... | collective-permute-start | bytes 2703368 | tf_op jit(solution)/shard_map/ppermute | solution.py:186
  39.3 22.3 %collective-permute-start.6 = (bf16[3520,128]{1,0:T(8,128)(2,1)}, bf16[3520,128]{1,0:T(8,128)(2,1)}, u32[]{:S(2)}, u32[]{:S(2)}) collective-permute-start(bf16[3520,128]{1,0:T(8,128)(2,1)} %collective-permute-done.rest_2_), channel_id=1, source_target_pairs={{0,1},{1,0},{2,3},{3,2},{4,5},{5,4},{6,7},{7,6},{8,9},{9,8},{10,11... | collective-permute-start | bytes 2703368 | tf_op jit(solution)/shard_map/ppermute | solution.py:186
  39.9 23.9 %collective-permute-start.7 = (bf16[3520,128]{1,0:T(8,128)(2,1)S(1)}, bf16[3520,128]{1,0:T(8,128)(2,1)S(1)}, u32[]{:S(2)}, u32[]{:S(2)}) collective-permute-start(bf16[3520,128]{1,0:T(8,128)(2,1)S(1)} %collective-permute-done.1.rest_3_), channel_id=1, source_target_pairs={{0,1},{1,0},{2,3},{3,2},{4,5},{5,4},{6,7},{7,6},{8,9},{9,8},{10,11... | collective-permute-start | bytes 2703368 | tf_op jit(solution)/shard_map/ppermute | solution.py:186
  55.3 8.5 %collective-permute-start.9 = (bf16[3520,128]{1,0:T(8,128)(2,1)}, bf16[3520,128]{1,0:T(8,128)(2,1)}, u32[]{:S(2)}, u32[]{:S(2)}) collective-permute-start(bf16[3520,128]{1,0:T(8,128)(2,1)} %collective-permute-done.3.rest_5_), channel_id=1, source_target_pairs={{0,1},{1,0},{2,3},{3,2},{4,5},{5,4},{6,7},{7,6},{8,9},{9,8},{10,11... | collective-permute-start | bytes 2703368 | tf_op jit(solution)/shard_map/ppermute | solution.py:186
  59.1 4.6 collective-permute-start.8
  59.1 1.0 copy-start.3
  60.1 27.6 %collective-permute-start.11 = (bf16[3520,128]{1,0:T(8,128)(2,1)}, bf16[3520,128]{1,0:T(8,128)(2,1)S(1)}, u32[]{:S(2)}, u32[]{:S(2)}) collective-permute-start(bf16[3520,128]{1,0:T(8,128)(2,1)} %get-tuple-element.87), channel_id=1, source_target_pairs={{0,2},{1,3},{2,0},{3,1},{4,6},{5,7},{6,4},{7,5},{8,10},{9,11},{10,... | collective-permute-start | bytes 2703368 | tf_op jit(solution)/shard_map/ppermute | solution.py:186
  61.6 26.1 %collective-permute-start.10 = (bf16[3520,128]{1,0:T(8,128)(2,1)}, bf16[3520,128]{1,0:T(8,128)(2,1)}, u32[]{:S(2)}, u32[]{:S(2)}) collective-permute-start(bf16[3520,128]{1,0:T(8,128)(2,1)} %get-tuple-element.89), channel_id=1, source_target_pairs={{0,4},{1,5},{2,6},{3,7},{4,0},{5,1},{6,2},{7,3},{8,12},{9,13},{10,... | collective-permute-start | bytes 2703368 | tf_op jit(solution)/shard_map/ppermute | solution.py:186
  63.8 1.0 copy-start.4
  69.5 18.8 %copy-start.11 = (s32[8]{0:T(128)S(1)}, s32[8]{0:T(128)}, u32[]{:S(2)}) copy-start(s32[8]{0:T(128)} %constant.42.clone) | copy-start | bytes 100
  69.5 18.8 %copy-start.12 = (s32[8]{0:T(128)S(1)}, s32[8]{0:T(128)}, u32[]{:S(2)}) copy-start(s32[8]{0:T(128)} %constant.41.clone) | copy-start | bytes 100
  69.5 18.8 %copy-start.13 = (s32[8]{0:T(128)S(1)}, s32[8]{0:T(128)}, u32[]{:S(2)}) copy-start(s32[8]{0:T(128)} %constant.40.clone) | copy-start | bytes 100
  69.5 18.8 %copy-start.14 = (s32[8]{0:T(128)S(1)}, s32[8]{0:T(128)}, u32[]{:S(2)}) copy-start(s32[8]{0:T(128)} %constant.39.clone) | copy-start | bytes 100
  69.6 19.3 %copy-start.9 = (s32[2,8]{1,0:T(2,128)S(1)}, s32[2,8]{1,0:T(2,128)}, u32[]{:S(2)}) copy-start(s32[2,8]{1,0:T(2,128)} %param.15) | copy-start | bytes 196
  69.6 19.3 %copy-start.10 = (s32[2,8]{1,0:T(2,128)S(1)}, s32[2,8]{1,0:T(2,128)}, u32[]{:S(2)}) copy-start(s32[2,8]{1,0:T(2,128)} %param.14) | copy-start | bytes 196
  87.7 20.1 %copy-start.5 = (bf16[3520,128]{1,0:T(8,128)(2,1)}, bf16[3520,128]{1,0:T(8,128)(2,1)S(1)}, u32[]{:S(2)}) copy-start(bf16[3520,128]{1,0:T(8,128)(2,1)S(1)} %collective-permute-done.11.rest_7_) | copy-start | bytes 2703364
  87.7 20.1 %collective-permute-start.12 = (bf16[3520,128]{1,0:T(8,128)(2,1)}, bf16[3520,128]{1,0:T(8,128)(2,1)S(1)}, u32[]{:S(2)}, u32[]{:S(2)}) collective-permute-start(bf16[3520,128]{1,0:T(8,128)(2,1)} %collective-permute-done.10.rest_6_), channel_id=1, source_target_pairs={{0,1},{1,0},{2,3},{3,2},{4,5},{5,4},{6,7},{7,6},{8,9},{9,8},{10,11... | collective-permute-start | bytes 2703368 | tf_op jit(solution)/shard_map/ppermute | solution.py:186
  87.8 20.0 %collective-permute-start.13 = (bf16[3520,128]{1,0:T(8,128)(2,1)S(1)}, bf16[3520,128]{1,0:T(8,128)(2,1)S(1)}, u32[]{:S(2)}, u32[]{:S(2)}) collective-permute-start(bf16[3520,128]{1,0:T(8,128)(2,1)S(1)} %collective-permute-done.11.rest_7_), channel_id=1, source_target_pairs={{0,1},{1,0},{2,3},{3,2},{4,5},{5,4},{6,7},{7,6},{8,9},{9,8},{10,11... | collective-permute-start | bytes 2703368 | tf_op jit(solution)/shard_map/ppermute | solution.py:186
  107.8 0.9 copy-start.6
  108.8 1.0 copy-start.7
  276.3 181.8 %all-reduce.5.cloned.1.call-start = ((), (), s32[]{:S(2)}) async-start(), calls=%async_computation.2 | async-start | bytes 3604480 | tf_op jit(solution)/shard_map/psum | solution.py:929
Sparse Core Ops, SparseCore 0:
  276.4 102.4 reduce-scatter.1
  381.5 76.5 all-reduce.4

commit v2 on v1

--- a/solution.py
+++ b/solution.py
@@ -670,11 +670,8 @@
     )(x, att, segc, hot, cot, wout, win, wback, wstu, wmid, vec, small, wcls)
 
 
-def retreat_kernel(qkv_ref, p_ref, datt_ref, dh1_ref, w_ref, dproj_ref, dx_ref, bg_ref, dk, dv):
-    @pl.when(pl.program_id(0) == 0)
-    def _():
-        bg_ref[...] = jnp.zeros_like(bg_ref)
-
+def retreat_kernel(begun, qkv_ref, p_ref, datt_ref, dproj_ref, bg_ref, dk, dv):
+    bg_ref[...] = jnp.zeros_like(bg_ref) if begun is None else begun[...]
     masks = half_masks()
 
     def pair(p, _):
@@ -709,6 +706,30 @@
 
     lax.fori_loop(0, PAIRS, pair, 0)
 
+
+def retreat(row, qkv, probs, datt, done):
+    rows = qkv.shape[0]
+    only = lambda *shape: pl.BlockSpec((1, *shape), lambda _: (row,) + (0,) * len(shape))
+
+    def kernel(qkv_ref, p_ref, datt_ref, *refs):
+        begun = refs[1] if done else None
+        retreat_kernel(begun, qkv_ref, p_ref, datt_ref, *refs[len(done) :])
+
+    return pl.pallas_call(
+        kernel,
+        grid=(1,),
+        in_specs=[only(LEN, 3 * D), only(HEADS, QB, WIDE), only(LEN, D)] + ([ANY, VM] if done else []),
+        out_specs=[only(LEN, 3 * D), VM],
+        out_shape=[SDS((rows, LEN, 3 * D), BF), SDS((8, D), F32)],
+        scratch_shapes=[pltpu.VMEM((LEN, LANE), F32), pltpu.VMEM((LEN, LANE), F32)],
+        input_output_aliases={3: 0} if done else {},
+        compiler_params=params_of(),
+        cost_estimate=pl.CostEstimate(flops=6 * 10**9, bytes_accessed=12 << 20, transcendentals=0),
+        name="retreat",
+    )(qkv, probs, datt, *done)
+
+
+def project_kernel(dproj_ref, dh1_ref, w_ref, dx_ref):
     def back(t, _):
         cols = at(t, 256)
         dx_ref[0, :, cols] = (dh1_ref[0, :, cols] + dot(dproj_ref[0], w_ref[cols, :], NT)).astype(BF)
@@ -717,24 +738,18 @@
     lax.fori_loop(0, D // 256, back, 0)
 
 
-def retreat(qkv, probs, datt, dh1, wqkv):
-    rows = qkv.shape[0]
-    return pl.pallas_call(
-        retreat_kernel,
+def project_back(dproj, dh1, wqkv):
+    rows = dproj.shape[0]
+    return pl.pallas_call(
+        project_kernel,
         grid=(rows,),
-        in_specs=[
-            row_spec(LEN, 3 * D),
-            row_spec(HEADS, QB, WIDE),
-            row_spec(LEN, D),
-            row_spec(LEN, D),
-            once(D, 3 * D),
-        ],
-        out_specs=[row_spec(LEN, 3 * D), row_spec(LEN, D), whole(8, D)],
-        out_shape=[SDS((rows, LEN, 3 * D), BF), SDS((rows, LEN, D), BF), SDS((8, D), F32)],
-        scratch_shapes=[pltpu.VMEM((LEN, LANE), F32), pltpu.VMEM((LEN, LANE), F32)],
-        compiler_params=params_of(),
-        name="retreat",
-    )(qkv, probs, datt, dh1, wqkv)
+        in_specs=[row_spec(LEN, 3 * D), row_spec(LEN, D), once(D, 3 * D)],
+        out_specs=row_spec(LEN, D),
+        out_shape=SDS((rows, LEN, D), BF),
+        compiler_params=params_of(),
+        cost_estimate=pl.CostEstimate(flops=4 * 10**9, bytes_accessed=16 << 20, transcendentals=0),
+        name="project_back",
+    )(dproj, dh1, wqkv)
 
 
 def store_product(flat, first, lhs_ref, rhs_ref, turned, step=256):
@@ -760,36 +775,37 @@
     lax.fori_loop(0, tall // block, rows_of, 0)
 
 
-def send_shards(flat, base, stop, shard_rows, out_ref, stage, sems):
-    count, padded, _ = out_ref.shape
+def send_shards(flat, origin, base, stop, shard_rows, padded, stage, sems, targets):
     plan = []
-    for d in range(count):
+    for d in range(base // shard_rows, -(-stop // shard_rows)):
         lo, hi = max(base, d * shard_rows), min(stop, (d + 1) * shard_rows)
-        if hi <= lo:
-            continue
         first = (lo - d * shard_rows) // 16 * 16
         last = min(padded, -(-(hi - d * shard_rows) // 16) * 16)
-        plan.append((d, first, last))
-    for n, (d, first, last) in enumerate(plan):
-        slot = n % 2
+        plan.append((d, first, last - first))
+
+    def copy(n, out_ref):
+        d, first, size = plan[n]
+        span = pl.ds(first, size)
+        return pltpu.make_async_copy(stage.at[n % 2, span], out_ref.at[span], sems.at[n % 2])
+
+    for n, (d, first, size) in enumerate(plan):
         if n >= 2:
-            e, f, g = plan[n - 2]
-            pltpu.make_async_copy(stage.at[slot, pl.ds(f, g - f)], out_ref.at[e, pl.ds(f, g - f)], sems.at[slot]).wait()
-        size = math.gcd(last - first, CHUNK)
-
-        def narrow(m, _, d=d, first=first, size=size, slot=slot):
-            src = d * shard_rows - base + first + m * size + 16
-            stage[slot, pl.ds(pl.multiple_of(first + m * size, 16), size), :] = flat[pl.ds(src, size), :].astype(BF)
+            copy(n - 2, targets(plan[n - 2][0])[0][1]).wait()
+        step = math.gcd(size, CHUNK)
+
+        def narrow(m, _, d=d, first=first, step=step, slot=n % 2):
+            src = d * shard_rows - origin + first + m * step + 16
+            stage[slot, pl.ds(pl.multiple_of(first + m * step, 16), step), :] = flat[pl.ds(src, step), :].astype(BF)
             return 0
 
-        lax.fori_loop(0, (last - first) // size, narrow, 0)
-        pltpu.make_async_copy(
-            stage.at[slot, pl.ds(first, last - first)], out_ref.at[d, pl.ds(first, last - first)], sems.at[slot]
-        ).start()
+        lax.fori_loop(0, size // step, narrow, 0)
+        for when, out_ref in targets(d):
+            if when is None:
+                copy(n, out_ref).start()
+            else:
+                pl.when(when)(lambda n=n, out_ref=out_ref: copy(n, out_ref).start())
     for n in range(max(0, len(plan) - 2), len(plan)):
-        e, f, g = plan[n]
-        slot = n % 2
-        pltpu.make_async_copy(stage.at[slot, pl.ds(f, g - f)], out_ref.at[e, pl.ds(f, g - f)], sems.at[slot]).wait()
+        copy(n, targets(plan[n][0])[0][1]).wait()
 
 
 def put_line(flat, first, src_ref, row):
@@ -797,9 +813,7 @@
         flat[first + j : first + j + 1, :] = src_ref[row : row + 1, j * LANE : (j + 1) * LANE]
 
 
-def late_kernel(
-    shard_rows, att, dbr, nbf, dinner, act, dffn, outb, dstu, vg, sg, gmid, gcls, out_ref, edge_ref, flat, turned, stage, sems
-):
+def fill_late(flat, att, dbr, nbf, dinner, act, dffn, outb, dstu, vg, sg, gmid, gcls, turned):
     first = lambda name: TABLE[name] - SPLIT + 16
     store_product(flat, first("w_out"), att, dbr, turned)
     store_product(flat, first("w_in"), nbf, dinner, turned)
@@ -820,16 +834,38 @@
     tail = USED - SPLIT + 16
     flat[tail:, :] = jnp.zeros((flat.shape[0] - tail, LANE), F32)
     flat[0:16, :] = jnp.zeros((16, LANE), F32)
-    edge_ref[...] = flat[16:32, :]
-    send_shards(flat, SPLIT, out_ref.shape[0] * shard_rows, shard_rows, out_ref, stage, sems)
-
-
-def early_kernel(shard_rows, x, dproj, bg, edge, _, out_ref, flat, turned, stage, sems):
+
+
+def fill_early(flat, x, dproj, bg, edge, turned):
     store_product(flat, 16, x, dproj, turned)
     put_line(flat, 16 + TABLE["b_qv"], bg, 0)
     put_line(flat, 16 + TABLE["b_qv"] + D // LANE, bg, 1)
-    flat[16 + SPLIT : 32 + SPLIT, :] = edge[...]
-    send_shards(flat, 0, SPLIT, shard_rows, out_ref, stage, sems)
+    flat[16 + SPLIT : 16 + SPLIT + edge.shape[0], :] = edge[...]
+
+
+GRAD_COST = pl.CostEstimate(flops=4 * 10**9, bytes_accessed=24 << 20, transcendentals=0)
+
+
+def scratch_of(rows, tokens, padded):
+    return [
+        pltpu.VMEM((16 + rows + 48, LANE), F32),
+        pltpu.VMEM((D, tokens), BF),
+        pltpu.VMEM((2, padded, LANE), BF),
+        pltpu.SemaphoreType.DMA((2,)),
+    ]
+
+
+def late_kernel(shard_rows, *refs):
+    ins, (out_ref, edge_ref, flat, turned, stage, sems) = refs[:12], refs[12:]
+    fill_late(flat, *ins, turned)
+    edge_ref[...] = flat[16:32, :]
+    count, padded, _ = out_ref.shape
+    send_shards(flat, SPLIT, SPLIT, count * shard_rows, shard_rows, padded, stage, sems, lambda d: [(None, out_ref.at[d])])
+
+
+def early_kernel(shard_rows, x, dproj, bg, edge, _, out_ref, flat, turned, stage, sems):
+    fill_early(flat, x, dproj, bg, edge, turned)
+    send_shards(flat, 0, 0, SPLIT, shard_rows, out_ref.shape[1], stage, sems, lambda d: [(None, out_ref.at[d])])
 
 
 def late_grads(shard_rows, count, padded, *arrays):
@@ -839,34 +875,231 @@
         in_specs=[VM] * len(arrays),
         out_specs=[ANY, VM],
         out_shape=[SDS((count, padded, LANE), BF), SDS((16, LANE), F32)],
-        scratch_shapes=[
-            pltpu.VMEM((16 + rows + 48, LANE), F32),
-            pltpu.VMEM((D, arrays[0].shape[0]), BF),
-            pltpu.VMEM((2, padded, LANE), BF),
-            pltpu.SemaphoreType.DMA((2,)),
-        ],
+        scratch_shapes=scratch_of(rows, arrays[0].shape[0], padded),
         compiler_params=params_of(),
         name="late_grads",
     )(*arrays)
 
 
 def early_grads(shard_rows, x, dproj, bg, edge, partial):
-    count, padded, _ = partial.shape
     return pl.pallas_call(
         functools.partial(early_kernel, shard_rows),
         in_specs=[VM] * 4 + [ANY],
         out_specs=ANY,
         out_shape=SDS(partial.shape, BF),
-        scratch_shapes=[
-            pltpu.VMEM((16 + SPLIT + 48, LANE), F32),
-            pltpu.VMEM((D, x.shape[0]), BF),
-            pltpu.VMEM((2, padded, LANE), BF),
-            pltpu.SemaphoreType.DMA((2,)),
-        ],
+        scratch_shapes=scratch_of(SPLIT, x.shape[0], partial.shape[1]),
         input_output_aliases={4: 0},
         compiler_params=params_of(),
         name="early_grads",
     )(x, dproj, bg, edge, partial)
+
+
+def by_core(core, d, chip, keep, give):
+    return [(core == (d & 1), keep.at[chip]), (core != (d & 1), give.at[chip])]
+
+
+def late_pair_kernel(shard_rows, me_ref, *refs):
+    ins, (keep, give, edge_ref, flat, turned, stage, sems) = refs[:12], refs[12:]
+    fill_late(flat, *ins, turned)
+    edge_ref[...] = flat[16 : 16 + edge_ref.shape[0], :]
+    core = me_ref[0] & 1
+    send_shards(
+        flat,
+        SPLIT,
+        2 * shard_rows,
+        8 * shard_rows,
+        shard_rows,
+        keep.shape[1],
+        stage,
+        sems,
+        lambda d: by_core(core, d, d // 2 - 1, keep, give),
+    )
+
+
+def late_pairs(me, shard_rows, padded, *arrays):
+    shape = SDS((3, padded, LANE), BF)
+    edge = -(-(2 * shard_rows - SPLIT) // 8) * 8
+    return pl.pallas_call(
+        functools.partial(late_pair_kernel, shard_rows),
+        in_specs=[SM] + [VM] * len(arrays),
+        out_specs=[ANY, ANY, VM],
+        out_shape=[shape, shape, SDS((edge, LANE), F32)],
+        scratch_shapes=scratch_of(8 * shard_rows - SPLIT, arrays[0].shape[0], padded),
+        compiler_params=params_of(),
+        cost_estimate=GRAD_COST,
+        name="late_grads",
+    )(me, *arrays)
+
+
+def early_pair_kernel(shard_rows, me_ref, x, dproj, bg, edge, keep, give, flat, turned, stage, sems):
+    fill_early(flat, x, dproj, bg, edge, turned)
+    core = me_ref[0] & 1
+    send_shards(
+        flat, 0, 0, 2 * shard_rows, shard_rows, keep.shape[1], stage, sems, lambda d: by_core(core, d, 0, keep, give)
+    )
+
+
+def early_pairs(me, shard_rows, padded, x, dproj, bg, edge):
+    shape = SDS((1, padded, LANE), BF)
+    return pl.pallas_call(
+        functools.partial(early_pair_kernel, shard_rows),
+        in_specs=[SM] + [VM] * 4,
+        out_specs=[ANY, ANY],
+        out_shape=[shape, shape],
+        scratch_shapes=scratch_of(SPLIT + edge.shape[0], x.shape[0], padded),
+        compiler_params=params_of(),
+        cost_estimate=GRAD_COST,
+        name="early_grads",
+    )(me, x, dproj, bg, edge)
+
+
+def merge_late_kernel(me_ref, keep, got, sums, along_y, along_x):
+    chip, half = pl.program_id(0) + 1, pl.program_id(1)
+    x, y = (me_ref[0] >> 1) & 1, me_ref[0] >> 2
+    total = keep[0] + got[0]
+    sums[0, 0] = total
+
+    @pl.when((half == 0) & (chip == 3 - 2 * y))
+    def _():
+        along_y[...] = total
+
+    @pl.when((half == 1) & (chip == 3 - x))
+    def _():
+        along_x[...] = total
+
+
+def merge_late(me, keep, got):
+    half = keep.shape[1] // 2
+    block = pl.BlockSpec((1, half, LANE), lambda c, h: (c, h, 0))
+    return pl.pallas_call(
+        merge_late_kernel,
+        grid=(3, 2),
+        in_specs=[SM, block, block],
+        out_specs=[pl.BlockSpec((1, 1, half, LANE), lambda c, h: (c + 1, h, 0, 0)), whole(half, LANE), whole(half, LANE)],
+        out_shape=[SDS((4, 2, half, LANE), BF), SDS((half, LANE), BF), SDS((half, LANE), BF)],
+        compiler_params=params_of(),
+        cost_estimate=pl.CostEstimate(flops=0, bytes_accessed=18 << 20, transcendentals=0),
+        name="merge_late",
+    )(me, keep, got)
+
+
+def merge_early_kernel(me_ref, keep, got, old, sums, along_y, along_x, total, sems):
+    x, y = (me_ref[0] >> 1) & 1, me_ref[0] >> 2
+    half = total.shape[1]
+    for h in range(2):
+        total[h] = keep[0, h * half : (h + 1) * half] + got[0, h * half : (h + 1) * half]
+    put = pltpu.make_async_copy(total, sums.at[0], sems.at[0])
+    put.start()
+    fetch_y = pltpu.make_async_copy(sums.at[2, 0], along_y, sems.at[1])
+    fetch_x = pltpu.make_async_copy(sums.at[1, 1], along_x, sems.at[2])
+
+    @pl.when(y == 0)
+    def _():
+        fetch_y.start()
+
+    @pl.when(y == 1)
+    def _():
+        along_y[...] = total[0]
+
+    @pl.when(x == 0)
+    def _():
+        fetch_x.start()
+
+    @pl.when(x == 1)
+    def _():
+        along_x[...] = total[1]
+
+    put.wait()
+
+    @pl.when(y == 0)
+    def _():
+        fetch_y.wait()
+
+    @pl.when(x == 0)
+    def _():
+        fetch_x.wait()
+
+
+def merge_early(me, keep, got, sums):
+    half = keep.shape[1] // 2
+    return pl.pallas_call(
+        merge_early_kernel,
+        in_specs=[SM, VM, VM, ANY],
+        out_specs=[ANY, VM, VM],
+        out_shape=[SDS(sums.shape, BF), SDS((half, LANE), BF), SDS((half, LANE), BF)],
+        scratch_shapes=[pltpu.VMEM((2, half, LANE), BF), pltpu.SemaphoreType.DMA((3,))],
+        input_output_aliases={3: 0},
+        compiler_params=params_of(),
+        cost_estimate=pl.CostEstimate(flops=0, bytes_accessed=9 << 20, transcendentals=0),
+        name="merge_early",
+    )(me, keep, got, sums)
+
+
+def merge_next_kernel(me_ref, sums, y_one, y_two, x_one, x_two, own_a, own_b, along_x, along_y, buf, sems):
+    x, y = (me_ref[0] >> 1) & 1, me_ref[0] >> 2
+    chip = me_ref[0] >> 1
+    reads = [
+        pltpu.make_async_copy(sums.at[c, h], buf.at[n], sems.at[n])
+        for n, (c, h) in enumerate(((chip, 0), (chip, 1), (chip ^ 1, 0), (chip ^ 2, 1)))
+    ]
+    for read in reads:
+        read.start()
+    for read in reads:
+        read.wait()
+
+    @pl.when(x == 0)
+    def _():
+        own_a[...] = buf[0] + y_two[...]
+        along_x[...] = buf[2] + y_one[...]
+
+    @pl.when(x == 1)
+    def _():
+        own_a[...] = buf[0] + y_one[...]
+        along_x[...] = buf[2] + y_two[...]
+
+    @pl.when(y == 0)
+    def _():
+        own_b[...] = buf[1] + x_two[...]
+        along_y[...] = buf[3] + x_one[...]
+
+    @pl.when(y == 1)
+    def _():
+        own_b[...] = buf[1] + x_one[...]
+        along_y[...] = buf[3] + x_two[...]
+
+
+def merge_next(me, sums, y_one, y_two, x_one, x_two):
+    half = sums.shape[2]
+    return pl.pallas_call(
+        merge_next_kernel,
+        in_specs=[SM, ANY, VM, VM, VM, VM],
+        out_specs=[VM] * 4,
+        out_shape=[SDS((half, LANE), BF)] * 4,
+        scratch_shapes=[pltpu.VMEM((4, half, LANE), BF), pltpu.SemaphoreType.DMA((4,))],
+        compiler_params=params_of(),
+        cost_estimate=pl.CostEstimate(flops=0, bytes_accessed=10 << 20, transcendentals=0),
+        name="merge_next",
+    )(me, sums, y_one, y_two, x_one, x_two)
+
+
+def part(v, pieces, i):
+    return lax.dynamic_index_in_dim(v.reshape(pieces, -1, LANE), i, keepdims=False)
+
+
+def join(own, other, first):
+    return jnp.where(first == 0, jnp.concatenate([own, other]), jnp.concatenate([other, own]))
+
+
+def sum_replicas(one, two):
+    z = lax.axis_index("rep")
+    low, high = z & 1, z >> 1
+    turn = lambda v, bit: lax.ppermute(v, "rep", [(i, i ^ bit) for i in range(4)])
+    got_one, got_two = turn(part(one, 2, 1 - low), 1), turn(part(two, 2, 1 - high), 2)
+    one, two = part(one, 2, low) + got_one, part(two, 2, high) + got_two
+    got_one, got_two = turn(part(one, 2, 1 - high), 2), turn(part(two, 2, 1 - low), 1)
+    one, two = part(one, 2, high) + got_one, part(two, 2, low) + got_two
+    one, two = join(one, turn(one, 2), high), join(two, turn(two, 1), low)
+    return join(one, turn(one, 1), low), join(two, turn(two, 2), high)
 
 
 def adam_update(first_part, second_part, grad_part):
@@ -906,27 +1139,42 @@
     )
     gcls = jnp.pad(gcls[:, :CLASSES].reshape(CLASSES, LANE), ((0, 2), (0, 0)))
     flat2 = lambda v: v.reshape(rows * LEN, v.shape[-1])
-    partial, edge = late_grads(
-        shard_rows,
-        count,
-        padded,
-        flat2(att),
-        flat2(dbr),
-        flat2(nbf),
-        flat2(dinner),
-        flat2(act),
-        flat2(dffn),
-        flat2(out),
-        flat2(dstu),
-        vg,
-        sg,
-        gmid,
-        gcls,
-    )
-    dproj, dx, bg = retreat(qkv, probs, datt, dh1, wqkv)
-    grads = early_grads(shard_rows, flat2(inputs), flat2(dproj), bg, edge, partial)
-    owned = lax.psum_scatter(grads, "fsdp", scatter_dimension=0, tiled=False)
-    owned = lax.psum(owned, "rep")
+    late = [flat2(v) for v in (att, dbr, nbf, dinner, act, dffn, out, dstu)] + [vg, sg, gmid, gcls]
+    if count == 8:
+        me = lax.axis_index("fsdp").reshape(1)
+        keep, give, edge = late_pairs(me, shard_rows, padded, *late)
+        got = swap(give, 1)
+        back = retreat(0, qkv, probs, datt, ())
+        got, back = lax.optimization_barrier((got, tuple(back)))
+        sums, along_y, along_x = merge_late(me, keep, got)
+        y_one, x_one = swap(along_y, 4), swap(along_x, 2)
+        back, _ = lax.optimization_barrier((back, along_y))
+        for row in range(1, rows):
+            back = retreat(row, qkv, probs, datt, tuple(back))
+        y_one, x_one, (dproj, bg) = lax.optimization_barrier((y_one, x_one, tuple(back)))
+        keep, give = early_pairs(me, shard_rows, padded, flat2(inputs), flat2(dproj), bg, edge)
+        sums, along_y, along_x = merge_early(me, keep, swap(give, 1), sums)
+        y_two, x_two = swap(along_y, 4), swap(along_x, 2)
+        dproj, _ = lax.optimization_barrier((dproj, along_y))
+        dx = project_back(dproj, dh1, wqkv)
+        y_two, _ = lax.optimization_barrier((y_two, dx))
+        own_a, own_b, along_x, along_y = merge_next(me, sums, y_one, y_two, x_one, x_two)
+        own_a, own_b = own_a + swap(along_x, 2), own_b + swap(along_y, 4)
+    else:
+        partial, edge = late_grads(shard_rows, count, padded, *late)
+        back = ()
+        for row in range(rows):
+            back = tuple(retreat(row, qkv, probs, datt, back))
+        dproj, bg = back
+        grads = early_grads(shard_rows, flat2(inputs), flat2(dproj), bg, edge, partial)
+        owned = lax.psum_scatter(grads, "fsdp", scatter_dimension=0, tiled=False)
+        dx = project_back(dproj, dh1, wqkv)
+    if count != 8:
+        owned = lax.psum(owned, "rep")
+    elif lax.axis_size("rep") == 4:
+        owned = jnp.concatenate(sum_replicas(own_a, own_b))
+    else:
+        owned = lax.psum(jnp.concatenate([own_a, own_b]), "rep")
     grad = owned[:shard_rows].astype(F32).reshape(-1)
     step_dir, first_new, second_new = adam_update(moment_one, moment_two, grad)
     return (out, logits, dx, step_dir, first_new, second_new)

time: 472 us -> 436 us (0.924)
  waiting for transfers between devices: 219 us -> 141 us
  Pallas kernels: 204 us -> 231 us
  starting transfers between devices: 11 us -> 28.4 us
  between operations: 14.2 us -> 1.01 us
  other arithmetic: 14.1 us -> 21.5 us
    reduce_scatter x1 -> x0, waiting for transfers between devices: 103 us -> none  [shards(): owned = lax.psum_scatter(grads, 'fsdp', scatter_dimension=0, tiled=False)]
    psum x1 -> x0, waiting for transfers between devices: 79.1 us -> none  [shards(): owned = lax.psum(owned, 'rep')]
    ppermute x0 -> x8, waiting for transfers between devices: none -> 64 us  [sum_replicas(): lax.ppermute(v, 'rep', [(i, i ^ bit) for i in range(4)])]
    ppermute x14 -> x22, waiting for transfers between devices: 37.7 us -> 77.3 us  [swap(): return lax.ppermute(v, 'fsdp', [(d, d ^ bit) for d in range(8)])]
    pallas_call x3 -> x8, Pallas kernels: 79 us -> 106 us  [the longest x2 32.6 us: retreat(): pl.pallas_call(kernel, grid=(1,), in_specs=[only(LEN, 3 * D), only(HEADS,...]
    ppermute x0 -> x8, starting transfers between devices: none -> 10.7 us  [sum_replicas(): lax.ppermute(v, 'rep', [(i, i ^ bit) for i in range(4)])]
    ppermute x14 -> x22, starting transfers between devices: 10.9 us -> 17.7 us  [swap(): return lax.ppermute(v, 'fsdp', [(d, d ^ bit) for d in range(8)])]
  transfers between devices with their start and end apart: 16 -> 30, of which waited for: 5 -> 16; matrix products, arithmetic and copies ran while one was open for 1% -> 2% of each run, Pallas kernels for 9% -> 19%
where the time goes in v2:
time: 436 us; the launch traced here: 435 us
  Pallas kernels  231 us (53%)
  waiting for transfers between devices  141 us (32%)
  starting transfers between devices  28.4 us (7%)
  other arithmetic  21.5 us (5%)
  local copies, waits for them, and re-layouts  11.7 us (3%)
    ppermute x22, waiting for transfers between devices, swap(): return lax.ppermute(v, 'fsdp', [(d, d ^ bit) for d in range(8)])  77.3 us
    pallas_call x1, Pallas kernels, middle(): pl.pallas_call(middle_kernel, grid=(rows,), in_specs=[row_spec(LEN, D), r...  69.7 us
    ppermute x8, waiting for transfers between devices, sum_replicas(): lax.ppermute(v, 'rep', [(i, i ^ bit) for i in range(4)])  64 us
    pallas_call x2, Pallas kernels, attend(): pl.pallas_call(kernel, grid=(1,), in_specs=[only(LEN, D), only(LEN, 1), o...  36.2 us
    pallas_call x2, Pallas kernels, retreat(): pl.pallas_call(kernel, grid=(1,), in_specs=[only(LEN, 3 * D), only(HEADS,...  32.6 us
    pallas_call x1, Pallas kernels, late_pairs(): pl.pallas_call(functools.partial(late_pair_kernel, shard_rows), in_specs=...  32.4 us
    ppermute x22, starting transfers between devices, swap(): return lax.ppermute(v, 'fsdp', [(d, d ^ bit) for d in range(8)])  17.7 us
    pallas_call x1, Pallas kernels, unpack_rest(): pl.pallas_call(functools.partial(unpack_rest_kernel, shard_rows), in_spec...  14.8 us
  transfers between devices with their start and end apart: 30, of which 16 were waited for; matrix products, arithmetic and copies ran while one was open for 2% of the time, Pallas kernels for 19%

profile of v2, /device:TPU:0, one launch (start us, length us, event | category | flops | bytes accessed | tf_op | source)
XLA Modules:
  0.0 435.4 jit_solution(12461237138505210428)
XLA Ops:
  0.6 2.2 convert.5
  3.1 3.0 collective-permute-start
  6.1 1.5 collective-permute-start.1
  7.6 18.5 %collective-permute-done.rest_2_ = bf16[3520,128]{1,0:T(8,128)(2,1)S(1)} collective-permute-done((bf16[3520,128]{1,0:T(8,128)(2,1)S(1)}, bf16[3520,128]{1,0:T(8,128)(2,1)S(1)}, u32[]{:S(2)}, u32[]{:S(2)}) %collective-permute-start) | collective-permute-done | bytes 901152 | tf_op jit(solution)/shard_map/ppermute | solution.py:186
  26.1 1.2 broadcast_select_fusion.2
  27.2 1.8 collective-permute-start.2
  29.0 2.3 broadcast_select_fusion
  31.3 1.5 collective-permute-start.3
  33.4 15.3 %collective-permute-done.2.rest_4_ = bf16[3520,128]{1,0:T(8,128)(2,1)} collective-permute-done((bf16[3520,128]{1,0:T(8,128)(2,1)S(1)}, bf16[3520,128]{1,0:T(8,128)(2,1)}, u32[]{:S(2)}, u32[]{:S(2)}) %collective-permute-start.2) | collective-permute-done | bytes 901152 | tf_op jit(solution)/shard_map/ppermute | solution.py:186
  48.6 4.0 collective-permute-done.3.rest_5_
  52.6 1.6 collective-permute-start.10
  56.3 1.0 copy.27.refs_1_.segc_ref
  58.3 4.8 %unpack_first.1 = (bf16[768,2304]{1,0:T(8,128)(2,1)}, f32[8,2304]{1,0:T(8,128)}) custom-call(s32[1]{0:T(128)} %bitcast.1.me_ref, bf16[3520,128]{1,0:T(8,128)(2,1)} %copy-done, bf16[3520,128]{1,0:T(8,128)(2,1)} %copy-done.1, bf16[3520,128]{1,0:T(8,128)(2,1)} %copy-done.2, bf16[3520,128]{1,0:T(8,128)(2,1)} %collective-permute-done.1.rest_3_, ...), custom_call_target="tpu_custom_call" | custom-call | bytes 20971520 | tf_op jit(solution)/shard_map/unpack_first/pallas_call | solution.py:235
  63.1 18.1 %attend.2 = (bf16[2,512,2304]{2,1,0:T(8,128)(2,1)}, bf16[2,12,128,1280]{3,2,1,0:T(8,128)(2,1)}, bf16[2,512,768]{2,1,0:T(8,128)(2,1)}) custom-call(bf16[2,512,768]{2,1,0:T(8,128)(2,1)} %x_ref.1, s32[2,512,1]{2,1,0:T(8,128)} %copy.27.refs_1_.segc_ref, s32[2,1,512]{2,1,0:T(1,128)} %broadcast_in_dim.24.refs_2_, ...), custom_call_target="tpu_custom_call" | custom-call | flops 6000000000 | bytes 12582912 | tf_op jit(solution)/shard_map/attend/pallas_call | solution.py:365
  83.3 18.1 %attend.3 = (bf16[2,512,2304]{2,1,0:T(8,128)(2,1)}, bf16[2,12,128,1280]{3,2,1,0:T(8,128)(2,1)}, bf16[2,512,768]{2,1,0:T(8,128)(2,1)}) custom-call(bf16[2,512,768]{2,1,0:T(8,128)(2,1)} %x_ref.1, s32[2,512,1]{2,1,0:T(8,128)} %copy.27.refs_1_.segc_ref, ...), custom_call_target="tpu_custom_call", output_to_operand_aliasing={{0}: (5, {}), {1}: (6, {}), {2}: (7, {})} | custom-call | flops 6000000000 | bytes 12582912 | tf_op jit(solution)/shard_map/attend/pallas_call | solution.py:365
  102.4 14.8 %unpack_rest.1 = (bf16[768,768]{1,0:T(8,128)(2,1)}, bf16[768,3072]{1,0:T(8,128)(2,1)}, bf16[3072,768]{1,0:T(8,128)(2,1)}, bf16[768,128]{1,0:T(8,128)(2,1)}, f32[...) custom-call(s32[8]{0:T(128)} %fusion.4.owner_ref, bf16[3520,128]{1,0:T(8,128)(2,1)} %copy-done, ...), custom_call_target="tpu_custom_call" | custom-call | bytes 62914560 | tf_op jit(solution)/shard_map/unpack_rest/pallas_call | solution.py:271
  118.7 69.7 %middle.1 = (bf16[2,512,768]{2,1,0:T(8,128)(2,1)}, f32[2,8,14]{2,1,0:T(8,128)}, bf16[2,512,768]{2,1,0:T(8,128)(2,1)}, bf16[2,512,3072]{2,1,0:T(8,128)(2,1)}, bf1...) custom-call(bf16[2,512,768]{2,1,0:T(8,128)(2,1)} %x_ref.1, ...), custom_call_target="tpu_custom_call" | custom-call | tf_op jit(solution)/shard_map/middle/pallas_call | solution.py:607
  188.3 1.0 reshape.108
  189.9 32.4 %late_grads.1 = (bf16[3,7040,128]{2,1,0:T(8,128)(2,1)}, bf16[3,7040,128]{2,1,0:T(8,128)(2,1)}, f32[240,128]{1,0:T(8,128)}) custom-call(s32[1]{0:T(128)} %bitcast.1.me_ref, bf16[1024,768]{1,0:T(8,128)(2,1)} %bitcast.49, bf16[1024,768]{1,0:T(8,128)(2,1)} %bitcast.62, bf16[1024,768]{1,0:T(8,128)(2,1)} %bitcast.60, bf16[1024,3072]{1,0:T(8,128)(2,1)} %bitcast.48, ...), custom_call_target="tpu_custom_call" | custom-call | flops 4000000000 | bytes 25165824 | tf_op jit(solution)/shard_map/late_grads/pallas_call | solution.py:922
  222.4 16.3 %retreat.2 = (bf16[2,512,2304]{2,1,0:T(8,128)(2,1)}, f32[8,768]{1,0:T(8,128)}) custom-call(bf16[2,512,2304]{2,1,0:T(8,128)(2,1)} %get-tuple-element.102.qkv_ref, bf16[2,12,128,1280]{3,2,1,0:T(8,128)(2,1)} %get-tuple-element.103.p_ref, bf16[2,512,768]{2,1,0:T(8,128)(2,1)} %get-tuple-element.104.datt_ref), custom_call_target="tpu_custom_call" | custom-call | flops 6000000000 | bytes 12582912 | tf_op jit(solution)/shard_map/retreat/pallas_call | solution.py:718
  238.7 8.5 %merge_late.1 = (bf16[4,2,3520,128]{3,2,1,0:T(8,128)(2,1)}, bf16[3520,128]{1,0:T(8,128)(2,1)}, bf16[3520,128]{1,0:T(8,128)(2,1)}) custom-call(s32[1]{0:T(128)} %bitcast.1.me_ref, bf16[3,7040,128]{2,1,0:T(8,128)(2,1)} %get-tuple-element.100.keep, bf16[3,7040,128]{2,1,0:T(8,128)(2,1)} %collective-permute-done.14.got), custom_call_target="tpu_custom_call" | custom-call | bytes 18874368 | tf_op jit(solution)/shard_map/merge_late/pallas_call | solution.py:974
  247.3 1.0 collective-permute-start.15
  248.3 1.4 collective-permute-start.16
  249.8 16.3 %retreat.3 = (bf16[2,512,2304]{2,1,0:T(8,128)(2,1)}, f32[8,768]{1,0:T(8,128)}) custom-call(bf16[2,512,2304]{2,1,0:T(8,128)(2,1)} %get-tuple-element.102.qkv_ref, bf16[2,12,128,1280]{3,2,1,0:T(8,128)(2,1)} %get-tuple-element.103.p_ref, bf16[2,512,768]{2,1,0:T(8,128)(2,1)} %get-tuple-element.104.datt_ref, ...), custom_call_target="tpu_custom_call", output_to_operand_aliasing={{0}: (3, {})} | custom-call | flops 6000000000 | bytes 12582912 | tf_op jit(solution)/shard_map/retreat/pallas_call | solution.py:718
  266.1 3.8 collective-permute-done.15.y_one
  270.6 11.1 %early_grads.1 = (bf16[1,7040,128]{2,1,0:T(8,128)(2,1)}, bf16[1,7040,128]{2,1,0:T(8,128)(2,1)}) custom-call(s32[1]{0:T(128)} %bitcast.1.me_ref, bf16[1024,768]{1,0:T(8,128)(2,1)} %bitcast.58, bf16[1024,2304]{1,0:T(8,128)(2,1)} %bitcast.67, f32[8,768]{1,0:T(8,128)} %get-tuple-element.117.bg, f32[240,128]{1,0:T(8,128)} %get-tuple-element.118.edge), custom_call_target="tpu_custom_call" | custom-call | flops 4000000000 | bytes 25165824 | tf_op jit(solution)/shard_map/early_grads/pallas_call | solution.py:944
  281.8 3.9 collective-permute-done.17.got
  285.7 1.2 copy-done.7
  287.0 5.8 %merge_early.1 = (bf16[4,2,3520,128]{3,2,1,0:T(8,128)(2,1)}, bf16[3520,128]{1,0:T(8,128)(2,1)}, bf16[3520,128]{1,0:T(8,128)(2,1)}) custom-call(s32[1]{0:T(128)} %bitcast.1.me_ref, bf16[1,7040,128]{2,1,0:T(8,128)(2,1)} %get-tuple-element.119.keep, bf16[1,7040,128]{2,1,0:T(8,128)(2,1)} %copy-done.7, ...), custom_call_target="tpu_custom_call", output_to_operand_aliasing={{0}: (3, {})} | custom-call | bytes 9437184 | tf_op jit(solution)/shard_map/merge_early/pallas_call | solution.py:1025
  294.4 9.0 %project_back.1 = bf16[2,512,768]{2,1,0:T(8,128)(2,1)} custom-call(bf16[2,512,2304]{2,1,0:T(8,128)(2,1)} %get-tuple-element.123.dproj_ref, f32[2,512,768]{2,1,0:T(8,128)} %get-tuple-element.124.dh1_ref, bf16[768,2304]{1,0:T(8,128)(2,1)} %get-tuple-element.72.refs_3_.w_ref), custom_call_target="tpu_custom_call" | custom-call | flops 4000000000 | bytes 16777216 | tf_op jit(solution)/shard_map/project_back/pallas_call | solution.py:743
  303.4 11.7 %collective-permute-done.18.y_two = bf16[3520,128]{1,0:T(8,128)(2,1)S(1)} collective-permute-done((bf16[3520,128]{1,0:T(8,128)(2,1)}, bf16[3520,128]{1,0:T(8,128)(2,1)S(1)}, u32[]{:S(2)}, u32[]{:S(2)}) %collective-permute-start.18) | collective-permute-done | bytes 901152 | tf_op jit(solution)/shard_map/ppermute | solution.py:186
  316.5 6.6 %merge_next.1 = (bf16[3520,128]{1,0:T(8,128)(2,1)}, bf16[3520,128]{1,0:T(8,128)(2,1)}, bf16[3520,128]{1,0:T(8,128)(2,1)}, bf16[3520,128]{1,0:T(8,128)(2,1)}) custom-call(s32[1]{0:T(128)} %bitcast.1.me_ref, bf16[4,2,3520,128]{3,2,1,0:T(8,128)(2,1)} %get-tuple-element.125.sums, bf16[3520,128]{1,0:T(8,128)(2,1)} %copy-done.13, bf16[3520,128]{1,0:T(8,128)(2,1)} %copy-done.15, ...), custom_call_target="tpu_custom_call" | custom-call | bytes 10485760 | tf_op jit(solution)/shard_map/merge_next/pallas_call | solution.py:1073
  323.1 1.3 collective-permute-start.25
  324.4 1.0 collective-permute-start.20
  325.4 18.9 %collective-permute-done.25 = bf16[3520,128]{1,0:T(8,128)(2,1)S(1)} collective-permute-done((bf16[3520,128]{1,0:T(8,128)(2,1)}, bf16[3520,128]{1,0:T(8,128)(2,1)S(1)}, u32[]{:S(2)}, u32[]{:S(2)}) %collective-permute-start.25) | collective-permute-done | bytes 901152 | tf_op jit(solution)/shard_map/ppermute | solution.py:186
  345.3 1.7 add.67
  347.8 2.6 collective-permute-start.26
  350.6 1.6 collective-permute-start.21
  352.3 16.8 %collective-permute-done.26 = bf16[1760,128]{1,0:T(8,128)(2,1)S(1)} collective-permute-done((bf16[1760,128]{1,0:T(8,128)(2,1)}, bf16[1760,128]{1,0:T(8,128)(2,1)S(1)}, u32[]{:S(2)}, u32[]{:S(2)}) %collective-permute-start.26) | collective-permute-done | bytes 450592 | tf_op jit(solution)/shard_map/ppermute | solution.py:1096
  370.0 3.3 collective-permute-start.22
  373.3 8.3 %collective-permute-done.27 = bf16[880,128]{1,0:T(8,128)(2,1)S(1)} collective-permute-done((bf16[880,128]{1,0:T(8,128)(2,1)S(1)}, bf16[880,128]{1,0:T(8,128)(2,1)S(1)}, u32[]{:S(2)}, u32[]{:S(2)}) %collective-permute-start.27) | collective-permute-done | bytes 225312 | tf_op jit(solution)/shard_map/ppermute | solution.py:1096
  381.7 2.1 collective-permute-done.22
  384.1 4.5 %collective-permute-done.28 = bf16[880,128]{1,0:T(8,128)(2,1)S(1)} collective-permute-done((bf16[880,128]{1,0:T(8,128)(2,1)S(1)}, bf16[880,128]{1,0:T(8,128)(2,1)S(1)}, u32[]{:S(2)}, u32[]{:S(2)}) %collective-permute-start.28) | collective-permute-done | bytes 225312 | tf_op jit(solution)/shard_map/ppermute | solution.py:1096
  388.7 2.0 collective-permute-start.29
  390.7 15.4 %collective-permute-done.23 = bf16[880,128]{1,0:T(8,128)(2,1)S(1)} collective-permute-done((bf16[880,128]{1,0:T(8,128)(2,1)S(1)}, bf16[880,128]{1,0:T(8,128)(2,1)S(1)}, u32[]{:S(2)}, u32[]{:S(2)}) %collective-permute-start.23) | collective-permute-done | bytes 225312 | tf_op jit(solution)/shard_map/ppermute | solution.py:1096
  406.3 7.8 %collective-permute-done.29 = bf16[1760,128]{1,0:T(8,128)(2,1)S(1)} collective-permute-done((bf16[1760,128]{1,0:T(8,128)(2,1)S(1)}, bf16[1760,128]{1,0:T(8,128)(2,1)S(1)}, u32[]{:S(2)}, u32[]{:S(2)}) %collective-permute-start.29) | collective-permute-done | bytes 450592 | tf_op jit(solution)/shard_map/ppermute | solution.py:1096
  414.3 9.3 %collective-permute-done.24 = bf16[1760,128]{1,0:T(8,128)(2,1)S(1)} collective-permute-done((bf16[1760,128]{1,0:T(8,128)(2,1)S(1)}, bf16[1760,128]{1,0:T(8,128)(2,1)S(1)}, u32[]{:S(2)}, u32[]{:S(2)}) %collective-permute-start.24) | collective-permute-done | bytes 450592 | tf_op jit(solution)/shard_map/ppermute | solution.py:1096
  423.9 11.5 %add_divide_fusion = (f32[900608]{0:T(1024)}, f32[900608]{0:T(1024)}, f32[900608]{0:T(1024)}) fusion(bf16[3520,128]{1,0:T(8,128)(2,1)S(1)} %maximum_select_fusion.1, bf16[3520,128]{1,0:T(8,128)(2,1)S(1)} %maximum_select_fusion, f32[900608]{0:T(1024)S(1)} %copy-done.3, f32[900608]{0:T(1024)} %param.19), kind=kLoop, calls=%fused_computation.5 | loop fusion | flops 14409728 | bytes 19814400 | tf_op jit(solution)/shard_map/div | solution.py:1108
  (103 shorter events, 17.0 us)
Async XLA Ops:
  2.9 24.3 %copy-start = (bf16[3520,128]{1,0:T(8,128)(2,1)}, bf16[3520,128]{1,0:T(8,128)(2,1)S(1)}, u32[]{:S(2)}) copy-start(bf16[3520,128]{1,0:T(8,128)(2,1)S(1)} %slice_bitcast_fusion.1.rest_0_) | copy-start | bytes 2703364
  3.0 29.7 %copy-start.1 = (bf16[3520,128]{1,0:T(8,128)(2,1)}, bf16[3520,128]{1,0:T(8,128)(2,1)S(1)}, u32[]{:S(2)}) copy-start(bf16[3520,128]{1,0:T(8,128)(2,1)S(1)} %pad.12.rest_1_) | copy-start | bytes 2703364
  3.1 23.0 %collective-permute-start = (bf16[3520,128]{1,0:T(8,128)(2,1)S(1)}, bf16[3520,128]{1,0:T(8,128)(2,1)S(1)}, u32[]{:S(2)}, u32[]{:S(2)}) collective-permute-start(bf16[3520,128]{1,0:T(8,128)(2,1)S(1)} %slice_bitcast_fusion.1.rest_0_), channel_id=1, source_target_pairs={{0,2},{1,3},{2,0},{3,1},{4,6},{5,7},{6,4},{7,5},{8,10},{9,11},{10,... | collective-permute-start | bytes 2703368 | tf_op jit(solution)/shard_map/ppermute | solution.py:186
  6.1 27.2 %collective-permute-start.4 = (bf16[3520,128]{1,0:T(8,128)(2,1)S(1)}, bf16[3520,128]{1,0:T(8,128)(2,1)}, u32[]{:S(2)}, u32[]{:S(2)}) collective-permute-start(bf16[3520,128]{1,0:T(8,128)(2,1)S(1)} %slice_bitcast_fusion.1.rest_0_), channel_id=1, source_target_pairs={{0,1},{1,0},{2,3},{3,2},{4,5},{5,4},{6,7},{7,6},{8,9},{9,8},{10,11... | collective-permute-start | bytes 2703368 | tf_op jit(solution)/shard_map/ppermute | solution.py:186
  6.1 22.9 %collective-permute-start.1 = (bf16[3520,128]{1,0:T(8,128)(2,1)S(1)}, bf16[3520,128]{1,0:T(8,128)(2,1)}, u32[]{:S(2)}, u32[]{:S(2)}) collective-permute-start(bf16[3520,128]{1,0:T(8,128)(2,1)S(1)} %pad.12.rest_1_), channel_id=1, source_target_pairs={{0,4},{1,5},{2,6},{3,7},{4,0},{5,1},{6,2},{7,3},{8,12},{9,13},{10,... | collective-permute-start | bytes 2703368 | tf_op jit(solution)/shard_map/ppermute | solution.py:186
  7.6 48.1 %copy-start.17 = (s32[2,512]{1,0:T(2,128)S(1)}, s32[2,512]{1,0:T(2,128)}, u32[]{:S(2)}) copy-start(s32[2,512]{1,0:T(2,128)} %param.13) | copy-start | bytes 12292
  26.1 6.7 %copy-start.2 = (bf16[3520,128]{1,0:T(8,128)(2,1)}, bf16[3520,128]{1,0:T(8,128)(2,1)S(1)}, u32[]{:S(2)}) copy-start(bf16[3520,128]{1,0:T(8,128)(2,1)S(1)} %collective-permute-done.rest_2_) | copy-start | bytes 2703364
  27.2 21.4 %collective-permute-start.2 = (bf16[3520,128]{1,0:T(8,128)(2,1)S(1)}, bf16[3520,128]{1,0:T(8,128)(2,1)}, u32[]{:S(2)}, u32[]{:S(2)}) collective-permute-start(bf16[3520,128]{1,0:T(8,128)(2,1)S(1)} %get-tuple-element.140), channel_id=1, source_target_pairs={{0,4},{1,5},{2,6},{3,7},{4,0},{5,1},{6,2},{7,3},{8,12},{9,13},{10,... | collective-permute-start | bytes 2703368 | tf_op jit(solution)/shard_map/ppermute | solution.py:186
  31.3 21.3 %collective-permute-start.3 = (bf16[3520,128]{1,0:T(8,128)(2,1)S(1)}, bf16[3520,128]{1,0:T(8,128)(2,1)}, u32[]{:S(2)}, u32[]{:S(2)}) collective-permute-start(bf16[3520,128]{1,0:T(8,128)(2,1)S(1)} %get-tuple-element.138), channel_id=1, source_target_pairs={{0,2},{1,3},{2,0},{3,1},{4,6},{5,7},{6,4},{7,5},{8,10},{9,11},{10,... | collective-permute-start | bytes 2703368 | tf_op jit(solution)/shard_map/ppermute | solution.py:186
  32.8 19.8 %collective-permute-start.5 = (bf16[3520,128]{1,0:T(8,128)(2,1)S(1)}, bf16[3520,128]{1,0:T(8,128)(2,1)S(1)}, u32[]{:S(2)}, u32[]{:S(2)}) collective-permute-start(bf16[3520,128]{1,0:T(8,128)(2,1)S(1)} %pad.12.rest_1_), channel_id=1, source_target_pairs={{0,1},{1,0},{2,3},{3,2},{4,5},{5,4},{6,7},{7,6},{8,9},{9,8},{10,11... | collective-permute-start | bytes 2703368 | tf_op jit(solution)/shard_map/ppermute | solution.py:186
  32.8 21.4 %collective-permute-start.6 = (bf16[3520,128]{1,0:T(8,128)(2,1)S(1)}, bf16[3520,128]{1,0:T(8,128)(2,1)S(1)}, u32[]{:S(2)}, u32[]{:S(2)}) collective-permute-start(bf16[3520,128]{1,0:T(8,128)(2,1)S(1)} %collective-permute-done.rest_2_), channel_id=1, source_target_pairs={{0,1},{1,0},{2,3},{3,2},{4,5},{5,4},{6,7},{7,6},{8,9},{9,8},{10,11... | collective-permute-start | bytes 2703368 | tf_op jit(solution)/shard_map/ppermute | solution.py:186
  33.3 24.0 %collective-permute-start.7 = (bf16[3520,128]{1,0:T(8,128)(2,1)}, bf16[3520,128]{1,0:T(8,128)(2,1)S(1)}, u32[]{:S(2)}, u32[]{:S(2)}) collective-permute-start(bf16[3520,128]{1,0:T(8,128)(2,1)} %collective-permute-done.1.rest_3_), channel_id=1, source_target_pairs={{0,1},{1,0},{2,3},{3,2},{4,5},{5,4},{6,7},{7,6},{8,9},{9,8},{10,11... | collective-permute-start | bytes 2703368 | tf_op jit(solution)/shard_map/ppermute | solution.py:186
  48.6 8.7 %collective-permute-start.8 = (bf16[3520,128]{1,0:T(8,128)(2,1)}, bf16[3520,128]{1,0:T(8,128)(2,1)}, u32[]{:S(2)}, u32[]{:S(2)}) collective-permute-start(bf16[3520,128]{1,0:T(8,128)(2,1)} %collective-permute-done.2.rest_4_), channel_id=1, source_target_pairs={{0,1},{1,0},{2,3},{3,2},{4,5},{5,4},{6,7},{7,6},{8,9},{9,8},{10,11... | collective-permute-start | bytes 2703368 | tf_op jit(solution)/shard_map/ppermute | solution.py:186
  52.6 4.7 %collective-permute-start.9 = (bf16[3520,128]{1,0:T(8,128)(2,1)}, bf16[3520,128]{1,0:T(8,128)(2,1)}, u32[]{:S(2)}, u32[]{:S(2)}) collective-permute-start(bf16[3520,128]{1,0:T(8,128)(2,1)} %collective-permute-done.3.rest_5_), channel_id=1, source_target_pairs={{0,1},{1,0},{2,3},{3,2},{4,5},{5,4},{6,7},{7,6},{8,9},{9,8},{10,11... | collective-permute-start | bytes 2703368 | tf_op jit(solution)/shard_map/ppermute | solution.py:186
  52.6 1.6 copy-start.4
  52.6 28.6 %collective-permute-start.10 = (bf16[3520,128]{1,0:T(8,128)(2,1)}, bf16[3520,128]{1,0:T(8,128)(2,1)S(1)}, u32[]{:S(2)}, u32[]{:S(2)}) collective-permute-start(bf16[3520,128]{1,0:T(8,128)(2,1)} %get-tuple-element.139), channel_id=1, source_target_pairs={{0,4},{1,5},{2,6},{3,7},{4,0},{5,1},{6,2},{7,3},{8,12},{9,13},{10,... | collective-permute-start | bytes 2703368 | tf_op jit(solution)/shard_map/ppermute | solution.py:186
  55.2 26.1 %collective-permute-start.11 = (bf16[3520,128]{1,0:T(8,128)(2,1)}, bf16[3520,128]{1,0:T(8,128)(2,1)S(1)}, u32[]{:S(2)}, u32[]{:S(2)}) collective-permute-start(bf16[3520,128]{1,0:T(8,128)(2,1)} %get-tuple-element.137), channel_id=1, source_target_pairs={{0,2},{1,3},{2,0},{3,1},{4,6},{5,7},{6,4},{7,5},{8,10},{9,11},{10,... | collective-permute-start | bytes 2703368 | tf_op jit(solution)/shard_map/ppermute | solution.py:186
  63.0 18.8 %copy-start.20 = (s32[8]{0:T(128)S(1)}, s32[8]{0:T(128)}, u32[]{:S(2)}) copy-start(s32[8]{0:T(128)} %constant.67.clone) | copy-start | bytes 100
  63.1 18.8 %copy-start.21 = (s32[8]{0:T(128)S(1)}, s32[8]{0:T(128)}, u32[]{:S(2)}) copy-start(s32[8]{0:T(128)} %constant.66.clone) | copy-start | bytes 100
  63.1 18.8 %copy-start.22 = (s32[8]{0:T(128)S(1)}, s32[8]{0:T(128)}, u32[]{:S(2)}) copy-start(s32[8]{0:T(128)} %constant.69.clone) | copy-start | bytes 100
  63.1 18.8 %copy-start.23 = (s32[8]{0:T(128)S(1)}, s32[8]{0:T(128)}, u32[]{:S(2)}) copy-start(s32[8]{0:T(128)} %constant.68.clone) | copy-start | bytes 100
  63.1 19.3 %copy-start.18 = (s32[2,8]{1,0:T(2,128)S(1)}, s32[2,8]{1,0:T(2,128)}, u32[]{:S(2)}) copy-start(s32[2,8]{1,0:T(2,128)} %param.15) | copy-start | bytes 196
  63.1 19.3 %copy-start.19 = (s32[2,8]{1,0:T(2,128)S(1)}, s32[2,8]{1,0:T(2,128)}, u32[]{:S(2)}) copy-start(s32[2,8]{1,0:T(2,128)} %param.14) | copy-start | bytes 196
  81.2 20.2 %copy-start.8 = (bf16[3520,128]{1,0:T(8,128)(2,1)}, bf16[3520,128]{1,0:T(8,128)(2,1)S(1)}, u32[]{:S(2)}) copy-start(bf16[3520,128]{1,0:T(8,128)(2,1)S(1)} %collective-permute-done.10.rest_6_) | copy-start | bytes 2703364
  81.3 20.2 %copy-start.9 = (bf16[3520,128]{1,0:T(8,128)(2,1)}, bf16[3520,128]{1,0:T(8,128)(2,1)S(1)}, u32[]{:S(2)}) copy-start(bf16[3520,128]{1,0:T(8,128)(2,1)S(1)} %collective-permute-done.11.rest_7_) | copy-start | bytes 2703364
  81.3 20.2 %collective-permute-start.12 = (bf16[3520,128]{1,0:T(8,128)(2,1)S(1)}, bf16[3520,128]{1,0:T(8,128)(2,1)S(1)}, u32[]{:S(2)}, u32[]{:S(2)}) collective-permute-start(bf16[3520,128]{1,0:T(8,128)(2,1)S(1)} %collective-permute-done.10.rest_6_), channel_id=1, source_target_pairs={{0,1},{1,0},{2,3},{3,2},{4,5},{5,4},{6,7},{7,6},{8,9},{9,8},{10,11... | collective-permute-start | bytes 2703368 | tf_op jit(solution)/shard_map/ppermute | solution.py:186
  81.3 20.1 %collective-permute-start.13 = (bf16[3520,128]{1,0:T(8,128)(2,1)S(1)}, bf16[3520,128]{1,0:T(8,128)(2,1)}, u32[]{:S(2)}, u32[]{:S(2)}) collective-permute-start(bf16[3520,128]{1,0:T(8,128)(2,1)S(1)} %collective-permute-done.11.rest_7_), channel_id=1, source_target_pairs={{0,1},{1,0},{2,3},{3,2},{4,5},{5,4},{6,7},{7,6},{8,9},{9,8},{10,11... | collective-permute-start | bytes 2703368 | tf_op jit(solution)/shard_map/ppermute | solution.py:186
  222.3 16.4 %collective-permute-start.14 = (bf16[3,7040,128]{2,1,0:T(8,128)(2,1)}, bf16[3,7040,128]{2,1,0:T(8,128)(2,1)}, u32[]{:S(2)}, u32[]{:S(2)}) collective-permute-start(bf16[3,7040,128]{2,1,0:T(8,128)(2,1)} %get-tuple-element.101), channel_id=1, source_target_pairs={{0,1},{1,0},{2,3},{3,2},{4,5},{5,4},{6,7},{7,6},{8,9},{9,8},{10,11... | collective-permute-start | bytes 16220168 | tf_op jit(solution)/shard_map/ppermute | solution.py:186
  247.3 22.6 %collective-permute-start.15 = (bf16[3520,128]{1,0:T(8,128)(2,1)}, bf16[3520,128]{1,0:T(8,128)(2,1)S(1)}, u32[]{:S(2)}, u32[]{:S(2)}) collective-permute-start(bf16[3520,128]{1,0:T(8,128)(2,1)} %get-tuple-element.108), channel_id=1, source_target_pairs={{0,4},{1,5},{2,6},{3,7},{4,0},{5,1},{6,2},{7,3},{8,12},{9,13},{10,... | collective-permute-start | bytes 2703368 | tf_op jit(solution)/shard_map/ppermute | solution.py:186
  248.3 22.3 %collective-permute-start.16 = (bf16[3520,128]{1,0:T(8,128)(2,1)}, bf16[3520,128]{1,0:T(8,128)(2,1)S(1)}, u32[]{:S(2)}, u32[]{:S(2)}) collective-permute-start(bf16[3520,128]{1,0:T(8,128)(2,1)} %get-tuple-element.109), channel_id=1, source_target_pairs={{0,2},{1,3},{2,0},{3,1},{4,6},{5,7},{6,4},{7,5},{8,10},{9,11},{10,... | collective-permute-start | bytes 2703368 | tf_op jit(solution)/shard_map/ppermute | solution.py:186
  269.9 11.8 %copy-start.13 = (bf16[3520,128]{1,0:T(8,128)(2,1)}, bf16[3520,128]{1,0:T(8,128)(2,1)S(1)}, u32[]{:S(2)}) copy-start(bf16[3520,128]{1,0:T(8,128)(2,1)S(1)} %collective-permute-done.15.y_one) | copy-start | bytes 2703364
  270.6 11.1 %copy-start.14 = (bf16[3520,128]{1,0:T(8,128)(2,1)}, bf16[3520,128]{1,0:T(8,128)(2,1)S(1)}, u32[]{:S(2)}) copy-start(bf16[3520,128]{1,0:T(8,128)(2,1)S(1)} %collective-permute-done.16.x_one) | copy-start | bytes 2703364
  281.7 4.0 collective-permute-start.17
  285.7 1.2 copy-start.7
  292.7 22.3 %collective-permute-start.18 = (bf16[3520,128]{1,0:T(8,128)(2,1)}, bf16[3520,128]{1,0:T(8,128)(2,1)S(1)}, u32[]{:S(2)}, u32[]{:S(2)}) collective-permute-start(bf16[3520,128]{1,0:T(8,128)(2,1)} %get-tuple-element.122), channel_id=1, source_target_pairs={{0,4},{1,5},{2,6},{3,7},{4,0},{5,1},{6,2},{7,3},{8,12},{9,13},{10,... | collective-permute-start | bytes 2703368 | tf_op jit(solution)/shard_map/ppermute | solution.py:186
  293.6 22.0 %collective-permute-start.19 = (bf16[3520,128]{1,0:T(8,128)(2,1)}, bf16[3520,128]{1,0:T(8,128)(2,1)S(1)}, u32[]{:S(2)}, u32[]{:S(2)}) collective-permute-start(bf16[3520,128]{1,0:T(8,128)(2,1)} %get-tuple-element.129), channel_id=1, source_target_pairs={{0,2},{1,3},{2,0},{3,1},{4,6},{5,7},{6,4},{7,5},{8,10},{9,11},{10,... | collective-permute-start | bytes 2703368 | tf_op jit(solution)/shard_map/ppermute | solution.py:186
  323.1 27.3 %copy-start.11 = (bf16[3520,128]{1,0:T(8,128)(2,1)S(1)}, bf16[3520,128]{1,0:T(8,128)(2,1)}, u32[]{:S(2)}) copy-start(bf16[3520,128]{1,0:T(8,128)(2,1)} %get-tuple-element.130) | copy-start | bytes 2703364
  323.1 21.3 %collective-permute-start.25 = (bf16[3520,128]{1,0:T(8,128)(2,1)}, bf16[3520,128]{1,0:T(8,128)(2,1)S(1)}, u32[]{:S(2)}, u32[]{:S(2)}) collective-permute-start(bf16[3520,128]{1,0:T(8,128)(2,1)} %get-tuple-element.133), channel_id=1, source_target_pairs={{0,4},{1,5},{2,6},{3,7},{4,0},{5,1},{6,2},{7,3},{8,12},{9,13},{10,... | collective-permute-start | bytes 2703368 | tf_op jit(solution)/shard_map/ppermute | solution.py:186
  324.4 25.9 %collective-permute-start.20 = (bf16[3520,128]{1,0:T(8,128)(2,1)}, bf16[3520,128]{1,0:T(8,128)(2,1)S(1)}, u32[]{:S(2)}, u32[]{:S(2)}) collective-permute-start(bf16[3520,128]{1,0:T(8,128)(2,1)} %get-tuple-element.131), channel_id=1, source_target_pairs={{0,2},{1,3},{2,0},{3,1},{4,6},{5,7},{6,4},{7,5},{8,10},{9,11},{10,... | collective-permute-start | bytes 2703368 | tf_op jit(solution)/shard_map/ppermute | solution.py:186
  347.8 21.3 %collective-permute-start.26 = (bf16[1760,128]{1,0:T(8,128)(2,1)}, bf16[1760,128]{1,0:T(8,128)(2,1)S(1)}, u32[]{:S(2)}, u32[]{:S(2)}) collective-permute-start(bf16[1760,128]{1,0:T(8,128)(2,1)} %dynamic-slice_bitcast_fusion), channel_id=1, source_target_pairs={{0,16},{8,24},{16,0},{24,8},{1,17},{9,25},{17,1},{25,9},{2,18},{10... | collective-permute-start | bytes 1351688 | tf_op jit(solution)/shard_map/ppermute | solution.py:1096
  350.6 19.2 %collective-permute-start.21 = (bf16[1760,128]{1,0:T(8,128)(2,1)S(1)}, bf16[1760,128]{1,0:T(8,128)(2,1)S(1)}, u32[]{:S(2)}, u32[]{:S(2)}) collective-permute-start(bf16[1760,128]{1,0:T(8,128)(2,1)S(1)} %dynamic-slice_bitcast_fusion.1), channel_id=1, source_target_pairs={{0,8},{8,0},{16,24},{24,16},{1,9},{9,1},{17,25},{25,17},{2,10},{10... | collective-permute-start | bytes 1351688 | tf_op jit(solution)/shard_map/ppermute | solution.py:1096
  369.2 12.4 %collective-permute-start.27 = (bf16[880,128]{1,0:T(8,128)(2,1)S(1)}, bf16[880,128]{1,0:T(8,128)(2,1)S(1)}, u32[]{:S(2)}, u32[]{:S(2)}) collective-permute-start(bf16[880,128]{1,0:T(8,128)(2,1)S(1)} %dynamic-slice_bitcast_fusion.2), channel_id=1, source_target_pairs={{0,8},{8,0},{16,24},{24,16},{1,9},{9,1},{17,25},{25,17},{2,10},{10... | collective-permute-start | bytes 675848 | tf_op jit(solution)/shard_map/ppermute | solution.py:1096
  370.0 13.8 %collective-permute-start.22 = (bf16[880,128]{1,0:T(8,128)(2,1)S(1)}, bf16[880,128]{1,0:T(8,128)(2,1)S(1)}, u32[]{:S(2)}, u32[]{:S(2)}) collective-permute-start(bf16[880,128]{1,0:T(8,128)(2,1)S(1)} %dynamic-slice_bitcast_fusion.3), channel_id=1, source_target_pairs={{0,16},{8,24},{16,0},{24,8},{1,17},{9,25},{17,1},{25,9},{2,18},{10... | collective-permute-start | bytes 675848 | tf_op jit(solution)/shard_map/ppermute | solution.py:1096
  381.6 7.0 %collective-permute-start.28 = (bf16[880,128]{1,0:T(8,128)(2,1)S(1)}, bf16[880,128]{1,0:T(8,128)(2,1)S(1)}, u32[]{:S(2)}, u32[]{:S(2)}) collective-permute-start(bf16[880,128]{1,0:T(8,128)(2,1)S(1)} %bitcast_add_fusion.2), channel_id=1, source_target_pairs={{0,8},{8,0},{16,24},{24,16},{1,9},{9,1},{17,25},{25,17},{2,10},{10... | collective-permute-start | bytes 675848 | tf_op jit(solution)/shard_map/ppermute | solution.py:1096
  383.8 22.3 %collective-permute-start.23 = (bf16[880,128]{1,0:T(8,128)(2,1)S(1)}, bf16[880,128]{1,0:T(8,128)(2,1)S(1)}, u32[]{:S(2)}, u32[]{:S(2)}) collective-permute-start(bf16[880,128]{1,0:T(8,128)(2,1)S(1)} %bitcast_add_fusion.3), channel_id=1, source_target_pairs={{0,16},{8,24},{16,0},{24,8},{1,17},{9,25},{17,1},{25,9},{2,18},{10... | collective-permute-start | bytes 675848 | tf_op jit(solution)/shard_map/ppermute | solution.py:1096
  388.7 25.4 %collective-permute-start.29 = (bf16[1760,128]{1,0:T(8,128)(2,1)S(1)}, bf16[1760,128]{1,0:T(8,128)(2,1)S(1)}, u32[]{:S(2)}, u32[]{:S(2)}) collective-permute-start(bf16[1760,128]{1,0:T(8,128)(2,1)S(1)} %maximum_select_fusion.3), channel_id=1, source_target_pairs={{0,16},{8,24},{16,0},{24,8},{1,17},{9,25},{17,1},{25,9},{2,18},{10... | collective-permute-start | bytes 1351688 | tf_op jit(solution)/shard_map/ppermute | solution.py:1096
  390.7 33.2 %copy-start.3 = (f32[900608]{0:T(1024)S(1)}, f32[900608]{0:T(1024)}, u32[]{:S(2)}) copy-start(f32[900608]{0:T(1024)} %param.18) | copy-start | bytes 10807300
  406.2 17.4 %collective-permute-start.24 = (bf16[1760,128]{1,0:T(8,128)(2,1)S(1)}, bf16[1760,128]{1,0:T(8,128)(2,1)S(1)}, u32[]{:S(2)}, u32[]{:S(2)}) collective-permute-start(bf16[1760,128]{1,0:T(8,128)(2,1)S(1)} %maximum_select_fusion.2), channel_id=1, source_target_pairs={{0,8},{8,0},{16,24},{24,16},{1,9},{9,1},{17,25},{25,17},{2,10},{10... | collective-permute-start | bytes 1351688 | tf_op jit(solution)/shard_map/ppermute | solution.py:1096
  (6 other events, 5.6 us)

commit v3 on v2

--- a/solution.py
+++ b/solution.py
@@ -18,7 +18,7 @@
 SEGS = 8
 EXR = 8
 LANE = 128
-CHUNK = 160
+CHUNK = 352
 
 NORM_EPS = 1e-12
 MASKED = -1e30
@@ -69,6 +69,8 @@
 VM = pl.BlockSpec(memory_space=pltpu.VMEM)
 ANY = pl.BlockSpec(memory_space=pl.ANY)
 
+TINY = pl.CostEstimate(flops=1, bytes_accessed=1, transcendentals=0)
+
 NN = (((1,), (0,)), ((), ()))
 NT = (((1,), (1,)), ((), ()))
 TN = (((0,), (0,)), ((), ()))
@@ -243,7 +245,7 @@
             pltpu.SemaphoreType.DMA((4,)),
         ],
         compiler_params=params_of(),
-        cost_estimate=pl.CostEstimate(flops=0, bytes_accessed=20 << 20, transcendentals=0),
+        cost_estimate=TINY,
         name="unpack_first",
     )(me, *pieces)
 
@@ -279,7 +281,7 @@
             pltpu.SemaphoreType.DMA((4,)),
         ],
         compiler_params=params_of(),
-        cost_estimate=pl.CostEstimate(flops=0, bytes_accessed=60 << 20, transcendentals=0),
+        cost_estimate=TINY,
         name="unpack_rest",
     )(owners, *pieces)
 
@@ -310,70 +312,68 @@
     return first, finish
 
 
-def half_masks():
+def both_heads(v):
     lane = lax.broadcasted_iota(jnp.int32, (1, LANE), 1)
-    return ((lane < 64).astype(F32).astype(BF), (lane >= 64).astype(F32).astype(BF))
-
-
-def attend_kernel(x_ref, segc_ref, segr_ref, w_ref, bq_ref, qkv_ref, p_ref, att_ref, bias):
-    def project(t, _):
-        cols = at(t, 256)
-        r = dot(x_ref[0], w_ref[:, cols])
-        qkv_ref[0, :, cols] = ((r + bq_ref[0:1, cols]) * bq_ref[1:2, cols]).astype(BF)
-        return 0
-
-    lax.fori_loop(0, 3 * D // 256, project, 0)
-
-    for i, (lo, hi) in enumerate(WINDOWS):
-        bias[:, OFFSETS[i] : OFFSETS[i] + hi - lo] = jnp.where(
-            segc_ref[0, i * QB : (i + 1) * QB, :] == segr_ref[0, :, lo:hi], 0.0, MASKED
-        )
-
-    masks = half_masks()
-
-    def pair(p, _):
-        q2 = qkv_ref[0, :, at(p, LANE)]
-        k2 = qkv_ref[0, :, at(p + PAIRS, LANE)]
-        v2 = qkv_ref[0, :, at(p + 2 * PAIRS, LANE)]
+    left, right = (lane < 64).astype(F32).astype(BF), (lane >= 64).astype(F32).astype(BF)
+    return jnp.concatenate([v * left, v * right], axis=0)
+
+
+def own_lanes(v):
+    n = v.shape[0] // 2
+    lane = lax.broadcasted_iota(jnp.int32, (1, LANE), 1)
+    return jnp.where(lane < 64, v[:n], v[n:])
+
+
+def attend_kernel(x_ref, segc_ref, segr_ref, wq_ref, wk_ref, wv_ref, bq_ref, q_ref, k_ref, v_ref, p_ref, att_ref, bias):
+    step = pl.program_id(1)
+
+    @pl.when(step == 0)
+    def _():
         for i, (lo, hi) in enumerate(WINDOWS):
-            out = jnp.zeros((QB, LANE), F32)
+            here = jnp.where(segc_ref[0, i * QB : (i + 1) * QB, :] == segr_ref[0, :, lo:hi], 0.0, MASKED)
             for h in range(2):
-                s = dot(q2[i * QB : (i + 1) * QB] * masks[h], k2[lo:hi], NT)
-                s = s + bias[:, OFFSETS[i] : OFFSETS[i] + hi - lo]
-                e = jnp.exp(s - jnp.max(s, axis=-1, keepdims=True))
-                a = (e * (1.0 / jnp.sum(e, axis=-1, keepdims=True))).astype(BF)
-                p_ref[0, 2 * p + h, :, OFFSETS[i] : OFFSETS[i] + hi - lo] = a
-                out = out + dot(a, v2[lo:hi] * masks[h])
-            att_ref[0, i * QB : (i + 1) * QB, at(p, LANE)] = out.astype(BF)
-        return 0
-
-    lax.fori_loop(0, PAIRS, pair, 0)
+                bias[h * QB : (h + 1) * QB, OFFSETS[i] : OFFSETS[i] + hi - lo] = here
+
+    for n, (w_ref, out_ref) in enumerate(((wq_ref, q_ref), (wk_ref, k_ref), (wv_ref, v_ref))):
+        cols = at(step + n * (D // 256), 256)
+        out_ref[0] = ((dot(x_ref[0], w_ref[...]) + bq_ref[0:1, cols]) * bq_ref[1:2, cols]).astype(BF)
+
+    for p in range(2):
+        lanes = slice(p * LANE, (p + 1) * LANE)
+        soft = []
+        for i, (lo, hi) in enumerate(WINDOWS):
+            span = slice(OFFSETS[i], OFFSETS[i] + hi - lo)
+            s = dot(both_heads(q_ref[0, i * QB : (i + 1) * QB, lanes]), k_ref[0, lo:hi, lanes], NT) + bias[:, span]
+            e = jnp.exp(s - jnp.max(s, axis=-1, keepdims=True))
+            a = (e * (1.0 / jnp.sum(e, axis=-1, keepdims=True))).astype(BF)
+            p_ref[0, p, :, span] = a
+            soft.append(a)
+        for i, (lo, hi) in enumerate(WINDOWS):
+            att_ref[0, i * QB : (i + 1) * QB, lanes] = own_lanes(dot(soft[i], v_ref[0, lo:hi, lanes])).astype(BF)
 
 
 def row_spec(*shape):
     return pl.BlockSpec((1, *shape), lambda r: (r,) + (0,) * len(shape))
 
 
-def attend(row, x, segc, segr, wqkv, bq, done):
+def attend(x, segc, segr, wqkv, bq):
     rows = x.shape[0]
-    only = lambda *shape: pl.BlockSpec((1, *shape), lambda _: (row,) + (0,) * len(shape))
-    outs = [SDS((rows, LEN, 3 * D), BF), SDS((rows, HEADS, QB, WIDE), BF), SDS((rows, LEN, D), BF)]
-
-    def kernel(*refs):
-        attend_kernel(*refs[:5], *refs[5 + len(done) :])
-
-    return pl.pallas_call(
-        kernel,
-        grid=(1,),
-        in_specs=[only(LEN, D), only(LEN, 1), only(1, LEN), VM, VM] + [ANY] * len(done),
-        out_specs=[only(LEN, 3 * D), only(HEADS, QB, WIDE), only(LEN, D)],
-        out_shape=outs,
-        scratch_shapes=[pltpu.VMEM((QB, WIDE), F32)],
-        input_output_aliases={5 + i: i for i in range(len(done))},
-        compiler_params=params_of(),
-        cost_estimate=pl.CostEstimate(flops=6 * 10**9, bytes_accessed=12 << 20, transcendentals=4 * 10**6),
+    only = lambda *shape: pl.BlockSpec((1, *shape), lambda r, g: (r,) + (0,) * len(shape))
+    tall = pl.BlockSpec((1, LEN, 256), lambda r, g: (r, 0, g))
+    weights = [pl.BlockSpec((D, 256), lambda r, g, n=n: (0, g + n * (D // 256))) for n in range(3)]
+    probs = pl.BlockSpec((1, 2, 2 * QB, WIDE), lambda r, g: (r, g, 0, 0))
+    token = SDS((rows, LEN, D), BF)
+    return pl.pallas_call(
+        attend_kernel,
+        grid=(rows, D // 256),
+        in_specs=[only(LEN, D), only(LEN, 1), only(1, LEN)] + weights + [whole(8, 3 * D)],
+        out_specs=[tall, tall, tall, probs, tall],
+        out_shape=[token, token, token, SDS((rows, PAIRS, 2 * QB, WIDE), BF), token],
+        scratch_shapes=[pltpu.VMEM((2 * QB, WIDE), F32)],
+        compiler_params=params_of(),
+        cost_estimate=TINY,
         name="attend",
-    )(x, segc, segr, wqkv, bq, *done)
+    )(x, segc, segr, wqkv, wqkv, wqkv, bq)
 
 
 TB = 64
@@ -432,11 +432,11 @@
         gcls_ref[...] = jnp.zeros_like(gcls_ref)
 
     def first(t, _):
-        cols = at(t, 256)
+        cols = at(t, 384)
         hid[:, cols] = x_ref[0, :, cols].astype(F32) + (dot(att_ref[0], wout[:, cols]) + vec[0:1, cols])
         return 0
 
-    lax.fori_loop(0, D // 256, first, 0)
+    lax.fori_loop(0, D // 384, first, 0)
 
     def norm_one(b, _):
         rows = at(b, TB)
@@ -454,15 +454,15 @@
     lax.fori_loop(0, LEN // TB, norm_one, 0)
 
     def inner(t, _):
-        cols = at(t, 256)
-        bias = vec[pl.ds(8 + t // 3, 1), at(t % 3, 256)]
+        cols = at(t, D)
+        bias = vec[pl.ds(8 + t, 1), :]
         u = dot(nbf_ref[0], win[:, cols]) + bias
         cdf = 0.5 * (1.0 + lax.erf(u * (0.5**0.5)))
         act_ref[0, :, cols] = (u * cdf).astype(BF)
         gp[:, cols] = cdf + u * (jnp.exp(-0.5 * u * u) * (1.0 / math.sqrt(2.0 * math.pi)))
         return 0
 
-    lax.fori_loop(0, FF // 256, inner, 0)
+    lax.fori_loop(0, FF // D, inner, 0)
 
     def second(t, _):
         cols = at(t, 256)
@@ -525,11 +525,11 @@
     sg_ref[3:4, :] += jnp.sum(dl, axis=0, keepdims=True)
 
     def spread(t, _):
-        cols = at(t, 256)
+        cols = at(t, 384)
         hid[:, cols] = cot_ref[0, :, cols].astype(F32) + dot(dstu_ref[0], wstu[cols, :], NT)
         return 0
 
-    lax.fori_loop(0, D // 256, spread, 0)
+    lax.fori_loop(0, D // 384, spread, 0)
 
     def back_two(b, _):
         rows = at(b, TB)
@@ -549,20 +549,20 @@
     lax.fori_loop(0, LEN // TB, back_two, 0)
 
     def outer(t, _):
-        cols = at(t, 256)
+        cols = at(t, D)
         d = dot(dffn_ref[0], wback[cols, :], NT) * gp[:, cols]
         accb[:, cols] += fold(d)
         dinner_ref[0, :, cols] = d.astype(BF)
         return 0
 
-    lax.fori_loop(0, FF // 256, outer, 0)
+    lax.fori_loop(0, FF // D, outer, 0)
 
     def third(t, _):
-        cols = at(t, 256)
+        cols = at(t, D)
         hid[:, cols] += dot(dinner_ref[0], win[cols, :], NT)
         return 0
 
-    lax.fori_loop(0, D // 256, third, 0)
+    lax.fori_loop(0, D // D, third, 0)
 
     def back_one(b, _):
         rows = at(b, TB)
@@ -582,11 +582,11 @@
     lax.fori_loop(0, LEN // TB, back_one, 0)
 
     def fourth(t, _):
-        cols = at(t, 256)
+        cols = at(t, 384)
         datt_ref[0, :, cols] = dot(dbr_ref[0], wout[cols, :], NT).astype(BF)
         return 0
 
-    lax.fori_loop(0, D // 256, fourth, 0)
+    lax.fori_loop(0, D // 384, fourth, 0)
 
     @pl.when(r == pl.num_programs(0) - 1)
     def _():
@@ -666,110 +666,108 @@
             pltpu.VMEM((8, FF), F32),
         ],
         compiler_params=params_of(),
+        cost_estimate=TINY,
         name="middle",
     )(x, att, segc, hot, cot, wout, win, wback, wstu, wmid, vec, small, wcls)
 
 
-def retreat_kernel(begun, qkv_ref, p_ref, datt_ref, dproj_ref, bg_ref, dk, dv):
-    bg_ref[...] = jnp.zeros_like(bg_ref) if begun is None else begun[...]
-    masks = half_masks()
-
-    def pair(p, _):
-        q2 = qkv_ref[0, :, at(p, LANE)]
-        k2 = qkv_ref[0, :, at(p + PAIRS, LANE)]
-        v2 = qkv_ref[0, :, at(p + 2 * PAIRS, LANE)]
-        d2 = datt_ref[0, :, at(p, LANE)]
+def retreat_kernel(q_ref, k_ref, v_ref, p_ref, datt_ref, dq_ref, dk_ref, dv_ref, bg_ref, dk, dv):
+    for p in range(2):
+        lanes = slice(p * LANE, (p + 1) * LANE)
         dk[...] = jnp.zeros_like(dk)
         dv[...] = jnp.zeros_like(dv)
         bq = jnp.zeros((1, LANE), F32)
+        diffs = []
         for i, (lo, hi) in enumerate(WINDOWS):
-            dq = jnp.zeros((QB, LANE), F32)
-            for h in range(2):
-                a = p_ref[0, 2 * p + h, :, OFFSETS[i] : OFFSETS[i] + hi - lo]
-                da = d2[i * QB : (i + 1) * QB] * masks[h]
-                qh = q2[i * QB : (i + 1) * QB] * masks[h]
-                wide = a.astype(F32)
-                dp = dot(da, v2[lo:hi], NT)
-                t = wide * dp
-                ds = (t - wide * jnp.sum(t, axis=-1, keepdims=True)).astype(BF)
-                dq = dq + dot(ds, k2[lo:hi] * masks[h])
-                dk[lo:hi, :] += dot(ds, qh, TN)
-                dv[lo:hi, :] += dot(a, da, TN)
-            dq = dq * 0.125
+            a = p_ref[0, p, :, OFFSETS[i] : OFFSETS[i] + hi - lo]
+            da = both_heads(datt_ref[0, i * QB : (i + 1) * QB, lanes])
+            wide = a.astype(F32)
+            t = wide * dot(da, v_ref[0, lo:hi, lanes], NT)
+            diffs.append((t - wide * jnp.sum(t, axis=-1, keepdims=True)).astype(BF))
+            dv[lo:hi, :] += dot(a, da, TN)
+        for i, (lo, hi) in enumerate(WINDOWS):
+            dq = own_lanes(dot(diffs[i], k_ref[0, lo:hi, lanes])) * 0.125
+            dk[lo:hi, :] += dot(diffs[i], both_heads(q_ref[0, i * QB : (i + 1) * QB, lanes]), TN)
             bq = bq + jnp.sum(dq, axis=0, keepdims=True)
-            dproj_ref[0, i * QB : (i + 1) * QB, at(p, LANE)] = dq.astype(BF)
-        dproj_ref[0, :, at(p + PAIRS, LANE)] = dk[...].astype(BF)
-        dproj_ref[0, :, at(p + 2 * PAIRS, LANE)] = dv[...].astype(BF)
-        bg_ref[0:1, at(p, LANE)] += bq
-        bg_ref[1:2, at(p, LANE)] += jnp.sum(dv[...], axis=0, keepdims=True)
-        return 0
-
-    lax.fori_loop(0, PAIRS, pair, 0)
-
-
-def retreat(row, qkv, probs, datt, done):
-    rows = qkv.shape[0]
-    only = lambda *shape: pl.BlockSpec((1, *shape), lambda _: (row,) + (0,) * len(shape))
-
-    def kernel(qkv_ref, p_ref, datt_ref, *refs):
-        begun = refs[1] if done else None
-        retreat_kernel(begun, qkv_ref, p_ref, datt_ref, *refs[len(done) :])
+            dq_ref[0, i * QB : (i + 1) * QB, lanes] = dq.astype(BF)
+        dk_ref[0, :, lanes] = dk[...].astype(BF)
+        dv_ref[0, :, lanes] = dv[...].astype(BF)
+        bg_ref[0:1, lanes] += bq
+        bg_ref[1:2, lanes] += jnp.sum(dv[...], axis=0, keepdims=True)
+
+
+def retreat(row, q, k, v, probs, datt, done):
+    rows = q.shape[0]
+    tall = pl.BlockSpec((1, LEN, 256), lambda g: (row, 0, g))
+    sums = pl.BlockSpec((8, 256), lambda g: (0, g))
+    block = pl.BlockSpec((1, 2, 2 * QB, WIDE), lambda g: (row, g, 0, 0))
+    token = SDS((rows, LEN, D), BF)
+
+    def kernel(*refs):
+        ins, outs = refs[:5], refs[5 + len(done) :]
+        outs[3][...] = refs[8][...] if done else jnp.zeros_like(outs[3])
+        retreat_kernel(*ins, *outs)
 
     return pl.pallas_call(
         kernel,
-        grid=(1,),
-        in_specs=[only(LEN, 3 * D), only(HEADS, QB, WIDE), only(LEN, D)] + ([ANY, VM] if done else []),
-        out_specs=[only(LEN, 3 * D), VM],
-        out_shape=[SDS((rows, LEN, 3 * D), BF), SDS((8, D), F32)],
+        grid=(D // 256,),
+        in_specs=[tall, tall, tall, block, tall] + ([ANY, ANY, ANY, sums] if done else []),
+        out_specs=[tall, tall, tall, sums],
+        out_shape=[token, token, token, SDS((8, D), F32)],
         scratch_shapes=[pltpu.VMEM((LEN, LANE), F32), pltpu.VMEM((LEN, LANE), F32)],
-        input_output_aliases={3: 0} if done else {},
-        compiler_params=params_of(),
-        cost_estimate=pl.CostEstimate(flops=6 * 10**9, bytes_accessed=12 << 20, transcendentals=0),
+        input_output_aliases={5: 0, 6: 1, 7: 2} if done else {},
+        compiler_params=params_of(),
+        cost_estimate=TINY,
         name="retreat",
-    )(qkv, probs, datt, *done)
-
-
-def project_kernel(dproj_ref, dh1_ref, w_ref, dx_ref):
+    )(q, k, v, probs, datt, *done)
+
+
+def project_kernel(dq_ref, dk_ref, dv_ref, dh1_ref, w_ref, dx_ref):
     def back(t, _):
         cols = at(t, 256)
-        dx_ref[0, :, cols] = (dh1_ref[0, :, cols] + dot(dproj_ref[0], w_ref[cols, :], NT)).astype(BF)
+        total = dh1_ref[0, :, cols]
+        for n, ref in enumerate((dq_ref, dk_ref, dv_ref)):
+            total = total + dot(ref[0], w_ref[cols, n * D : (n + 1) * D], NT)
+        dx_ref[0, :, cols] = total.astype(BF)
         return 0
 
     lax.fori_loop(0, D // 256, back, 0)
 
 
-def project_back(dproj, dh1, wqkv):
-    rows = dproj.shape[0]
+def project_back(dq, dk, dv, dh1, wqkv):
+    rows = dq.shape[0]
     return pl.pallas_call(
         project_kernel,
         grid=(rows,),
-        in_specs=[row_spec(LEN, 3 * D), row_spec(LEN, D), once(D, 3 * D)],
+        in_specs=[row_spec(LEN, D)] * 4 + [once(D, 3 * D)],
         out_specs=row_spec(LEN, D),
         out_shape=SDS((rows, LEN, D), BF),
         compiler_params=params_of(),
-        cost_estimate=pl.CostEstimate(flops=4 * 10**9, bytes_accessed=16 << 20, transcendentals=0),
+        cost_estimate=TINY,
         name="project_back",
-    )(dproj, dh1, wqkv)
-
-
-def store_product(flat, first, lhs_ref, rhs_ref, turned, step=256):
+    )(dq, dk, dv, dh1, wqkv)
+
+
+def store_product(flat, first, lhs_ref, rhs_refs, turned, step=768):
     tokens, tall = lhs_ref.shape
-    broad = rhs_ref.shape[1]
-    cols = broad // LANE
+    broad = rhs_refs[0].shape[1]
+    cols = len(rhs_refs) * broad // LANE
     block = min(tall, turned.shape[0])
 
     def rows_of(m, _):
         for b in range(block // 256):
             turned[b * 256 : (b + 1) * 256, :] = lhs_ref[:, pl.ds(pl.multiple_of(m * block + b * 256, 256), 256)].T
 
-        def cols_of(t, _):
-            r = dot(turned[0:block, :], rhs_ref[:, at(t, step)])
-            for j in range(step // LANE):
-                place = first + m * (block * cols) + t * (step // LANE) + j
-                flat[pl.ds(place, block, stride=cols), :] = r[:, j * LANE : (j + 1) * LANE]
-            return 0
-
-        lax.fori_loop(0, broad // step, cols_of, 0)
+        for n, rhs_ref in enumerate(rhs_refs):
+
+            def cols_of(t, _, n=n, rhs_ref=rhs_ref):
+                r = dot(turned[0:block, :], rhs_ref[:, at(t, step)])
+                for j in range(step // LANE):
+                    place = first + m * (block * cols) + n * (broad // LANE) + t * (step // LANE) + j
+                    flat[pl.ds(place, block, stride=cols), :] = r[:, j * LANE : (j + 1) * LANE]
+                return 0
+
+            lax.fori_loop(0, broad // step, cols_of, 0)
         return 0
 
     lax.fori_loop(0, tall // block, rows_of, 0)
@@ -813,11 +811,15 @@
         flat[first + j : first + j + 1, :] = src_ref[row : row + 1, j * LANE : (j + 1) * LANE]
 
 
-def fill_late(flat, att, dbr, nbf, dinner, act, dffn, outb, dstu, vg, sg, gmid, gcls, turned):
+def fill_late(flat, wait, att, dbr, nbf, dinner, act, dffn, outb, dstu, vg, sg, gmid, gcls, turned):
     first = lambda name: TABLE[name] - SPLIT + 16
-    store_product(flat, first("w_out"), att, dbr, turned)
-    store_product(flat, first("w_in"), nbf, dinner, turned)
-    store_product(flat, first("w_back"), act, dffn, turned)
+    wait(0, 1)
+    store_product(flat, first("w_out"), att, [dbr], turned)
+    wait(2, 3)
+    store_product(flat, first("w_in"), nbf, [dinner], turned)
+    wait(4, 5)
+    store_product(flat, first("w_back"), act, [dffn], turned)
+    wait(6, 7)
     for b in range(D // 256):
         turned[b * 256 : (b + 1) * 256, :] = outb[:, b * 256 : (b + 1) * 256].T
     flat[first("w_stu") : first("w_stu") + D, :] = dot(turned[...], dstu[...])
@@ -836,14 +838,34 @@
     flat[0:16, :] = jnp.zeros((16, LANE), F32)
 
 
-def fill_early(flat, x, dproj, bg, edge, turned):
-    store_product(flat, 16, x, dproj, turned)
+MOVED = 8
+
+
+def fetch_late(ins, bufs, sems):
+    copies = [pltpu.make_async_copy(ins[n], bufs[n], sems.at[n]) for n in range(MOVED)]
+    for copy in copies:
+        copy.start()
+
+    def wait(*which):
+        for n in which:
+            copies[n].wait()
+
+    return wait
+
+
+def late_scratch(arrays):
+    return [pltpu.VMEM(v.shape, BF) for v in arrays[:MOVED]] + [pltpu.SemaphoreType.DMA((MOVED,))]
+
+
+def late_specs(arrays):
+    return [ANY] * MOVED + [VM] * (len(arrays) - MOVED)
+
+
+def fill_early(flat, x, dq, dk, dv, bg, edge, turned):
+    store_product(flat, 16, x, [dq, dk, dv], turned)
     put_line(flat, 16 + TABLE["b_qv"], bg, 0)
     put_line(flat, 16 + TABLE["b_qv"] + D // LANE, bg, 1)
     flat[16 + SPLIT : 16 + SPLIT + edge.shape[0], :] = edge[...]
-
-
-GRAD_COST = pl.CostEstimate(flops=4 * 10**9, bytes_accessed=24 << 20, transcendentals=0)
 
 
 def scratch_of(rows, tokens, padded):
@@ -856,15 +878,15 @@
 
 
 def late_kernel(shard_rows, *refs):
-    ins, (out_ref, edge_ref, flat, turned, stage, sems) = refs[:12], refs[12:]
-    fill_late(flat, *ins, turned)
+    ins, (out_ref, edge_ref, flat, turned, stage, sems, *bufs, in_sems) = refs[:12], refs[12:]
+    fill_late(flat, fetch_late(ins, bufs, in_sems), *bufs, *ins[MOVED:], turned)
     edge_ref[...] = flat[16:32, :]
     count, padded, _ = out_ref.shape
     send_shards(flat, SPLIT, SPLIT, count * shard_rows, shard_rows, padded, stage, sems, lambda d: [(None, out_ref.at[d])])
 
 
-def early_kernel(shard_rows, x, dproj, bg, edge, _, out_ref, flat, turned, stage, sems):
-    fill_early(flat, x, dproj, bg, edge, turned)
+def early_kernel(shard_rows, x, dq, dk, dv, bg, edge, _, out_ref, flat, turned, stage, sems):
+    fill_early(flat, x, dq, dk, dv, bg, edge, turned)
     send_shards(flat, 0, 0, SPLIT, shard_rows, out_ref.shape[1], stage, sems, lambda d: [(None, out_ref.at[d])])
 
 
@@ -872,26 +894,26 @@
     rows = count * shard_rows - SPLIT
     return pl.pallas_call(
         functools.partial(late_kernel, shard_rows),
-        in_specs=[VM] * len(arrays),
+        in_specs=late_specs(arrays),
         out_specs=[ANY, VM],
         out_shape=[SDS((count, padded, LANE), BF), SDS((16, LANE), F32)],
-        scratch_shapes=scratch_of(rows, arrays[0].shape[0], padded),
+        scratch_shapes=scratch_of(rows, arrays[0].shape[0], padded) + late_scratch(arrays),
         compiler_params=params_of(),
         name="late_grads",
     )(*arrays)
 
 
-def early_grads(shard_rows, x, dproj, bg, edge, partial):
+def early_grads(shard_rows, x, dq, dk, dv, bg, edge, partial):
     return pl.pallas_call(
         functools.partial(early_kernel, shard_rows),
-        in_specs=[VM] * 4 + [ANY],
+        in_specs=[VM] * 6 + [ANY],
         out_specs=ANY,
         out_shape=SDS(partial.shape, BF),
         scratch_shapes=scratch_of(SPLIT, x.shape[0], partial.shape[1]),
-        input_output_aliases={4: 0},
+        input_output_aliases={6: 0},
         compiler_params=params_of(),
         name="early_grads",
-    )(x, dproj, bg, edge, partial)
+    )(x, dq, dk, dv, bg, edge, partial)
 
 
 def by_core(core, d, chip, keep, give):
@@ -899,8 +921,8 @@
 
 
 def late_pair_kernel(shard_rows, me_ref, *refs):
-    ins, (keep, give, edge_ref, flat, turned, stage, sems) = refs[:12], refs[12:]
-    fill_late(flat, *ins, turned)
+    ins, (keep, give, edge_ref, flat, turned, stage, sems, *bufs, in_sems) = refs[:12], refs[12:]
+    fill_late(flat, fetch_late(ins, bufs, in_sems), *bufs, *ins[MOVED:], turned)
     edge_ref[...] = flat[16 : 16 + edge_ref.shape[0], :]
     core = me_ref[0] & 1
     send_shards(
@@ -921,36 +943,36 @@
     edge = -(-(2 * shard_rows - SPLIT) // 8) * 8
     return pl.pallas_call(
         functools.partial(late_pair_kernel, shard_rows),
-        in_specs=[SM] + [VM] * len(arrays),
+        in_specs=[SM] + late_specs(arrays),
         out_specs=[ANY, ANY, VM],
         out_shape=[shape, shape, SDS((edge, LANE), F32)],
-        scratch_shapes=scratch_of(8 * shard_rows - SPLIT, arrays[0].shape[0], padded),
-        compiler_params=params_of(),
-        cost_estimate=GRAD_COST,
+        scratch_shapes=scratch_of(8 * shard_rows - SPLIT, arrays[0].shape[0], padded) + late_scratch(arrays),
+        compiler_params=params_of(),
+        cost_estimate=TINY,
         name="late_grads",
     )(me, *arrays)
 
 
-def early_pair_kernel(shard_rows, me_ref, x, dproj, bg, edge, keep, give, flat, turned, stage, sems):
-    fill_early(flat, x, dproj, bg, edge, turned)
+def early_pair_kernel(shard_rows, me_ref, x, dq, dk, dv, bg, edge, keep, give, flat, turned, stage, sems):
+    fill_early(flat, x, dq, dk, dv, bg, edge, turned)
     core = me_ref[0] & 1
     send_shards(
         flat, 0, 0, 2 * shard_rows, shard_rows, keep.shape[1], stage, sems, lambda d: by_core(core, d, 0, keep, give)
     )
 
 
-def early_pairs(me, shard_rows, padded, x, dproj, bg, edge):
+def early_pairs(me, shard_rows, padded, x, dq, dk, dv, bg, edge):
     shape = SDS((1, padded, LANE), BF)
     return pl.pallas_call(
         functools.partial(early_pair_kernel, shard_rows),
-        in_specs=[SM] + [VM] * 4,
+        in_specs=[SM] + [VM] * 6,
         out_specs=[ANY, ANY],
         out_shape=[shape, shape],
         scratch_shapes=scratch_of(SPLIT + edge.shape[0], x.shape[0], padded),
         compiler_params=params_of(),
-        cost_estimate=GRAD_COST,
+        cost_estimate=TINY,
         name="early_grads",
-    )(me, x, dproj, bg, edge)
+    )(me, x, dq, dk, dv, bg, edge)
 
 
 def merge_late_kernel(me_ref, keep, got, sums, along_y, along_x):
@@ -978,7 +1000,7 @@
         out_specs=[pl.BlockSpec((1, 1, half, LANE), lambda c, h: (c + 1, h, 0, 0)), whole(half, LANE), whole(half, LANE)],
         out_shape=[SDS((4, 2, half, LANE), BF), SDS((half, LANE), BF), SDS((half, LANE), BF)],
         compiler_params=params_of(),
-        cost_estimate=pl.CostEstimate(flops=0, bytes_accessed=18 << 20, transcendentals=0),
+        cost_estimate=TINY,
         name="merge_late",
     )(me, keep, got)
 
@@ -1030,7 +1052,7 @@
         scratch_shapes=[pltpu.VMEM((2, half, LANE), BF), pltpu.SemaphoreType.DMA((3,))],
         input_output_aliases={3: 0},
         compiler_params=params_of(),
-        cost_estimate=pl.CostEstimate(flops=0, bytes_accessed=9 << 20, transcendentals=0),
+        cost_estimate=TINY,
         name="merge_early",
     )(me, keep, got, sums)
 
@@ -1077,7 +1099,7 @@
         out_shape=[SDS((half, LANE), BF)] * 4,
         scratch_shapes=[pltpu.VMEM((4, half, LANE), BF), pltpu.SemaphoreType.DMA((4,))],
         compiler_params=params_of(),
-        cost_estimate=pl.CostEstimate(flops=0, bytes_accessed=10 << 20, transcendentals=0),
+        cost_estimate=TINY,
         name="merge_next",
     )(me, sums, y_one, y_two, x_one, x_two)
 
@@ -1126,13 +1148,8 @@
         both = unpack(lax.all_gather(mine, "fsdp", axis=0, tiled=False), shard_rows)
         first, finish = both[:2], lambda after: both[2:]
     wqkv, bq = first
-    done = ()
-    for row in range(rows):
-        done = attend(row, inputs, segc, segr, wqkv, bq, done)
-        if row == 0:
-            rest = finish(done[2])
-    qkv, probs, att = done
-    wout, win, wback, wstu, wmid, vec, small, wcls = rest
+    q, k, v, probs, att = attend(inputs, segc, segr, wqkv, bq)
+    wout, win, wback, wstu, wmid, vec, small, wcls = finish(att)
     wcls = jnp.pad(wcls[:CLASSES].reshape(STU, CLASSES), ((0, 0), (0, LANE - CLASSES)))
     out, logits, nbf, act, dffn, dinner, dstu, dh1, dbr, datt, vg, sg, gmid, gcls = middle(
         inputs, att, segc, hot, out_cotangent, wout, win, wback, wstu, wmid, vec, small, wcls
@@ -1144,19 +1161,20 @@
         me = lax.axis_index("fsdp").reshape(1)
         keep, give, edge = late_pairs(me, shard_rows, padded, *late)
         got = swap(give, 1)
-        back = retreat(0, qkv, probs, datt, ())
+        back = retreat(0, q, k, v, probs, datt, ())
         got, back = lax.optimization_barrier((got, tuple(back)))
         sums, along_y, along_x = merge_late(me, keep, got)
         y_one, x_one = swap(along_y, 4), swap(along_x, 2)
         back, _ = lax.optimization_barrier((back, along_y))
         for row in range(1, rows):
-            back = retreat(row, qkv, probs, datt, tuple(back))
-        y_one, x_one, (dproj, bg) = lax.optimization_barrier((y_one, x_one, tuple(back)))
-        keep, give = early_pairs(me, shard_rows, padded, flat2(inputs), flat2(dproj), bg, edge)
+            back = retreat(row, q, k, v, probs, datt, tuple(back))
+        *dproj, bg = back
+        keep, give = early_pairs(me, shard_rows, padded, flat2(inputs), *map(flat2, dproj), bg, edge)
+        y_one, x_one, give = lax.optimization_barrier((y_one, x_one, give))
         sums, along_y, along_x = merge_early(me, keep, swap(give, 1), sums)
         y_two, x_two = swap(along_y, 4), swap(along_x, 2)
         dproj, _ = lax.optimization_barrier((dproj, along_y))
-        dx = project_back(dproj, dh1, wqkv)
+        dx = project_back(*dproj, dh1, wqkv)
         y_two, _ = lax.optimization_barrier((y_two, dx))
         own_a, own_b, along_x, along_y = merge_next(me, sums, y_one, y_two, x_one, x_two)
         own_a, own_b = own_a + swap(along_x, 2), own_b + swap(along_y, 4)
@@ -1164,11 +1182,11 @@
         partial, edge = late_grads(shard_rows, count, padded, *late)
         back = ()
         for row in range(rows):
-            back = tuple(retreat(row, qkv, probs, datt, back))
-        dproj, bg = back
-        grads = early_grads(shard_rows, flat2(inputs), flat2(dproj), bg, edge, partial)
+            back = tuple(retreat(row, q, k, v, probs, datt, back))
+        *dproj, bg = back
+        grads = early_grads(shard_rows, flat2(inputs), *map(flat2, dproj), bg, edge, partial)
         owned = lax.psum_scatter(grads, "fsdp", scatter_dimension=0, tiled=False)
-        dx = project_back(dproj, dh1, wqkv)
+        dx = project_back(*dproj, dh1, wqkv)
     if count != 8:
         owned = lax.psum(owned, "rep")
     elif lax.axis_size("rep") == 4:

time: 436 us -> 384 us (0.88)
  Pallas kernels: 231 us -> 178 us
    pallas_call x5 -> x4, Pallas kernels: 77.8 us -> 42 us  [the longest x1 16.7 us: attend(): pl.pallas_call(attend_kernel, grid=(rows, D // 256), in_specs=[only(LEN,...]
    pallas_call x1, Pallas kernels: 32.4 us -> 23.8 us  [late_pairs(): pl.pallas_call(functools.partial(late_pair_kernel, shard_rows), in_specs=...]
    pallas_call x1, Pallas kernels: 69.7 us -> 63.5 us  [middle(): pl.pallas_call(middle_kernel, grid=(rows,), in_specs=[row_spec(LEN, D), r...]
  transfers between devices with their start and end apart: 30 -> 30, of which waited for: 16 -> 19; matrix products, arithmetic and copies ran while one was open for 2% -> 3% of each run, Pallas kernels for 19% -> 14%
where the time goes in v3:
time: 384 us; the launch traced here: 383 us
  Pallas kernels  178 us (46%)
  waiting for transfers between devices  143 us (37%)
  starting transfers between devices  28.4 us (7%)
  other arithmetic  21.2 us (6%)
  local copies, waits for them, and re-layouts  10.8 us (3%)
    ppermute x22, waiting for transfers between devices, swap(): return lax.ppermute(v, 'fsdp', [(d, d ^ bit) for d in range(8)])  79.2 us
    ppermute x8, waiting for transfers between devices, sum_replicas(): lax.ppermute(v, 'rep', [(i, i ^ bit) for i in range(4)])  64 us
    pallas_call x1, Pallas kernels, middle(): pl.pallas_call(middle_kernel, grid=(rows,), in_specs=[row_spec(LEN, D), r...  63.5 us
    pallas_call x1, Pallas kernels, late_pairs(): pl.pallas_call(functools.partial(late_pair_kernel, shard_rows), in_specs=...  23.8 us
    ppermute x22, starting transfers between devices, swap(): return lax.ppermute(v, 'fsdp', [(d, d ^ bit) for d in range(8)])  17.7 us
    pallas_call x1, Pallas kernels, attend(): pl.pallas_call(attend_kernel, grid=(rows, D // 256), in_specs=[only(LEN,...  16.7 us
    pallas_call x2, Pallas kernels, retreat(): pl.pallas_call(kernel, grid=(D // 256,), in_specs=[tall, tall, tall, bloc...  15.8 us
    pallas_call x1, Pallas kernels, unpack_rest(): pl.pallas_call(functools.partial(unpack_rest_kernel, shard_rows), in_spec...  14.6 us
  transfers between devices with their start and end apart: 30, of which 19 were waited for; matrix products, arithmetic and copies ran while one was open for 3% of the time, Pallas kernels for 14%

profile of v3, /device:TPU:0, one launch (start us, length us, event | category | flops | bytes accessed | tf_op | source)
XLA Modules:
  0.0 382.9 jit_solution(13430846959492920992)
XLA Ops:
  0.6 2.2 convert.5
  3.1 3.0 collective-permute-start
  6.1 1.5 collective-permute-start.1
  7.6 18.5 %collective-permute-done.rest_2_ = bf16[3520,128]{1,0:T(8,128)(2,1)S(1)} collective-permute-done((bf16[3520,128]{1,0:T(8,128)(2,1)S(1)}, bf16[3520,128]{1,0:T(8,128)(2,1)S(1)}, u32[]{:S(2)}, u32[]{:S(2)}) %collective-permute-start) | collective-permute-done | bytes 901152 | tf_op jit(solution)/shard_map/ppermute | solution.py:188
  26.1 1.2 broadcast_select_fusion.2
  27.3 1.8 collective-permute-start.2
  29.0 2.2 broadcast_select_fusion
  31.3 1.5 collective-permute-start.3
  33.4 15.3 %collective-permute-done.2.rest_4_ = bf16[3520,128]{1,0:T(8,128)(2,1)} collective-permute-done((bf16[3520,128]{1,0:T(8,128)(2,1)S(1)}, bf16[3520,128]{1,0:T(8,128)(2,1)}, u32[]{:S(2)}, u32[]{:S(2)}) %collective-permute-start.2) | collective-permute-done | bytes 901152 | tf_op jit(solution)/shard_map/ppermute | solution.py:188
  48.7 3.9 %collective-permute-done.3.rest_5_ = bf16[3520,128]{1,0:T(8,128)(2,1)} collective-permute-done((bf16[3520,128]{1,0:T(8,128)(2,1)S(1)}, bf16[3520,128]{1,0:T(8,128)(2,1)}, u32[]{:S(2)}, u32[]{:S(2)}) %collective-permute-start.3) | collective-permute-done | bytes 901152 | tf_op jit(solution)/shard_map/ppermute | solution.py:188
  52.6 1.6 collective-permute-start.10
  56.2 1.0 copy.24.segc_ref
  58.2 4.7 %unpack_first.1 = (bf16[768,2304]{1,0:T(8,128)(2,1)}, f32[8,2304]{1,0:T(8,128)}) custom-call(s32[1]{0:T(128)} %bitcast.1.me_ref, bf16[3520,128]{1,0:T(8,128)(2,1)} %copy-done, bf16[3520,128]{1,0:T(8,128)(2,1)} %copy-done.1, bf16[3520,128]{1,0:T(8,128)(2,1)} %copy-done.2, bf16[3520,128]{1,0:T(8,128)(2,1)} %collective-permute-done.1.rest_3_, ...), custom_call_target="tpu_custom_call" | custom-call | flops 1 | bytes 1 | tf_op jit(solution)/shard_map/unpack_first/pallas_call | solution.py:237
  63.0 16.7 %attend.1 = (bf16[2,512,768]{2,1,0:T(8,128)(2,1)}, bf16[2,512,768]{2,1,0:T(8,128)(2,1)}, bf16[2,512,768]{2,1,0:T(8,128)(2,1)}, bf16[2,6,256,1280]{3,2,1,0:T(8,128)(2,1)}, bf16[2,512,768]{2,1,0:T(8,128)(2,1)}) custom-call(bf16[2,512,768]{2,1,0:T(8,128)(2,1)} %x_ref.3, s32[2,512,1]{2,1,0:T(8,128)} %copy.24.segc_ref, s32[2,1,512]{2,1,0:T(1,128)} %broadcast_in_dim.24.segr_ref, ...), custom_call_target="tpu_custom_call" | custom-call | flops 1 | bytes 1 | tf_op jit(solution)/shard_map/attend/pallas_call | solution.py:366
  83.7 14.6 %unpack_rest.1 = (bf16[768,768]{1,0:T(8,128)(2,1)}, bf16[768,3072]{1,0:T(8,128)(2,1)}, bf16[3072,768]{1,0:T(8,128)(2,1)}, bf16[768,128]{1,0:T(8,128)(2,1)}, f32[...) custom-call(s32[8]{0:T(128)} %fusion.4.owner_ref, bf16[3520,128]{1,0:T(8,128)(2,1)} %copy-done, ...), custom_call_target="tpu_custom_call" | custom-call | flops 1 | bytes 1 | tf_op jit(solution)/shard_map/unpack_rest/pallas_call | solution.py:273
  99.7 63.5 %middle.1 = (bf16[2,512,768]{2,1,0:T(8,128)(2,1)}, f32[2,8,14]{2,1,0:T(8,128)}, bf16[2,512,768]{2,1,0:T(8,128)(2,1)}, bf16[2,512,3072]{2,1,0:T(8,128)(2,1)}, bf1...) custom-call(bf16[2,512,768]{2,1,0:T(8,128)(2,1)} %x_ref.3, ...), custom_call_target="tpu_custom_call" | custom-call | flops 1 | bytes 1 | tf_op jit(solution)/shard_map/middle/pallas_call | solution.py:607
  163.2 1.0 reshape.114
  164.8 23.8 %late_grads.1 = (bf16[3,7040,128]{2,1,0:T(8,128)(2,1)}, bf16[3,7040,128]{2,1,0:T(8,128)(2,1)}, f32[240,128]{1,0:T(8,128)}) custom-call(s32[1]{0:T(128)} %bitcast.1.me_ref, bf16[1024,768]{1,0:T(8,128)(2,1)} %bitcast.55, bf16[1024,768]{1,0:T(8,128)(2,1)} %bitcast.67, bf16[1024,768]{1,0:T(8,128)(2,1)} %bitcast.65, bf16[1024,3072]{1,0:T(8,128)(2,1)} %bitcast.54, ...), custom_call_target="tpu_custom_call" | custom-call | flops 1 | bytes 1 | tf_op jit(solution)/shard_map/late_grads/pallas_call | solution.py:944
  188.8 7.9 %retreat.2 = (bf16[2,512,768]{2,1,0:T(8,128)(2,1)}, bf16[2,512,768]{2,1,0:T(8,128)(2,1)}, bf16[2,512,768]{2,1,0:T(8,128)(2,1)}, f32[8,768]{1,0:T(8,128)}) custom-call(bf16[2,512,768]{2,1,0:T(8,128)(2,1)} %get-tuple-element.95.refs_0_, bf16[2,512,768]{2,1,0:T(8,128)(2,1)} %get-tuple-element.96.refs_1_, bf16[2,512,768]{2,1,0:T(8,128)(2,1)} %get-tuple-element.97.refs_2_, ...), custom_call_target="tpu_custom_call" | custom-call | flops 1 | bytes 1 | tf_op jit(solution)/shard_map/retreat/pallas_call | solution.py:711
  196.7 1.2 collective-permute-done.14.got
  197.9 8.5 %merge_late.1 = (bf16[4,2,3520,128]{3,2,1,0:T(8,128)(2,1)}, bf16[3520,128]{1,0:T(8,128)(2,1)}, bf16[3520,128]{1,0:T(8,128)(2,1)}) custom-call(s32[1]{0:T(128)} %bitcast.1.me_ref, bf16[3,7040,128]{2,1,0:T(8,128)(2,1)} %get-tuple-element.119.keep, bf16[3,7040,128]{2,1,0:T(8,128)(2,1)} %collective-permute-done.14.got), custom_call_target="tpu_custom_call" | custom-call | flops 1 | bytes 1 | tf_op jit(solution)/shard_map/merge_late/pallas_call | solution.py:996
  206.4 1.1 collective-permute-start.15
  207.5 1.3 collective-permute-start.16
  208.8 7.9 %retreat.3 = (bf16[2,512,768]{2,1,0:T(8,128)(2,1)}, bf16[2,512,768]{2,1,0:T(8,128)(2,1)}, bf16[2,512,768]{2,1,0:T(8,128)(2,1)}, f32[8,768]{1,0:T(8,128)}) custom-call(bf16[2,512,768]{2,1,0:T(8,128)(2,1)} %get-tuple-element.95.refs_0_, bf16[2,512,768]{2,1,0:T(8,128)(2,1)} %get-tuple-element.96.refs_1_, ...), custom_call_target="tpu_custom_call", output_to_operand_aliasing={{0}: (5, {}), {1}: (6, {}), {2}: (7, {})} | custom-call | flops 1 | bytes 1 | tf_op jit(solution)/shard_map/retreat/pallas_call | solution.py:711
  216.7 8.8 %early_grads.1 = (bf16[1,7040,128]{2,1,0:T(8,128)(2,1)}, bf16[1,7040,128]{2,1,0:T(8,128)(2,1)}) custom-call(s32[1]{0:T(128)} %bitcast.1.me_ref, bf16[1024,768]{1,0:T(8,128)(2,1)} %bitcast.49, bf16[1024,768]{1,0:T(8,128)(2,1)} %bitcast.50, bf16[1024,768]{1,0:T(8,128)(2,1)} %bitcast.51, bf16[1024,768]{1,0:T(8,128)(2,1)} %bitcast.52, ...), custom_call_target="tpu_custom_call" | custom-call | flops 1 | bytes 1 | tf_op jit(solution)/shard_map/early_grads/pallas_call | solution.py:966
  225.6 3.1 collective-permute-done.15.y_one
  229.5 3.9 %collective-permute-done.17.got = bf16[1,7040,128]{2,1,0:T(8,128)(2,1)S(1)} collective-permute-done((bf16[1,7040,128]{2,1,0:T(8,128)(2,1)}, bf16[1,7040,128]{2,1,0:T(8,128)(2,1)S(1)}, u32[]{:S(2)}, u32[]{:S(2)}) %collective-permute-start.17) | collective-permute-done | bytes 1802272 | tf_op jit(solution)/shard_map/ppermute | solution.py:188
  233.4 1.2 copy-done.7
  234.7 5.8 %merge_early.1 = (bf16[4,2,3520,128]{3,2,1,0:T(8,128)(2,1)}, bf16[3520,128]{1,0:T(8,128)(2,1)}, bf16[3520,128]{1,0:T(8,128)(2,1)}) custom-call(s32[1]{0:T(128)} %bitcast.1.me_ref, bf16[1,7040,128]{2,1,0:T(8,128)(2,1)} %get-tuple-element.131.keep, bf16[1,7040,128]{2,1,0:T(8,128)(2,1)} %copy-done.7, ...), custom_call_target="tpu_custom_call", output_to_operand_aliasing={{0}: (3, {})} | custom-call | flops 1 | bytes 1 | tf_op jit(solution)/shard_map/merge_early/pallas_call | solution.py:1047
  242.1 9.5 %project_back.1 = bf16[2,512,768]{2,1,0:T(8,128)(2,1)} custom-call(bf16[2,512,768]{2,1,0:T(8,128)(2,1)} %get-tuple-element.137.dq_ref, bf16[2,512,768]{2,1,0:T(8,128)(2,1)} %get-tuple-element.138.dk_ref, bf16[2,512,768]{2,1,0:T(8,128)(2,1)} %get-tuple-element.139.dv_ref, f32[2,512,768]{2,1,0:T(8,128)} %get-tuple-element.140.dh1_ref, ...), custom_call_target="tpu_custom_call" | custom-call | flops 1 | bytes 1 | tf_op jit(solution)/shard_map/project_back/pallas_call | solution.py:739
  251.6 11.2 %collective-permute-done.18.y_two = bf16[3520,128]{1,0:T(8,128)(2,1)S(1)} collective-permute-done((bf16[3520,128]{1,0:T(8,128)(2,1)}, bf16[3520,128]{1,0:T(8,128)(2,1)S(1)}, u32[]{:S(2)}, u32[]{:S(2)}) %collective-permute-start.18) | collective-permute-done | bytes 901152 | tf_op jit(solution)/shard_map/ppermute | solution.py:188
  264.1 6.6 %merge_next.1 = (bf16[3520,128]{1,0:T(8,128)(2,1)}, bf16[3520,128]{1,0:T(8,128)(2,1)}, bf16[3520,128]{1,0:T(8,128)(2,1)}, bf16[3520,128]{1,0:T(8,128)(2,1)}) custom-call(s32[1]{0:T(128)} %bitcast.1.me_ref, bf16[4,2,3520,128]{3,2,1,0:T(8,128)(2,1)} %get-tuple-element.141.sums, bf16[3520,128]{1,0:T(8,128)(2,1)} %copy-done.13, bf16[3520,128]{1,0:T(8,128)(2,1)} %copy-done.15, ...), custom_call_target="tpu_custom_call" | custom-call | flops 1 | bytes 1 | tf_op jit(solution)/shard_map/merge_next/pallas_call | solution.py:1095
  270.8 1.4 collective-permute-start.25
  272.1 1.1 collective-permute-start.20
  273.2 18.9 %collective-permute-done.25 = bf16[3520,128]{1,0:T(8,128)(2,1)S(1)} collective-permute-done((bf16[3520,128]{1,0:T(8,128)(2,1)}, bf16[3520,128]{1,0:T(8,128)(2,1)S(1)}, u32[]{:S(2)}, u32[]{:S(2)}) %collective-permute-start.25) | collective-permute-done | bytes 901152 | tf_op jit(solution)/shard_map/ppermute | solution.py:188
  293.0 1.7 add.67
  295.5 2.6 collective-permute-start.26
  298.4 1.7 collective-permute-start.21
  300.0 16.8 %collective-permute-done.26 = bf16[1760,128]{1,0:T(8,128)(2,1)S(1)} collective-permute-done((bf16[1760,128]{1,0:T(8,128)(2,1)}, bf16[1760,128]{1,0:T(8,128)(2,1)S(1)}, u32[]{:S(2)}, u32[]{:S(2)}) %collective-permute-start.26) | collective-permute-done | bytes 450592 | tf_op jit(solution)/shard_map/ppermute | solution.py:1118
  317.7 3.3 collective-permute-start.22
  321.1 8.3 %collective-permute-done.27 = bf16[880,128]{1,0:T(8,128)(2,1)S(1)} collective-permute-done((bf16[880,128]{1,0:T(8,128)(2,1)S(1)}, bf16[880,128]{1,0:T(8,128)(2,1)S(1)}, u32[]{:S(2)}, u32[]{:S(2)}) %collective-permute-start.27) | collective-permute-done | bytes 225312 | tf_op jit(solution)/shard_map/ppermute | solution.py:1118
  329.5 2.0 collective-permute-done.22
  331.9 4.5 %collective-permute-done.28 = bf16[880,128]{1,0:T(8,128)(2,1)S(1)} collective-permute-done((bf16[880,128]{1,0:T(8,128)(2,1)S(1)}, bf16[880,128]{1,0:T(8,128)(2,1)S(1)}, u32[]{:S(2)}, u32[]{:S(2)}) %collective-permute-start.28) | collective-permute-done | bytes 225312 | tf_op jit(solution)/shard_map/ppermute | solution.py:1118
  336.4 2.0 collective-permute-start.29
  338.5 15.3 %collective-permute-done.23 = bf16[880,128]{1,0:T(8,128)(2,1)S(1)} collective-permute-done((bf16[880,128]{1,0:T(8,128)(2,1)S(1)}, bf16[880,128]{1,0:T(8,128)(2,1)S(1)}, u32[]{:S(2)}, u32[]{:S(2)}) %collective-permute-start.23) | collective-permute-done | bytes 225312 | tf_op jit(solution)/shard_map/ppermute | solution.py:1118
  354.0 7.8 %collective-permute-done.29 = bf16[1760,128]{1,0:T(8,128)(2,1)S(1)} collective-permute-done((bf16[1760,128]{1,0:T(8,128)(2,1)S(1)}, bf16[1760,128]{1,0:T(8,128)(2,1)S(1)}, u32[]{:S(2)}, u32[]{:S(2)}) %collective-permute-start.29) | collective-permute-done | bytes 450592 | tf_op jit(solution)/shard_map/ppermute | solution.py:1118
  362.1 9.3 %collective-permute-done.24 = bf16[1760,128]{1,0:T(8,128)(2,1)S(1)} collective-permute-done((bf16[1760,128]{1,0:T(8,128)(2,1)S(1)}, bf16[1760,128]{1,0:T(8,128)(2,1)S(1)}, u32[]{:S(2)}, u32[]{:S(2)}) %collective-permute-start.24) | collective-permute-done | bytes 450592 | tf_op jit(solution)/shard_map/ppermute | solution.py:1118
  371.6 11.3 %add_divide_fusion = (f32[900608]{0:T(1024)}, f32[900608]{0:T(1024)}, f32[900608]{0:T(1024)}) fusion(bf16[3520,128]{1,0:T(8,128)(2,1)S(1)} %maximum_select_fusion.1, bf16[3520,128]{1,0:T(8,128)(2,1)S(1)} %maximum_select_fusion, f32[900608]{0:T(1024)S(1)} %copy-done.3, f32[900608]{0:T(1024)} %param.19), kind=kLoop, calls=%fused_computation.5 | loop fusion | flops 14409728 | bytes 19814400 | tf_op jit(solution)/shard_map/div | solution.py:1130
  (102 shorter events, 17.9 us)
Async XLA Ops:
  2.9 24.4 %copy-start = (bf16[3520,128]{1,0:T(8,128)(2,1)}, bf16[3520,128]{1,0:T(8,128)(2,1)S(1)}, u32[]{:S(2)}) copy-start(bf16[3520,128]{1,0:T(8,128)(2,1)S(1)} %slice_bitcast_fusion.1.rest_0_) | copy-start | bytes 2703364
  3.0 29.7 %copy-start.1 = (bf16[3520,128]{1,0:T(8,128)(2,1)}, bf16[3520,128]{1,0:T(8,128)(2,1)S(1)}, u32[]{:S(2)}) copy-start(bf16[3520,128]{1,0:T(8,128)(2,1)S(1)} %pad.12.rest_1_) | copy-start | bytes 2703364
  3.1 23.0 %collective-permute-start = (bf16[3520,128]{1,0:T(8,128)(2,1)S(1)}, bf16[3520,128]{1,0:T(8,128)(2,1)S(1)}, u32[]{:S(2)}, u32[]{:S(2)}) collective-permute-start(bf16[3520,128]{1,0:T(8,128)(2,1)S(1)} %slice_bitcast_fusion.1.rest_0_), channel_id=1, source_target_pairs={{0,2},{1,3},{2,0},{3,1},{4,6},{5,7},{6,4},{7,5},{8,10},{9,11},{10,... | collective-permute-start | bytes 2703368 | tf_op jit(solution)/shard_map/ppermute | solution.py:188
  6.1 27.2 %collective-permute-start.4 = (bf16[3520,128]{1,0:T(8,128)(2,1)S(1)}, bf16[3520,128]{1,0:T(8,128)(2,1)}, u32[]{:S(2)}, u32[]{:S(2)}) collective-permute-start(bf16[3520,128]{1,0:T(8,128)(2,1)S(1)} %slice_bitcast_fusion.1.rest_0_), channel_id=1, source_target_pairs={{0,1},{1,0},{2,3},{3,2},{4,5},{5,4},{6,7},{7,6},{8,9},{9,8},{10,11... | collective-permute-start | bytes 2703368 | tf_op jit(solution)/shard_map/ppermute | solution.py:188
  6.1 23.0 %collective-permute-start.1 = (bf16[3520,128]{1,0:T(8,128)(2,1)S(1)}, bf16[3520,128]{1,0:T(8,128)(2,1)}, u32[]{:S(2)}, u32[]{:S(2)}) collective-permute-start(bf16[3520,128]{1,0:T(8,128)(2,1)S(1)} %pad.12.rest_1_), channel_id=1, source_target_pairs={{0,4},{1,5},{2,6},{3,7},{4,0},{5,1},{6,2},{7,3},{8,12},{9,13},{10,... | collective-permute-start | bytes 2703368 | tf_op jit(solution)/shard_map/ppermute | solution.py:188
  7.6 48.0 %copy-start.17 = (s32[2,512]{1,0:T(2,128)S(1)}, s32[2,512]{1,0:T(2,128)}, u32[]{:S(2)}) copy-start(s32[2,512]{1,0:T(2,128)} %param.13) | copy-start | bytes 12292
  26.1 6.7 %copy-start.2 = (bf16[3520,128]{1,0:T(8,128)(2,1)}, bf16[3520,128]{1,0:T(8,128)(2,1)S(1)}, u32[]{:S(2)}) copy-start(bf16[3520,128]{1,0:T(8,128)(2,1)S(1)} %collective-permute-done.rest_2_) | copy-start | bytes 2703364
  27.3 21.4 %collective-permute-start.2 = (bf16[3520,128]{1,0:T(8,128)(2,1)S(1)}, bf16[3520,128]{1,0:T(8,128)(2,1)}, u32[]{:S(2)}, u32[]{:S(2)}) collective-permute-start(bf16[3520,128]{1,0:T(8,128)(2,1)S(1)} %get-tuple-element.156), channel_id=1, source_target_pairs={{0,4},{1,5},{2,6},{3,7},{4,0},{5,1},{6,2},{7,3},{8,12},{9,13},{10,... | collective-permute-start | bytes 2703368 | tf_op jit(solution)/shard_map/ppermute | solution.py:188
  31.3 21.3 %collective-permute-start.3 = (bf16[3520,128]{1,0:T(8,128)(2,1)S(1)}, bf16[3520,128]{1,0:T(8,128)(2,1)}, u32[]{:S(2)}, u32[]{:S(2)}) collective-permute-start(bf16[3520,128]{1,0:T(8,128)(2,1)S(1)} %get-tuple-element.154), channel_id=1, source_target_pairs={{0,2},{1,3},{2,0},{3,1},{4,6},{5,7},{6,4},{7,5},{8,10},{9,11},{10,... | collective-permute-start | bytes 2703368 | tf_op jit(solution)/shard_map/ppermute | solution.py:188
  32.8 19.8 %collective-permute-start.5 = (bf16[3520,128]{1,0:T(8,128)(2,1)S(1)}, bf16[3520,128]{1,0:T(8,128)(2,1)S(1)}, u32[]{:S(2)}, u32[]{:S(2)}) collective-permute-start(bf16[3520,128]{1,0:T(8,128)(2,1)S(1)} %pad.12.rest_1_), channel_id=1, source_target_pairs={{0,1},{1,0},{2,3},{3,2},{4,5},{5,4},{6,7},{7,6},{8,9},{9,8},{10,11... | collective-permute-start | bytes 2703368 | tf_op jit(solution)/shard_map/ppermute | solution.py:188
  32.8 21.4 %collective-permute-start.6 = (bf16[3520,128]{1,0:T(8,128)(2,1)S(1)}, bf16[3520,128]{1,0:T(8,128)(2,1)S(1)}, u32[]{:S(2)}, u32[]{:S(2)}) collective-permute-start(bf16[3520,128]{1,0:T(8,128)(2,1)S(1)} %collective-permute-done.rest_2_), channel_id=1, source_target_pairs={{0,1},{1,0},{2,3},{3,2},{4,5},{5,4},{6,7},{7,6},{8,9},{9,8},{10,11... | collective-permute-start | bytes 2703368 | tf_op jit(solution)/shard_map/ppermute | solution.py:188
  33.3 24.0 %collective-permute-start.7 = (bf16[3520,128]{1,0:T(8,128)(2,1)}, bf16[3520,128]{1,0:T(8,128)(2,1)S(1)}, u32[]{:S(2)}, u32[]{:S(2)}) collective-permute-start(bf16[3520,128]{1,0:T(8,128)(2,1)} %collective-permute-done.1.rest_3_), channel_id=1, source_target_pairs={{0,1},{1,0},{2,3},{3,2},{4,5},{5,4},{6,7},{7,6},{8,9},{9,8},{10,11... | collective-permute-start | bytes 2703368 | tf_op jit(solution)/shard_map/ppermute | solution.py:188
  48.7 8.6 %collective-permute-start.8 = (bf16[3520,128]{1,0:T(8,128)(2,1)}, bf16[3520,128]{1,0:T(8,128)(2,1)}, u32[]{:S(2)}, u32[]{:S(2)}) collective-permute-start(bf16[3520,128]{1,0:T(8,128)(2,1)} %collective-permute-done.2.rest_4_), channel_id=1, source_target_pairs={{0,1},{1,0},{2,3},{3,2},{4,5},{5,4},{6,7},{7,6},{8,9},{9,8},{10,11... | collective-permute-start | bytes 2703368 | tf_op jit(solution)/shard_map/ppermute | solution.py:188
  52.6 4.7 %collective-permute-start.9 = (bf16[3520,128]{1,0:T(8,128)(2,1)}, bf16[3520,128]{1,0:T(8,128)(2,1)}, u32[]{:S(2)}, u32[]{:S(2)}) collective-permute-start(bf16[3520,128]{1,0:T(8,128)(2,1)} %collective-permute-done.3.rest_5_), channel_id=1, source_target_pairs={{0,1},{1,0},{2,3},{3,2},{4,5},{5,4},{6,7},{7,6},{8,9},{9,8},{10,11... | collective-permute-start | bytes 2703368 | tf_op jit(solution)/shard_map/ppermute | solution.py:188
  52.6 1.6 copy-start.4
  52.6 27.1 %collective-permute-start.10 = (bf16[3520,128]{1,0:T(8,128)(2,1)}, bf16[3520,128]{1,0:T(8,128)(2,1)S(1)}, u32[]{:S(2)}, u32[]{:S(2)}) collective-permute-start(bf16[3520,128]{1,0:T(8,128)(2,1)} %get-tuple-element.155), channel_id=1, source_target_pairs={{0,4},{1,5},{2,6},{3,7},{4,0},{5,1},{6,2},{7,3},{8,12},{9,13},{10,... | collective-permute-start | bytes 2703368 | tf_op jit(solution)/shard_map/ppermute | solution.py:188
  55.1 24.6 %collective-permute-start.11 = (bf16[3520,128]{1,0:T(8,128)(2,1)}, bf16[3520,128]{1,0:T(8,128)(2,1)S(1)}, u32[]{:S(2)}, u32[]{:S(2)}) collective-permute-start(bf16[3520,128]{1,0:T(8,128)(2,1)} %get-tuple-element.153), channel_id=1, source_target_pairs={{0,2},{1,3},{2,0},{3,1},{4,6},{5,7},{6,4},{7,5},{8,10},{9,11},{10,... | collective-permute-start | bytes 2703368 | tf_op jit(solution)/shard_map/ppermute | solution.py:188
  62.9 17.4 %copy-start.18 = (s32[2,8]{1,0:T(2,128)S(1)}, s32[2,8]{1,0:T(2,128)}, u32[]{:S(2)}) copy-start(s32[2,8]{1,0:T(2,128)} %param.15) | copy-start | bytes 196
  62.9 17.4 %copy-start.19 = (s32[2,8]{1,0:T(2,128)S(1)}, s32[2,8]{1,0:T(2,128)}, u32[]{:S(2)}) copy-start(s32[2,8]{1,0:T(2,128)} %param.14) | copy-start | bytes 196
  62.9 17.6 %copy-start.20 = (s32[8]{0:T(128)S(1)}, s32[8]{0:T(128)}, u32[]{:S(2)}) copy-start(s32[8]{0:T(128)} %constant.67.clone) | copy-start | bytes 100
  63.0 17.6 %copy-start.21 = (s32[8]{0:T(128)S(1)}, s32[8]{0:T(128)}, u32[]{:S(2)}) copy-start(s32[8]{0:T(128)} %constant.66.clone) | copy-start | bytes 100
  63.0 17.6 %copy-start.22 = (s32[8]{0:T(128)S(1)}, s32[8]{0:T(128)}, u32[]{:S(2)}) copy-start(s32[8]{0:T(128)} %constant.69.clone) | copy-start | bytes 100
  63.0 17.6 %copy-start.23 = (s32[8]{0:T(128)S(1)}, s32[8]{0:T(128)}, u32[]{:S(2)}) copy-start(s32[8]{0:T(128)} %constant.68.clone) | copy-start | bytes 100
  79.7 4.0 %copy-start.8 = (bf16[3520,128]{1,0:T(8,128)(2,1)}, bf16[3520,128]{1,0:T(8,128)(2,1)S(1)}, u32[]{:S(2)}) copy-start(bf16[3520,128]{1,0:T(8,128)(2,1)S(1)} %collective-permute-done.10.rest_6_) | copy-start | bytes 2703364
  79.7 4.0 %copy-start.9 = (bf16[3520,128]{1,0:T(8,128)(2,1)}, bf16[3520,128]{1,0:T(8,128)(2,1)S(1)}, u32[]{:S(2)}) copy-start(bf16[3520,128]{1,0:T(8,128)(2,1)S(1)} %collective-permute-done.11.rest_7_) | copy-start | bytes 2703364
  79.7 3.0 collective-permute-start.12
  79.8 3.8 collective-permute-start.13
  188.6 9.3 %collective-permute-start.14 = (bf16[3,7040,128]{2,1,0:T(8,128)(2,1)}, bf16[3,7040,128]{2,1,0:T(8,128)(2,1)}, u32[]{:S(2)}, u32[]{:S(2)}) collective-permute-start(bf16[3,7040,128]{2,1,0:T(8,128)(2,1)} %get-tuple-element.110), channel_id=1, source_target_pairs={{0,1},{1,0},{2,3},{3,2},{4,5},{5,4},{6,7},{7,6},{8,9},{9,8},{10,11... | collective-permute-start | bytes 16220168 | tf_op jit(solution)/shard_map/ppermute | solution.py:188
  206.4 22.3 %collective-permute-start.15 = (bf16[3520,128]{1,0:T(8,128)(2,1)}, bf16[3520,128]{1,0:T(8,128)(2,1)S(1)}, u32[]{:S(2)}, u32[]{:S(2)}) collective-permute-start(bf16[3520,128]{1,0:T(8,128)(2,1)} %get-tuple-element.121), channel_id=1, source_target_pairs={{0,4},{1,5},{2,6},{3,7},{4,0},{5,1},{6,2},{7,3},{8,12},{9,13},{10,... | collective-permute-start | bytes 2703368 | tf_op jit(solution)/shard_map/ppermute | solution.py:188
  207.5 22.0 %collective-permute-start.16 = (bf16[3520,128]{1,0:T(8,128)(2,1)}, bf16[3520,128]{1,0:T(8,128)(2,1)S(1)}, u32[]{:S(2)}, u32[]{:S(2)}) collective-permute-start(bf16[3520,128]{1,0:T(8,128)(2,1)} %get-tuple-element.132), channel_id=1, source_target_pairs={{0,2},{1,3},{2,0},{3,1},{4,6},{5,7},{6,4},{7,5},{8,10},{9,11},{10,... | collective-permute-start | bytes 2703368 | tf_op jit(solution)/shard_map/ppermute | solution.py:188
  228.7 22.9 %copy-start.13 = (bf16[3520,128]{1,0:T(8,128)(2,1)}, bf16[3520,128]{1,0:T(8,128)(2,1)S(1)}, u32[]{:S(2)}) copy-start(bf16[3520,128]{1,0:T(8,128)(2,1)S(1)} %collective-permute-done.15.y_one) | copy-start | bytes 2703364
  229.5 22.1 %copy-start.14 = (bf16[3520,128]{1,0:T(8,128)(2,1)}, bf16[3520,128]{1,0:T(8,128)(2,1)S(1)}, u32[]{:S(2)}) copy-start(bf16[3520,128]{1,0:T(8,128)(2,1)S(1)} %collective-permute-done.16.x_one) | copy-start | bytes 2703364
  229.5 3.9 %collective-permute-start.17 = (bf16[1,7040,128]{2,1,0:T(8,128)(2,1)}, bf16[1,7040,128]{2,1,0:T(8,128)(2,1)S(1)}, u32[]{:S(2)}, u32[]{:S(2)}) collective-permute-start(bf16[1,7040,128]{2,1,0:T(8,128)(2,1)} %get-tuple-element.134), channel_id=1, source_target_pairs={{0,1},{1,0},{2,3},{3,2},{4,5},{5,4},{6,7},{7,6},{8,9},{9,8},{10,11... | collective-permute-start | bytes 5406728 | tf_op jit(solution)/shard_map/ppermute | solution.py:188
  233.4 1.2 copy-start.7
  240.4 22.3 %collective-permute-start.18 = (bf16[3520,128]{1,0:T(8,128)(2,1)}, bf16[3520,128]{1,0:T(8,128)(2,1)S(1)}, u32[]{:S(2)}, u32[]{:S(2)}) collective-permute-start(bf16[3520,128]{1,0:T(8,128)(2,1)} %get-tuple-element.136), channel_id=1, source_target_pairs={{0,4},{1,5},{2,6},{3,7},{4,0},{5,1},{6,2},{7,3},{8,12},{9,13},{10,... | collective-permute-start | bytes 2703368 | tf_op jit(solution)/shard_map/ppermute | solution.py:188
  241.2 22.0 %collective-permute-start.19 = (bf16[3520,128]{1,0:T(8,128)(2,1)}, bf16[3520,128]{1,0:T(8,128)(2,1)S(1)}, u32[]{:S(2)}, u32[]{:S(2)}) collective-permute-start(bf16[3520,128]{1,0:T(8,128)(2,1)} %get-tuple-element.145), channel_id=1, source_target_pairs={{0,2},{1,3},{2,0},{3,1},{4,6},{5,7},{6,4},{7,5},{8,10},{9,11},{10,... | collective-permute-start | bytes 2703368 | tf_op jit(solution)/shard_map/ppermute | solution.py:188
  270.7 27.3 %copy-start.11 = (bf16[3520,128]{1,0:T(8,128)(2,1)S(1)}, bf16[3520,128]{1,0:T(8,128)(2,1)}, u32[]{:S(2)}) copy-start(bf16[3520,128]{1,0:T(8,128)(2,1)} %get-tuple-element.146) | copy-start | bytes 2703364
  270.8 21.3 %collective-permute-start.25 = (bf16[3520,128]{1,0:T(8,128)(2,1)}, bf16[3520,128]{1,0:T(8,128)(2,1)S(1)}, u32[]{:S(2)}, u32[]{:S(2)}) collective-permute-start(bf16[3520,128]{1,0:T(8,128)(2,1)} %get-tuple-element.149), channel_id=1, source_target_pairs={{0,4},{1,5},{2,6},{3,7},{4,0},{5,1},{6,2},{7,3},{8,12},{9,13},{10,... | collective-permute-start | bytes 2703368 | tf_op jit(solution)/shard_map/ppermute | solution.py:188
  272.1 25.9 %collective-permute-start.20 = (bf16[3520,128]{1,0:T(8,128)(2,1)}, bf16[3520,128]{1,0:T(8,128)(2,1)S(1)}, u32[]{:S(2)}, u32[]{:S(2)}) collective-permute-start(bf16[3520,128]{1,0:T(8,128)(2,1)} %get-tuple-element.147), channel_id=1, source_target_pairs={{0,2},{1,3},{2,0},{3,1},{4,6},{5,7},{6,4},{7,5},{8,10},{9,11},{10,... | collective-permute-start | bytes 2703368 | tf_op jit(solution)/shard_map/ppermute | solution.py:188
  295.5 21.4 %collective-permute-start.26 = (bf16[1760,128]{1,0:T(8,128)(2,1)}, bf16[1760,128]{1,0:T(8,128)(2,1)S(1)}, u32[]{:S(2)}, u32[]{:S(2)}) collective-permute-start(bf16[1760,128]{1,0:T(8,128)(2,1)} %dynamic-slice_bitcast_fusion), channel_id=1, source_target_pairs={{0,16},{8,24},{16,0},{24,8},{1,17},{9,25},{17,1},{25,9},{2,18},{10... | collective-permute-start | bytes 1351688 | tf_op jit(solution)/shard_map/ppermute | solution.py:1118
  298.4 19.2 %collective-permute-start.21 = (bf16[1760,128]{1,0:T(8,128)(2,1)S(1)}, bf16[1760,128]{1,0:T(8,128)(2,1)S(1)}, u32[]{:S(2)}, u32[]{:S(2)}) collective-permute-start(bf16[1760,128]{1,0:T(8,128)(2,1)S(1)} %dynamic-slice_bitcast_fusion.1), channel_id=1, source_target_pairs={{0,8},{8,0},{16,24},{24,16},{1,9},{9,1},{17,25},{25,17},{2,10},{10... | collective-permute-start | bytes 1351688 | tf_op jit(solution)/shard_map/ppermute | solution.py:1118
  317.0 12.4 %collective-permute-start.27 = (bf16[880,128]{1,0:T(8,128)(2,1)S(1)}, bf16[880,128]{1,0:T(8,128)(2,1)S(1)}, u32[]{:S(2)}, u32[]{:S(2)}) collective-permute-start(bf16[880,128]{1,0:T(8,128)(2,1)S(1)} %dynamic-slice_bitcast_fusion.2), channel_id=1, source_target_pairs={{0,8},{8,0},{16,24},{24,16},{1,9},{9,1},{17,25},{25,17},{2,10},{10... | collective-permute-start | bytes 675848 | tf_op jit(solution)/shard_map/ppermute | solution.py:1118
  317.7 13.8 %collective-permute-start.22 = (bf16[880,128]{1,0:T(8,128)(2,1)S(1)}, bf16[880,128]{1,0:T(8,128)(2,1)S(1)}, u32[]{:S(2)}, u32[]{:S(2)}) collective-permute-start(bf16[880,128]{1,0:T(8,128)(2,1)S(1)} %dynamic-slice_bitcast_fusion.3), channel_id=1, source_target_pairs={{0,16},{8,24},{16,0},{24,8},{1,17},{9,25},{17,1},{25,9},{2,18},{10... | collective-permute-start | bytes 675848 | tf_op jit(solution)/shard_map/ppermute | solution.py:1118
  329.4 6.9 %collective-permute-start.28 = (bf16[880,128]{1,0:T(8,128)(2,1)S(1)}, bf16[880,128]{1,0:T(8,128)(2,1)S(1)}, u32[]{:S(2)}, u32[]{:S(2)}) collective-permute-start(bf16[880,128]{1,0:T(8,128)(2,1)S(1)} %bitcast_add_fusion.2), channel_id=1, source_target_pairs={{0,8},{8,0},{16,24},{24,16},{1,9},{9,1},{17,25},{25,17},{2,10},{10... | collective-permute-start | bytes 675848 | tf_op jit(solution)/shard_map/ppermute | solution.py:1118
  331.5 22.3 %collective-permute-start.23 = (bf16[880,128]{1,0:T(8,128)(2,1)S(1)}, bf16[880,128]{1,0:T(8,128)(2,1)S(1)}, u32[]{:S(2)}, u32[]{:S(2)}) collective-permute-start(bf16[880,128]{1,0:T(8,128)(2,1)S(1)} %bitcast_add_fusion.3), channel_id=1, source_target_pairs={{0,16},{8,24},{16,0},{24,8},{1,17},{9,25},{17,1},{25,9},{2,18},{10... | collective-permute-start | bytes 675848 | tf_op jit(solution)/shard_map/ppermute | solution.py:1118
  336.4 25.4 %collective-permute-start.29 = (bf16[1760,128]{1,0:T(8,128)(2,1)S(1)}, bf16[1760,128]{1,0:T(8,128)(2,1)S(1)}, u32[]{:S(2)}, u32[]{:S(2)}) collective-permute-start(bf16[1760,128]{1,0:T(8,128)(2,1)S(1)} %maximum_select_fusion.3), channel_id=1, source_target_pairs={{0,16},{8,24},{16,0},{24,8},{1,17},{9,25},{17,1},{25,9},{2,18},{10... | collective-permute-start | bytes 1351688 | tf_op jit(solution)/shard_map/ppermute | solution.py:1118
  338.5 33.1 %copy-start.3 = (f32[900608]{0:T(1024)S(1)}, f32[900608]{0:T(1024)}, u32[]{:S(2)}) copy-start(f32[900608]{0:T(1024)} %param.18) | copy-start | bytes 10807300
  354.0 17.4 %collective-permute-start.24 = (bf16[1760,128]{1,0:T(8,128)(2,1)S(1)}, bf16[1760,128]{1,0:T(8,128)(2,1)S(1)}, u32[]{:S(2)}, u32[]{:S(2)}) collective-permute-start(bf16[1760,128]{1,0:T(8,128)(2,1)S(1)} %maximum_select_fusion.2), channel_id=1, source_target_pairs={{0,8},{8,0},{16,24},{24,16},{1,9},{9,1},{17,25},{25,17},{2,10},{10... | collective-permute-start | bytes 1351688 | tf_op jit(solution)/shard_map/ppermute | solution.py:1118
  (6 other events, 5.5 us)

commit v4 on v3

--- a/solution.py
+++ b/solution.py
@@ -975,133 +975,55 @@
     )(me, x, dq, dk, dv, bg, edge)
 
 
-def merge_late_kernel(me_ref, keep, got, sums, along_y, along_x):
-    chip, half = pl.program_id(0) + 1, pl.program_id(1)
+def combine_kernel(plan, extra, me_ref, *refs):
     x, y = (me_ref[0] >> 1) & 1, me_ref[0] >> 2
-    total = keep[0] + got[0]
-    sums[0, 0] = total
-
-    @pl.when((half == 0) & (chip == 3 - 2 * y))
-    def _():
-        along_y[...] = total
-
-    @pl.when((half == 1) & (chip == 3 - x))
-    def _():
-        along_x[...] = total
-
-
-def merge_late(me, keep, got):
-    half = keep.shape[1] // 2
-    block = pl.BlockSpec((1, half, LANE), lambda c, h: (c, h, 0))
-    return pl.pallas_call(
-        merge_late_kernel,
-        grid=(3, 2),
-        in_specs=[SM, block, block],
-        out_specs=[pl.BlockSpec((1, 1, half, LANE), lambda c, h: (c + 1, h, 0, 0)), whole(half, LANE), whole(half, LANE)],
-        out_shape=[SDS((4, 2, half, LANE), BF), SDS((half, LANE), BF), SDS((half, LANE), BF)],
+    late_keep, late_got, early_keep, early_got = refs[:4]
+    extras, outs = refs[4 : 4 + extra], refs[4 + extra : 4 + extra + len(plan)]
+    buf, sems = refs[-2:]
+
+    def into(n, src, side):
+        return pltpu.make_async_copy(src, buf.at[n, side], sems.at[n])
+
+    for n, (which, first, rows, added) in enumerate(plan):
+        chip, span = which(x, y), pl.ds(first, rows)
+
+        @pl.when(chip == 0)
+        def _(n=n, span=span):
+            into(n, early_keep.at[0, span], 0).start()
+            into(n, early_got.at[0, span], 1).start()
+
+        @pl.when(chip != 0)
+        def _(n=n, span=span, chip=chip):
+            into(n, late_keep.at[chip - 1, span], 0).start()
+            into(n, late_got.at[chip - 1, span], 1).start()
+
+        if added is not None:
+            bit, *options = added
+            for value, (array, row) in zip((1, 0), options):
+
+                @pl.when(bit(x, y) == value)
+                def _(n=n, rows=rows, array=array, row=row):
+                    into(n, extras[array].at[pl.ds(row, rows)], 2).start()
+
+    for n, (_, first, rows, added) in enumerate(plan):
+        for side in range(2 if added is None else 3):
+            into(n, late_keep.at[0, pl.ds(first, rows)], side).wait()
+        total = buf[n, 0] + buf[n, 1]
+        outs[n][...] = total if added is None else total + buf[n, 2]
+
+
+def combine(me, parts, extras, plan, name):
+    rows = plan[0][2]
+    return pl.pallas_call(
+        functools.partial(combine_kernel, plan, len(extras)),
+        in_specs=[SM] + [ANY] * (4 + len(extras)),
+        out_specs=[VM] * len(plan),
+        out_shape=[SDS((rows, LANE), BF)] * len(plan),
+        scratch_shapes=[pltpu.VMEM((len(plan), 3, rows, LANE), BF), pltpu.SemaphoreType.DMA((len(plan),))],
         compiler_params=params_of(),
         cost_estimate=TINY,
-        name="merge_late",
-    )(me, keep, got)
-
-
-def merge_early_kernel(me_ref, keep, got, old, sums, along_y, along_x, total, sems):
-    x, y = (me_ref[0] >> 1) & 1, me_ref[0] >> 2
-    half = total.shape[1]
-    for h in range(2):
-        total[h] = keep[0, h * half : (h + 1) * half] + got[0, h * half : (h + 1) * half]
-    put = pltpu.make_async_copy(total, sums.at[0], sems.at[0])
-    put.start()
-    fetch_y = pltpu.make_async_copy(sums.at[2, 0], along_y, sems.at[1])
-    fetch_x = pltpu.make_async_copy(sums.at[1, 1], along_x, sems.at[2])
-
-    @pl.when(y == 0)
-    def _():
-        fetch_y.start()
-
-    @pl.when(y == 1)
-    def _():
-        along_y[...] = total[0]
-
-    @pl.when(x == 0)
-    def _():
-        fetch_x.start()
-
-    @pl.when(x == 1)
-    def _():
-        along_x[...] = total[1]
-
-    put.wait()
-
-    @pl.when(y == 0)
-    def _():
-        fetch_y.wait()
-
-    @pl.when(x == 0)
-    def _():
-        fetch_x.wait()
-
-
-def merge_early(me, keep, got, sums):
-    half = keep.shape[1] // 2
-    return pl.pallas_call(
-        merge_early_kernel,
-        in_specs=[SM, VM, VM, ANY],
-        out_specs=[ANY, VM, VM],
-        out_shape=[SDS(sums.shape, BF), SDS((half, LANE), BF), SDS((half, LANE), BF)],
-        scratch_shapes=[pltpu.VMEM((2, half, LANE), BF), pltpu.SemaphoreType.DMA((3,))],
-        input_output_aliases={3: 0},
-        compiler_params=params_of(),
-        cost_estimate=TINY,
-        name="merge_early",
-    )(me, keep, got, sums)
-
-
-def merge_next_kernel(me_ref, sums, y_one, y_two, x_one, x_two, own_a, own_b, along_x, along_y, buf, sems):
-    x, y = (me_ref[0] >> 1) & 1, me_ref[0] >> 2
-    chip = me_ref[0] >> 1
-    reads = [
-        pltpu.make_async_copy(sums.at[c, h], buf.at[n], sems.at[n])
-        for n, (c, h) in enumerate(((chip, 0), (chip, 1), (chip ^ 1, 0), (chip ^ 2, 1)))
-    ]
-    for read in reads:
-        read.start()
-    for read in reads:
-        read.wait()
-
-    @pl.when(x == 0)
-    def _():
-        own_a[...] = buf[0] + y_two[...]
-        along_x[...] = buf[2] + y_one[...]
-
-    @pl.when(x == 1)
-    def _():
-        own_a[...] = buf[0] + y_one[...]
-        along_x[...] = buf[2] + y_two[...]
-
-    @pl.when(y == 0)
-    def _():
-        own_b[...] = buf[1] + x_two[...]
-        along_y[...] = buf[3] + x_one[...]
-
-    @pl.when(y == 1)
-    def _():
-        own_b[...] = buf[1] + x_one[...]
-        along_y[...] = buf[3] + x_two[...]
-
-
-def merge_next(me, sums, y_one, y_two, x_one, x_two):
-    half = sums.shape[2]
-    return pl.pallas_call(
-        merge_next_kernel,
-        in_specs=[SM, ANY, VM, VM, VM, VM],
-        out_specs=[VM] * 4,
-        out_shape=[SDS((half, LANE), BF)] * 4,
-        scratch_shapes=[pltpu.VMEM((4, half, LANE), BF), pltpu.SemaphoreType.DMA((4,))],
-        compiler_params=params_of(),
-        cost_estimate=TINY,
-        name="merge_next",
-    )(me, sums, y_one, y_two, x_one, x_two)
+        name=name,
+    )(me, *parts, *extras)
 
 
 def part(v, pieces, i):
@@ -1112,23 +1034,49 @@
     return jnp.where(first == 0, jnp.concatenate([own, other]), jnp.concatenate([other, own]))
 
 
-def sum_replicas(one, two):
+def sum_replicas(one, two, later):
     z = lax.axis_index("rep")
     low, high = z & 1, z >> 1
     turn = lambda v, bit: lax.ppermute(v, "rep", [(i, i ^ bit) for i in range(4)])
     got_one, got_two = turn(part(one, 2, 1 - low), 1), turn(part(two, 2, 1 - high), 2)
+    got_one, got_two, later = lax.optimization_barrier((got_one, got_two, later))
     one, two = part(one, 2, low) + got_one, part(two, 2, high) + got_two
     got_one, got_two = turn(part(one, 2, 1 - high), 2), turn(part(two, 2, 1 - low), 1)
     one, two = part(one, 2, high) + got_one, part(two, 2, low) + got_two
     one, two = join(one, turn(one, 2), high), join(two, turn(two, 1), low)
-    return join(one, turn(one, 1), low), join(two, turn(two, 2), high)
+    return (one, turn(one, 1), two, turn(two, 2)), later
 
 
 def adam_update(first_part, second_part, grad_part):
     first_new = BETA_ONE * first_part + (1.0 - BETA_ONE) * grad_part
     second_new = BETA_TWO * second_part + (1.0 - BETA_TWO) * grad_part * grad_part
-    step_dir = first_new / CORRECT_ONE / (jnp.sqrt(second_new / CORRECT_TWO) + ADAM_EPS)
+    step_dir = first_new * (1.0 / CORRECT_ONE) / (jnp.sqrt(second_new * (1.0 / CORRECT_TWO)) + ADAM_EPS)
     return (step_dir, first_new, second_new)
+
+
+def adam_part(z, chunk, pieces, moment_one, moment_two, done):
+    rows = moment_one.shape[0]
+    size = pieces[0].shape[0]
+    block = pl.BlockSpec((size, LANE), lambda i: ((i >> 1) * 4 + chunk * 2 + (i & 1), 0))
+
+    def kernel(z_ref, one, one_other, two, two_other, m_one, m_two, *refs):
+        step_ref, first_ref, second_ref = refs[len(done) :]
+        i = pl.program_id(0)
+        own = (i & 1) == jnp.where(i < 2, z_ref[0] & 1, z_ref[0] >> 1)
+        grad = jnp.where(i < 2, jnp.where(own, one[...], one_other[...]), jnp.where(own, two[...], two_other[...]))
+        step_ref[...], first_ref[...], second_ref[...] = adam_update(m_one[...], m_two[...], grad.astype(F32))
+
+    return pl.pallas_call(
+        kernel,
+        grid=(4,),
+        in_specs=[SM] + [VM] * 4 + [block] * 2 + [ANY] * len(done),
+        out_specs=[block] * 3,
+        out_shape=[SDS((rows, LANE), F32)] * 3,
+        input_output_aliases={7 + i: i for i in range(len(done))},
+        compiler_params=params_of(12),
+        cost_estimate=TINY,
+        name="adam",
+    )(z, *pieces, moment_one, moment_two, *done)
 
 
 def shards(inputs, seg_ids, example_map, labels, out_cotangent, params, moment_one, moment_two):
@@ -1159,25 +1107,47 @@
     late = [flat2(v) for v in (att, dbr, nbf, dinner, act, dffn, out, dstu)] + [vg, sg, gmid, gcls]
     if count == 8:
         me = lax.axis_index("fsdp").reshape(1)
-        keep, give, edge = late_pairs(me, shard_rows, padded, *late)
-        got = swap(give, 1)
+        half, size = padded // 2, padded // 4
+        late_keep, give, edge = late_pairs(me, shard_rows, padded, *late)
+        late_got = swap(give, 1)
         back = retreat(0, q, k, v, probs, datt, ())
-        got, back = lax.optimization_barrier((got, tuple(back)))
-        sums, along_y, along_x = merge_late(me, keep, got)
+        late_got, back = lax.optimization_barrier((late_got, tuple(back)))
+        parts = (late_keep, late_got, late_keep, late_got)
+        plan = [(lambda x, y: 3 - 2 * y, 0, half, None), (lambda x, y: 3 - x, half, half, None)]
+        along_y, along_x = combine(me, parts, (), plan, "combine_one")
         y_one, x_one = swap(along_y, 4), swap(along_x, 2)
         back, _ = lax.optimization_barrier((back, along_y))
         for row in range(1, rows):
             back = retreat(row, q, k, v, probs, datt, tuple(back))
         *dproj, bg = back
-        keep, give = early_pairs(me, shard_rows, padded, flat2(inputs), *map(flat2, dproj), bg, edge)
+        early_keep, give = early_pairs(me, shard_rows, padded, flat2(inputs), *map(flat2, dproj), bg, edge)
         y_one, x_one, give = lax.optimization_barrier((y_one, x_one, give))
-        sums, along_y, along_x = merge_early(me, keep, swap(give, 1), sums)
-        y_two, x_two = swap(along_y, 4), swap(along_x, 2)
-        dproj, _ = lax.optimization_barrier((dproj, along_y))
+        parts = (late_keep, late_got, early_keep, swap(give, 1))
+        plan = [(lambda x, y: 2 - 2 * y, 0, size, None), (lambda x, y: 1 - x, half, size, None)]
+        plan += [(which, first + size, size, None) for which, first, *_ in plan]
+        *pairs, = combine(me, parts, (), plan, "combine_two")
+        arrived = [(swap(pairs[2 * c], 4), swap(pairs[2 * c + 1], 2)) for c in range(2)]
+        dproj, _ = lax.optimization_barrier((dproj, pairs[0]))
         dx = project_back(*dproj, dh1, wqkv)
-        y_two, _ = lax.optimization_barrier((y_two, dx))
-        own_a, own_b, along_x, along_y = merge_next(me, sums, y_one, y_two, x_one, x_two)
-        own_a, own_b = own_a + swap(along_x, 2), own_b + swap(along_y, 4)
+        sent, own, after = [], [], dx
+        here = lambda x, y: y * 2 + x
+        for c in range(2):
+            arrived_c, _ = lax.optimization_barrier((arrived[c], after))
+            extras = (y_one, x_one, *arrived_c)
+            plan = [
+                (lambda x, y: y * 2 + 1 - x, c * size, size, (lambda x, y: x, (2, 0), (0, c * size))),
+                (lambda x, y: (1 - y) * 2 + x, half + c * size, size, (lambda x, y: y, (3, 0), (1, c * size))),
+            ]
+            along_x, along_y = combine(me, parts, extras, plan, "combine_three")
+            sent.append((swap(along_x, 2), swap(along_y, 4)))
+            plan = [
+                (here, c * size, size, (lambda x, y: x, (0, c * size), (2, 0))),
+                (here, half + c * size, size, (lambda x, y: y, (1, c * size), (3, 0))),
+            ]
+            extras, _ = lax.optimization_barrier((extras, sent[0] if c else along_x))
+            after = combine(me, parts, extras, plan, "combine_own")
+            own.append(after)
+        sums = [(own[c][0] + sent[c][0], own[c][1] + sent[c][1]) for c in range(2)]
     else:
         partial, edge = late_grads(shard_rows, count, padded, *late)
         back = ()
@@ -1187,14 +1157,20 @@
         grads = early_grads(shard_rows, flat2(inputs), *map(flat2, dproj), bg, edge, partial)
         owned = lax.psum_scatter(grads, "fsdp", scatter_dimension=0, tiled=False)
         dx = project_back(*dproj, dh1, wqkv)
-    if count != 8:
+    if count == 8 and lax.axis_size("rep") == 4:
+        tall = lambda v: v.reshape(shard_rows, LANE)
+        z = lax.axis_index("rep").reshape(1)
+        done = ()
+        for c in range(2):
+            pieces, sums[1] = sum_replicas(*sums[c], sums[1])
+            done = adam_part(z, c, pieces, tall(moment_one), tall(moment_two), tuple(done))
+        step_dir, first_new, second_new = (v.reshape(-1) for v in done)
+    else:
+        if count == 8:
+            owned = jnp.concatenate([sums[0][0], sums[1][0], sums[0][1], sums[1][1]])
         owned = lax.psum(owned, "rep")
-    elif lax.axis_size("rep") == 4:
-        owned = jnp.concatenate(sum_replicas(own_a, own_b))
-    else:
-        owned = lax.psum(jnp.concatenate([own_a, own_b]), "rep")
-    grad = owned[:shard_rows].astype(F32).reshape(-1)
-    step_dir, first_new, second_new = adam_update(moment_one, moment_two, grad)
+        grad = owned[:shard_rows].astype(F32).reshape(-1)
+        step_dir, first_new, second_new = adam_update(moment_one, moment_two, grad)
     return (out, logits, dx, step_dir, first_new, second_new)
 
 

time: 384 us -> 340 us (0.89)
  waiting for transfers between devices: 143 us -> 95.8 us
  starting transfers between devices: 28.4 us -> 39.6 us
  other arithmetic: 21.2 us -> 10 us
  Pallas kernels: 178 us -> 182 us
    ppermute x22 -> x26, waiting for transfers between devices: 79.2 us -> 55.2 us  [swap(): return lax.ppermute(v, 'fsdp', [(d, d ^ bit) for d in range(8)])]
    ppermute x8 -> x16, waiting for transfers between devices: 64 us -> 40.6 us  [sum_replicas(): lax.ppermute(v, 'rep', [(i, i ^ bit) for i in range(4)])]
    div x1 -> x0, other arithmetic: 11.3 us -> none  [adam_update(): first_new / CORRECT_ONE / (jnp.sqrt(second_new / CORRECT_TWO) + ADAM_EPS)]
    ppermute x8 -> x16, starting transfers between devices: 10.8 us -> 16.9 us  [sum_replicas(): lax.ppermute(v, 'rep', [(i, i ^ bit) for i in range(4)])]
    ppermute x22 -> x26, starting transfers between devices: 17.7 us -> 22.7 us  [swap(): return lax.ppermute(v, 'fsdp', [(d, d ^ bit) for d in range(8)])]
    pallas_call x3 -> x8, Pallas kernels: 20.9 us -> 24.6 us  [the longest x6 17.9 us: combine(): pl.pallas_call(functools.partial(combine_kernel, plan, len(extras)), in_s...]
  transfers between devices with their start and end apart: 30 -> 42, of which waited for: 19 -> 22; matrix products, arithmetic and copies ran while one was open for 3% -> 3% of each run, Pallas kernels for 14% -> 21%
where the time goes in v4:
time: 340 us; the launch traced here: 339 us
  Pallas kernels  182 us (54%)
  waiting for transfers between devices  95.8 us (28%)
  starting transfers between devices  39.6 us (12%)
  local copies, waits for them, and re-layouts  10.6 us (3%)
  other arithmetic  10 us (3%)
    pallas_call x1, Pallas kernels, middle(): pl.pallas_call(middle_kernel, grid=(rows,), in_specs=[row_spec(LEN, D), r...  63.5 us
    ppermute x26, waiting for transfers between devices, swap(): return lax.ppermute(v, 'fsdp', [(d, d ^ bit) for d in range(8)])  55.2 us
    ppermute x16, waiting for transfers between devices, sum_replicas(): lax.ppermute(v, 'rep', [(i, i ^ bit) for i in range(4)])  40.6 us
    pallas_call x1, Pallas kernels, late_pairs(): pl.pallas_call(functools.partial(late_pair_kernel, shard_rows), in_specs=...  23.8 us
    ppermute x26, starting transfers between devices, swap(): return lax.ppermute(v, 'fsdp', [(d, d ^ bit) for d in range(8)])  22.7 us
    pallas_call x6, Pallas kernels, combine(): pl.pallas_call(functools.partial(combine_kernel, plan, len(extras)), in_s...  17.9 us
    ppermute x16, starting transfers between devices, sum_replicas(): lax.ppermute(v, 'rep', [(i, i ^ bit) for i in range(4)])  16.9 us
    pallas_call x1, Pallas kernels, attend(): pl.pallas_call(attend_kernel, grid=(rows, D // 256), in_specs=[only(LEN,...  16.7 us
  transfers between devices with their start and end apart: 42, of which 22 were waited for; matrix products, arithmetic and copies ran while one was open for 3% of the time, Pallas kernels for 21%

profile of v4, /device:TPU:0, one launch (start us, length us, event | category | flops | bytes accessed | tf_op | source)
XLA Modules:
  0.0 339.1 jit_solution(1121424018878039213)
XLA Ops:
  0.6 2.2 convert.4
  3.1 3.0 collective-permute-start
  6.1 1.5 collective-permute-start.1
  7.6 18.5 %collective-permute-done.rest_2_ = bf16[3520,128]{1,0:T(8,128)(2,1)S(1)} collective-permute-done((bf16[3520,128]{1,0:T(8,128)(2,1)S(1)}, bf16[3520,128]{1,0:T(8,128)(2,1)S(1)}, u32[]{:S(2)}, u32[]{:S(2)}) %collective-permute-start) | collective-permute-done | bytes 901152 | tf_op jit(solution)/shard_map/ppermute | solution.py:188
  27.3 1.8 collective-permute-start.2
  29.0 2.2 broadcast_select_fusion
  31.2 1.5 collective-permute-start.3
  33.3 15.3 %collective-permute-done.2.rest_4_ = bf16[3520,128]{1,0:T(8,128)(2,1)} collective-permute-done((bf16[3520,128]{1,0:T(8,128)(2,1)S(1)}, bf16[3520,128]{1,0:T(8,128)(2,1)}, u32[]{:S(2)}, u32[]{:S(2)}) %collective-permute-start.2) | collective-permute-done | bytes 901152 | tf_op jit(solution)/shard_map/ppermute | solution.py:188
  48.7 3.9 %collective-permute-done.3.rest_5_ = bf16[3520,128]{1,0:T(8,128)(2,1)} collective-permute-done((bf16[3520,128]{1,0:T(8,128)(2,1)S(1)}, bf16[3520,128]{1,0:T(8,128)(2,1)}, u32[]{:S(2)}, u32[]{:S(2)}) %collective-permute-start.3) | collective-permute-done | bytes 901152 | tf_op jit(solution)/shard_map/ppermute | solution.py:188
  52.6 1.6 collective-permute-start.10
  58.2 4.7 %unpack_first.1 = (bf16[768,2304]{1,0:T(8,128)(2,1)}, f32[8,2304]{1,0:T(8,128)}) custom-call(s32[1]{0:T(128)} %bitcast.1.me_ref, bf16[3520,128]{1,0:T(8,128)(2,1)} %copy-done.3, bf16[3520,128]{1,0:T(8,128)(2,1)} %copy-done.4, bf16[3520,128]{1,0:T(8,128)(2,1)} %copy-done.7, bf16[3520,128]{1,0:T(8,128)(2,1)} %collective-permute-done.1.rest_3_, ...), custom_call_target="tpu_custom_call" | custom-call | flops 1 | bytes 1 | tf_op jit(solution)/shard_map/unpack_first/pallas_call | solution.py:237
  63.0 16.7 %attend.1 = (bf16[2,512,768]{2,1,0:T(8,128)(2,1)}, bf16[2,512,768]{2,1,0:T(8,128)(2,1)}, bf16[2,512,768]{2,1,0:T(8,128)(2,1)}, bf16[2,6,256,1280]{3,2,1,0:T(8,128)(2,1)}, bf16[2,512,768]{2,1,0:T(8,128)(2,1)}) custom-call(bf16[2,512,768]{2,1,0:T(8,128)(2,1)} %x_ref.3, s32[2,512,1]{2,1,0:T(8,128)} %copy.26.segc_ref, s32[2,1,512]{2,1,0:T(1,128)} %broadcast_in_dim.24.segr_ref, ...), custom_call_target="tpu_custom_call" | custom-call | flops 1 | bytes 1 | tf_op jit(solution)/shard_map/attend/pallas_call | solution.py:366
  83.7 14.6 %unpack_rest.1 = (bf16[768,768]{1,0:T(8,128)(2,1)}, bf16[768,3072]{1,0:T(8,128)(2,1)}, bf16[3072,768]{1,0:T(8,128)(2,1)}, bf16[768,128]{1,0:T(8,128)(2,1)}, f32[...) custom-call(s32[8]{0:T(128)} %fusion.1.owner_ref, bf16[3520,128]{1,0:T(8,128)(2,1)} %copy-done.3, ...), custom_call_target="tpu_custom_call" | custom-call | flops 1 | bytes 1 | tf_op jit(solution)/shard_map/unpack_rest/pallas_call | solution.py:273
  99.7 63.5 %middle.1 = (bf16[2,512,768]{2,1,0:T(8,128)(2,1)}, f32[2,8,14]{2,1,0:T(8,128)}, bf16[2,512,768]{2,1,0:T(8,128)(2,1)}, bf16[2,512,3072]{2,1,0:T(8,128)(2,1)}, bf1...) custom-call(bf16[2,512,768]{2,1,0:T(8,128)(2,1)} %x_ref.3, ...), custom_call_target="tpu_custom_call" | custom-call | flops 1 | bytes 1 | tf_op jit(solution)/shard_map/middle/pallas_call | solution.py:607
  164.8 23.8 %late_grads.1 = (bf16[3,7040,128]{2,1,0:T(8,128)(2,1)}, bf16[3,7040,128]{2,1,0:T(8,128)(2,1)}, f32[240,128]{1,0:T(8,128)}) custom-call(s32[1]{0:T(128)} %bitcast.1.me_ref, bf16[1024,768]{1,0:T(8,128)(2,1)} %bitcast.76, bf16[1024,768]{1,0:T(8,128)(2,1)} %bitcast.91, bf16[1024,768]{1,0:T(8,128)(2,1)} %bitcast.89, bf16[1024,3072]{1,0:T(8,128)(2,1)} %bitcast.75, ...), custom_call_target="tpu_custom_call" | custom-call | flops 1 | bytes 1 | tf_op jit(solution)/shard_map/late_grads/pallas_call | solution.py:944
  188.7 7.8 %retreat.2 = (bf16[2,512,768]{2,1,0:T(8,128)(2,1)}, bf16[2,512,768]{2,1,0:T(8,128)(2,1)}, bf16[2,512,768]{2,1,0:T(8,128)(2,1)}, f32[8,768]{1,0:T(8,128)}) custom-call(bf16[2,512,768]{2,1,0:T(8,128)(2,1)} %get-tuple-element.122.refs_0_, bf16[2,512,768]{2,1,0:T(8,128)(2,1)} %get-tuple-element.123.refs_1_, bf16[2,512,768]{2,1,0:T(8,128)(2,1)} %get-tuple-element.124.refs_2_, ...), custom_call_target="tpu_custom_call" | custom-call | flops 1 | bytes 1 | tf_op jit(solution)/shard_map/retreat/pallas_call | solution.py:711
  197.9 3.4 %combine_one.1 = (bf16[3520,128]{1,0:T(8,128)(2,1)}, bf16[3520,128]{1,0:T(8,128)(2,1)}) custom-call(s32[1]{0:T(128)} %bitcast.1.me_ref, bf16[3,7040,128]{2,1,0:T(8,128)(2,1)} %get-tuple-element.146.refs_0_.refs_2_, bf16[3,7040,128]{2,1,0:T(8,128)(2,1)} %collective-permute-done.14.refs_1_.refs_3_, bf16[3,7040,128]{2,1,0:T(8,128)(2,1)} %get-tuple-element.146.refs_0_.refs_2_, ...), custom_call_target="tpu_custom_call" | custom-call | flops 1 | bytes 1 | tf_op jit(solution)/shard_map/combine_one/pallas_call | solution.py:1017
  203.7 7.9 %retreat.3 = (bf16[2,512,768]{2,1,0:T(8,128)(2,1)}, bf16[2,512,768]{2,1,0:T(8,128)(2,1)}, bf16[2,512,768]{2,1,0:T(8,128)(2,1)}, f32[8,768]{1,0:T(8,128)}) custom-call(bf16[2,512,768]{2,1,0:T(8,128)(2,1)} %get-tuple-element.122.refs_0_, bf16[2,512,768]{2,1,0:T(8,128)(2,1)} %get-tuple-element.123.refs_1_, ...), custom_call_target="tpu_custom_call", output_to_operand_aliasing={{0}: (5, {}), {1}: (6, {}), {2}: (7, {})} | custom-call | flops 1 | bytes 1 | tf_op jit(solution)/shard_map/retreat/pallas_call | solution.py:711
  211.6 8.8 %early_grads.1 = (bf16[1,7040,128]{2,1,0:T(8,128)(2,1)}, bf16[1,7040,128]{2,1,0:T(8,128)(2,1)}) custom-call(s32[1]{0:T(128)} %bitcast.1.me_ref, bf16[1024,768]{1,0:T(8,128)(2,1)} %bitcast.70, bf16[1024,768]{1,0:T(8,128)(2,1)} %bitcast.71, bf16[1024,768]{1,0:T(8,128)(2,1)} %bitcast.72, bf16[1024,768]{1,0:T(8,128)(2,1)} %bitcast.73, ...), custom_call_target="tpu_custom_call" | custom-call | flops 1 | bytes 1 | tf_op jit(solution)/shard_map/early_grads/pallas_call | solution.py:966
  220.4 3.2 collective-permute-done.15.refs_4_
  225.2 3.9 %collective-permute-done.17.refs_3_ = bf16[1,7040,128]{2,1,0:T(8,128)(2,1)S(1)} collective-permute-done((bf16[1,7040,128]{2,1,0:T(8,128)(2,1)}, bf16[1,7040,128]{2,1,0:T(8,128)(2,1)S(1)}, u32[]{:S(2)}, u32[]{:S(2)}) %collective-permute-start.17) | collective-permute-done | bytes 1802272 | tf_op jit(solution)/shard_map/ppermute | solution.py:188
  230.4 3.3 combine_two.1
  234.8 1.5 collective-permute-start.19
  237.8 9.5 %project_back.1 = bf16[2,512,768]{2,1,0:T(8,128)(2,1)} custom-call(bf16[2,512,768]{2,1,0:T(8,128)(2,1)} %get-tuple-element.163.dq_ref, bf16[2,512,768]{2,1,0:T(8,128)(2,1)} %get-tuple-element.164.dk_ref, bf16[2,512,768]{2,1,0:T(8,128)(2,1)} %get-tuple-element.165.dv_ref, f32[2,512,768]{2,1,0:T(8,128)} %get-tuple-element.166.dh1_ref, ...), custom_call_target="tpu_custom_call" | custom-call | flops 1 | bytes 1 | tf_op jit(solution)/shard_map/project_back/pallas_call | solution.py:739
  249.0 2.8 combine_three.2
  251.8 1.6 collective-permute-start.20
  254.3 2.8 combine_own.2
  258.7 2.8 combine_three.3
  261.5 1.6 collective-permute-start.26
  264.0 3.6 %collective-permute-done.20 = bf16[1760,128]{1,0:T(8,128)(2,1)S(1)} collective-permute-done((bf16[1760,128]{1,0:T(8,128)(2,1)}, bf16[1760,128]{1,0:T(8,128)(2,1)S(1)}, u32[]{:S(2)}, u32[]{:S(2)}) %collective-permute-start.20) | collective-permute-done | bytes 450592 | tf_op jit(solution)/shard_map/ppermute | solution.py:188
  267.7 1.7 collective-permute-start.21
  269.6 2.6 collective-permute-start.23
  272.2 2.8 combine_own.3
  278.4 2.0 collective-permute-done.23
  280.7 2.9 collective-permute-start.29
  283.9 1.9 collective-permute-start.39
  285.7 12.1 %collective-permute-done.36 = bf16[440,128]{1,0:T(8,128)(2,1)S(1)} collective-permute-done((bf16[440,128]{1,0:T(8,128)(2,1)S(1)}, bf16[440,128]{1,0:T(8,128)(2,1)S(1)}, u32[]{:S(2)}, u32[]{:S(2)}) %collective-permute-start.36) | collective-permute-done | bytes 112672 | tf_op jit(solution)/shard_map/ppermute | solution.py:1040
  298.0 3.3 collective-permute-start.40
  301.6 1.7 collective-permute-start.33
  303.3 3.5 %collective-permute-done.37 = bf16[440,128]{1,0:T(8,128)(2,1)S(1)} collective-permute-done((bf16[440,128]{1,0:T(8,128)(2,1)S(1)}, bf16[440,128]{1,0:T(8,128)(2,1)S(1)}, u32[]{:S(2)}, u32[]{:S(2)}) %collective-permute-start.37) | collective-permute-done | bytes 112672 | tf_op jit(solution)/shard_map/ppermute | solution.py:1040
  306.9 2.2 collective-permute-done.40
  310.4 1.9 collective-permute-start.31
  312.3 3.4 collective-permute-done.33
  315.8 8.3 %collective-permute-done.31 = bf16[440,128]{1,0:T(8,128)(2,1)S(1)} collective-permute-done((bf16[440,128]{1,0:T(8,128)(2,1)S(1)}, bf16[440,128]{1,0:T(8,128)(2,1)S(1)}, u32[]{:S(2)}, u32[]{:S(2)}) %collective-permute-start.31) | collective-permute-done | bytes 112672 | tf_op jit(solution)/shard_map/ppermute | solution.py:1040
  324.2 2.6 collective-permute-done.34
  327.0 3.3 adam.2
  330.3 5.4 %collective-permute-done.35.two_other = bf16[880,128]{1,0:T(8,128)(2,1)S(1)} collective-permute-done((bf16[880,128]{1,0:T(8,128)(2,1)S(1)}, bf16[880,128]{1,0:T(8,128)(2,1)S(1)}, u32[]{:S(2)}, u32[]{:S(2)}) %collective-permute-start.35) | collective-permute-done | bytes 225312 | tf_op jit(solution)/shard_map/ppermute | solution.py:1040
  335.7 3.4 %adam.3 = (f32[7036,128]{1,0:T(8,128)}, f32[7036,128]{1,0:T(8,128)}, f32[7036,128]{1,0:T(8,128)}) custom-call(s32[1]{0:T(128)} %bitcast.16.z_ref, bf16[880,128]{1,0:T(8,128)(2,1)S(1)} %maximum_select_fusion.one, bf16[880,128]{1,0:T(8,128)(2,1)S(1)} %collective-permute-done.32.one_other, ...), custom_call_target="tpu_custom_call", output_to_operand_aliasing={{0}: (7, {}), {1}: (8, {}), {2}: (9, {})} | custom-call | flops 1 | bytes 1 | tf_op jit(solution)/shard_map/adam/pallas_call | solution.py:1069
  (146 shorter events, 34.0 us)
Async XLA Ops:
  2.9 23.2 %copy-start.3 = (bf16[3520,128]{1,0:T(8,128)(2,1)}, bf16[3520,128]{1,0:T(8,128)(2,1)S(1)}, u32[]{:S(2)}) copy-start(bf16[3520,128]{1,0:T(8,128)(2,1)S(1)} %slice_bitcast_fusion.1.rest_0_) | copy-start | bytes 2703364
  3.0 29.7 %copy-start.4 = (bf16[3520,128]{1,0:T(8,128)(2,1)}, bf16[3520,128]{1,0:T(8,128)(2,1)S(1)}, u32[]{:S(2)}) copy-start(bf16[3520,128]{1,0:T(8,128)(2,1)S(1)} %pad.12.rest_1_) | copy-start | bytes 2703364
  3.1 23.0 %collective-permute-start = (bf16[3520,128]{1,0:T(8,128)(2,1)S(1)}, bf16[3520,128]{1,0:T(8,128)(2,1)S(1)}, u32[]{:S(2)}, u32[]{:S(2)}) collective-permute-start(bf16[3520,128]{1,0:T(8,128)(2,1)S(1)} %slice_bitcast_fusion.1.rest_0_), channel_id=1, source_target_pairs={{0,2},{1,3},{2,0},{3,1},{4,6},{5,7},{6,4},{7,5},{8,10},{9,11},{10,... | collective-permute-start | bytes 2703368 | tf_op jit(solution)/shard_map/ppermute | solution.py:188
  6.1 27.2 %collective-permute-start.4 = (bf16[3520,128]{1,0:T(8,128)(2,1)S(1)}, bf16[3520,128]{1,0:T(8,128)(2,1)}, u32[]{:S(2)}, u32[]{:S(2)}) collective-permute-start(bf16[3520,128]{1,0:T(8,128)(2,1)S(1)} %slice_bitcast_fusion.1.rest_0_), channel_id=1, source_target_pairs={{0,1},{1,0},{2,3},{3,2},{4,5},{5,4},{6,7},{7,6},{8,9},{9,8},{10,11... | collective-permute-start | bytes 2703368 | tf_op jit(solution)/shard_map/ppermute | solution.py:188
  6.1 23.0 %collective-permute-start.1 = (bf16[3520,128]{1,0:T(8,128)(2,1)S(1)}, bf16[3520,128]{1,0:T(8,128)(2,1)}, u32[]{:S(2)}, u32[]{:S(2)}) collective-permute-start(bf16[3520,128]{1,0:T(8,128)(2,1)S(1)} %pad.12.rest_1_), channel_id=1, source_target_pairs={{0,4},{1,5},{2,6},{3,7},{4,0},{5,1},{6,2},{7,3},{8,12},{9,13},{10,... | collective-permute-start | bytes 2703368 | tf_op jit(solution)/shard_map/ppermute | solution.py:188
  27.3 28.4 %copy-start.20 = (s32[2,512]{1,0:T(2,128)S(1)}, s32[2,512]{1,0:T(2,128)}, u32[]{:S(2)}) copy-start(s32[2,512]{1,0:T(2,128)} %param.13) | copy-start | bytes 12292
  27.3 21.4 %collective-permute-start.2 = (bf16[3520,128]{1,0:T(8,128)(2,1)S(1)}, bf16[3520,128]{1,0:T(8,128)(2,1)}, u32[]{:S(2)}, u32[]{:S(2)}) collective-permute-start(bf16[3520,128]{1,0:T(8,128)(2,1)S(1)} %get-tuple-element.207), channel_id=1, source_target_pairs={{0,4},{1,5},{2,6},{3,7},{4,0},{5,1},{6,2},{7,3},{8,12},{9,13},{10,... | collective-permute-start | bytes 2703368 | tf_op jit(solution)/shard_map/ppermute | solution.py:188
  31.2 21.3 %collective-permute-start.3 = (bf16[3520,128]{1,0:T(8,128)(2,1)S(1)}, bf16[3520,128]{1,0:T(8,128)(2,1)}, u32[]{:S(2)}, u32[]{:S(2)}) collective-permute-start(bf16[3520,128]{1,0:T(8,128)(2,1)S(1)} %get-tuple-element.205), channel_id=1, source_target_pairs={{0,2},{1,3},{2,0},{3,1},{4,6},{5,7},{6,4},{7,5},{8,10},{9,11},{10,... | collective-permute-start | bytes 2703368 | tf_op jit(solution)/shard_map/ppermute | solution.py:188
  32.7 19.8 %collective-permute-start.5 = (bf16[3520,128]{1,0:T(8,128)(2,1)S(1)}, bf16[3520,128]{1,0:T(8,128)(2,1)S(1)}, u32[]{:S(2)}, u32[]{:S(2)}) collective-permute-start(bf16[3520,128]{1,0:T(8,128)(2,1)S(1)} %pad.12.rest_1_), channel_id=1, source_target_pairs={{0,1},{1,0},{2,3},{3,2},{4,5},{5,4},{6,7},{7,6},{8,9},{9,8},{10,11... | collective-permute-start | bytes 2703368 | tf_op jit(solution)/shard_map/ppermute | solution.py:188
  32.7 21.4 %collective-permute-start.6 = (bf16[3520,128]{1,0:T(8,128)(2,1)S(1)}, bf16[3520,128]{1,0:T(8,128)(2,1)S(1)}, u32[]{:S(2)}, u32[]{:S(2)}) collective-permute-start(bf16[3520,128]{1,0:T(8,128)(2,1)S(1)} %collective-permute-done.rest_2_), channel_id=1, source_target_pairs={{0,1},{1,0},{2,3},{3,2},{4,5},{5,4},{6,7},{7,6},{8,9},{9,8},{10,11... | collective-permute-start | bytes 2703368 | tf_op jit(solution)/shard_map/ppermute | solution.py:188
  33.3 24.0 %collective-permute-start.7 = (bf16[3520,128]{1,0:T(8,128)(2,1)}, bf16[3520,128]{1,0:T(8,128)(2,1)S(1)}, u32[]{:S(2)}, u32[]{:S(2)}) collective-permute-start(bf16[3520,128]{1,0:T(8,128)(2,1)} %collective-permute-done.1.rest_3_), channel_id=1, source_target_pairs={{0,1},{1,0},{2,3},{3,2},{4,5},{5,4},{6,7},{7,6},{8,9},{9,8},{10,11... | collective-permute-start | bytes 2703368 | tf_op jit(solution)/shard_map/ppermute | solution.py:188
  48.6 8.6 %collective-permute-start.8 = (bf16[3520,128]{1,0:T(8,128)(2,1)}, bf16[3520,128]{1,0:T(8,128)(2,1)}, u32[]{:S(2)}, u32[]{:S(2)}) collective-permute-start(bf16[3520,128]{1,0:T(8,128)(2,1)} %collective-permute-done.2.rest_4_), channel_id=1, source_target_pairs={{0,1},{1,0},{2,3},{3,2},{4,5},{5,4},{6,7},{7,6},{8,9},{9,8},{10,11... | collective-permute-start | bytes 2703368 | tf_op jit(solution)/shard_map/ppermute | solution.py:188
  52.5 4.7 %collective-permute-start.9 = (bf16[3520,128]{1,0:T(8,128)(2,1)}, bf16[3520,128]{1,0:T(8,128)(2,1)}, u32[]{:S(2)}, u32[]{:S(2)}) collective-permute-start(bf16[3520,128]{1,0:T(8,128)(2,1)} %collective-permute-done.3.rest_5_), channel_id=1, source_target_pairs={{0,1},{1,0},{2,3},{3,2},{4,5},{5,4},{6,7},{7,6},{8,9},{9,8},{10,11... | collective-permute-start | bytes 2703368 | tf_op jit(solution)/shard_map/ppermute | solution.py:188
  52.6 27.1 %collective-permute-start.10 = (bf16[3520,128]{1,0:T(8,128)(2,1)}, bf16[3520,128]{1,0:T(8,128)(2,1)S(1)}, u32[]{:S(2)}, u32[]{:S(2)}) collective-permute-start(bf16[3520,128]{1,0:T(8,128)(2,1)} %get-tuple-element.206), channel_id=1, source_target_pairs={{0,4},{1,5},{2,6},{3,7},{4,0},{5,1},{6,2},{7,3},{8,12},{9,13},{10,... | collective-permute-start | bytes 2703368 | tf_op jit(solution)/shard_map/ppermute | solution.py:188
  55.1 24.6 %collective-permute-start.11 = (bf16[3520,128]{1,0:T(8,128)(2,1)}, bf16[3520,128]{1,0:T(8,128)(2,1)S(1)}, u32[]{:S(2)}, u32[]{:S(2)}) collective-permute-start(bf16[3520,128]{1,0:T(8,128)(2,1)} %get-tuple-element.204), channel_id=1, source_target_pairs={{0,2},{1,3},{2,0},{3,1},{4,6},{5,7},{6,4},{7,5},{8,10},{9,11},{10,... | collective-permute-start | bytes 2703368 | tf_op jit(solution)/shard_map/ppermute | solution.py:188
  63.0 17.6 %copy-start.23 = (s32[8]{0:T(128)S(1)}, s32[8]{0:T(128)}, u32[]{:S(2)}) copy-start(s32[8]{0:T(128)} %constant.67.clone) | copy-start | bytes 100
  79.7 3.0 collective-permute-start.12
  79.8 3.9 %collective-permute-start.13 = (bf16[3520,128]{1,0:T(8,128)(2,1)S(1)}, bf16[3520,128]{1,0:T(8,128)(2,1)}, u32[]{:S(2)}, u32[]{:S(2)}) collective-permute-start(bf16[3520,128]{1,0:T(8,128)(2,1)S(1)} %collective-permute-done.11.rest_7_), channel_id=1, source_target_pairs={{0,1},{1,0},{2,3},{3,2},{4,5},{5,4},{6,7},{7,6},{8,9},{9,8},{10,11... | collective-permute-start | bytes 2703368 | tf_op jit(solution)/shard_map/ppermute | solution.py:188
  188.6 9.3 %collective-permute-start.14 = (bf16[3,7040,128]{2,1,0:T(8,128)(2,1)}, bf16[3,7040,128]{2,1,0:T(8,128)(2,1)}, u32[]{:S(2)}, u32[]{:S(2)}) collective-permute-start(bf16[3,7040,128]{2,1,0:T(8,128)(2,1)} %get-tuple-element.137), channel_id=1, source_target_pairs={{0,1},{1,0},{2,3},{3,2},{4,5},{5,4},{6,7},{7,6},{8,9},{9,8},{10,11... | collective-permute-start | bytes 16220168 | tf_op jit(solution)/shard_map/ppermute | solution.py:188
  201.3 22.3 %collective-permute-start.15 = (bf16[3520,128]{1,0:T(8,128)(2,1)}, bf16[3520,128]{1,0:T(8,128)(2,1)S(1)}, u32[]{:S(2)}, u32[]{:S(2)}) collective-permute-start(bf16[3520,128]{1,0:T(8,128)(2,1)} %get-tuple-element.148), channel_id=1, source_target_pairs={{0,4},{1,5},{2,6},{3,7},{4,0},{5,1},{6,2},{7,3},{8,12},{9,13},{10,... | collective-permute-start | bytes 2703368 | tf_op jit(solution)/shard_map/ppermute | solution.py:188
  202.3 22.0 %collective-permute-start.16 = (bf16[3520,128]{1,0:T(8,128)(2,1)}, bf16[3520,128]{1,0:T(8,128)(2,1)S(1)}, u32[]{:S(2)}, u32[]{:S(2)}) collective-permute-start(bf16[3520,128]{1,0:T(8,128)(2,1)} %get-tuple-element.159), channel_id=1, source_target_pairs={{0,2},{1,3},{2,0},{3,1},{4,6},{5,7},{6,4},{7,5},{8,10},{9,11},{10,... | collective-permute-start | bytes 2703368 | tf_op jit(solution)/shard_map/ppermute | solution.py:188
  225.2 3.9 %collective-permute-start.17 = (bf16[1,7040,128]{2,1,0:T(8,128)(2,1)}, bf16[1,7040,128]{2,1,0:T(8,128)(2,1)S(1)}, u32[]{:S(2)}, u32[]{:S(2)}) collective-permute-start(bf16[1,7040,128]{2,1,0:T(8,128)(2,1)} %get-tuple-element.161), channel_id=1, source_target_pairs={{0,1},{1,0},{2,3},{3,2},{4,5},{5,4},{6,7},{7,6},{8,9},{9,8},{10,11... | collective-permute-start | bytes 5406728 | tf_op jit(solution)/shard_map/ppermute | solution.py:188
  233.7 13.6 %collective-permute-start.18 = (bf16[1760,128]{1,0:T(8,128)(2,1)}, bf16[1760,128]{1,0:T(8,128)(2,1)S(1)}, u32[]{:S(2)}, u32[]{:S(2)}) collective-permute-start(bf16[1760,128]{1,0:T(8,128)(2,1)} %get-tuple-element.162), channel_id=1, source_target_pairs={{0,4},{1,5},{2,6},{3,7},{4,0},{5,1},{6,2},{7,3},{8,12},{9,13},{10,... | collective-permute-start | bytes 1351688 | tf_op jit(solution)/shard_map/ppermute | solution.py:188
  234.8 13.4 %collective-permute-start.19 = (bf16[1760,128]{1,0:T(8,128)(2,1)}, bf16[1760,128]{1,0:T(8,128)(2,1)S(1)}, u32[]{:S(2)}, u32[]{:S(2)}) collective-permute-start(bf16[1760,128]{1,0:T(8,128)(2,1)} %get-tuple-element.169), channel_id=1, source_target_pairs={{0,2},{1,3},{2,0},{3,1},{4,6},{5,7},{6,4},{7,5},{8,10},{9,11},{10,... | collective-permute-start | bytes 1351688 | tf_op jit(solution)/shard_map/ppermute | solution.py:188
  236.3 20.7 %collective-permute-start.24 = (bf16[1760,128]{1,0:T(8,128)(2,1)}, bf16[1760,128]{1,0:T(8,128)(2,1)S(1)}, u32[]{:S(2)}, u32[]{:S(2)}) collective-permute-start(bf16[1760,128]{1,0:T(8,128)(2,1)} %get-tuple-element.180), channel_id=1, source_target_pairs={{0,4},{1,5},{2,6},{3,7},{4,0},{5,1},{6,2},{7,3},{8,12},{9,13},{10,... | collective-permute-start | bytes 1351688 | tf_op jit(solution)/shard_map/ppermute | solution.py:188
  237.2 20.7 %collective-permute-start.25 = (bf16[1760,128]{1,0:T(8,128)(2,1)}, bf16[1760,128]{1,0:T(8,128)(2,1)S(1)}, u32[]{:S(2)}, u32[]{:S(2)}) collective-permute-start(bf16[1760,128]{1,0:T(8,128)(2,1)} %get-tuple-element.181), channel_id=1, source_target_pairs={{0,2},{1,3},{2,0},{3,1},{4,6},{5,7},{6,4},{7,5},{8,10},{9,11},{10,... | collective-permute-start | bytes 1351688 | tf_op jit(solution)/shard_map/ppermute | solution.py:188
  251.8 15.7 %collective-permute-start.20 = (bf16[1760,128]{1,0:T(8,128)(2,1)}, bf16[1760,128]{1,0:T(8,128)(2,1)S(1)}, u32[]{:S(2)}, u32[]{:S(2)}) collective-permute-start(bf16[1760,128]{1,0:T(8,128)(2,1)} %get-tuple-element.172), channel_id=1, source_target_pairs={{0,2},{1,3},{2,0},{3,1},{4,6},{5,7},{6,4},{7,5},{8,10},{9,11},{10,... | collective-permute-start | bytes 1351688 | tf_op jit(solution)/shard_map/ppermute | solution.py:188
  253.4 16.0 %collective-permute-start.22 = (bf16[1760,128]{1,0:T(8,128)(2,1)}, bf16[1760,128]{1,0:T(8,128)(2,1)S(1)}, u32[]{:S(2)}, u32[]{:S(2)}) collective-permute-start(bf16[1760,128]{1,0:T(8,128)(2,1)} %get-tuple-element.179), channel_id=1, source_target_pairs={{0,4},{1,5},{2,6},{3,7},{4,0},{5,1},{6,2},{7,3},{8,12},{9,13},{10,... | collective-permute-start | bytes 1351688 | tf_op jit(solution)/shard_map/ppermute | solution.py:188
  261.5 14.6 %collective-permute-start.26 = (bf16[1760,128]{1,0:T(8,128)(2,1)}, bf16[1760,128]{1,0:T(8,128)(2,1)S(1)}, u32[]{:S(2)}, u32[]{:S(2)}) collective-permute-start(bf16[1760,128]{1,0:T(8,128)(2,1)} %get-tuple-element.189), channel_id=1, source_target_pairs={{0,2},{1,3},{2,0},{3,1},{4,6},{5,7},{6,4},{7,5},{8,10},{9,11},{10,... | collective-permute-start | bytes 1351688 | tf_op jit(solution)/shard_map/ppermute | solution.py:188
  263.1 14.1 %collective-permute-start.27 = (bf16[1760,128]{1,0:T(8,128)(2,1)}, bf16[1760,128]{1,0:T(8,128)(2,1)S(1)}, u32[]{:S(2)}, u32[]{:S(2)}) collective-permute-start(bf16[1760,128]{1,0:T(8,128)(2,1)} %get-tuple-element.191), channel_id=1, source_target_pairs={{0,4},{1,5},{2,6},{3,7},{4,0},{5,1},{6,2},{7,3},{8,12},{9,13},{10,... | collective-permute-start | bytes 1351688 | tf_op jit(solution)/shard_map/ppermute | solution.py:188
  267.7 10.7 %collective-permute-start.21 = (bf16[880,128]{1,0:T(8,128)(2,1)S(1)}, bf16[880,128]{1,0:T(8,128)(2,1)S(1)}, u32[]{:S(2)}, u32[]{:S(2)}) collective-permute-start(bf16[880,128]{1,0:T(8,128)(2,1)S(1)} %dynamic-slice_bitcast_fusion.3), channel_id=1, source_target_pairs={{0,8},{8,0},{16,24},{24,16},{1,9},{9,1},{17,25},{25,17},{2,10},{10... | collective-permute-start | bytes 675848 | tf_op jit(solution)/shard_map/ppermute | solution.py:1040
  269.6 10.8 %collective-permute-start.23 = (bf16[880,128]{1,0:T(8,128)(2,1)S(1)}, bf16[880,128]{1,0:T(8,128)(2,1)S(1)}, u32[]{:S(2)}, u32[]{:S(2)}) collective-permute-start(bf16[880,128]{1,0:T(8,128)(2,1)S(1)} %dynamic-slice_bitcast_fusion.2), channel_id=1, source_target_pairs={{0,16},{8,24},{16,0},{24,8},{1,17},{9,25},{17,1},{25,9},{2,18},{10... | collective-permute-start | bytes 675848 | tf_op jit(solution)/shard_map/ppermute | solution.py:1040
  280.4 21.0 %collective-permute-start.28 = (bf16[880,128]{1,0:T(8,128)(2,1)S(1)}, bf16[880,128]{1,0:T(8,128)(2,1)S(1)}, u32[]{:S(2)}, u32[]{:S(2)}) collective-permute-start(bf16[880,128]{1,0:T(8,128)(2,1)S(1)} %dynamic-slice_bitcast_fusion.1), channel_id=1, source_target_pairs={{0,8},{8,0},{16,24},{24,16},{1,9},{9,1},{17,25},{25,17},{2,10},{10... | collective-permute-start | bytes 675848 | tf_op jit(solution)/shard_map/ppermute | solution.py:1040
  280.7 46.2 %copy-start.1 = (f32[900608]{0:T(1024)S(1)}, f32[900608]{0:T(1024)}, u32[]{:S(2)}) copy-start(f32[900608]{0:T(1024)} %param.19) | copy-start | bytes 10807300
  280.7 20.7 %collective-permute-start.29 = (bf16[880,128]{1,0:T(8,128)(2,1)S(1)}, bf16[880,128]{1,0:T(8,128)(2,1)S(1)}, u32[]{:S(2)}, u32[]{:S(2)}) collective-permute-start(bf16[880,128]{1,0:T(8,128)(2,1)S(1)} %dynamic-slice_bitcast_fusion), channel_id=1, source_target_pairs={{0,16},{8,24},{16,0},{24,8},{1,17},{9,25},{17,1},{25,9},{2,18},{10... | collective-permute-start | bytes 675848 | tf_op jit(solution)/shard_map/ppermute | solution.py:1040
  283.7 14.2 %collective-permute-start.36 = (bf16[440,128]{1,0:T(8,128)(2,1)S(1)}, bf16[440,128]{1,0:T(8,128)(2,1)S(1)}, u32[]{:S(2)}, u32[]{:S(2)}) collective-permute-start(bf16[440,128]{1,0:T(8,128)(2,1)S(1)} %dynamic-slice_bitcast_fusion.5), channel_id=1, source_target_pairs={{0,16},{8,24},{16,0},{24,8},{1,17},{9,25},{17,1},{25,9},{2,18},{10... | collective-permute-start | bytes 337928 | tf_op jit(solution)/shard_map/ppermute | solution.py:1040
  283.9 14.1 %collective-permute-start.39 = (bf16[440,128]{1,0:T(8,128)(2,1)S(1)}, bf16[440,128]{1,0:T(8,128)(2,1)S(1)}, u32[]{:S(2)}, u32[]{:S(2)}) collective-permute-start(bf16[440,128]{1,0:T(8,128)(2,1)S(1)} %dynamic-slice_bitcast_fusion.4), channel_id=1, source_target_pairs={{0,8},{8,0},{16,24},{24,16},{1,9},{9,1},{17,25},{25,17},{2,10},{10... | collective-permute-start | bytes 337928 | tf_op jit(solution)/shard_map/ppermute | solution.py:1040
  297.9 8.9 %collective-permute-start.37 = (bf16[440,128]{1,0:T(8,128)(2,1)S(1)}, bf16[440,128]{1,0:T(8,128)(2,1)S(1)}, u32[]{:S(2)}, u32[]{:S(2)}) collective-permute-start(bf16[440,128]{1,0:T(8,128)(2,1)S(1)} %bitcast_add_fusion.5), channel_id=1, source_target_pairs={{0,16},{8,24},{16,0},{24,8},{1,17},{9,25},{17,1},{25,9},{2,18},{10... | collective-permute-start | bytes 337928 | tf_op jit(solution)/shard_map/ppermute | solution.py:1040
  298.0 11.1 %collective-permute-start.40 = (bf16[440,128]{1,0:T(8,128)(2,1)S(1)}, bf16[440,128]{1,0:T(8,128)(2,1)S(1)}, u32[]{:S(2)}, u32[]{:S(2)}) collective-permute-start(bf16[440,128]{1,0:T(8,128)(2,1)S(1)} %bitcast_add_fusion.4), channel_id=1, source_target_pairs={{0,8},{8,0},{16,24},{24,16},{1,9},{9,1},{17,25},{25,17},{2,10},{10... | collective-permute-start | bytes 337928 | tf_op jit(solution)/shard_map/ppermute | solution.py:1040
  301.4 25.5 %copy-start = (f32[900608]{0:T(1024)S(1)}, f32[900608]{0:T(1024)}, u32[]{:S(2)}) copy-start(f32[900608]{0:T(1024)} %param.18) | copy-start | bytes 10807300
  301.4 8.9 %collective-permute-start.30 = (bf16[440,128]{1,0:T(8,128)(2,1)S(1)}, bf16[440,128]{1,0:T(8,128)(2,1)S(1)}, u32[]{:S(2)}, u32[]{:S(2)}) collective-permute-start(bf16[440,128]{1,0:T(8,128)(2,1)S(1)} %dynamic-slice_bitcast_fusion.7), channel_id=1, source_target_pairs={{0,16},{8,24},{16,0},{24,8},{1,17},{9,25},{17,1},{25,9},{2,18},{10... | collective-permute-start | bytes 337928 | tf_op jit(solution)/shard_map/ppermute | solution.py:1040
  301.6 14.0 %collective-permute-start.33 = (bf16[440,128]{1,0:T(8,128)(2,1)S(1)}, bf16[440,128]{1,0:T(8,128)(2,1)S(1)}, u32[]{:S(2)}, u32[]{:S(2)}) collective-permute-start(bf16[440,128]{1,0:T(8,128)(2,1)S(1)} %dynamic-slice_bitcast_fusion.6), channel_id=1, source_target_pairs={{0,8},{8,0},{16,24},{24,16},{1,9},{9,1},{17,25},{25,17},{2,10},{10... | collective-permute-start | bytes 337928 | tf_op jit(solution)/shard_map/ppermute | solution.py:1040
  306.8 20.1 %collective-permute-start.38 = (bf16[880,128]{1,0:T(8,128)(2,1)S(1)}, bf16[880,128]{1,0:T(8,128)(2,1)S(1)}, u32[]{:S(2)}, u32[]{:S(2)}) collective-permute-start(bf16[880,128]{1,0:T(8,128)(2,1)S(1)} %maximum_select_fusion.2.one), channel_id=1, source_target_pairs={{0,8},{8,0},{16,24},{24,16},{1,9},{9,1},{17,25},{25,17},{2,10},{10... | collective-permute-start | bytes 675848 | tf_op jit(solution)/shard_map/ppermute | solution.py:1040
  309.2 17.8 %collective-permute-start.41 = (bf16[880,128]{1,0:T(8,128)(2,1)S(1)}, bf16[880,128]{1,0:T(8,128)(2,1)S(1)}, u32[]{:S(2)}, u32[]{:S(2)}) collective-permute-start(bf16[880,128]{1,0:T(8,128)(2,1)S(1)} %maximum_select_fusion.3.two), channel_id=1, source_target_pairs={{0,16},{8,24},{16,0},{24,8},{1,17},{9,25},{17,1},{25,9},{2,18},{10... | collective-permute-start | bytes 675848 | tf_op jit(solution)/shard_map/ppermute | solution.py:1040
  310.4 13.6 %collective-permute-start.31 = (bf16[440,128]{1,0:T(8,128)(2,1)S(1)}, bf16[440,128]{1,0:T(8,128)(2,1)S(1)}, u32[]{:S(2)}, u32[]{:S(2)}) collective-permute-start(bf16[440,128]{1,0:T(8,128)(2,1)S(1)} %bitcast_add_fusion.7), channel_id=1, source_target_pairs={{0,16},{8,24},{16,0},{24,8},{1,17},{9,25},{17,1},{25,9},{2,18},{10... | collective-permute-start | bytes 337928 | tf_op jit(solution)/shard_map/ppermute | solution.py:1040
  315.7 11.1 %collective-permute-start.34 = (bf16[440,128]{1,0:T(8,128)(2,1)S(1)}, bf16[440,128]{1,0:T(8,128)(2,1)S(1)}, u32[]{:S(2)}, u32[]{:S(2)}) collective-permute-start(bf16[440,128]{1,0:T(8,128)(2,1)S(1)} %bitcast_add_fusion.6), channel_id=1, source_target_pairs={{0,8},{8,0},{16,24},{24,16},{1,9},{9,1},{17,25},{25,17},{2,10},{10... | collective-permute-start | bytes 337928 | tf_op jit(solution)/shard_map/ppermute | solution.py:1040
  324.1 6.1 %collective-permute-start.32 = (bf16[880,128]{1,0:T(8,128)(2,1)S(1)}, bf16[880,128]{1,0:T(8,128)(2,1)S(1)}, u32[]{:S(2)}, u32[]{:S(2)}) collective-permute-start(bf16[880,128]{1,0:T(8,128)(2,1)S(1)} %maximum_select_fusion.one), channel_id=1, source_target_pairs={{0,8},{8,0},{16,24},{24,16},{1,9},{9,1},{17,25},{25,17},{2,10},{10... | collective-permute-start | bytes 675848 | tf_op jit(solution)/shard_map/ppermute | solution.py:1040
  326.8 8.8 %collective-permute-start.35 = (bf16[880,128]{1,0:T(8,128)(2,1)S(1)}, bf16[880,128]{1,0:T(8,128)(2,1)S(1)}, u32[]{:S(2)}, u32[]{:S(2)}) collective-permute-start(bf16[880,128]{1,0:T(8,128)(2,1)S(1)} %maximum_select_fusion.1.two), channel_id=1, source_target_pairs={{0,16},{8,24},{16,0},{24,8},{1,17},{9,25},{17,1},{25,9},{2,18},{10... | collective-permute-start | bytes 675848 | tf_op jit(solution)/shard_map/ppermute | solution.py:1040
  (21 other events, 138.8 us)

commit v5 on v4

--- a/solution.py
+++ b/solution.py
@@ -250,40 +250,89 @@
     )(me, *pieces)
 
 
-def unpack_rest_kernel(shard_rows, owner_ref, *rest):
-    pieces, (*outs, flat, buf, sems) = rest[:16], rest[16:]
-    plan = [(src, n % 2, owner_ref[n % 8] ^ (n // 8)) for n, src in enumerate(pieces)]
-
-    def copy(n):
-        return pltpu.make_async_copy(plan[n][0], buf.at[n % 4], sems.at[n % 4])
-
-    for n in range(3):
-        copy(n).start()
-    for n in range(len(plan)):
-        if n + 3 < len(plan):
-            copy(n + 3).start()
-        copy(n).wait()
-        _, half, owner = plan[n]
-        widen_half(flat, owner * shard_rows, buf.at[n % 4], half, shard_rows)
-    put_rest(flat, *outs)
-
-
-def unpack_rest(owners, shard_rows, *pieces):
-    n = pieces[0].shape[0]
-    return pl.pallas_call(
-        functools.partial(unpack_rest_kernel, shard_rows),
-        in_specs=[SM] + [ANY] * len(pieces),
-        out_specs=[VM] * len(REST),
-        out_shape=REST,
-        scratch_shapes=[
-            pltpu.VMEM((8 * shard_rows + 16, LANE), F32),
-            pltpu.VMEM((4, n, LANE), BF),
-            pltpu.SemaphoreType.DMA((4,)),
-        ],
-        compiler_params=params_of(),
-        cost_estimate=TINY,
-        name="unpack_rest",
-    )(owners, *pieces)
+def widen_rows(flat, place, src, first, last):
+    whole_steps = (last - first) // CHUNK
+
+    def widen(m, _):
+        rows = pl.ds(pl.multiple_of(first + m * CHUNK, 16), CHUNK)
+        flat[pl.ds(place + m * CHUNK, CHUNK), :] = src[rows, :].astype(F32)
+        return 0
+
+    lax.fori_loop(0, whole_steps, widen, 0)
+    done = first + whole_steps * CHUNK
+    if done < last:
+        flat[pl.ds(place + done - first, last - done), :] = src[done:last, :].astype(F32)
+
+
+def class_places(c):
+    at_row = lax.broadcasted_iota(jnp.int32, (STU, LANE), 0) * CLASSES + c
+    lane = lax.broadcasted_iota(jnp.int32, (STU, LANE), 1)
+    return ((at_row >> 7) == lane)[:, :16].astype(F32), ((at_row & (LANE - 1)) == lane).astype(F32)
+
+
+def unpack_rest(shard_rows, owner_ref, pieces, flat, buf, sems, wout, win, wback, wstu, wmid, vec, small, wcls):
+    half = pieces[0].shape[0]
+    targets = [(d, h) for d in range(8) for h in range(2) if d * shard_rows + min((h + 1) * half, shard_rows) > SPLIT]
+
+    def start(t):
+        for n, src in enumerate(pieces):
+            if n % 2 == targets[t][1]:
+
+                @pl.when(owner_ref[n % 8] ^ (n // 8) == targets[t][0])
+                def _(src=src):
+                    pltpu.make_async_copy(src, buf.at[t % 4], sems.at[t % 4]).start()
+
+    nb = D // LANE
+
+    def region_out(first):
+        put_matrix(wout, flat, 16, 64)
+        for row, name in enumerate(("b_out", "gain_one", "shift_one")):
+            put_row(vec, row, flat, 16 + TABLE[name] - first, nb)
+
+    def region_in(first):
+        put_matrix(win, flat, 16, 32)
+        for q in range(4):
+            put_row(vec, 8 + q, flat, 16 + TABLE["b_in"] - first + q * nb, nb)
+
+    def region_back(first):
+        row_of = lambda name: 16 + TABLE[name] - first
+        put_matrix(wback, flat, 16, 64)
+        for row, name in enumerate(("b_back", "gain_two", "shift_two")):
+            put_row(vec, 3 + row, flat, row_of(name), nb)
+        wstu[...] = flat[row_of("w_stu") : row_of("w_stu") + D, :].astype(BF)
+        wmid[...] = flat[row_of("w_mid") : row_of("w_mid") + STU, :]
+        put_row(small, 0, flat, row_of("b_stu"), 1)
+        put_row(small, 1, flat, row_of("pool_query"), 1)
+        put_row(small, 2, flat, row_of("b_mid"), 1)
+        lane = lax.broadcasted_iota(jnp.int32, (1, LANE), 1)
+        small[3:4, :] = jnp.where(lane < CLASSES, flat[row_of("b_cls") : row_of("b_cls") + 1, :], 0.0)
+        rows = lax.broadcasted_iota(jnp.int32, (16, LANE), 0)
+        classes = jnp.where(rows < CLASSES, flat[row_of("w_cls") : row_of("w_cls") + 16, :], 0.0).astype(BF)
+        total = jnp.zeros((STU, LANE), F32)
+        for c in range(CLASSES):
+            to_row, to_lane = class_places(c)
+            column = jnp.sum(dot(to_row.astype(BF), classes) * to_lane, axis=-1, keepdims=True)
+            total = total + jnp.where(lane == c, column, 0.0)
+        wcls[...] = total
+
+    ends = (TABLE["w_in"], TABLE["w_back"], 8 * shard_rows)
+    regions = list(zip((SPLIT, *ends), ends, (region_out, region_in, region_back)))
+    for t in range(3):
+        start(t)
+    for t, (d, h) in enumerate(targets):
+        if t + 3 < len(targets):
+            start(t + 3)
+        pltpu.make_async_copy(pieces[0], buf.at[t % 4], sems.at[t % 4]).wait()
+        origin = d * shard_rows + h * half
+        size = min(half, shard_rows - h * half)
+        for first, last, put in regions:
+            lo, hi = max(first, origin) - origin, min(last, origin + size) - origin
+            if lo >= hi:
+                continue
+            lo, hi = lo // 16 * 16, min(half, -(-hi // 16) * 16)
+            widen_rows(flat, 16 + origin + lo - first, buf.at[t % 4], lo, hi)
+            if last <= origin + size:
+                put(first)
 
 
 def exchange_weights(params, shard_rows, padded):
@@ -307,7 +356,7 @@
         turned = jnp.array([0, 0, 2, 4, 6, 6, 4, 2], jnp.int32)
         swapped = jnp.array([0, 0, 0, 0, 1, 0, 1, 0], jnp.int32) * x + jnp.array([0, 0, 0, 0, 0, 1, 0, 1], jnp.int32) * y
         owners = me ^ jnp.where(swapped == 1, turned, bits)
-        return unpack_rest(owners, shard_rows, *early, *late, *early_c, *late_c)
+        return owners, (*early, *late, *early_c, *late_c)
 
     return first, finish
 
@@ -383,44 +432,11 @@
     return jnp.sum(v.reshape(v.shape[0] // 8, 8, v.shape[1]), axis=0)
 
 
-def middle_kernel(
-    x_ref,
-    att_ref,
-    segc_ref,
-    hot_ref,
-    cot_ref,
-    wout,
-    win,
-    wback,
-    wstu,
-    wmid,
-    vec,
-    small,
-    wcls,
-    out_ref,
-    logit_ref,
-    nbf_ref,
-    act_ref,
-    dffn_ref,
-    dinner_ref,
-    dstu_ref,
-    dh1_ref,
-    dbr_ref,
-    datt_ref,
-    vg_ref,
-    sg_ref,
-    gmid_ref,
-    gcls_ref,
-    hid,
-    n1,
-    nrm,
-    n2,
-    q1,
-    q2,
-    gp,
-    acc,
-    accb,
-):
+def middle_kernel(ins, weights, moved, outs, scratch):
+    x_ref, att_ref, segc_ref, hot_ref, cot_ref = ins
+    wout, win, wback, wstu, wmid, vec, small, wcls = weights
+    logit_ref, dstu_ref, dh1_ref, dbr_ref, datt_ref, vg_ref, sg_ref, gmid_ref, gcls_ref = outs
+    hid, n1, nrm, n2, q1, q2, gp, acc, accb, out_ref, nbf_ref, act_ref, dffn_ref, dinner_ref, sems = scratch
     r = pl.program_id(0)
 
     @pl.when(r == 0)
@@ -430,6 +446,14 @@
         sg_ref[...] = jnp.zeros_like(sg_ref)
         gmid_ref[...] = jnp.zeros_like(gmid_ref)
         gcls_ref[...] = jnp.zeros_like(gcls_ref)
+
+    bufs = (out_ref, nbf_ref, act_ref, dffn_ref, dinner_ref)
+
+    def copy(n, row):
+        return pltpu.make_async_copy(bufs[n], moved[n].at[row], sems.at[n])
+
+    def reuse(n):
+        pl.when(r > 0)(lambda: copy(n, r - 1).wait())
 
     def first(t, _):
         cols = at(t, 384)
@@ -448,25 +472,31 @@
         q1[rows, :] = jnp.broadcast_to(q, (TB, LANE))
         y = n * vec[1:2, :] + vec[2:3, :]
         nrm[rows, :] = y
-        nbf_ref[0, rows, :] = y.astype(BF)
-        return 0
-
+        nbf_ref[rows, :] = y.astype(BF)
+        return 0
+
+    reuse(1)
     lax.fori_loop(0, LEN // TB, norm_one, 0)
+    copy(1, r).start()
 
     def inner(t, _):
         cols = at(t, D)
         bias = vec[pl.ds(8 + t, 1), :]
-        u = dot(nbf_ref[0], win[:, cols]) + bias
+        u = dot(nbf_ref[...], win[:, cols]) + bias
         cdf = 0.5 * (1.0 + lax.erf(u * (0.5**0.5)))
-        act_ref[0, :, cols] = (u * cdf).astype(BF)
-        gp[:, cols] = cdf + u * (jnp.exp(-0.5 * u * u) * (1.0 / math.sqrt(2.0 * math.pi)))
-        return 0
-
+        act_ref[:, cols] = (u * cdf).astype(BF)
+        slope = cdf + u * (jnp.exp(-0.5 * u * u) * (1.0 / math.sqrt(2.0 * math.pi)))
+        for j in range(D // LANE):
+            gp[at(t * (D // LANE) + j, LEN), :] = slope[:, j * LANE : (j + 1) * LANE]
+        return 0
+
+    reuse(2)
     lax.fori_loop(0, FF // D, inner, 0)
+    copy(2, r).start()
 
     def second(t, _):
         cols = at(t, 256)
-        hid[:, cols] = nrm[:, cols] + (dot(act_ref[0], wback[:, cols]) + vec[3:4, cols])
+        hid[:, cols] = nrm[:, cols] + (dot(act_ref[...], wback[:, cols]) + vec[3:4, cols])
         return 0
 
     lax.fori_loop(0, D // 256, second, 0)
@@ -479,14 +509,16 @@
         n = c * q
         n2[rows, :] = n
         q2[rows, :] = jnp.broadcast_to(q, (TB, LANE))
-        out_ref[0, rows, :] = (n * vec[4:5, :] + vec[5:6, :]).astype(BF)
-        return 0
-
+        out_ref[rows, :] = (n * vec[4:5, :] + vec[5:6, :]).astype(BF)
+        return 0
+
+    reuse(0)
     lax.fori_loop(0, LEN // TB, norm_two, 0)
+    copy(0, r).start()
 
     lane = lax.broadcasted_iota(jnp.int32, (1, LANE), 1)
     left = lane < 64
-    stu = dot(out_ref[0], wstu[...]) + small[0:1, :]
+    stu = dot(out_ref[...], wstu[...]) + small[0:1, :]
     pq = small[1:2, :] * 0.125
     sp = stu * pq
     s0 = jnp.sum(jnp.where(left, sp, 0.0), axis=-1, keepdims=True)
@@ -543,23 +575,28 @@
         )
         acc[3] += fold(d)
         hid[rows, :] = d
-        dffn_ref[0, rows, :] = d.astype(BF)
-        return 0
-
+        dffn_ref[rows, :] = d.astype(BF)
+        return 0
+
+    reuse(3)
     lax.fori_loop(0, LEN // TB, back_two, 0)
+    copy(3, r).start()
 
     def outer(t, _):
         cols = at(t, D)
-        d = dot(dffn_ref[0], wback[cols, :], NT) * gp[:, cols]
+        slope = jnp.concatenate([gp[at(t * (D // LANE) + j, LEN), :] for j in range(D // LANE)], axis=1)
+        d = dot(dffn_ref[...], wback[cols, :], NT) * slope
         accb[:, cols] += fold(d)
-        dinner_ref[0, :, cols] = d.astype(BF)
-        return 0
-
+        dinner_ref[:, cols] = d.astype(BF)
+        return 0
+
+    reuse(4)
     lax.fori_loop(0, FF // D, outer, 0)
+    copy(4, r).start()
 
     def third(t, _):
         cols = at(t, D)
-        hid[:, cols] += dot(dinner_ref[0], win[cols, :], NT)
+        hid[:, cols] += dot(dinner_ref[...], win[cols, :], NT)
         return 0
 
     lax.fori_loop(0, D // D, third, 0)
@@ -590,6 +627,8 @@
 
     @pl.when(r == pl.num_programs(0) - 1)
     def _():
+        for n in range(len(bufs)):
+            copy(n, r).wait()
         vg_ref[...] = jnp.zeros_like(vg_ref)
         for i in range(6):
             vg_ref[i : i + 1, :] = jnp.sum(acc[i], axis=0, keepdims=True)
@@ -601,34 +640,42 @@
     return pl.BlockSpec(shape, lambda *_: (0,) * len(shape), pipeline_mode=pl.Buffered(1))
 
 
-def middle(x, att, segc, hot, cot, wout, win, wback, wstu, wmid, vec, small, wcls):
+def middle(x, att, segc, hot, cot, weights, pieces=None, shard_rows=0):
     rows = x.shape[0]
     tok = lambda n, dt: SDS((rows, LEN, n), dt)
+    held = REST[:-1] + (SDS((STU, LANE), F32),)
+    if pieces is None:
+        pieces, weight_specs, own = (), [once(*w.shape) for w in weights], []
+        flat_rows = LEN * FF // LANE
+    else:
+        weight_specs = [SM] + [ANY] * len(pieces)
+        half = pieces[0].shape[0]
+        own = [pltpu.VMEM(w.shape, w.dtype) for w in held]
+        own += [pltpu.VMEM((4, half, LANE), BF), pltpu.SemaphoreType.DMA((4,))]
+        flat_rows = 8 * shard_rows - TABLE["w_back"] + 32 + half
+    widths = (D, D, FF, D, FF)
+
+    def kernel(*refs):
+        ins, refs = refs[:5], refs[5:]
+        given, refs = refs[: len(weight_specs)], refs[len(weight_specs) :]
+        moved, outs, refs = refs[:5], refs[5:14], refs[14:]
+        scratch, kept = refs[:15], refs[15:]
+        if pieces:
+
+            @pl.when(pl.program_id(0) == 0)
+            def _():
+                unpack_rest(shard_rows, given[0], given[1:], scratch[6], *kept[8:], *kept[:8])
+
+            given = kept[:8]
+        middle_kernel(ins, given, moved, outs, scratch)
+
     return pl.pallas_call(
-        middle_kernel,
+        kernel,
         grid=(rows,),
-        in_specs=[
-            row_spec(LEN, D),
-            row_spec(LEN, D),
-            row_spec(LEN, 1),
-            row_spec(SEGS, LANE),
-            row_spec(LEN, D),
-            once(D, D),
-            once(D, FF),
-            once(FF, D),
-            once(D, STU),
-            once(STU, STU),
-            once(16, D),
-            once(8, LANE),
-            once(STU, LANE),
-        ],
-        out_specs=[
-            row_spec(LEN, D),
+        in_specs=[row_spec(LEN, D), row_spec(LEN, D), row_spec(LEN, 1), row_spec(SEGS, LANE), row_spec(LEN, D)] + weight_specs,
+        out_specs=[ANY] * 5
+        + [
             row_spec(SEGS, CLASSES),
-            row_spec(LEN, D),
-            row_spec(LEN, FF),
-            row_spec(LEN, D),
-            row_spec(LEN, FF),
             row_spec(LEN, STU),
             row_spec(LEN, D),
             row_spec(LEN, D),
@@ -638,13 +685,9 @@
             whole(STU, STU),
             whole(STU, LANE),
         ],
-        out_shape=[
-            tok(D, BF),
+        out_shape=[tok(n, BF) for n in widths]
+        + [
             SDS((rows, SEGS, CLASSES), F32),
-            tok(D, BF),
-            tok(FF, BF),
-            tok(D, BF),
-            tok(FF, BF),
             tok(STU, BF),
             tok(D, F32),
             tok(D, BF),
@@ -661,14 +704,17 @@
             pltpu.VMEM((LEN, D), F32),
             pltpu.VMEM((LEN, LANE), F32),
             pltpu.VMEM((LEN, LANE), F32),
-            pltpu.VMEM((LEN, FF), F32),
+            pltpu.VMEM((flat_rows, LANE), F32),
             pltpu.VMEM((6, 8, D), F32),
             pltpu.VMEM((8, FF), F32),
-        ],
+        ]
+        + [pltpu.VMEM((LEN, n), BF) for n in widths]
+        + [pltpu.SemaphoreType.DMA((5,))]
+        + own,
         compiler_params=params_of(),
         cost_estimate=TINY,
         name="middle",
-    )(x, att, segc, hot, cot, wout, win, wback, wstu, wmid, vec, small, wcls)
+    )(x, att, segc, hot, cot, *weights, *pieces)
 
 
 def retreat_kernel(q_ref, k_ref, v_ref, p_ref, datt_ref, dq_ref, dk_ref, dv_ref, bg_ref, dk, dv):
@@ -832,7 +878,11 @@
     put_line(flat, first("b_mid"), sg, 2)
     put_line(flat, first("b_cls"), sg, 3)
     flat[first("w_mid") : first("w_mid") + STU, :] = gmid[...]
-    flat[first("w_cls") : first("w_cls") + CLASSES, :] = gcls[0:CLASSES, :]
+    total = jnp.zeros((16, LANE), F32)
+    for c in range(CLASSES):
+        to_row, to_lane = class_places(c)
+        total = total + dot((to_row * gcls[:, c : c + 1]).astype(BF), to_lane.astype(BF), TN)
+    flat[first("w_cls") : first("w_cls") + CLASSES, :] = total[0:CLASSES, :]
     tail = USED - SPLIT + 16
     flat[tail:, :] = jnp.zeros((flat.shape[0] - tail, LANE), F32)
     flat[0:16, :] = jnp.zeros((16, LANE), F32)
@@ -1097,12 +1147,14 @@
         first, finish = both[:2], lambda after: both[2:]
     wqkv, bq = first
     q, k, v, probs, att = attend(inputs, segc, segr, wqkv, bq)
-    wout, win, wback, wstu, wmid, vec, small, wcls = finish(att)
-    wcls = jnp.pad(wcls[:CLASSES].reshape(STU, CLASSES), ((0, 0), (0, LANE - CLASSES)))
-    out, logits, nbf, act, dffn, dinner, dstu, dh1, dbr, datt, vg, sg, gmid, gcls = middle(
-        inputs, att, segc, hot, out_cotangent, wout, win, wback, wstu, wmid, vec, small, wcls
-    )
-    gcls = jnp.pad(gcls[:, :CLASSES].reshape(CLASSES, LANE), ((0, 2), (0, 0)))
+    if count == 8:
+        owners, pieces = finish(att)
+        results = middle(inputs, att, segc, hot, out_cotangent, (owners,), pieces, shard_rows)
+    else:
+        *rest, wcls = finish(att)
+        wcls = jnp.pad(wcls[:CLASSES].reshape(STU, CLASSES), ((0, 0), (0, LANE - CLASSES)))
+        results = middle(inputs, att, segc, hot, out_cotangent, (*rest, wcls))
+    out, nbf, act, dffn, dinner, logits, dstu, dh1, dbr, datt, vg, sg, gmid, gcls = results
     flat2 = lambda v: v.reshape(rows * LEN, v.shape[-1])
     late = [flat2(v) for v in (att, dbr, nbf, dinner, act, dffn, out, dstu)] + [vg, sg, gmid, gcls]
     if count == 8:

time: 340 us -> 326 us (0.959)
  Pallas kernels: 182 us -> 171 us
    pallas_call x2 -> x1, Pallas kernels: 78 us -> 66.6 us  [middle(): pl.pallas_call(kernel, grid=(rows,), in_specs=[row_spec(LEN, D), row_spec...]
where the time goes in v5:
time: 326 us
  Pallas kernels  171 us (52%)
  waiting for transfers between devices  95.7 us (29%)
  starting transfers between devices  39.6 us (12%)
  other arithmetic  10 us (3%)
  local copies, waits for them, and re-layouts  7.65 us (2%)
    pallas_call x1, Pallas kernels, middle(): pl.pallas_call(kernel, grid=(rows,), in_specs=[row_spec(LEN, D), row_spec...  66.6 us
    ppermute x26, waiting for transfers between devices, swap(): return lax.ppermute(v, 'fsdp', [(d, d ^ bit) for d in range(8)])  55.3 us
    ppermute x16, waiting for transfers between devices, sum_replicas(): lax.ppermute(v, 'rep', [(i, i ^ bit) for i in range(4)])  40.4 us
    pallas_call x1, Pallas kernels, late_pairs(): pl.pallas_call(functools.partial(late_pair_kernel, shard_rows), in_specs=...  24.7 us
    ppermute x26, starting transfers between devices, swap(): return lax.ppermute(v, 'fsdp', [(d, d ^ bit) for d in range(8)])  22.5 us
    pallas_call x6, Pallas kernels, combine(): pl.pallas_call(functools.partial(combine_kernel, plan, len(extras)), in_s...  18 us
    ppermute x16, starting transfers between devices, sum_replicas(): lax.ppermute(v, 'rep', [(i, i ^ bit) for i in range(4)])  17 us
    pallas_call x1, Pallas kernels, attend(): pl.pallas_call(attend_kernel, grid=(rows, D // 256), in_specs=[only(LEN,...  16.7 us
  transfers between devices with their start and end apart: 42, of which 22 were waited for; matrix products, arithmetic and copies ran while one was open for 3% of the time, Pallas kernels for 21%

profile of v5, /device:TPU:0, one launch (start us, length us, event | category | flops | bytes accessed | tf_op | source)
XLA Modules:
  0.0 325.5 jit_solution(8324581578983136956)
XLA Ops:
  0.6 2.2 convert.4
  3.1 3.0 collective-permute-start
  6.1 1.5 collective-permute-start.1
  7.6 18.5 %collective-permute-done.rest_2_.refs_8_ = bf16[3520,128]{1,0:T(8,128)(2,1)S(1)} collective-permute-done((bf16[3520,128]{1,0:T(8,128)(2,1)S(1)}, bf16[3520,128]{1,0:T(8,128)(2,1)S(1)}, u32[]{:S(2)}, u32[]{:S(2)}) %collective-permute-start) | collective-permute-done | bytes 901152 | tf_op jit(solution)/shard_map/ppermute | solution.py:188
  27.2 1.8 collective-permute-start.2
  29.0 2.2 broadcast_select_fusion
  31.2 1.5 collective-permute-start.3
  33.3 15.3 %collective-permute-done.2.rest_4_.refs_10_ = bf16[3520,128]{1,0:T(8,128)(2,1)} collective-permute-done((bf16[3520,128]{1,0:T(8,128)(2,1)S(1)}, bf16[3520,128]{1,0:T(8,128)(2,1)}, u32[]{:S(2)}, u32[]{:S(2)}) %collective-permute-start.2) | collective-permute-done | bytes 901152 | tf_op jit(solution)/shard_map/ppermute | solution.py:188
  48.6 3.9 %collective-permute-done.3.rest_5_.refs_11_ = bf16[3520,128]{1,0:T(8,128)(2,1)} collective-permute-done((bf16[3520,128]{1,0:T(8,128)(2,1)S(1)}, bf16[3520,128]{1,0:T(8,128)(2,1)}, u32[]{:S(2)}, u32[]{:S(2)}) %collective-permute-start.3) | collective-permute-done | bytes 901152 | tf_op jit(solution)/shard_map/ppermute | solution.py:188
  52.5 1.6 collective-permute-start.10
  58.2 4.7 %unpack_first.1 = (bf16[768,2304]{1,0:T(8,128)(2,1)}, f32[8,2304]{1,0:T(8,128)}) custom-call(s32[1]{0:T(128)} %bitcast.1.me_ref, bf16[3520,128]{1,0:T(8,128)(2,1)} %copy-done.3, bf16[3520,128]{1,0:T(8,128)(2,1)} %copy-done.4, bf16[3520,128]{1,0:T(8,128)(2,1)} %copy-done.7, bf16[3520,128]{1,0:T(8,128)(2,1)} %collective-permute-done.1.rest_3_.refs_9_, ...), custom_call_target="tpu_custom_call" | custom-call | flops 1 | bytes 1 | tf_op jit(solution)/shard_map/unpack_first/pallas_call | solution.py:237
  63.0 16.7 %attend.1 = (bf16[2,512,768]{2,1,0:T(8,128)(2,1)}, bf16[2,512,768]{2,1,0:T(8,128)(2,1)}, bf16[2,512,768]{2,1,0:T(8,128)(2,1)}, bf16[2,6,256,1280]{3,2,1,0:T(8,128)(2,1)}, bf16[2,512,768]{2,1,0:T(8,128)(2,1)}) custom-call(bf16[2,512,768]{2,1,0:T(8,128)(2,1)} %refs_0_.1, s32[2,512,1]{2,1,0:T(8,128)} %copy.26.segc_ref.refs_2_, ...), custom_call_target="tpu_custom_call" | custom-call | flops 1 | bytes 1 | tf_op jit(solution)/shard_map/attend/pallas_call | solution.py:415
  83.7 66.6 %middle.1 = (bf16[2,512,768]{2,1,0:T(8,128)(2,1)}, bf16[2,512,768]{2,1,0:T(8,128)(2,1)}, bf16[2,512,3072]{2,1,0:T(8,128)(2,1)}, bf16[2,512,768]{2,1,0:T(8,128)(2...) custom-call(bf16[2,512,768]{2,1,0:T(8,128)(2,1)} %refs_0_.1, ...), custom_call_target="tpu_custom_call" | custom-call | flops 1 | bytes 1 | tf_op jit(solution)/shard_map/middle/pallas_call | solution.py:672
  150.3 24.7 %late_grads.1 = (bf16[3,7040,128]{2,1,0:T(8,128)(2,1)}, bf16[3,7040,128]{2,1,0:T(8,128)(2,1)}, f32[240,128]{1,0:T(8,128)}) custom-call(s32[1]{0:T(128)} %bitcast.1.me_ref, bf16[1024,768]{1,0:T(8,128)(2,1)} %bitcast.74, bf16[1024,768]{1,0:T(8,128)(2,1)} %bitcast.89, bf16[1024,768]{1,0:T(8,128)(2,1)} %bitcast.87, bf16[1024,3072]{1,0:T(8,128)(2,1)} %bitcast.73, ...), custom_call_target="tpu_custom_call" | custom-call | flops 1 | bytes 1 | tf_op jit(solution)/shard_map/late_grads/pallas_call | solution.py:994
  175.1 7.8 %retreat.2 = (bf16[2,512,768]{2,1,0:T(8,128)(2,1)}, bf16[2,512,768]{2,1,0:T(8,128)(2,1)}, bf16[2,512,768]{2,1,0:T(8,128)(2,1)}, f32[8,768]{1,0:T(8,128)}) custom-call(bf16[2,512,768]{2,1,0:T(8,128)(2,1)} %get-tuple-element.106.refs_0_, bf16[2,512,768]{2,1,0:T(8,128)(2,1)} %get-tuple-element.107.refs_1_, bf16[2,512,768]{2,1,0:T(8,128)(2,1)} %get-tuple-element.108.refs_2_, ...), custom_call_target="tpu_custom_call" | custom-call | flops 1 | bytes 1 | tf_op jit(solution)/shard_map/retreat/pallas_call | solution.py:757
  183.0 1.3 collective-permute-done.14.refs_1_.refs_3_
  184.3 3.4 %combine_one.1 = (bf16[3520,128]{1,0:T(8,128)(2,1)}, bf16[3520,128]{1,0:T(8,128)(2,1)}) custom-call(s32[1]{0:T(128)} %bitcast.1.me_ref, bf16[3,7040,128]{2,1,0:T(8,128)(2,1)} %get-tuple-element.130.refs_0_.refs_2_, bf16[3,7040,128]{2,1,0:T(8,128)(2,1)} %collective-permute-done.14.refs_1_.refs_3_, bf16[3,7040,128]{2,1,0:T(8,128)(2,1)} %get-tuple-element.130.refs_0_.refs_2_, ...), custom_call_target="tpu_custom_call" | custom-call | flops 1 | bytes 1 | tf_op jit(solution)/shard_map/combine_one/pallas_call | solution.py:1067
  190.1 7.9 %retreat.3 = (bf16[2,512,768]{2,1,0:T(8,128)(2,1)}, bf16[2,512,768]{2,1,0:T(8,128)(2,1)}, bf16[2,512,768]{2,1,0:T(8,128)(2,1)}, f32[8,768]{1,0:T(8,128)}) custom-call(bf16[2,512,768]{2,1,0:T(8,128)(2,1)} %get-tuple-element.106.refs_0_, bf16[2,512,768]{2,1,0:T(8,128)(2,1)} %get-tuple-element.107.refs_1_, ...), custom_call_target="tpu_custom_call", output_to_operand_aliasing={{0}: (5, {}), {1}: (6, {}), {2}: (7, {})} | custom-call | flops 1 | bytes 1 | tf_op jit(solution)/shard_map/retreat/pallas_call | solution.py:757
  198.0 8.8 %early_grads.1 = (bf16[1,7040,128]{2,1,0:T(8,128)(2,1)}, bf16[1,7040,128]{2,1,0:T(8,128)(2,1)}) custom-call(s32[1]{0:T(128)} %bitcast.1.me_ref, bf16[1024,768]{1,0:T(8,128)(2,1)} %bitcast.71, bf16[1024,768]{1,0:T(8,128)(2,1)} %bitcast.68, bf16[1024,768]{1,0:T(8,128)(2,1)} %bitcast.69, bf16[1024,768]{1,0:T(8,128)(2,1)} %bitcast.70, ...), custom_call_target="tpu_custom_call" | custom-call | flops 1 | bytes 1 | tf_op jit(solution)/shard_map/early_grads/pallas_call | solution.py:1016
  206.8 3.2 collective-permute-done.15.refs_4_
  211.7 3.9 %collective-permute-done.17.refs_3_ = bf16[1,7040,128]{2,1,0:T(8,128)(2,1)S(1)} collective-permute-done((bf16[1,7040,128]{2,1,0:T(8,128)(2,1)}, bf16[1,7040,128]{2,1,0:T(8,128)(2,1)S(1)}, u32[]{:S(2)}, u32[]{:S(2)}) %collective-permute-start.17) | collective-permute-done | bytes 1802272 | tf_op jit(solution)/shard_map/ppermute | solution.py:188
  216.9 3.4 %combine_two.1 = (bf16[1760,128]{1,0:T(8,128)(2,1)}, bf16[1760,128]{1,0:T(8,128)(2,1)}, bf16[1760,128]{1,0:T(8,128)(2,1)}, bf16[1760,128]{1,0:T(8,128)(2,1)}) custom-call(s32[1]{0:T(128)} %bitcast.1.me_ref, bf16[3,7040,128]{2,1,0:T(8,128)(2,1)} %get-tuple-element.130.refs_0_.refs_2_, bf16[3,7040,128]{2,1,0:T(8,128)(2,1)} %collective-permute-done.14.refs_1_.refs_3_, ...), custom_call_target="tpu_custom_call" | custom-call | flops 1 | bytes 1 | tf_op jit(solution)/shard_map/combine_two/pallas_call | solution.py:1067
  221.3 1.5 collective-permute-start.19
  224.4 9.5 %project_back.1 = bf16[2,512,768]{2,1,0:T(8,128)(2,1)} custom-call(bf16[2,512,768]{2,1,0:T(8,128)(2,1)} %get-tuple-element.147.dq_ref, bf16[2,512,768]{2,1,0:T(8,128)(2,1)} %get-tuple-element.148.dk_ref, bf16[2,512,768]{2,1,0:T(8,128)(2,1)} %get-tuple-element.149.dv_ref, f32[2,512,768]{2,1,0:T(8,128)} %get-tuple-element.150.dh1_ref, ...), custom_call_target="tpu_custom_call" | custom-call | flops 1 | bytes 1 | tf_op jit(solution)/shard_map/project_back/pallas_call | solution.py:785
  235.5 2.8 combine_three.2
  238.4 1.5 collective-permute-start.20
  240.8 2.8 combine_own.2
  245.2 2.8 combine_three.3
  248.0 1.5 collective-permute-start.26
  250.5 3.6 %collective-permute-done.20 = bf16[1760,128]{1,0:T(8,128)(2,1)S(1)} collective-permute-done((bf16[1760,128]{1,0:T(8,128)(2,1)}, bf16[1760,128]{1,0:T(8,128)(2,1)S(1)}, u32[]{:S(2)}, u32[]{:S(2)}) %collective-permute-start.20) | collective-permute-done | bytes 450592 | tf_op jit(solution)/shard_map/ppermute | solution.py:188
  254.2 1.6 collective-permute-start.21
  256.0 2.7 collective-permute-start.23
  258.7 2.8 combine_own.3
  264.9 1.9 collective-permute-done.23
  267.2 2.9 collective-permute-start.29
  270.3 1.8 collective-permute-start.39
  272.2 12.2 %collective-permute-done.36 = bf16[440,128]{1,0:T(8,128)(2,1)S(1)} collective-permute-done((bf16[440,128]{1,0:T(8,128)(2,1)S(1)}, bf16[440,128]{1,0:T(8,128)(2,1)S(1)}, u32[]{:S(2)}, u32[]{:S(2)}) %collective-permute-start.36) | collective-permute-done | bytes 112672 | tf_op jit(solution)/shard_map/ppermute | solution.py:1090
  284.5 3.3 %collective-permute-start.40 = (bf16[440,128]{1,0:T(8,128)(2,1)S(1)}, bf16[440,128]{1,0:T(8,128)(2,1)S(1)}, u32[]{:S(2)}, u32[]{:S(2)}) collective-permute-start(bf16[440,128]{1,0:T(8,128)(2,1)S(1)} %bitcast_add_fusion.4), channel_id=1, source_target_pairs={{0,8},{8,0},{16,24},{24,16},{1,9},{9,1},{17,25},{25,17},{2,10},{10... | collective-permute-start | bytes 337928 | tf_op jit(solution)/shard_map/ppermute | solution.py:1090
  288.1 1.7 collective-permute-start.33
  289.8 3.4 %collective-permute-done.37 = bf16[440,128]{1,0:T(8,128)(2,1)S(1)} collective-permute-done((bf16[440,128]{1,0:T(8,128)(2,1)S(1)}, bf16[440,128]{1,0:T(8,128)(2,1)S(1)}, u32[]{:S(2)}, u32[]{:S(2)}) %collective-permute-start.37) | collective-permute-done | bytes 112672 | tf_op jit(solution)/shard_map/ppermute | solution.py:1090
  293.3 2.3 collective-permute-done.40
  296.9 2.0 collective-permute-start.31
  298.8 3.3 %collective-permute-done.33 = bf16[440,128]{1,0:T(8,128)(2,1)S(1)} collective-permute-done((bf16[440,128]{1,0:T(8,128)(2,1)S(1)}, bf16[440,128]{1,0:T(8,128)(2,1)S(1)}, u32[]{:S(2)}, u32[]{:S(2)}) %collective-permute-start.33) | collective-permute-done | bytes 112672 | tf_op jit(solution)/shard_map/ppermute | solution.py:1090
  302.2 8.4 %collective-permute-done.31 = bf16[440,128]{1,0:T(8,128)(2,1)S(1)} collective-permute-done((bf16[440,128]{1,0:T(8,128)(2,1)S(1)}, bf16[440,128]{1,0:T(8,128)(2,1)S(1)}, u32[]{:S(2)}, u32[]{:S(2)}) %collective-permute-start.31) | collective-permute-done | bytes 112672 | tf_op jit(solution)/shard_map/ppermute | solution.py:1090
  310.8 2.5 collective-permute-done.34
  313.4 3.3 %adam.2 = (f32[7036,128]{1,0:T(8,128)}, f32[7036,128]{1,0:T(8,128)}, f32[7036,128]{1,0:T(8,128)}) custom-call(s32[1]{0:T(128)} %bitcast.16.z_ref, bf16[880,128]{1,0:T(8,128)(2,1)S(1)} %maximum_select_fusion.2.one, bf16[880,128]{1,0:T(8,128)(2,1)S(1)} %collective-permute-done.38.one_other, bf16[880,128]{1,0:T(8,128)(2,1)S(1)} %maximum_select_fusion.3.two, ...), custom_call_target="tpu_custom_call" | custom-call | flops 1 | bytes 1 | tf_op jit(solution)/shard_map/adam/pallas_call | solution.py:1119
  316.7 5.4 %collective-permute-done.35.two_other = bf16[880,128]{1,0:T(8,128)(2,1)S(1)} collective-permute-done((bf16[880,128]{1,0:T(8,128)(2,1)S(1)}, bf16[880,128]{1,0:T(8,128)(2,1)S(1)}, u32[]{:S(2)}, u32[]{:S(2)}) %collective-permute-start.35) | collective-permute-done | bytes 225312 | tf_op jit(solution)/shard_map/ppermute | solution.py:1090
  322.1 3.4 %adam.3 = (f32[7036,128]{1,0:T(8,128)}, f32[7036,128]{1,0:T(8,128)}, f32[7036,128]{1,0:T(8,128)}) custom-call(s32[1]{0:T(128)} %bitcast.16.z_ref, bf16[880,128]{1,0:T(8,128)(2,1)S(1)} %maximum_select_fusion.one, bf16[880,128]{1,0:T(8,128)(2,1)S(1)} %collective-permute-done.32.one_other, ...), custom_call_target="tpu_custom_call", output_to_operand_aliasing={{0}: (7, {}), {1}: (8, {}), {2}: (9, {})} | custom-call | flops 1 | bytes 1 | tf_op jit(solution)/shard_map/adam/pallas_call | solution.py:1119
  (141 shorter events, 29.5 us)
Async XLA Ops:
  2.9 23.2 %copy-start.3 = (bf16[3520,128]{1,0:T(8,128)(2,1)}, bf16[3520,128]{1,0:T(8,128)(2,1)S(1)}, u32[]{:S(2)}) copy-start(bf16[3520,128]{1,0:T(8,128)(2,1)S(1)} %slice_bitcast_fusion.1.rest_0_.refs_6_) | copy-start | bytes 2703364
  3.0 29.7 %copy-start.4 = (bf16[3520,128]{1,0:T(8,128)(2,1)}, bf16[3520,128]{1,0:T(8,128)(2,1)S(1)}, u32[]{:S(2)}) copy-start(bf16[3520,128]{1,0:T(8,128)(2,1)S(1)} %pad.4.rest_1_.refs_7_) | copy-start | bytes 2703364
  3.1 23.0 %collective-permute-start = (bf16[3520,128]{1,0:T(8,128)(2,1)S(1)}, bf16[3520,128]{1,0:T(8,128)(2,1)S(1)}, u32[]{:S(2)}, u32[]{:S(2)}) collective-permute-start(bf16[3520,128]{1,0:T(8,128)(2,1)S(1)} %slice_bitcast_fusion.1.rest_0_.refs_6_), channel_id=1, source_target_pairs={{0,2},{1,3},{2,0},{3,1},{4,6},{5,7},{6,4},{7,5},{8,10},{9,11},{10,... | collective-permute-start | bytes 2703368 | tf_op jit(solution)/shard_map/ppermute | solution.py:188
  6.1 27.2 %collective-permute-start.4 = (bf16[3520,128]{1,0:T(8,128)(2,1)S(1)}, bf16[3520,128]{1,0:T(8,128)(2,1)}, u32[]{:S(2)}, u32[]{:S(2)}) collective-permute-start(bf16[3520,128]{1,0:T(8,128)(2,1)S(1)} %slice_bitcast_fusion.1.rest_0_.refs_6_), channel_id=1, source_target_pairs={{0,1},{1,0},{2,3},{3,2},{4,5},{5,4},{6,7},{7,6},{8,9},{9,8},{10,11... | collective-permute-start | bytes 2703368 | tf_op jit(solution)/shard_map/ppermute | solution.py:188
  6.1 23.0 %collective-permute-start.1 = (bf16[3520,128]{1,0:T(8,128)(2,1)S(1)}, bf16[3520,128]{1,0:T(8,128)(2,1)}, u32[]{:S(2)}, u32[]{:S(2)}) collective-permute-start(bf16[3520,128]{1,0:T(8,128)(2,1)S(1)} %pad.4.rest_1_.refs_7_), channel_id=1, source_target_pairs={{0,4},{1,5},{2,6},{3,7},{4,0},{5,1},{6,2},{7,3},{8,12},{9,13},{10,... | collective-permute-start | bytes 2703368 | tf_op jit(solution)/shard_map/ppermute | solution.py:188
  27.2 28.4 %copy-start.20 = (s32[2,512]{1,0:T(2,128)S(1)}, s32[2,512]{1,0:T(2,128)}, u32[]{:S(2)}) copy-start(s32[2,512]{1,0:T(2,128)} %param.13) | copy-start | bytes 12292
  27.2 21.4 %collective-permute-start.2 = (bf16[3520,128]{1,0:T(8,128)(2,1)S(1)}, bf16[3520,128]{1,0:T(8,128)(2,1)}, u32[]{:S(2)}, u32[]{:S(2)}) collective-permute-start(bf16[3520,128]{1,0:T(8,128)(2,1)S(1)} %get-tuple-element.191), channel_id=1, source_target_pairs={{0,4},{1,5},{2,6},{3,7},{4,0},{5,1},{6,2},{7,3},{8,12},{9,13},{10,... | collective-permute-start | bytes 2703368 | tf_op jit(solution)/shard_map/ppermute | solution.py:188
  31.2 21.3 %collective-permute-start.3 = (bf16[3520,128]{1,0:T(8,128)(2,1)S(1)}, bf16[3520,128]{1,0:T(8,128)(2,1)}, u32[]{:S(2)}, u32[]{:S(2)}) collective-permute-start(bf16[3520,128]{1,0:T(8,128)(2,1)S(1)} %get-tuple-element.189), channel_id=1, source_target_pairs={{0,2},{1,3},{2,0},{3,1},{4,6},{5,7},{6,4},{7,5},{8,10},{9,11},{10,... | collective-permute-start | bytes 2703368 | tf_op jit(solution)/shard_map/ppermute | solution.py:188
  32.7 19.8 %collective-permute-start.5 = (bf16[3520,128]{1,0:T(8,128)(2,1)S(1)}, bf16[3520,128]{1,0:T(8,128)(2,1)S(1)}, u32[]{:S(2)}, u32[]{:S(2)}) collective-permute-start(bf16[3520,128]{1,0:T(8,128)(2,1)S(1)} %pad.4.rest_1_.refs_7_), channel_id=1, source_target_pairs={{0,1},{1,0},{2,3},{3,2},{4,5},{5,4},{6,7},{7,6},{8,9},{9,8},{10,11... | collective-permute-start | bytes 2703368 | tf_op jit(solution)/shard_map/ppermute | solution.py:188
  32.7 21.4 %collective-permute-start.6 = (bf16[3520,128]{1,0:T(8,128)(2,1)S(1)}, bf16[3520,128]{1,0:T(8,128)(2,1)S(1)}, u32[]{:S(2)}, u32[]{:S(2)}) collective-permute-start(bf16[3520,128]{1,0:T(8,128)(2,1)S(1)} %collective-permute-done.rest_2_.refs_8_), channel_id=1, source_target_pairs={{0,1},{1,0},{2,3},{3,2},{4,5},{5,4},{6,7},{7,6},{8,9},{9,8},{10,11... | collective-permute-start | bytes 2703368 | tf_op jit(solution)/shard_map/ppermute | solution.py:188
  33.2 24.0 %collective-permute-start.7 = (bf16[3520,128]{1,0:T(8,128)(2,1)}, bf16[3520,128]{1,0:T(8,128)(2,1)S(1)}, u32[]{:S(2)}, u32[]{:S(2)}) collective-permute-start(bf16[3520,128]{1,0:T(8,128)(2,1)} %collective-permute-done.1.rest_3_.refs_9_), channel_id=1, source_target_pairs={{0,1},{1,0},{2,3},{3,2},{4,5},{5,4},{6,7},{7,6},{8,9},{9,8},{10,11... | collective-permute-start | bytes 2703368 | tf_op jit(solution)/shard_map/ppermute | solution.py:188
  48.6 8.6 %collective-permute-start.8 = (bf16[3520,128]{1,0:T(8,128)(2,1)}, bf16[3520,128]{1,0:T(8,128)(2,1)}, u32[]{:S(2)}, u32[]{:S(2)}) collective-permute-start(bf16[3520,128]{1,0:T(8,128)(2,1)} %collective-permute-done.2.rest_4_.refs_10_), channel_id=1, source_target_pairs={{0,1},{1,0},{2,3},{3,2},{4,5},{5,4},{6,7},{7,6},{8,9},{9,8},{10,11... | collective-permute-start | bytes 2703368 | tf_op jit(solution)/shard_map/ppermute | solution.py:188
  52.5 4.7 %collective-permute-start.9 = (bf16[3520,128]{1,0:T(8,128)(2,1)}, bf16[3520,128]{1,0:T(8,128)(2,1)}, u32[]{:S(2)}, u32[]{:S(2)}) collective-permute-start(bf16[3520,128]{1,0:T(8,128)(2,1)} %collective-permute-done.3.rest_5_.refs_11_), channel_id=1, source_target_pairs={{0,1},{1,0},{2,3},{3,2},{4,5},{5,4},{6,7},{7,6},{8,9},{9,8},{10,11... | collective-permute-start | bytes 2703368 | tf_op jit(solution)/shard_map/ppermute | solution.py:188
  52.5 27.2 %collective-permute-start.10 = (bf16[3520,128]{1,0:T(8,128)(2,1)}, bf16[3520,128]{1,0:T(8,128)(2,1)S(1)}, u32[]{:S(2)}, u32[]{:S(2)}) collective-permute-start(bf16[3520,128]{1,0:T(8,128)(2,1)} %get-tuple-element.190), channel_id=1, source_target_pairs={{0,4},{1,5},{2,6},{3,7},{4,0},{5,1},{6,2},{7,3},{8,12},{9,13},{10,... | collective-permute-start | bytes 2703368 | tf_op jit(solution)/shard_map/ppermute | solution.py:188
  55.1 24.6 %collective-permute-start.11 = (bf16[3520,128]{1,0:T(8,128)(2,1)}, bf16[3520,128]{1,0:T(8,128)(2,1)S(1)}, u32[]{:S(2)}, u32[]{:S(2)}) collective-permute-start(bf16[3520,128]{1,0:T(8,128)(2,1)} %get-tuple-element.188), channel_id=1, source_target_pairs={{0,2},{1,3},{2,0},{3,1},{4,6},{5,7},{6,4},{7,5},{8,10},{9,11},{10,... | collective-permute-start | bytes 2703368 | tf_op jit(solution)/shard_map/ppermute | solution.py:188
  63.0 17.6 %copy-start.23 = (s32[8]{0:T(128)S(1)}, s32[8]{0:T(128)}, u32[]{:S(2)}) copy-start(s32[8]{0:T(128)} %constant.65.clone) | copy-start | bytes 100
  79.7 3.0 collective-permute-start.12
  79.8 3.9 %collective-permute-start.13 = (bf16[3520,128]{1,0:T(8,128)(2,1)S(1)}, bf16[3520,128]{1,0:T(8,128)(2,1)}, u32[]{:S(2)}, u32[]{:S(2)}) collective-permute-start(bf16[3520,128]{1,0:T(8,128)(2,1)S(1)} %collective-permute-done.11.refs_13_), channel_id=1, source_target_pairs={{0,1},{1,0},{2,3},{3,2},{4,5},{5,4},{6,7},{7,6},{8,9},{9,8},{10,11... | collective-permute-start | bytes 2703368 | tf_op jit(solution)/shard_map/ppermute | solution.py:188
  175.0 9.3 %collective-permute-start.14 = (bf16[3,7040,128]{2,1,0:T(8,128)(2,1)}, bf16[3,7040,128]{2,1,0:T(8,128)(2,1)}, u32[]{:S(2)}, u32[]{:S(2)}) collective-permute-start(bf16[3,7040,128]{2,1,0:T(8,128)(2,1)} %get-tuple-element.121), channel_id=1, source_target_pairs={{0,1},{1,0},{2,3},{3,2},{4,5},{5,4},{6,7},{7,6},{8,9},{9,8},{10,11... | collective-permute-start | bytes 16220168 | tf_op jit(solution)/shard_map/ppermute | solution.py:188
  187.7 22.3 %collective-permute-start.15 = (bf16[3520,128]{1,0:T(8,128)(2,1)}, bf16[3520,128]{1,0:T(8,128)(2,1)S(1)}, u32[]{:S(2)}, u32[]{:S(2)}) collective-permute-start(bf16[3520,128]{1,0:T(8,128)(2,1)} %get-tuple-element.132), channel_id=1, source_target_pairs={{0,4},{1,5},{2,6},{3,7},{4,0},{5,1},{6,2},{7,3},{8,12},{9,13},{10,... | collective-permute-start | bytes 2703368 | tf_op jit(solution)/shard_map/ppermute | solution.py:188
  188.8 22.0 %collective-permute-start.16 = (bf16[3520,128]{1,0:T(8,128)(2,1)}, bf16[3520,128]{1,0:T(8,128)(2,1)S(1)}, u32[]{:S(2)}, u32[]{:S(2)}) collective-permute-start(bf16[3520,128]{1,0:T(8,128)(2,1)} %get-tuple-element.143), channel_id=1, source_target_pairs={{0,2},{1,3},{2,0},{3,1},{4,6},{5,7},{6,4},{7,5},{8,10},{9,11},{10,... | collective-permute-start | bytes 2703368 | tf_op jit(solution)/shard_map/ppermute | solution.py:188
  211.7 3.9 %collective-permute-start.17 = (bf16[1,7040,128]{2,1,0:T(8,128)(2,1)}, bf16[1,7040,128]{2,1,0:T(8,128)(2,1)S(1)}, u32[]{:S(2)}, u32[]{:S(2)}) collective-permute-start(bf16[1,7040,128]{2,1,0:T(8,128)(2,1)} %get-tuple-element.145), channel_id=1, source_target_pairs={{0,1},{1,0},{2,3},{3,2},{4,5},{5,4},{6,7},{7,6},{8,9},{9,8},{10,11... | collective-permute-start | bytes 5406728 | tf_op jit(solution)/shard_map/ppermute | solution.py:188
  220.2 13.6 %collective-permute-start.18 = (bf16[1760,128]{1,0:T(8,128)(2,1)}, bf16[1760,128]{1,0:T(8,128)(2,1)S(1)}, u32[]{:S(2)}, u32[]{:S(2)}) collective-permute-start(bf16[1760,128]{1,0:T(8,128)(2,1)} %get-tuple-element.146), channel_id=1, source_target_pairs={{0,4},{1,5},{2,6},{3,7},{4,0},{5,1},{6,2},{7,3},{8,12},{9,13},{10,... | collective-permute-start | bytes 1351688 | tf_op jit(solution)/shard_map/ppermute | solution.py:188
  221.3 13.4 %collective-permute-start.19 = (bf16[1760,128]{1,0:T(8,128)(2,1)}, bf16[1760,128]{1,0:T(8,128)(2,1)S(1)}, u32[]{:S(2)}, u32[]{:S(2)}) collective-permute-start(bf16[1760,128]{1,0:T(8,128)(2,1)} %get-tuple-element.153), channel_id=1, source_target_pairs={{0,2},{1,3},{2,0},{3,1},{4,6},{5,7},{6,4},{7,5},{8,10},{9,11},{10,... | collective-permute-start | bytes 1351688 | tf_op jit(solution)/shard_map/ppermute | solution.py:188
  222.8 20.8 %collective-permute-start.24 = (bf16[1760,128]{1,0:T(8,128)(2,1)}, bf16[1760,128]{1,0:T(8,128)(2,1)S(1)}, u32[]{:S(2)}, u32[]{:S(2)}) collective-permute-start(bf16[1760,128]{1,0:T(8,128)(2,1)} %get-tuple-element.164), channel_id=1, source_target_pairs={{0,4},{1,5},{2,6},{3,7},{4,0},{5,1},{6,2},{7,3},{8,12},{9,13},{10,... | collective-permute-start | bytes 1351688 | tf_op jit(solution)/shard_map/ppermute | solution.py:188
  223.7 20.7 %collective-permute-start.25 = (bf16[1760,128]{1,0:T(8,128)(2,1)}, bf16[1760,128]{1,0:T(8,128)(2,1)S(1)}, u32[]{:S(2)}, u32[]{:S(2)}) collective-permute-start(bf16[1760,128]{1,0:T(8,128)(2,1)} %get-tuple-element.165), channel_id=1, source_target_pairs={{0,2},{1,3},{2,0},{3,1},{4,6},{5,7},{6,4},{7,5},{8,10},{9,11},{10,... | collective-permute-start | bytes 1351688 | tf_op jit(solution)/shard_map/ppermute | solution.py:188
  238.4 15.7 %collective-permute-start.20 = (bf16[1760,128]{1,0:T(8,128)(2,1)}, bf16[1760,128]{1,0:T(8,128)(2,1)S(1)}, u32[]{:S(2)}, u32[]{:S(2)}) collective-permute-start(bf16[1760,128]{1,0:T(8,128)(2,1)} %get-tuple-element.156), channel_id=1, source_target_pairs={{0,2},{1,3},{2,0},{3,1},{4,6},{5,7},{6,4},{7,5},{8,10},{9,11},{10,... | collective-permute-start | bytes 1351688 | tf_op jit(solution)/shard_map/ppermute | solution.py:188
  239.9 16.0 %collective-permute-start.22 = (bf16[1760,128]{1,0:T(8,128)(2,1)}, bf16[1760,128]{1,0:T(8,128)(2,1)S(1)}, u32[]{:S(2)}, u32[]{:S(2)}) collective-permute-start(bf16[1760,128]{1,0:T(8,128)(2,1)} %get-tuple-element.163), channel_id=1, source_target_pairs={{0,4},{1,5},{2,6},{3,7},{4,0},{5,1},{6,2},{7,3},{8,12},{9,13},{10,... | collective-permute-start | bytes 1351688 | tf_op jit(solution)/shard_map/ppermute | solution.py:188
  248.0 14.6 %collective-permute-start.26 = (bf16[1760,128]{1,0:T(8,128)(2,1)}, bf16[1760,128]{1,0:T(8,128)(2,1)S(1)}, u32[]{:S(2)}, u32[]{:S(2)}) collective-permute-start(bf16[1760,128]{1,0:T(8,128)(2,1)} %get-tuple-element.173), channel_id=1, source_target_pairs={{0,2},{1,3},{2,0},{3,1},{4,6},{5,7},{6,4},{7,5},{8,10},{9,11},{10,... | collective-permute-start | bytes 1351688 | tf_op jit(solution)/shard_map/ppermute | solution.py:188
  249.6 14.2 %collective-permute-start.27 = (bf16[1760,128]{1,0:T(8,128)(2,1)}, bf16[1760,128]{1,0:T(8,128)(2,1)S(1)}, u32[]{:S(2)}, u32[]{:S(2)}) collective-permute-start(bf16[1760,128]{1,0:T(8,128)(2,1)} %get-tuple-element.175), channel_id=1, source_target_pairs={{0,4},{1,5},{2,6},{3,7},{4,0},{5,1},{6,2},{7,3},{8,12},{9,13},{10,... | collective-permute-start | bytes 1351688 | tf_op jit(solution)/shard_map/ppermute | solution.py:188
  254.2 10.7 %collective-permute-start.21 = (bf16[880,128]{1,0:T(8,128)(2,1)S(1)}, bf16[880,128]{1,0:T(8,128)(2,1)S(1)}, u32[]{:S(2)}, u32[]{:S(2)}) collective-permute-start(bf16[880,128]{1,0:T(8,128)(2,1)S(1)} %dynamic-slice_bitcast_fusion.3), channel_id=1, source_target_pairs={{0,8},{8,0},{16,24},{24,16},{1,9},{9,1},{17,25},{25,17},{2,10},{10... | collective-permute-start | bytes 675848 | tf_op jit(solution)/shard_map/ppermute | solution.py:1090
  256.0 10.8 %collective-permute-start.23 = (bf16[880,128]{1,0:T(8,128)(2,1)S(1)}, bf16[880,128]{1,0:T(8,128)(2,1)S(1)}, u32[]{:S(2)}, u32[]{:S(2)}) collective-permute-start(bf16[880,128]{1,0:T(8,128)(2,1)S(1)} %dynamic-slice_bitcast_fusion.2), channel_id=1, source_target_pairs={{0,16},{8,24},{16,0},{24,8},{1,17},{9,25},{17,1},{25,9},{2,18},{10... | collective-permute-start | bytes 675848 | tf_op jit(solution)/shard_map/ppermute | solution.py:1090
  266.9 21.0 %collective-permute-start.28 = (bf16[880,128]{1,0:T(8,128)(2,1)S(1)}, bf16[880,128]{1,0:T(8,128)(2,1)S(1)}, u32[]{:S(2)}, u32[]{:S(2)}) collective-permute-start(bf16[880,128]{1,0:T(8,128)(2,1)S(1)} %dynamic-slice_bitcast_fusion.1), channel_id=1, source_target_pairs={{0,8},{8,0},{16,24},{24,16},{1,9},{9,1},{17,25},{25,17},{2,10},{10... | collective-permute-start | bytes 675848 | tf_op jit(solution)/shard_map/ppermute | solution.py:1090
  267.2 46.2 %copy-start.1 = (f32[900608]{0:T(1024)S(1)}, f32[900608]{0:T(1024)}, u32[]{:S(2)}) copy-start(f32[900608]{0:T(1024)} %param.19) | copy-start | bytes 10807300
  267.2 20.7 %collective-permute-start.29 = (bf16[880,128]{1,0:T(8,128)(2,1)S(1)}, bf16[880,128]{1,0:T(8,128)(2,1)S(1)}, u32[]{:S(2)}, u32[]{:S(2)}) collective-permute-start(bf16[880,128]{1,0:T(8,128)(2,1)S(1)} %dynamic-slice_bitcast_fusion), channel_id=1, source_target_pairs={{0,16},{8,24},{16,0},{24,8},{1,17},{9,25},{17,1},{25,9},{2,18},{10... | collective-permute-start | bytes 675848 | tf_op jit(solution)/shard_map/ppermute | solution.py:1090
  270.1 14.2 %collective-permute-start.36 = (bf16[440,128]{1,0:T(8,128)(2,1)S(1)}, bf16[440,128]{1,0:T(8,128)(2,1)S(1)}, u32[]{:S(2)}, u32[]{:S(2)}) collective-permute-start(bf16[440,128]{1,0:T(8,128)(2,1)S(1)} %dynamic-slice_bitcast_fusion.5), channel_id=1, source_target_pairs={{0,16},{8,24},{16,0},{24,8},{1,17},{9,25},{17,1},{25,9},{2,18},{10... | collective-permute-start | bytes 337928 | tf_op jit(solution)/shard_map/ppermute | solution.py:1090
  270.3 14.1 %collective-permute-start.39 = (bf16[440,128]{1,0:T(8,128)(2,1)S(1)}, bf16[440,128]{1,0:T(8,128)(2,1)S(1)}, u32[]{:S(2)}, u32[]{:S(2)}) collective-permute-start(bf16[440,128]{1,0:T(8,128)(2,1)S(1)} %dynamic-slice_bitcast_fusion.4), channel_id=1, source_target_pairs={{0,8},{8,0},{16,24},{24,16},{1,9},{9,1},{17,25},{25,17},{2,10},{10... | collective-permute-start | bytes 337928 | tf_op jit(solution)/shard_map/ppermute | solution.py:1090
  284.4 8.8 %collective-permute-start.37 = (bf16[440,128]{1,0:T(8,128)(2,1)S(1)}, bf16[440,128]{1,0:T(8,128)(2,1)S(1)}, u32[]{:S(2)}, u32[]{:S(2)}) collective-permute-start(bf16[440,128]{1,0:T(8,128)(2,1)S(1)} %bitcast_add_fusion.5), channel_id=1, source_target_pairs={{0,16},{8,24},{16,0},{24,8},{1,17},{9,25},{17,1},{25,9},{2,18},{10... | collective-permute-start | bytes 337928 | tf_op jit(solution)/shard_map/ppermute | solution.py:1090
  284.5 11.1 %collective-permute-start.40 = (bf16[440,128]{1,0:T(8,128)(2,1)S(1)}, bf16[440,128]{1,0:T(8,128)(2,1)S(1)}, u32[]{:S(2)}, u32[]{:S(2)}) collective-permute-start(bf16[440,128]{1,0:T(8,128)(2,1)S(1)} %bitcast_add_fusion.4), channel_id=1, source_target_pairs={{0,8},{8,0},{16,24},{24,16},{1,9},{9,1},{17,25},{25,17},{2,10},{10... | collective-permute-start | bytes 337928 | tf_op jit(solution)/shard_map/ppermute | solution.py:1090
  287.9 25.5 %copy-start = (f32[900608]{0:T(1024)S(1)}, f32[900608]{0:T(1024)}, u32[]{:S(2)}) copy-start(f32[900608]{0:T(1024)} %param.18) | copy-start | bytes 10807300
  287.9 8.9 %collective-permute-start.30 = (bf16[440,128]{1,0:T(8,128)(2,1)S(1)}, bf16[440,128]{1,0:T(8,128)(2,1)S(1)}, u32[]{:S(2)}, u32[]{:S(2)}) collective-permute-start(bf16[440,128]{1,0:T(8,128)(2,1)S(1)} %dynamic-slice_bitcast_fusion.7), channel_id=1, source_target_pairs={{0,16},{8,24},{16,0},{24,8},{1,17},{9,25},{17,1},{25,9},{2,18},{10... | collective-permute-start | bytes 337928 | tf_op jit(solution)/shard_map/ppermute | solution.py:1090
  288.1 14.0 %collective-permute-start.33 = (bf16[440,128]{1,0:T(8,128)(2,1)S(1)}, bf16[440,128]{1,0:T(8,128)(2,1)S(1)}, u32[]{:S(2)}, u32[]{:S(2)}) collective-permute-start(bf16[440,128]{1,0:T(8,128)(2,1)S(1)} %dynamic-slice_bitcast_fusion.6), channel_id=1, source_target_pairs={{0,8},{8,0},{16,24},{24,16},{1,9},{9,1},{17,25},{25,17},{2,10},{10... | collective-permute-start | bytes 337928 | tf_op jit(solution)/shard_map/ppermute | solution.py:1090
  293.3 20.1 %collective-permute-start.38 = (bf16[880,128]{1,0:T(8,128)(2,1)S(1)}, bf16[880,128]{1,0:T(8,128)(2,1)S(1)}, u32[]{:S(2)}, u32[]{:S(2)}) collective-permute-start(bf16[880,128]{1,0:T(8,128)(2,1)S(1)} %maximum_select_fusion.2.one), channel_id=1, source_target_pairs={{0,8},{8,0},{16,24},{24,16},{1,9},{9,1},{17,25},{25,17},{2,10},{10... | collective-permute-start | bytes 675848 | tf_op jit(solution)/shard_map/ppermute | solution.py:1090
  295.7 17.7 %collective-permute-start.41 = (bf16[880,128]{1,0:T(8,128)(2,1)S(1)}, bf16[880,128]{1,0:T(8,128)(2,1)S(1)}, u32[]{:S(2)}, u32[]{:S(2)}) collective-permute-start(bf16[880,128]{1,0:T(8,128)(2,1)S(1)} %maximum_select_fusion.3.two), channel_id=1, source_target_pairs={{0,16},{8,24},{16,0},{24,8},{1,17},{9,25},{17,1},{25,9},{2,18},{10... | collective-permute-start | bytes 675848 | tf_op jit(solution)/shard_map/ppermute | solution.py:1090
  296.9 13.8 %collective-permute-start.31 = (bf16[440,128]{1,0:T(8,128)(2,1)S(1)}, bf16[440,128]{1,0:T(8,128)(2,1)S(1)}, u32[]{:S(2)}, u32[]{:S(2)}) collective-permute-start(bf16[440,128]{1,0:T(8,128)(2,1)S(1)} %bitcast_add_fusion.7), channel_id=1, source_target_pairs={{0,16},{8,24},{16,0},{24,8},{1,17},{9,25},{17,1},{25,9},{2,18},{10... | collective-permute-start | bytes 337928 | tf_op jit(solution)/shard_map/ppermute | solution.py:1090
  302.1 11.1 %collective-permute-start.34 = (bf16[440,128]{1,0:T(8,128)(2,1)S(1)}, bf16[440,128]{1,0:T(8,128)(2,1)S(1)}, u32[]{:S(2)}, u32[]{:S(2)}) collective-permute-start(bf16[440,128]{1,0:T(8,128)(2,1)S(1)} %bitcast_add_fusion.6), channel_id=1, source_target_pairs={{0,8},{8,0},{16,24},{24,16},{1,9},{9,1},{17,25},{25,17},{2,10},{10... | collective-permute-start | bytes 337928 | tf_op jit(solution)/shard_map/ppermute | solution.py:1090
  310.7 6.0 %collective-permute-start.32 = (bf16[880,128]{1,0:T(8,128)(2,1)S(1)}, bf16[880,128]{1,0:T(8,128)(2,1)S(1)}, u32[]{:S(2)}, u32[]{:S(2)}) collective-permute-start(bf16[880,128]{1,0:T(8,128)(2,1)S(1)} %maximum_select_fusion.one), channel_id=1, source_target_pairs={{0,8},{8,0},{16,24},{24,16},{1,9},{9,1},{17,25},{25,17},{2,10},{10... | collective-permute-start | bytes 675848 | tf_op jit(solution)/shard_map/ppermute | solution.py:1090
  313.3 8.8 %collective-permute-start.35 = (bf16[880,128]{1,0:T(8,128)(2,1)S(1)}, bf16[880,128]{1,0:T(8,128)(2,1)S(1)}, u32[]{:S(2)}, u32[]{:S(2)}) collective-permute-start(bf16[880,128]{1,0:T(8,128)(2,1)S(1)} %maximum_select_fusion.1.two), channel_id=1, source_target_pairs={{0,16},{8,24},{16,0},{24,8},{1,17},{9,25},{17,1},{25,9},{2,18},{10... | collective-permute-start | bytes 675848 | tf_op jit(solution)/shard_map/ppermute | solution.py:1090
  (21 other events, 138.9 us)

commit v6 on v5

--- a/solution.py
+++ b/solution.py
@@ -30,7 +30,7 @@
 
 F32 = jnp.float32
 BF = jnp.bfloat16
-HIGH = lax.Precision.HIGHEST
+HIGH = lax.Precision.HIGH
 SDS = jax.ShapeDtypeStruct
 
 QB = 128
@@ -250,6 +250,9 @@
     )(me, *pieces)
 
 
+SLOTS = 8
+
+
 def widen_rows(flat, place, src, first, last):
     whole_steps = (last - first) // CHUNK
 
@@ -280,7 +283,7 @@
 
                 @pl.when(owner_ref[n % 8] ^ (n // 8) == targets[t][0])
                 def _(src=src):
-                    pltpu.make_async_copy(src, buf.at[t % 4], sems.at[t % 4]).start()
+                    pltpu.make_async_copy(src, buf.at[t % SLOTS], sems.at[t % SLOTS]).start()
 
     nb = D // LANE
 
@@ -317,12 +320,12 @@
 
     ends = (TABLE["w_in"], TABLE["w_back"], 8 * shard_rows)
     regions = list(zip((SPLIT, *ends), ends, (region_out, region_in, region_back)))
-    for t in range(3):
+    for t in range(SLOTS - 1):
         start(t)
     for t, (d, h) in enumerate(targets):
-        if t + 3 < len(targets):
-            start(t + 3)
-        pltpu.make_async_copy(pieces[0], buf.at[t % 4], sems.at[t % 4]).wait()
+        if t + SLOTS - 1 < len(targets):
+            start(t + SLOTS - 1)
+        pltpu.make_async_copy(pieces[0], buf.at[t % SLOTS], sems.at[t % SLOTS]).wait()
         origin = d * shard_rows + h * half
         size = min(half, shard_rows - h * half)
         for first, last, put in regions:
@@ -330,7 +333,7 @@
             if lo >= hi:
                 continue
             lo, hi = lo // 16 * 16, min(half, -(-hi // 16) * 16)
-            widen_rows(flat, 16 + origin + lo - first, buf.at[t % 4], lo, hi)
+            widen_rows(flat, 16 + origin + lo - first, buf.at[t % SLOTS], lo, hi)
             if last <= origin + size:
                 put(first)
 
@@ -344,7 +347,8 @@
     own = lax.optimization_barrier((mine[:half].astype(BF), own_b))
     near = (swap(own[0], 2), swap(own[1], 4))
     far = (swap(jnp.where(x == 1, near[0], own[0]), 4), swap(jnp.where(y == 1, near[1], own[1]), 2))
-    last = (swap(jnp.where(x == 1, own[0], near[0]), 4), swap(jnp.where(y == 1, own[1], near[1]), 2))
+    held, close, _ = lax.optimization_barrier((own, near, x))
+    last = (swap(jnp.where(x == 1, held[0], close[0]), 4), swap(jnp.where(y == 1, held[1], close[1]), 2))
     early = own + near + far
     early_c = tuple(swap(v, 1) for v in early)
     first = unpack_first(me.reshape(1), shard_rows, *early, *early_c)
@@ -425,7 +429,7 @@
     )(x, segc, segr, wqkv, wqkv, wqkv, bq)
 
 
-TB = 64
+TB = 512
 
 
 def fold(v):
@@ -651,7 +655,7 @@
         weight_specs = [SM] + [ANY] * len(pieces)
         half = pieces[0].shape[0]
         own = [pltpu.VMEM(w.shape, w.dtype) for w in held]
-        own += [pltpu.VMEM((4, half, LANE), BF), pltpu.SemaphoreType.DMA((4,))]
+        own += [pltpu.VMEM((SLOTS, half, LANE), BF), pltpu.SemaphoreType.DMA((SLOTS,))]
         flat_rows = 8 * shard_rows - TABLE["w_back"] + 32 + half
     widths = (D, D, FF, D, FF)
 

time: 326 us -> 316 us (0.969)
  Pallas kernels: 171 us -> 160 us
    pallas_call x1, Pallas kernels: 66.6 us -> 55.7 us  [middle(): pl.pallas_call(kernel, grid=(rows,), in_specs=[row_spec(LEN, D), row_spec...]
  transfers between devices with their start and end apart: 42 -> 42, of which waited for: 22 -> 24; matrix products, arithmetic and copies ran while one was open for 3% -> 3% of each run, Pallas kernels for 21% -> 22%
where the time goes in v6:
time: 316 us; the launch traced here: 315 us
  Pallas kernels  160 us (51%)
  waiting for transfers between devices  97.4 us (31%)
  starting transfers between devices  38.2 us (12%)
  other arithmetic  10 us (3%)
  local copies, waits for them, and re-layouts  7.73 us (2%)
    ppermute x26, waiting for transfers between devices, swap(): return lax.ppermute(v, 'fsdp', [(d, d ^ bit) for d in range(8)])  56.5 us
    pallas_call x1, Pallas kernels, middle(): pl.pallas_call(kernel, grid=(rows,), in_specs=[row_spec(LEN, D), row_spec...  55.7 us
    ppermute x16, waiting for transfers between devices, sum_replicas(): lax.ppermute(v, 'rep', [(i, i ^ bit) for i in range(4)])  40.9 us
    pallas_call x1, Pallas kernels, late_pairs(): pl.pallas_call(functools.partial(late_pair_kernel, shard_rows), in_specs=...  24.7 us
    ppermute x26, starting transfers between devices, swap(): return lax.ppermute(v, 'fsdp', [(d, d ^ bit) for d in range(8)])  21.4 us
    pallas_call x6, Pallas kernels, combine(): pl.pallas_call(functools.partial(combine_kernel, plan, len(extras)), in_s...  17.9 us
    ppermute x16, starting transfers between devices, sum_replicas(): lax.ppermute(v, 'rep', [(i, i ^ bit) for i in range(4)])  16.9 us
    pallas_call x1, Pallas kernels, attend(): pl.pallas_call(attend_kernel, grid=(rows, D // 256), in_specs=[only(LEN,...  16.7 us
  transfers between devices with their start and end apart: 42, of which 24 were waited for; matrix products, arithmetic and copies ran while one was open for 3% of the time, Pallas kernels for 22%

profile of v6, /device:TPU:0, one launch (start us, length us, event | category | flops | bytes accessed | tf_op | source)
XLA Modules:
  0.0 315.0 jit_solution(11506104384438354116)
XLA Ops:
  0.6 2.2 convert.4
  3.1 3.0 collective-permute-start
  6.1 1.5 collective-permute-start.1
  7.8 18.2 %collective-permute-done.rest_2_.refs_8_ = bf16[3520,128]{1,0:T(8,128)(2,1)S(1)} collective-permute-done((bf16[3520,128]{1,0:T(8,128)(2,1)S(1)}, bf16[3520,128]{1,0:T(8,128)(2,1)S(1)}, u32[]{:S(2)}, u32[]{:S(2)}) %collective-permute-start) | collective-permute-done | bytes 901152 | tf_op jit(solution)/shard_map/ppermute | solution.py:188
  26.2 1.8 collective-permute-start.2
  31.2 16.7 %collective-permute-done.2.rest_4_.refs_10_ = bf16[3520,128]{1,0:T(8,128)(2,1)} collective-permute-done((bf16[3520,128]{1,0:T(8,128)(2,1)S(1)}, bf16[3520,128]{1,0:T(8,128)(2,1)}, u32[]{:S(2)}, u32[]{:S(2)}) %collective-permute-start.2) | collective-permute-done | bytes 901152 | tf_op jit(solution)/shard_map/ppermute | solution.py:188
  47.9 2.6 collective-permute-done.3.rest_5_.refs_11_
  50.5 2.2 broadcast_select_fusion
  52.7 1.5 collective-permute-start.10
  58.3 4.7 %unpack_first.1 = (bf16[768,2304]{1,0:T(8,128)(2,1)}, f32[8,2304]{1,0:T(8,128)}) custom-call(s32[1]{0:T(128)} %bitcast.1.me_ref, bf16[3520,128]{1,0:T(8,128)(2,1)} %copy-done.3, bf16[3520,128]{1,0:T(8,128)(2,1)} %copy-done.4, bf16[3520,128]{1,0:T(8,128)(2,1)} %copy-done.5, bf16[3520,128]{1,0:T(8,128)(2,1)} %collective-permute-done.1.rest_3_.refs_9_, ...), custom_call_target="tpu_custom_call" | custom-call | flops 1 | bytes 1 | tf_op jit(solution)/shard_map/unpack_first/pallas_call | solution.py:237
  63.1 16.7 %attend.1 = (bf16[2,512,768]{2,1,0:T(8,128)(2,1)}, bf16[2,512,768]{2,1,0:T(8,128)(2,1)}, bf16[2,512,768]{2,1,0:T(8,128)(2,1)}, bf16[2,6,256,1280]{3,2,1,0:T(8,128)(2,1)}, bf16[2,512,768]{2,1,0:T(8,128)(2,1)}) custom-call(bf16[2,512,768]{2,1,0:T(8,128)(2,1)} %refs_0_.1, s32[2,512,1]{2,1,0:T(8,128)} %copy.26.segc_ref.refs_2_, ...), custom_call_target="tpu_custom_call" | custom-call | flops 1 | bytes 1 | tf_op jit(solution)/shard_map/attend/pallas_call | solution.py:419
  83.7 55.7 %middle.1 = (bf16[2,512,768]{2,1,0:T(8,128)(2,1)}, bf16[2,512,768]{2,1,0:T(8,128)(2,1)}, bf16[2,512,3072]{2,1,0:T(8,128)(2,1)}, bf16[2,512,768]{2,1,0:T(8,128)(2...) custom-call(bf16[2,512,768]{2,1,0:T(8,128)(2,1)} %refs_0_.1, ...), custom_call_target="tpu_custom_call" | custom-call | flops 1 | bytes 1 | tf_op jit(solution)/shard_map/middle/pallas_call | solution.py:676
  139.4 24.7 %late_grads.1 = (bf16[3,7040,128]{2,1,0:T(8,128)(2,1)}, bf16[3,7040,128]{2,1,0:T(8,128)(2,1)}, f32[240,128]{1,0:T(8,128)}) custom-call(s32[1]{0:T(128)} %bitcast.1.me_ref, bf16[1024,768]{1,0:T(8,128)(2,1)} %bitcast.74, bf16[1024,768]{1,0:T(8,128)(2,1)} %bitcast.89, bf16[1024,768]{1,0:T(8,128)(2,1)} %bitcast.87, bf16[1024,3072]{1,0:T(8,128)(2,1)} %bitcast.73, ...), custom_call_target="tpu_custom_call" | custom-call | flops 1 | bytes 1 | tf_op jit(solution)/shard_map/late_grads/pallas_call | solution.py:998
  164.2 7.8 %retreat.2 = (bf16[2,512,768]{2,1,0:T(8,128)(2,1)}, bf16[2,512,768]{2,1,0:T(8,128)(2,1)}, bf16[2,512,768]{2,1,0:T(8,128)(2,1)}, f32[8,768]{1,0:T(8,128)}) custom-call(bf16[2,512,768]{2,1,0:T(8,128)(2,1)} %get-tuple-element.114.refs_0_, bf16[2,512,768]{2,1,0:T(8,128)(2,1)} %get-tuple-element.115.refs_1_, bf16[2,512,768]{2,1,0:T(8,128)(2,1)} %get-tuple-element.116.refs_2_, ...), custom_call_target="tpu_custom_call" | custom-call | flops 1 | bytes 1 | tf_op jit(solution)/shard_map/retreat/pallas_call | solution.py:761
  173.4 3.4 %combine_one.1 = (bf16[3520,128]{1,0:T(8,128)(2,1)}, bf16[3520,128]{1,0:T(8,128)(2,1)}) custom-call(s32[1]{0:T(128)} %bitcast.1.me_ref, bf16[3,7040,128]{2,1,0:T(8,128)(2,1)} %get-tuple-element.138.refs_0_.refs_2_, bf16[3,7040,128]{2,1,0:T(8,128)(2,1)} %collective-permute-done.14.refs_1_.refs_3_, bf16[3,7040,128]{2,1,0:T(8,128)(2,1)} %get-tuple-element.138.refs_0_.refs_2_, ...), custom_call_target="tpu_custom_call" | custom-call | flops 1 | bytes 1 | tf_op jit(solution)/shard_map/combine_one/pallas_call | solution.py:1071
  177.2 1.6 collective-permute-start.16
  178.8 7.9 %retreat.3 = (bf16[2,512,768]{2,1,0:T(8,128)(2,1)}, bf16[2,512,768]{2,1,0:T(8,128)(2,1)}, bf16[2,512,768]{2,1,0:T(8,128)(2,1)}, f32[8,768]{1,0:T(8,128)}) custom-call(bf16[2,512,768]{2,1,0:T(8,128)(2,1)} %get-tuple-element.114.refs_0_, bf16[2,512,768]{2,1,0:T(8,128)(2,1)} %get-tuple-element.115.refs_1_, ...), custom_call_target="tpu_custom_call", output_to_operand_aliasing={{0}: (5, {}), {1}: (6, {}), {2}: (7, {})} | custom-call | flops 1 | bytes 1 | tf_op jit(solution)/shard_map/retreat/pallas_call | solution.py:761
  186.7 8.8 %early_grads.1 = (bf16[1,7040,128]{2,1,0:T(8,128)(2,1)}, bf16[1,7040,128]{2,1,0:T(8,128)(2,1)}) custom-call(s32[1]{0:T(128)} %bitcast.1.me_ref, bf16[1024,768]{1,0:T(8,128)(2,1)} %bitcast.71, bf16[1024,768]{1,0:T(8,128)(2,1)} %bitcast.68, bf16[1024,768]{1,0:T(8,128)(2,1)} %bitcast.69, bf16[1024,768]{1,0:T(8,128)(2,1)} %bitcast.70, ...), custom_call_target="tpu_custom_call" | custom-call | flops 1 | bytes 1 | tf_op jit(solution)/shard_map/early_grads/pallas_call | solution.py:1020
  195.6 3.5 %collective-permute-done.15.refs_4_ = bf16[3520,128]{1,0:T(8,128)(2,1)S(1)} collective-permute-done((bf16[3520,128]{1,0:T(8,128)(2,1)}, bf16[3520,128]{1,0:T(8,128)(2,1)S(1)}, u32[]{:S(2)}, u32[]{:S(2)}) %collective-permute-start.15) | collective-permute-done | bytes 901152 | tf_op jit(solution)/shard_map/ppermute | solution.py:188
  200.2 3.9 %collective-permute-done.17.refs_3_ = bf16[1,7040,128]{2,1,0:T(8,128)(2,1)S(1)} collective-permute-done((bf16[1,7040,128]{2,1,0:T(8,128)(2,1)}, bf16[1,7040,128]{2,1,0:T(8,128)(2,1)S(1)}, u32[]{:S(2)}, u32[]{:S(2)}) %collective-permute-start.17) | collective-permute-done | bytes 1802272 | tf_op jit(solution)/shard_map/ppermute | solution.py:188
  205.4 3.4 %combine_two.1 = (bf16[1760,128]{1,0:T(8,128)(2,1)}, bf16[1760,128]{1,0:T(8,128)(2,1)}, bf16[1760,128]{1,0:T(8,128)(2,1)}, bf16[1760,128]{1,0:T(8,128)(2,1)}) custom-call(s32[1]{0:T(128)} %bitcast.1.me_ref, bf16[3,7040,128]{2,1,0:T(8,128)(2,1)} %get-tuple-element.138.refs_0_.refs_2_, bf16[3,7040,128]{2,1,0:T(8,128)(2,1)} %collective-permute-done.14.refs_1_.refs_3_, ...), custom_call_target="tpu_custom_call" | custom-call | flops 1 | bytes 1 | tf_op jit(solution)/shard_map/combine_two/pallas_call | solution.py:1071
  208.8 1.6 collective-permute-start.18
  210.4 1.5 collective-permute-start.19
  212.9 9.5 %project_back.1 = bf16[2,512,768]{2,1,0:T(8,128)(2,1)} custom-call(bf16[2,512,768]{2,1,0:T(8,128)(2,1)} %get-tuple-element.155.dq_ref, bf16[2,512,768]{2,1,0:T(8,128)(2,1)} %get-tuple-element.156.dk_ref, bf16[2,512,768]{2,1,0:T(8,128)(2,1)} %get-tuple-element.157.dv_ref, f32[2,512,768]{2,1,0:T(8,128)} %get-tuple-element.158.dh1_ref, ...), custom_call_target="tpu_custom_call" | custom-call | flops 1 | bytes 1 | tf_op jit(solution)/shard_map/project_back/pallas_call | solution.py:789
  222.3 1.5 collective-permute-done.19.refs_7_
  224.6 2.8 combine_three.2
  227.4 1.6 collective-permute-start.20
  229.8 2.8 combine_own.2
  234.3 2.8 combine_three.3
  237.1 1.6 collective-permute-start.26
  239.3 3.9 %collective-permute-done.20 = bf16[1760,128]{1,0:T(8,128)(2,1)S(1)} collective-permute-done((bf16[1760,128]{1,0:T(8,128)(2,1)}, bf16[1760,128]{1,0:T(8,128)(2,1)S(1)}, u32[]{:S(2)}, u32[]{:S(2)}) %collective-permute-start.20) | collective-permute-done | bytes 450592 | tf_op jit(solution)/shard_map/ppermute | solution.py:188
  243.3 1.7 collective-permute-start.21
  245.1 2.6 collective-permute-start.23
  247.8 2.8 combine_own.3
  254.0 2.0 collective-permute-done.23
  256.3 2.8 collective-permute-start.29
  259.5 1.8 collective-permute-start.39
  261.3 12.3 %collective-permute-done.36 = bf16[440,128]{1,0:T(8,128)(2,1)S(1)} collective-permute-done((bf16[440,128]{1,0:T(8,128)(2,1)S(1)}, bf16[440,128]{1,0:T(8,128)(2,1)S(1)}, u32[]{:S(2)}, u32[]{:S(2)}) %collective-permute-start.36) | collective-permute-done | bytes 112672 | tf_op jit(solution)/shard_map/ppermute | solution.py:1094
  273.7 3.2 %collective-permute-start.40 = (bf16[440,128]{1,0:T(8,128)(2,1)S(1)}, bf16[440,128]{1,0:T(8,128)(2,1)S(1)}, u32[]{:S(2)}, u32[]{:S(2)}) collective-permute-start(bf16[440,128]{1,0:T(8,128)(2,1)S(1)} %bitcast_add_fusion.4), channel_id=1, source_target_pairs={{0,8},{8,0},{16,24},{24,16},{1,9},{9,1},{17,25},{25,17},{2,10},{10... | collective-permute-start | bytes 337928 | tf_op jit(solution)/shard_map/ppermute | solution.py:1094
  277.2 1.8 collective-permute-start.33
  279.0 3.6 %collective-permute-done.37 = bf16[440,128]{1,0:T(8,128)(2,1)S(1)} collective-permute-done((bf16[440,128]{1,0:T(8,128)(2,1)S(1)}, bf16[440,128]{1,0:T(8,128)(2,1)S(1)}, u32[]{:S(2)}, u32[]{:S(2)}) %collective-permute-start.37) | collective-permute-done | bytes 112672 | tf_op jit(solution)/shard_map/ppermute | solution.py:1094
  282.8 1.6 collective-permute-done.40
  287.5 3.7 %collective-permute-done.33 = bf16[440,128]{1,0:T(8,128)(2,1)S(1)} collective-permute-done((bf16[440,128]{1,0:T(8,128)(2,1)S(1)}, bf16[440,128]{1,0:T(8,128)(2,1)S(1)}, u32[]{:S(2)}, u32[]{:S(2)}) %collective-permute-start.33) | collective-permute-done | bytes 112672 | tf_op jit(solution)/shard_map/ppermute | solution.py:1094
  291.3 8.4 %collective-permute-done.31 = bf16[440,128]{1,0:T(8,128)(2,1)S(1)} collective-permute-done((bf16[440,128]{1,0:T(8,128)(2,1)S(1)}, bf16[440,128]{1,0:T(8,128)(2,1)S(1)}, u32[]{:S(2)}, u32[]{:S(2)}) %collective-permute-start.31) | collective-permute-done | bytes 112672 | tf_op jit(solution)/shard_map/ppermute | solution.py:1094
  299.8 2.6 collective-permute-done.34
  302.6 3.3 %adam.2 = (f32[7036,128]{1,0:T(8,128)}, f32[7036,128]{1,0:T(8,128)}, f32[7036,128]{1,0:T(8,128)}) custom-call(s32[1]{0:T(128)} %bitcast.16.z_ref, bf16[880,128]{1,0:T(8,128)(2,1)S(1)} %maximum_select_fusion.2.one, bf16[880,128]{1,0:T(8,128)(2,1)S(1)} %collective-permute-done.38.one_other, bf16[880,128]{1,0:T(8,128)(2,1)S(1)} %maximum_select_fusion.3.two, ...), custom_call_target="tpu_custom_call" | custom-call | flops 1 | bytes 1 | tf_op jit(solution)/shard_map/adam/pallas_call | solution.py:1123
  306.1 5.4 %collective-permute-done.35.two_other = bf16[880,128]{1,0:T(8,128)(2,1)S(1)} collective-permute-done((bf16[880,128]{1,0:T(8,128)(2,1)S(1)}, bf16[880,128]{1,0:T(8,128)(2,1)S(1)}, u32[]{:S(2)}, u32[]{:S(2)}) %collective-permute-start.35) | collective-permute-done | bytes 225312 | tf_op jit(solution)/shard_map/ppermute | solution.py:1094
  311.5 3.4 %adam.3 = (f32[7036,128]{1,0:T(8,128)}, f32[7036,128]{1,0:T(8,128)}, f32[7036,128]{1,0:T(8,128)}) custom-call(s32[1]{0:T(128)} %bitcast.16.z_ref, bf16[880,128]{1,0:T(8,128)(2,1)S(1)} %maximum_select_fusion.one, bf16[880,128]{1,0:T(8,128)(2,1)S(1)} %collective-permute-done.32.one_other, ...), custom_call_target="tpu_custom_call", output_to_operand_aliasing={{0}: (7, {}), {1}: (8, {}), {2}: (9, {})} | custom-call | flops 1 | bytes 1 | tf_op jit(solution)/shard_map/adam/pallas_call | solution.py:1123
  (141 shorter events, 29.3 us)
Async XLA Ops:
  2.9 26.8 %copy-start.3 = (bf16[3520,128]{1,0:T(8,128)(2,1)}, bf16[3520,128]{1,0:T(8,128)(2,1)S(1)}, u32[]{:S(2)}) copy-start(bf16[3520,128]{1,0:T(8,128)(2,1)S(1)} %slice_bitcast_fusion.1.rest_0_.refs_6_) | copy-start | bytes 2703364
  3.0 47.4 %copy-start.4 = (bf16[3520,128]{1,0:T(8,128)(2,1)}, bf16[3520,128]{1,0:T(8,128)(2,1)S(1)}, u32[]{:S(2)}) copy-start(bf16[3520,128]{1,0:T(8,128)(2,1)S(1)} %pad.4.rest_1_.refs_7_) | copy-start | bytes 2703364
  3.1 23.0 %collective-permute-start = (bf16[3520,128]{1,0:T(8,128)(2,1)S(1)}, bf16[3520,128]{1,0:T(8,128)(2,1)S(1)}, u32[]{:S(2)}, u32[]{:S(2)}) collective-permute-start(bf16[3520,128]{1,0:T(8,128)(2,1)S(1)} %slice_bitcast_fusion.1.rest_0_.refs_6_), channel_id=1, source_target_pairs={{0,2},{1,3},{2,0},{3,1},{4,6},{5,7},{6,4},{7,5},{8,10},{9,11},{10,... | collective-permute-start | bytes 2703368 | tf_op jit(solution)/shard_map/ppermute | solution.py:188
  6.1 24.6 %collective-permute-start.4 = (bf16[3520,128]{1,0:T(8,128)(2,1)S(1)}, bf16[3520,128]{1,0:T(8,128)(2,1)}, u32[]{:S(2)}, u32[]{:S(2)}) collective-permute-start(bf16[3520,128]{1,0:T(8,128)(2,1)S(1)} %slice_bitcast_fusion.1.rest_0_.refs_6_), channel_id=1, source_target_pairs={{0,1},{1,0},{2,3},{3,2},{4,5},{5,4},{6,7},{7,6},{8,9},{9,8},{10,11... | collective-permute-start | bytes 2703368 | tf_op jit(solution)/shard_map/ppermute | solution.py:188
  6.1 22.7 %collective-permute-start.1 = (bf16[3520,128]{1,0:T(8,128)(2,1)S(1)}, bf16[3520,128]{1,0:T(8,128)(2,1)}, u32[]{:S(2)}, u32[]{:S(2)}) collective-permute-start(bf16[3520,128]{1,0:T(8,128)(2,1)S(1)} %pad.4.rest_1_.refs_7_), channel_id=1, source_target_pairs={{0,4},{1,5},{2,6},{3,7},{4,0},{5,1},{6,2},{7,3},{8,12},{9,13},{10,... | collective-permute-start | bytes 2703368 | tf_op jit(solution)/shard_map/ppermute | solution.py:188
  7.6 45.1 %collective-permute-start.5 = (bf16[3520,128]{1,0:T(8,128)(2,1)S(1)}, bf16[3520,128]{1,0:T(8,128)(2,1)}, u32[]{:S(2)}, u32[]{:S(2)}) collective-permute-start(bf16[3520,128]{1,0:T(8,128)(2,1)S(1)} %pad.4.rest_1_.refs_7_), channel_id=1, source_target_pairs={{0,1},{1,0},{2,3},{3,2},{4,5},{5,4},{6,7},{7,6},{8,9},{9,8},{10,11... | collective-permute-start | bytes 2703368 | tf_op jit(solution)/shard_map/ppermute | solution.py:188
  26.2 21.7 %collective-permute-start.2 = (bf16[3520,128]{1,0:T(8,128)(2,1)S(1)}, bf16[3520,128]{1,0:T(8,128)(2,1)}, u32[]{:S(2)}, u32[]{:S(2)}) collective-permute-start(bf16[3520,128]{1,0:T(8,128)(2,1)S(1)} %broadcast_select_fusion.3), channel_id=1, source_target_pairs={{0,4},{1,5},{2,6},{3,7},{4,0},{5,1},{6,2},{7,3},{8,12},{9,13},{10,... | collective-permute-start | bytes 2703368 | tf_op jit(solution)/shard_map/ppermute | solution.py:188
  28.9 21.6 %collective-permute-start.3 = (bf16[3520,128]{1,0:T(8,128)(2,1)S(1)}, bf16[3520,128]{1,0:T(8,128)(2,1)}, u32[]{:S(2)}, u32[]{:S(2)}) collective-permute-start(bf16[3520,128]{1,0:T(8,128)(2,1)S(1)} %broadcast_select_fusion.1), channel_id=1, source_target_pairs={{0,2},{1,3},{2,0},{3,1},{4,6},{5,7},{6,4},{7,5},{8,10},{9,11},{10,... | collective-permute-start | bytes 2703368 | tf_op jit(solution)/shard_map/ppermute | solution.py:188
  29.7 24.5 %collective-permute-start.6 = (bf16[3520,128]{1,0:T(8,128)(2,1)S(1)}, bf16[3520,128]{1,0:T(8,128)(2,1)S(1)}, u32[]{:S(2)}, u32[]{:S(2)}) collective-permute-start(bf16[3520,128]{1,0:T(8,128)(2,1)S(1)} %collective-permute-done.rest_2_.refs_8_), channel_id=1, source_target_pairs={{0,1},{1,0},{2,3},{3,2},{4,5},{5,4},{6,7},{7,6},{8,9},{9,8},{10,11... | collective-permute-start | bytes 2703368 | tf_op jit(solution)/shard_map/ppermute | solution.py:188
  30.7 25.0 %copy-start.19 = (s32[2,512]{1,0:T(2,128)S(1)}, s32[2,512]{1,0:T(2,128)}, u32[]{:S(2)}) copy-start(s32[2,512]{1,0:T(2,128)} %param.13) | copy-start | bytes 12292
  30.7 26.6 %collective-permute-start.7 = (bf16[3520,128]{1,0:T(8,128)(2,1)}, bf16[3520,128]{1,0:T(8,128)(2,1)S(1)}, u32[]{:S(2)}, u32[]{:S(2)}) collective-permute-start(bf16[3520,128]{1,0:T(8,128)(2,1)} %collective-permute-done.1.rest_3_.refs_9_), channel_id=1, source_target_pairs={{0,1},{1,0},{2,3},{3,2},{4,5},{5,4},{6,7},{7,6},{8,9},{9,8},{10,11... | collective-permute-start | bytes 2703368 | tf_op jit(solution)/shard_map/ppermute | solution.py:188
  47.9 9.4 %collective-permute-start.8 = (bf16[3520,128]{1,0:T(8,128)(2,1)}, bf16[3520,128]{1,0:T(8,128)(2,1)}, u32[]{:S(2)}, u32[]{:S(2)}) collective-permute-start(bf16[3520,128]{1,0:T(8,128)(2,1)} %collective-permute-done.2.rest_4_.refs_10_), channel_id=1, source_target_pairs={{0,1},{1,0},{2,3},{3,2},{4,5},{5,4},{6,7},{7,6},{8,9},{9,8},{10,11... | collective-permute-start | bytes 2703368 | tf_op jit(solution)/shard_map/ppermute | solution.py:188
  50.5 6.8 %collective-permute-start.9 = (bf16[3520,128]{1,0:T(8,128)(2,1)}, bf16[3520,128]{1,0:T(8,128)(2,1)}, u32[]{:S(2)}, u32[]{:S(2)}) collective-permute-start(bf16[3520,128]{1,0:T(8,128)(2,1)} %collective-permute-done.3.rest_5_.refs_11_), channel_id=1, source_target_pairs={{0,1},{1,0},{2,3},{3,2},{4,5},{5,4},{6,7},{7,6},{8,9},{9,8},{10,11... | collective-permute-start | bytes 2703368 | tf_op jit(solution)/shard_map/ppermute | solution.py:188
  52.7 27.1 %collective-permute-start.10 = (bf16[3520,128]{1,0:T(8,128)(2,1)}, bf16[3520,128]{1,0:T(8,128)(2,1)S(1)}, u32[]{:S(2)}, u32[]{:S(2)}) collective-permute-start(bf16[3520,128]{1,0:T(8,128)(2,1)} %broadcast_select_fusion.2), channel_id=1, source_target_pairs={{0,4},{1,5},{2,6},{3,7},{4,0},{5,1},{6,2},{7,3},{8,12},{9,13},{10,... | collective-permute-start | bytes 2703368 | tf_op jit(solution)/shard_map/ppermute | solution.py:188
  55.2 24.6 %collective-permute-start.11 = (bf16[3520,128]{1,0:T(8,128)(2,1)}, bf16[3520,128]{1,0:T(8,128)(2,1)S(1)}, u32[]{:S(2)}, u32[]{:S(2)}) collective-permute-start(bf16[3520,128]{1,0:T(8,128)(2,1)} %broadcast_select_fusion), channel_id=1, source_target_pairs={{0,2},{1,3},{2,0},{3,1},{4,6},{5,7},{6,4},{7,5},{8,10},{9,11},{10,... | collective-permute-start | bytes 2703368 | tf_op jit(solution)/shard_map/ppermute | solution.py:188
  63.0 17.5 %copy-start.22 = (s32[8]{0:T(128)S(1)}, s32[8]{0:T(128)}, u32[]{:S(2)}) copy-start(s32[8]{0:T(128)} %constant.65.clone) | copy-start | bytes 100
  79.8 3.0 collective-permute-start.12
  79.9 3.9 %collective-permute-start.13 = (bf16[3520,128]{1,0:T(8,128)(2,1)S(1)}, bf16[3520,128]{1,0:T(8,128)(2,1)}, u32[]{:S(2)}, u32[]{:S(2)}) collective-permute-start(bf16[3520,128]{1,0:T(8,128)(2,1)S(1)} %collective-permute-done.11.refs_13_), channel_id=1, source_target_pairs={{0,1},{1,0},{2,3},{3,2},{4,5},{5,4},{6,7},{7,6},{8,9},{9,8},{10,11... | collective-permute-start | bytes 2703368 | tf_op jit(solution)/shard_map/ppermute | solution.py:188
  164.1 9.3 %collective-permute-start.14 = (bf16[3,7040,128]{2,1,0:T(8,128)(2,1)}, bf16[3,7040,128]{2,1,0:T(8,128)(2,1)}, u32[]{:S(2)}, u32[]{:S(2)}) collective-permute-start(bf16[3,7040,128]{2,1,0:T(8,128)(2,1)} %get-tuple-element.129), channel_id=1, source_target_pairs={{0,1},{1,0},{2,3},{3,2},{4,5},{5,4},{6,7},{7,6},{8,9},{9,8},{10,11... | collective-permute-start | bytes 16220168 | tf_op jit(solution)/shard_map/ppermute | solution.py:188
  176.8 22.3 %collective-permute-start.15 = (bf16[3520,128]{1,0:T(8,128)(2,1)}, bf16[3520,128]{1,0:T(8,128)(2,1)S(1)}, u32[]{:S(2)}, u32[]{:S(2)}) collective-permute-start(bf16[3520,128]{1,0:T(8,128)(2,1)} %get-tuple-element.140), channel_id=1, source_target_pairs={{0,4},{1,5},{2,6},{3,7},{4,0},{5,1},{6,2},{7,3},{8,12},{9,13},{10,... | collective-permute-start | bytes 2703368 | tf_op jit(solution)/shard_map/ppermute | solution.py:188
  177.2 22.0 %collective-permute-start.16 = (bf16[3520,128]{1,0:T(8,128)(2,1)}, bf16[3520,128]{1,0:T(8,128)(2,1)S(1)}, u32[]{:S(2)}, u32[]{:S(2)}) collective-permute-start(bf16[3520,128]{1,0:T(8,128)(2,1)} %get-tuple-element.151), channel_id=1, source_target_pairs={{0,2},{1,3},{2,0},{3,1},{4,6},{5,7},{6,4},{7,5},{8,10},{9,11},{10,... | collective-permute-start | bytes 2703368 | tf_op jit(solution)/shard_map/ppermute | solution.py:188
  200.2 3.9 %collective-permute-start.17 = (bf16[1,7040,128]{2,1,0:T(8,128)(2,1)}, bf16[1,7040,128]{2,1,0:T(8,128)(2,1)S(1)}, u32[]{:S(2)}, u32[]{:S(2)}) collective-permute-start(bf16[1,7040,128]{2,1,0:T(8,128)(2,1)} %get-tuple-element.153), channel_id=1, source_target_pairs={{0,1},{1,0},{2,3},{3,2},{4,5},{5,4},{6,7},{7,6},{8,9},{9,8},{10,11... | collective-permute-start | bytes 5406728 | tf_op jit(solution)/shard_map/ppermute | solution.py:188
  208.8 13.6 %collective-permute-start.18 = (bf16[1760,128]{1,0:T(8,128)(2,1)}, bf16[1760,128]{1,0:T(8,128)(2,1)S(1)}, u32[]{:S(2)}, u32[]{:S(2)}) collective-permute-start(bf16[1760,128]{1,0:T(8,128)(2,1)} %get-tuple-element.154), channel_id=1, source_target_pairs={{0,4},{1,5},{2,6},{3,7},{4,0},{5,1},{6,2},{7,3},{8,12},{9,13},{10,... | collective-permute-start | bytes 1351688 | tf_op jit(solution)/shard_map/ppermute | solution.py:188
  210.4 13.4 %collective-permute-start.19 = (bf16[1760,128]{1,0:T(8,128)(2,1)}, bf16[1760,128]{1,0:T(8,128)(2,1)S(1)}, u32[]{:S(2)}, u32[]{:S(2)}) collective-permute-start(bf16[1760,128]{1,0:T(8,128)(2,1)} %get-tuple-element.161), channel_id=1, source_target_pairs={{0,2},{1,3},{2,0},{3,1},{4,6},{5,7},{6,4},{7,5},{8,10},{9,11},{10,... | collective-permute-start | bytes 1351688 | tf_op jit(solution)/shard_map/ppermute | solution.py:188
  211.9 20.7 %collective-permute-start.24 = (bf16[1760,128]{1,0:T(8,128)(2,1)}, bf16[1760,128]{1,0:T(8,128)(2,1)S(1)}, u32[]{:S(2)}, u32[]{:S(2)}) collective-permute-start(bf16[1760,128]{1,0:T(8,128)(2,1)} %get-tuple-element.172), channel_id=1, source_target_pairs={{0,4},{1,5},{2,6},{3,7},{4,0},{5,1},{6,2},{7,3},{8,12},{9,13},{10,... | collective-permute-start | bytes 1351688 | tf_op jit(solution)/shard_map/ppermute | solution.py:188
  212.5 21.0 %collective-permute-start.25 = (bf16[1760,128]{1,0:T(8,128)(2,1)}, bf16[1760,128]{1,0:T(8,128)(2,1)S(1)}, u32[]{:S(2)}, u32[]{:S(2)}) collective-permute-start(bf16[1760,128]{1,0:T(8,128)(2,1)} %get-tuple-element.173), channel_id=1, source_target_pairs={{0,2},{1,3},{2,0},{3,1},{4,6},{5,7},{6,4},{7,5},{8,10},{9,11},{10,... | collective-permute-start | bytes 1351688 | tf_op jit(solution)/shard_map/ppermute | solution.py:188
  227.4 15.7 %collective-permute-start.20 = (bf16[1760,128]{1,0:T(8,128)(2,1)}, bf16[1760,128]{1,0:T(8,128)(2,1)S(1)}, u32[]{:S(2)}, u32[]{:S(2)}) collective-permute-start(bf16[1760,128]{1,0:T(8,128)(2,1)} %get-tuple-element.164), channel_id=1, source_target_pairs={{0,2},{1,3},{2,0},{3,1},{4,6},{5,7},{6,4},{7,5},{8,10},{9,11},{10,... | collective-permute-start | bytes 1351688 | tf_op jit(solution)/shard_map/ppermute | solution.py:188
  229.0 16.0 %collective-permute-start.22 = (bf16[1760,128]{1,0:T(8,128)(2,1)}, bf16[1760,128]{1,0:T(8,128)(2,1)S(1)}, u32[]{:S(2)}, u32[]{:S(2)}) collective-permute-start(bf16[1760,128]{1,0:T(8,128)(2,1)} %get-tuple-element.171), channel_id=1, source_target_pairs={{0,4},{1,5},{2,6},{3,7},{4,0},{5,1},{6,2},{7,3},{8,12},{9,13},{10,... | collective-permute-start | bytes 1351688 | tf_op jit(solution)/shard_map/ppermute | solution.py:188
  237.1 14.6 %collective-permute-start.26 = (bf16[1760,128]{1,0:T(8,128)(2,1)}, bf16[1760,128]{1,0:T(8,128)(2,1)S(1)}, u32[]{:S(2)}, u32[]{:S(2)}) collective-permute-start(bf16[1760,128]{1,0:T(8,128)(2,1)} %get-tuple-element.181), channel_id=1, source_target_pairs={{0,2},{1,3},{2,0},{3,1},{4,6},{5,7},{6,4},{7,5},{8,10},{9,11},{10,... | collective-permute-start | bytes 1351688 | tf_op jit(solution)/shard_map/ppermute | solution.py:188
  238.7 14.1 %collective-permute-start.27 = (bf16[1760,128]{1,0:T(8,128)(2,1)}, bf16[1760,128]{1,0:T(8,128)(2,1)S(1)}, u32[]{:S(2)}, u32[]{:S(2)}) collective-permute-start(bf16[1760,128]{1,0:T(8,128)(2,1)} %get-tuple-element.183), channel_id=1, source_target_pairs={{0,4},{1,5},{2,6},{3,7},{4,0},{5,1},{6,2},{7,3},{8,12},{9,13},{10,... | collective-permute-start | bytes 1351688 | tf_op jit(solution)/shard_map/ppermute | solution.py:188
  243.3 10.7 %collective-permute-start.21 = (bf16[880,128]{1,0:T(8,128)(2,1)S(1)}, bf16[880,128]{1,0:T(8,128)(2,1)S(1)}, u32[]{:S(2)}, u32[]{:S(2)}) collective-permute-start(bf16[880,128]{1,0:T(8,128)(2,1)S(1)} %dynamic-slice_bitcast_fusion.3), channel_id=1, source_target_pairs={{0,8},{8,0},{16,24},{24,16},{1,9},{9,1},{17,25},{25,17},{2,10},{10... | collective-permute-start | bytes 675848 | tf_op jit(solution)/shard_map/ppermute | solution.py:1094
  245.1 10.8 %collective-permute-start.23 = (bf16[880,128]{1,0:T(8,128)(2,1)S(1)}, bf16[880,128]{1,0:T(8,128)(2,1)S(1)}, u32[]{:S(2)}, u32[]{:S(2)}) collective-permute-start(bf16[880,128]{1,0:T(8,128)(2,1)S(1)} %dynamic-slice_bitcast_fusion.2), channel_id=1, source_target_pairs={{0,16},{8,24},{16,0},{24,8},{1,17},{9,25},{17,1},{25,9},{2,18},{10... | collective-permute-start | bytes 675848 | tf_op jit(solution)/shard_map/ppermute | solution.py:1094
  256.0 21.0 %collective-permute-start.28 = (bf16[880,128]{1,0:T(8,128)(2,1)S(1)}, bf16[880,128]{1,0:T(8,128)(2,1)S(1)}, u32[]{:S(2)}, u32[]{:S(2)}) collective-permute-start(bf16[880,128]{1,0:T(8,128)(2,1)S(1)} %dynamic-slice_bitcast_fusion.1), channel_id=1, source_target_pairs={{0,8},{8,0},{16,24},{24,16},{1,9},{9,1},{17,25},{25,17},{2,10},{10... | collective-permute-start | bytes 675848 | tf_op jit(solution)/shard_map/ppermute | solution.py:1094
  256.3 46.3 %copy-start.1 = (f32[900608]{0:T(1024)S(1)}, f32[900608]{0:T(1024)}, u32[]{:S(2)}) copy-start(f32[900608]{0:T(1024)} %param.19) | copy-start | bytes 10807300
  256.3 20.7 %collective-permute-start.29 = (bf16[880,128]{1,0:T(8,128)(2,1)S(1)}, bf16[880,128]{1,0:T(8,128)(2,1)S(1)}, u32[]{:S(2)}, u32[]{:S(2)}) collective-permute-start(bf16[880,128]{1,0:T(8,128)(2,1)S(1)} %dynamic-slice_bitcast_fusion), channel_id=1, source_target_pairs={{0,16},{8,24},{16,0},{24,8},{1,17},{9,25},{17,1},{25,9},{2,18},{10... | collective-permute-start | bytes 675848 | tf_op jit(solution)/shard_map/ppermute | solution.py:1094
  259.2 14.4 %collective-permute-start.36 = (bf16[440,128]{1,0:T(8,128)(2,1)S(1)}, bf16[440,128]{1,0:T(8,128)(2,1)S(1)}, u32[]{:S(2)}, u32[]{:S(2)}) collective-permute-start(bf16[440,128]{1,0:T(8,128)(2,1)S(1)} %dynamic-slice_bitcast_fusion.5), channel_id=1, source_target_pairs={{0,16},{8,24},{16,0},{24,8},{1,17},{9,25},{17,1},{25,9},{2,18},{10... | collective-permute-start | bytes 337928 | tf_op jit(solution)/shard_map/ppermute | solution.py:1094
  259.5 14.2 %collective-permute-start.39 = (bf16[440,128]{1,0:T(8,128)(2,1)S(1)}, bf16[440,128]{1,0:T(8,128)(2,1)S(1)}, u32[]{:S(2)}, u32[]{:S(2)}) collective-permute-start(bf16[440,128]{1,0:T(8,128)(2,1)S(1)} %dynamic-slice_bitcast_fusion.4), channel_id=1, source_target_pairs={{0,8},{8,0},{16,24},{24,16},{1,9},{9,1},{17,25},{25,17},{2,10},{10... | collective-permute-start | bytes 337928 | tf_op jit(solution)/shard_map/ppermute | solution.py:1094
  273.6 9.0 %collective-permute-start.37 = (bf16[440,128]{1,0:T(8,128)(2,1)S(1)}, bf16[440,128]{1,0:T(8,128)(2,1)S(1)}, u32[]{:S(2)}, u32[]{:S(2)}) collective-permute-start(bf16[440,128]{1,0:T(8,128)(2,1)S(1)} %bitcast_add_fusion.5), channel_id=1, source_target_pairs={{0,16},{8,24},{16,0},{24,8},{1,17},{9,25},{17,1},{25,9},{2,18},{10... | collective-permute-start | bytes 337928 | tf_op jit(solution)/shard_map/ppermute | solution.py:1094
  273.7 10.6 %collective-permute-start.40 = (bf16[440,128]{1,0:T(8,128)(2,1)S(1)}, bf16[440,128]{1,0:T(8,128)(2,1)S(1)}, u32[]{:S(2)}, u32[]{:S(2)}) collective-permute-start(bf16[440,128]{1,0:T(8,128)(2,1)S(1)} %bitcast_add_fusion.4), channel_id=1, source_target_pairs={{0,8},{8,0},{16,24},{24,16},{1,9},{9,1},{17,25},{25,17},{2,10},{10... | collective-permute-start | bytes 337928 | tf_op jit(solution)/shard_map/ppermute | solution.py:1094
  277.0 25.6 %copy-start = (f32[900608]{0:T(1024)S(1)}, f32[900608]{0:T(1024)}, u32[]{:S(2)}) copy-start(f32[900608]{0:T(1024)} %param.18) | copy-start | bytes 10807300
  277.1 9.2 %collective-permute-start.30 = (bf16[440,128]{1,0:T(8,128)(2,1)S(1)}, bf16[440,128]{1,0:T(8,128)(2,1)S(1)}, u32[]{:S(2)}, u32[]{:S(2)}) collective-permute-start(bf16[440,128]{1,0:T(8,128)(2,1)S(1)} %dynamic-slice_bitcast_fusion.7), channel_id=1, source_target_pairs={{0,16},{8,24},{16,0},{24,8},{1,17},{9,25},{17,1},{25,9},{2,18},{10... | collective-permute-start | bytes 337928 | tf_op jit(solution)/shard_map/ppermute | solution.py:1094
  277.2 14.0 %collective-permute-start.33 = (bf16[440,128]{1,0:T(8,128)(2,1)S(1)}, bf16[440,128]{1,0:T(8,128)(2,1)S(1)}, u32[]{:S(2)}, u32[]{:S(2)}) collective-permute-start(bf16[440,128]{1,0:T(8,128)(2,1)S(1)} %dynamic-slice_bitcast_fusion.6), channel_id=1, source_target_pairs={{0,8},{8,0},{16,24},{24,16},{1,9},{9,1},{17,25},{25,17},{2,10},{10... | collective-permute-start | bytes 337928 | tf_op jit(solution)/shard_map/ppermute | solution.py:1094
  282.7 19.9 %collective-permute-start.38 = (bf16[880,128]{1,0:T(8,128)(2,1)S(1)}, bf16[880,128]{1,0:T(8,128)(2,1)S(1)}, u32[]{:S(2)}, u32[]{:S(2)}) collective-permute-start(bf16[880,128]{1,0:T(8,128)(2,1)S(1)} %maximum_select_fusion.2.one), channel_id=1, source_target_pairs={{0,8},{8,0},{16,24},{24,16},{1,9},{9,1},{17,25},{25,17},{2,10},{10... | collective-permute-start | bytes 675848 | tf_op jit(solution)/shard_map/ppermute | solution.py:1094
  284.4 18.2 %collective-permute-start.41 = (bf16[880,128]{1,0:T(8,128)(2,1)S(1)}, bf16[880,128]{1,0:T(8,128)(2,1)S(1)}, u32[]{:S(2)}, u32[]{:S(2)}) collective-permute-start(bf16[880,128]{1,0:T(8,128)(2,1)S(1)} %maximum_select_fusion.3.two), channel_id=1, source_target_pairs={{0,16},{8,24},{16,0},{24,8},{1,17},{9,25},{17,1},{25,9},{2,18},{10... | collective-permute-start | bytes 675848 | tf_op jit(solution)/shard_map/ppermute | solution.py:1094
  286.3 13.4 %collective-permute-start.31 = (bf16[440,128]{1,0:T(8,128)(2,1)S(1)}, bf16[440,128]{1,0:T(8,128)(2,1)S(1)}, u32[]{:S(2)}, u32[]{:S(2)}) collective-permute-start(bf16[440,128]{1,0:T(8,128)(2,1)S(1)} %bitcast_add_fusion.7), channel_id=1, source_target_pairs={{0,16},{8,24},{16,0},{24,8},{1,17},{9,25},{17,1},{25,9},{2,18},{10... | collective-permute-start | bytes 337928 | tf_op jit(solution)/shard_map/ppermute | solution.py:1094
  291.2 11.2 %collective-permute-start.34 = (bf16[440,128]{1,0:T(8,128)(2,1)S(1)}, bf16[440,128]{1,0:T(8,128)(2,1)S(1)}, u32[]{:S(2)}, u32[]{:S(2)}) collective-permute-start(bf16[440,128]{1,0:T(8,128)(2,1)S(1)} %bitcast_add_fusion.6), channel_id=1, source_target_pairs={{0,8},{8,0},{16,24},{24,16},{1,9},{9,1},{17,25},{25,17},{2,10},{10... | collective-permute-start | bytes 337928 | tf_op jit(solution)/shard_map/ppermute | solution.py:1094
  299.7 6.4 %collective-permute-start.32 = (bf16[880,128]{1,0:T(8,128)(2,1)S(1)}, bf16[880,128]{1,0:T(8,128)(2,1)S(1)}, u32[]{:S(2)}, u32[]{:S(2)}) collective-permute-start(bf16[880,128]{1,0:T(8,128)(2,1)S(1)} %maximum_select_fusion.one), channel_id=1, source_target_pairs={{0,8},{8,0},{16,24},{24,16},{1,9},{9,1},{17,25},{25,17},{2,10},{10... | collective-permute-start | bytes 675848 | tf_op jit(solution)/shard_map/ppermute | solution.py:1094
  302.5 9.0 %collective-permute-start.35 = (bf16[880,128]{1,0:T(8,128)(2,1)S(1)}, bf16[880,128]{1,0:T(8,128)(2,1)S(1)}, u32[]{:S(2)}, u32[]{:S(2)}) collective-permute-start(bf16[880,128]{1,0:T(8,128)(2,1)S(1)} %maximum_select_fusion.1.two), channel_id=1, source_target_pairs={{0,16},{8,24},{16,0},{24,8},{1,17},{9,25},{17,1},{25,9},{2,18},{10... | collective-permute-start | bytes 675848 | tf_op jit(solution)/shard_map/ppermute | solution.py:1094
  (20 other events, 134.2 us)

commit v7 on v6

--- a/solution.py
+++ b/solution.py
@@ -378,31 +378,34 @@
 
 
 def attend_kernel(x_ref, segc_ref, segr_ref, wq_ref, wk_ref, wv_ref, bq_ref, q_ref, k_ref, v_ref, p_ref, att_ref, bias):
-    step = pl.program_id(1)
+    step, row = pl.program_id(0), pl.program_id(1)
 
     @pl.when(step == 0)
     def _():
         for i, (lo, hi) in enumerate(WINDOWS):
-            here = jnp.where(segc_ref[0, i * QB : (i + 1) * QB, :] == segr_ref[0, :, lo:hi], 0.0, MASKED)
+            here = jnp.where(segc_ref[row, i * QB : (i + 1) * QB, :] == segr_ref[row, :, lo:hi], 0.0, MASKED)
             for h in range(2):
-                bias[h * QB : (h + 1) * QB, OFFSETS[i] : OFFSETS[i] + hi - lo] = here
+                bias[row, h * QB : (h + 1) * QB, OFFSETS[i] : OFFSETS[i] + hi - lo] = here
 
     for n, (w_ref, out_ref) in enumerate(((wq_ref, q_ref), (wk_ref, k_ref), (wv_ref, v_ref))):
         cols = at(step + n * (D // 256), 256)
-        out_ref[0] = ((dot(x_ref[0], w_ref[...]) + bq_ref[0:1, cols]) * bq_ref[1:2, cols]).astype(BF)
-
-    for p in range(2):
-        lanes = slice(p * LANE, (p + 1) * LANE)
-        soft = []
-        for i, (lo, hi) in enumerate(WINDOWS):
-            span = slice(OFFSETS[i], OFFSETS[i] + hi - lo)
-            s = dot(both_heads(q_ref[0, i * QB : (i + 1) * QB, lanes]), k_ref[0, lo:hi, lanes], NT) + bias[:, span]
-            e = jnp.exp(s - jnp.max(s, axis=-1, keepdims=True))
-            a = (e * (1.0 / jnp.sum(e, axis=-1, keepdims=True))).astype(BF)
-            p_ref[0, p, :, span] = a
-            soft.append(a)
-        for i, (lo, hi) in enumerate(WINDOWS):
-            att_ref[0, i * QB : (i + 1) * QB, lanes] = own_lanes(dot(soft[i], v_ref[0, lo:hi, lanes])).astype(BF)
+        out_ref[0] = ((dot(x_ref[row], w_ref[...]) + bq_ref[0:1, cols]) * bq_ref[1:2, cols]).astype(BF)
+
+    blocks = [
+        (p, slice(p * LANE, (p + 1) * LANE), i, lo, hi, slice(OFFSETS[i], OFFSETS[i] + hi - lo))
+        for p in range(2)
+        for i, (lo, hi) in enumerate(WINDOWS)
+    ]
+    scores = []
+    for p, lanes, i, lo, hi, span in blocks:
+        scores.append(dot(both_heads(q_ref[0, i * QB : (i + 1) * QB, lanes]), k_ref[0, lo:hi, lanes], NT) + bias[row, :, span])
+    raised = [jnp.exp(s - jnp.max(s, axis=-1, keepdims=True)) for s in scores]
+    totals = [jnp.sum(e, axis=-1, keepdims=True) for e in raised]
+    soft = [(e * (1.0 / total)).astype(BF) for e, total in zip(raised, totals)]
+    for a, (p, lanes, i, lo, hi, span) in zip(soft, blocks):
+        p_ref[0, p, :, span] = a
+    for a, (p, lanes, i, lo, hi, span) in zip(soft, blocks):
+        att_ref[0, i * QB : (i + 1) * QB, lanes] = own_lanes(dot(a, v_ref[0, lo:hi, lanes])).astype(BF)
 
 
 def row_spec(*shape):
@@ -411,18 +414,17 @@
 
 def attend(x, segc, segr, wqkv, bq):
     rows = x.shape[0]
-    only = lambda *shape: pl.BlockSpec((1, *shape), lambda r, g: (r,) + (0,) * len(shape))
-    tall = pl.BlockSpec((1, LEN, 256), lambda r, g: (r, 0, g))
-    weights = [pl.BlockSpec((D, 256), lambda r, g, n=n: (0, g + n * (D // 256))) for n in range(3)]
-    probs = pl.BlockSpec((1, 2, 2 * QB, WIDE), lambda r, g: (r, g, 0, 0))
+    tall = pl.BlockSpec((1, LEN, 256), lambda g, r: (r, 0, g))
+    weights = [pl.BlockSpec((D, 256), lambda g, r, n=n: (0, g + n * (D // 256))) for n in range(3)]
+    probs = pl.BlockSpec((1, 2, 2 * QB, WIDE), lambda g, r: (r, g, 0, 0))
     token = SDS((rows, LEN, D), BF)
     return pl.pallas_call(
         attend_kernel,
-        grid=(rows, D // 256),
-        in_specs=[only(LEN, D), only(LEN, 1), only(1, LEN)] + weights + [whole(8, 3 * D)],
+        grid=(D // 256, rows),
+        in_specs=[once(*v.shape) for v in (x, segc, segr)] + weights + [once(8, 3 * D)],
         out_specs=[tall, tall, tall, probs, tall],
         out_shape=[token, token, token, SDS((rows, PAIRS, 2 * QB, WIDE), BF), token],
-        scratch_shapes=[pltpu.VMEM((2 * QB, WIDE), F32)],
+        scratch_shapes=[pltpu.VMEM((rows, 2 * QB, WIDE), F32)],
         compiler_params=params_of(),
         cost_estimate=TINY,
         name="attend",
@@ -1169,36 +1171,37 @@
         back = retreat(0, q, k, v, probs, datt, ())
         late_got, back = lax.optimization_barrier((late_got, tuple(back)))
         parts = (late_keep, late_got, late_keep, late_got)
-        plan = [(lambda x, y: 3 - 2 * y, 0, half, None), (lambda x, y: 3 - x, half, half, None)]
-        along_y, along_x = combine(me, parts, (), plan, "combine_one")
-        y_one, x_one = swap(along_y, 4), swap(along_x, 2)
-        back, _ = lax.optimization_barrier((back, along_y))
+        plan = [(lambda x, y: 3 - 2 * y, 0, size, None), (lambda x, y: 3 - x, half, size, None)]
+        plan += [(which, first + size, size, None) for which, first, *_ in plan]
+        *pairs, = combine(me, parts, (), plan, "combine_one")
+        one = [(swap(pairs[2 * c], 4), swap(pairs[2 * c + 1], 2)) for c in range(2)]
+        back, _ = lax.optimization_barrier((back, pairs[0]))
         for row in range(1, rows):
             back = retreat(row, q, k, v, probs, datt, tuple(back))
         *dproj, bg = back
         early_keep, give = early_pairs(me, shard_rows, padded, flat2(inputs), *map(flat2, dproj), bg, edge)
-        y_one, x_one, give = lax.optimization_barrier((y_one, x_one, give))
+        one[0], give = lax.optimization_barrier((one[0], give))
         parts = (late_keep, late_got, early_keep, swap(give, 1))
         plan = [(lambda x, y: 2 - 2 * y, 0, size, None), (lambda x, y: 1 - x, half, size, None)]
         plan += [(which, first + size, size, None) for which, first, *_ in plan]
         *pairs, = combine(me, parts, (), plan, "combine_two")
         arrived = [(swap(pairs[2 * c], 4), swap(pairs[2 * c + 1], 2)) for c in range(2)]
-        dproj, _ = lax.optimization_barrier((dproj, pairs[0]))
+        dproj, _, one[1] = lax.optimization_barrier((dproj, pairs[0], one[1]))
         dx = project_back(*dproj, dh1, wqkv)
         sent, own, after = [], [], dx
         here = lambda x, y: y * 2 + x
         for c in range(2):
             arrived_c, _ = lax.optimization_barrier((arrived[c], after))
-            extras = (y_one, x_one, *arrived_c)
+            extras = (*one[c], *arrived_c)
             plan = [
-                (lambda x, y: y * 2 + 1 - x, c * size, size, (lambda x, y: x, (2, 0), (0, c * size))),
-                (lambda x, y: (1 - y) * 2 + x, half + c * size, size, (lambda x, y: y, (3, 0), (1, c * size))),
+                (lambda x, y: y * 2 + 1 - x, c * size, size, (lambda x, y: x, (2, 0), (0, 0))),
+                (lambda x, y: (1 - y) * 2 + x, half + c * size, size, (lambda x, y: y, (3, 0), (1, 0))),
             ]
             along_x, along_y = combine(me, parts, extras, plan, "combine_three")
             sent.append((swap(along_x, 2), swap(along_y, 4)))
             plan = [
-                (here, c * size, size, (lambda x, y: x, (0, c * size), (2, 0))),
-                (here, half + c * size, size, (lambda x, y: y, (1, c * size), (3, 0))),
+                (here, c * size, size, (lambda x, y: x, (0, 0), (2, 0))),
+                (here, half + c * size, size, (lambda x, y: y, (1, 0), (3, 0))),
             ]
             extras, _ = lax.optimization_barrier((extras, sent[0] if c else along_x))
             after = combine(me, parts, extras, plan, "combine_own")

time: 316 us -> 312 us (0.987)
  waiting for transfers between devices: 97.4 us -> 92.9 us
    ppermute x26 -> x28, waiting for transfers between devices: 56.5 us -> 52.7 us  [swap(): return lax.ppermute(v, 'fsdp', [(d, d ^ bit) for d in range(8)])]
    ppermute x26 -> x28, starting transfers between devices: 21.4 us -> 22.1 us  [swap(): return lax.ppermute(v, 'fsdp', [(d, d ^ bit) for d in range(8)])]
  transfers between devices with their start and end apart: 42 -> 44, of which waited for: 24 -> 21; matrix products, arithmetic and copies ran while one was open for 3% -> 3% of each run, Pallas kernels for 22% -> 23%
where the time goes in v7:
time: 312 us; the launch traced here: 311 us
  Pallas kernels  160 us (51%)
  waiting for transfers between devices  92.9 us (30%)
  starting transfers between devices  39.5 us (13%)
  other arithmetic  10.1 us (3%)
  local copies, waits for them, and re-layouts  7.59 us (2%)
    pallas_call x1, Pallas kernels, middle(): pl.pallas_call(kernel, grid=(rows,), in_specs=[row_spec(LEN, D), row_spec...  55.7 us
    ppermute x28, waiting for transfers between devices, swap(): return lax.ppermute(v, 'fsdp', [(d, d ^ bit) for d in range(8)])  52.7 us
    ppermute x16, waiting for transfers between devices, sum_replicas(): lax.ppermute(v, 'rep', [(i, i ^ bit) for i in range(4)])  40.2 us
    pallas_call x1, Pallas kernels, late_pairs(): pl.pallas_call(functools.partial(late_pair_kernel, shard_rows), in_specs=...  24.7 us
    ppermute x28, starting transfers between devices, swap(): return lax.ppermute(v, 'fsdp', [(d, d ^ bit) for d in range(8)])  22.1 us
    pallas_call x6, Pallas kernels, combine(): pl.pallas_call(functools.partial(combine_kernel, plan, len(extras)), in_s...  17.8 us
    ppermute x16, starting transfers between devices, sum_replicas(): lax.ppermute(v, 'rep', [(i, i ^ bit) for i in range(4)])  17.5 us
    pallas_call x1, Pallas kernels, attend(): pl.pallas_call(attend_kernel, grid=(D // 256, rows), in_specs=[once(*v.sh...  16 us
  transfers between devices with their start and end apart: 44, of which 21 were waited for; matrix products, arithmetic and copies ran while one was open for 3% of the time, Pallas kernels for 23%

profile of v7, /device:TPU:0, one launch (start us, length us, event | category | flops | bytes accessed | tf_op | source)
XLA Modules:
  0.0 311.1 jit_solution(7628734747030541732)
XLA Ops:
  0.6 2.2 convert.4
  3.1 3.0 collective-permute-start
  6.1 1.5 collective-permute-start.1
  7.8 18.2 %collective-permute-done.rest_2_.refs_8_ = bf16[3520,128]{1,0:T(8,128)(2,1)S(1)} collective-permute-done((bf16[3520,128]{1,0:T(8,128)(2,1)S(1)}, bf16[3520,128]{1,0:T(8,128)(2,1)S(1)}, u32[]{:S(2)}, u32[]{:S(2)}) %collective-permute-start) | collective-permute-done | bytes 901152 | tf_op jit(solution)/shard_map/ppermute | solution.py:188
  26.2 1.8 collective-permute-start.2
  31.2 16.7 %collective-permute-done.2.rest_4_.refs_10_ = bf16[3520,128]{1,0:T(8,128)(2,1)} collective-permute-done((bf16[3520,128]{1,0:T(8,128)(2,1)S(1)}, bf16[3520,128]{1,0:T(8,128)(2,1)}, u32[]{:S(2)}, u32[]{:S(2)}) %collective-permute-start.2) | collective-permute-done | bytes 901152 | tf_op jit(solution)/shard_map/ppermute | solution.py:188
  47.9 2.6 collective-permute-done.3.rest_5_.refs_11_
  50.5 2.2 broadcast_select_fusion
  52.7 1.5 collective-permute-start.10
  58.3 4.7 %unpack_first.1 = (bf16[768,2304]{1,0:T(8,128)(2,1)}, f32[8,2304]{1,0:T(8,128)}) custom-call(s32[1]{0:T(128)} %bitcast.1.me_ref, bf16[3520,128]{1,0:T(8,128)(2,1)} %copy-done.3, bf16[3520,128]{1,0:T(8,128)(2,1)} %copy-done.4, bf16[3520,128]{1,0:T(8,128)(2,1)} %copy-done.5, bf16[3520,128]{1,0:T(8,128)(2,1)} %collective-permute-done.1.rest_3_.refs_9_, ...), custom_call_target="tpu_custom_call" | custom-call | flops 1 | bytes 1 | tf_op jit(solution)/shard_map/unpack_first/pallas_call | solution.py:237
  63.1 16.0 %attend.1 = (bf16[2,512,768]{2,1,0:T(8,128)(2,1)}, bf16[2,512,768]{2,1,0:T(8,128)(2,1)}, bf16[2,512,768]{2,1,0:T(8,128)(2,1)}, bf16[2,6,256,1280]{3,2,1,0:T(8,128)(2,1)}, bf16[2,512,768]{2,1,0:T(8,128)(2,1)}) custom-call(bf16[2,512,768]{2,1,0:T(8,128)(2,1)} %refs_0_.1, s32[2,512,1]{2,1,0:T(8,128)} %copy.26.segc_ref.refs_2_, ...), custom_call_target="tpu_custom_call" | custom-call | flops 1 | bytes 1 | tf_op jit(solution)/shard_map/attend/pallas_call | solution.py:421
  83.1 55.7 %middle.1 = (bf16[2,512,768]{2,1,0:T(8,128)(2,1)}, bf16[2,512,768]{2,1,0:T(8,128)(2,1)}, bf16[2,512,3072]{2,1,0:T(8,128)(2,1)}, bf16[2,512,768]{2,1,0:T(8,128)(2...) custom-call(bf16[2,512,768]{2,1,0:T(8,128)(2,1)} %refs_0_.1, ...), custom_call_target="tpu_custom_call" | custom-call | flops 1 | bytes 1 | tf_op jit(solution)/shard_map/middle/pallas_call | solution.py:678
  138.7 24.7 %late_grads.1 = (bf16[3,7040,128]{2,1,0:T(8,128)(2,1)}, bf16[3,7040,128]{2,1,0:T(8,128)(2,1)}, f32[240,128]{1,0:T(8,128)}) custom-call(s32[1]{0:T(128)} %bitcast.1.me_ref, bf16[1024,768]{1,0:T(8,128)(2,1)} %bitcast.74, bf16[1024,768]{1,0:T(8,128)(2,1)} %bitcast.89, bf16[1024,768]{1,0:T(8,128)(2,1)} %bitcast.87, bf16[1024,3072]{1,0:T(8,128)(2,1)} %bitcast.73, ...), custom_call_target="tpu_custom_call" | custom-call | flops 1 | bytes 1 | tf_op jit(solution)/shard_map/late_grads/pallas_call | solution.py:1000
  163.6 7.9 %retreat.2 = (bf16[2,512,768]{2,1,0:T(8,128)(2,1)}, bf16[2,512,768]{2,1,0:T(8,128)(2,1)}, bf16[2,512,768]{2,1,0:T(8,128)(2,1)}, f32[8,768]{1,0:T(8,128)}) custom-call(bf16[2,512,768]{2,1,0:T(8,128)(2,1)} %get-tuple-element.118.refs_0_, bf16[2,512,768]{2,1,0:T(8,128)(2,1)} %get-tuple-element.119.refs_1_, bf16[2,512,768]{2,1,0:T(8,128)(2,1)} %get-tuple-element.120.refs_2_, ...), custom_call_target="tpu_custom_call" | custom-call | flops 1 | bytes 1 | tf_op jit(solution)/shard_map/retreat/pallas_call | solution.py:763
  172.7 3.3 %combine_one.1 = (bf16[1760,128]{1,0:T(8,128)(2,1)}, bf16[1760,128]{1,0:T(8,128)(2,1)}, bf16[1760,128]{1,0:T(8,128)(2,1)}, bf16[1760,128]{1,0:T(8,128)(2,1)}) custom-call(s32[1]{0:T(128)} %bitcast.1.me_ref, bf16[3,7040,128]{2,1,0:T(8,128)(2,1)} %get-tuple-element.142.refs_0_.refs_2_, bf16[3,7040,128]{2,1,0:T(8,128)(2,1)} %collective-permute-done.14.refs_1_.refs_3_, ...), custom_call_target="tpu_custom_call" | custom-call | flops 1 | bytes 1 | tf_op jit(solution)/shard_map/combine_one/pallas_call | solution.py:1073
  176.5 1.6 collective-permute-start.16
  178.2 8.0 %retreat.3 = (bf16[2,512,768]{2,1,0:T(8,128)(2,1)}, bf16[2,512,768]{2,1,0:T(8,128)(2,1)}, bf16[2,512,768]{2,1,0:T(8,128)(2,1)}, f32[8,768]{1,0:T(8,128)}) custom-call(bf16[2,512,768]{2,1,0:T(8,128)(2,1)} %get-tuple-element.118.refs_0_, bf16[2,512,768]{2,1,0:T(8,128)(2,1)} %get-tuple-element.119.refs_1_, ...), custom_call_target="tpu_custom_call", output_to_operand_aliasing={{0}: (5, {}), {1}: (6, {}), {2}: (7, {})} | custom-call | flops 1 | bytes 1 | tf_op jit(solution)/shard_map/retreat/pallas_call | solution.py:763
  186.1 8.8 %early_grads.1 = (bf16[1,7040,128]{2,1,0:T(8,128)(2,1)}, bf16[1,7040,128]{2,1,0:T(8,128)(2,1)}) custom-call(s32[1]{0:T(128)} %bitcast.1.me_ref, bf16[1024,768]{1,0:T(8,128)(2,1)} %bitcast.71, bf16[1024,768]{1,0:T(8,128)(2,1)} %bitcast.68, bf16[1024,768]{1,0:T(8,128)(2,1)} %bitcast.69, bf16[1024,768]{1,0:T(8,128)(2,1)} %bitcast.70, ...), custom_call_target="tpu_custom_call" | custom-call | flops 1 | bytes 1 | tf_op jit(solution)/shard_map/early_grads/pallas_call | solution.py:1022
  195.1 1.6 collective-permute-start.18
  197.2 1.8 collective-permute-done.17.refs_3_
  200.3 3.3 %combine_two.1 = (bf16[1760,128]{1,0:T(8,128)(2,1)}, bf16[1760,128]{1,0:T(8,128)(2,1)}, bf16[1760,128]{1,0:T(8,128)(2,1)}, bf16[1760,128]{1,0:T(8,128)(2,1)}) custom-call(s32[1]{0:T(128)} %bitcast.1.me_ref, bf16[3,7040,128]{2,1,0:T(8,128)(2,1)} %get-tuple-element.142.refs_0_.refs_2_, bf16[3,7040,128]{2,1,0:T(8,128)(2,1)} %collective-permute-done.14.refs_1_.refs_3_, ...), custom_call_target="tpu_custom_call" | custom-call | flops 1 | bytes 1 | tf_op jit(solution)/shard_map/combine_two/pallas_call | solution.py:1073
  203.6 1.6 collective-permute-start.20
  205.7 2.8 collective-permute-done.18.refs_4_
  208.5 1.6 collective-permute-done.19.refs_5_
  211.0 9.5 %project_back.1 = bf16[2,512,768]{2,1,0:T(8,128)(2,1)} custom-call(bf16[2,512,768]{2,1,0:T(8,128)(2,1)} %get-tuple-element.161.dq_ref, bf16[2,512,768]{2,1,0:T(8,128)(2,1)} %get-tuple-element.162.dk_ref, bf16[2,512,768]{2,1,0:T(8,128)(2,1)} %get-tuple-element.163.dv_ref, f32[2,512,768]{2,1,0:T(8,128)} %get-tuple-element.164.dh1_ref, ...), custom_call_target="tpu_custom_call" | custom-call | flops 1 | bytes 1 | tf_op jit(solution)/shard_map/project_back/pallas_call | solution.py:791
  222.0 2.8 combine_three.2
  224.8 1.7 collective-permute-start.22
  228.0 2.8 combine_own.2
  231.7 2.8 combine_three.3
  235.5 3.5 %collective-permute-done.22 = bf16[1760,128]{1,0:T(8,128)(2,1)S(1)} collective-permute-done((bf16[1760,128]{1,0:T(8,128)(2,1)}, bf16[1760,128]{1,0:T(8,128)(2,1)S(1)}, u32[]{:S(2)}, u32[]{:S(2)}) %collective-permute-start.22) | collective-permute-done | bytes 450592 | tf_op jit(solution)/shard_map/ppermute | solution.py:188
  239.2 1.6 collective-permute-start.23
  241.0 2.6 collective-permute-start.25
  243.6 2.8 combine_own.3
  250.2 2.4 collective-permute-done.25
  252.8 3.0 collective-permute-start.31
  255.9 2.0 collective-permute-start.41
  257.9 12.0 %collective-permute-done.38 = bf16[440,128]{1,0:T(8,128)(2,1)S(1)} collective-permute-done((bf16[440,128]{1,0:T(8,128)(2,1)S(1)}, bf16[440,128]{1,0:T(8,128)(2,1)S(1)}, u32[]{:S(2)}, u32[]{:S(2)}) %collective-permute-start.38) | collective-permute-done | bytes 112672 | tf_op jit(solution)/shard_map/ppermute | solution.py:1096
  270.1 3.4 %collective-permute-start.42 = (bf16[440,128]{1,0:T(8,128)(2,1)S(1)}, bf16[440,128]{1,0:T(8,128)(2,1)S(1)}, u32[]{:S(2)}, u32[]{:S(2)}) collective-permute-start(bf16[440,128]{1,0:T(8,128)(2,1)S(1)} %bitcast_add_fusion.4), channel_id=1, source_target_pairs={{0,8},{8,0},{16,24},{24,16},{1,9},{9,1},{17,25},{25,17},{2,10},{10... | collective-permute-start | bytes 337928 | tf_op jit(solution)/shard_map/ppermute | solution.py:1096
  273.7 1.6 collective-permute-start.35
  275.3 3.4 %collective-permute-done.39 = bf16[440,128]{1,0:T(8,128)(2,1)S(1)} collective-permute-done((bf16[440,128]{1,0:T(8,128)(2,1)S(1)}, bf16[440,128]{1,0:T(8,128)(2,1)S(1)}, u32[]{:S(2)}, u32[]{:S(2)}) %collective-permute-start.39) | collective-permute-done | bytes 112672 | tf_op jit(solution)/shard_map/ppermute | solution.py:1096
  278.9 2.8 collective-permute-done.42
  282.4 2.4 collective-permute-start.33
  284.8 2.9 collective-permute-done.35
  287.8 8.5 %collective-permute-done.33 = bf16[440,128]{1,0:T(8,128)(2,1)S(1)} collective-permute-done((bf16[440,128]{1,0:T(8,128)(2,1)S(1)}, bf16[440,128]{1,0:T(8,128)(2,1)S(1)}, u32[]{:S(2)}, u32[]{:S(2)}) %collective-permute-start.33) | collective-permute-done | bytes 112672 | tf_op jit(solution)/shard_map/ppermute | solution.py:1096
  296.4 2.5 collective-permute-done.36
  299.1 3.3 %adam.2 = (f32[7036,128]{1,0:T(8,128)}, f32[7036,128]{1,0:T(8,128)}, f32[7036,128]{1,0:T(8,128)}) custom-call(s32[1]{0:T(128)} %bitcast.16.z_ref, bf16[880,128]{1,0:T(8,128)(2,1)S(1)} %maximum_select_fusion.2.one, bf16[880,128]{1,0:T(8,128)(2,1)S(1)} %collective-permute-done.40.one_other, bf16[880,128]{1,0:T(8,128)(2,1)S(1)} %maximum_select_fusion.3.two, ...), custom_call_target="tpu_custom_call" | custom-call | flops 1 | bytes 1 | tf_op jit(solution)/shard_map/adam/pallas_call | solution.py:1125
  302.4 5.3 %collective-permute-done.37.two_other = bf16[880,128]{1,0:T(8,128)(2,1)S(1)} collective-permute-done((bf16[880,128]{1,0:T(8,128)(2,1)S(1)}, bf16[880,128]{1,0:T(8,128)(2,1)S(1)}, u32[]{:S(2)}, u32[]{:S(2)}) %collective-permute-start.37) | collective-permute-done | bytes 225312 | tf_op jit(solution)/shard_map/ppermute | solution.py:1096
  307.7 3.4 %adam.3 = (f32[7036,128]{1,0:T(8,128)}, f32[7036,128]{1,0:T(8,128)}, f32[7036,128]{1,0:T(8,128)}) custom-call(s32[1]{0:T(128)} %bitcast.16.z_ref, bf16[880,128]{1,0:T(8,128)(2,1)S(1)} %maximum_select_fusion.one, bf16[880,128]{1,0:T(8,128)(2,1)S(1)} %collective-permute-done.34.one_other, ...), custom_call_target="tpu_custom_call", output_to_operand_aliasing={{0}: (7, {}), {1}: (8, {}), {2}: (9, {})} | custom-call | flops 1 | bytes 1 | tf_op jit(solution)/shard_map/adam/pallas_call | solution.py:1125
  (149 shorter events, 27.7 us)
Async XLA Ops:
  2.9 26.8 %copy-start.3 = (bf16[3520,128]{1,0:T(8,128)(2,1)}, bf16[3520,128]{1,0:T(8,128)(2,1)S(1)}, u32[]{:S(2)}) copy-start(bf16[3520,128]{1,0:T(8,128)(2,1)S(1)} %slice_bitcast_fusion.1.rest_0_.refs_6_) | copy-start | bytes 2703364
  3.0 47.4 %copy-start.4 = (bf16[3520,128]{1,0:T(8,128)(2,1)}, bf16[3520,128]{1,0:T(8,128)(2,1)S(1)}, u32[]{:S(2)}) copy-start(bf16[3520,128]{1,0:T(8,128)(2,1)S(1)} %pad.4.rest_1_.refs_7_) | copy-start | bytes 2703364
  3.1 23.0 %collective-permute-start = (bf16[3520,128]{1,0:T(8,128)(2,1)S(1)}, bf16[3520,128]{1,0:T(8,128)(2,1)S(1)}, u32[]{:S(2)}, u32[]{:S(2)}) collective-permute-start(bf16[3520,128]{1,0:T(8,128)(2,1)S(1)} %slice_bitcast_fusion.1.rest_0_.refs_6_), channel_id=1, source_target_pairs={{0,2},{1,3},{2,0},{3,1},{4,6},{5,7},{6,4},{7,5},{8,10},{9,11},{10,... | collective-permute-start | bytes 2703368 | tf_op jit(solution)/shard_map/ppermute | solution.py:188
  6.1 24.6 %collective-permute-start.4 = (bf16[3520,128]{1,0:T(8,128)(2,1)S(1)}, bf16[3520,128]{1,0:T(8,128)(2,1)}, u32[]{:S(2)}, u32[]{:S(2)}) collective-permute-start(bf16[3520,128]{1,0:T(8,128)(2,1)S(1)} %slice_bitcast_fusion.1.rest_0_.refs_6_), channel_id=1, source_target_pairs={{0,1},{1,0},{2,3},{3,2},{4,5},{5,4},{6,7},{7,6},{8,9},{9,8},{10,11... | collective-permute-start | bytes 2703368 | tf_op jit(solution)/shard_map/ppermute | solution.py:188
  6.1 22.7 %collective-permute-start.1 = (bf16[3520,128]{1,0:T(8,128)(2,1)S(1)}, bf16[3520,128]{1,0:T(8,128)(2,1)}, u32[]{:S(2)}, u32[]{:S(2)}) collective-permute-start(bf16[3520,128]{1,0:T(8,128)(2,1)S(1)} %pad.4.rest_1_.refs_7_), channel_id=1, source_target_pairs={{0,4},{1,5},{2,6},{3,7},{4,0},{5,1},{6,2},{7,3},{8,12},{9,13},{10,... | collective-permute-start | bytes 2703368 | tf_op jit(solution)/shard_map/ppermute | solution.py:188
  7.6 45.1 %collective-permute-start.5 = (bf16[3520,128]{1,0:T(8,128)(2,1)S(1)}, bf16[3520,128]{1,0:T(8,128)(2,1)}, u32[]{:S(2)}, u32[]{:S(2)}) collective-permute-start(bf16[3520,128]{1,0:T(8,128)(2,1)S(1)} %pad.4.rest_1_.refs_7_), channel_id=1, source_target_pairs={{0,1},{1,0},{2,3},{3,2},{4,5},{5,4},{6,7},{7,6},{8,9},{9,8},{10,11... | collective-permute-start | bytes 2703368 | tf_op jit(solution)/shard_map/ppermute | solution.py:188
  26.2 21.7 %collective-permute-start.2 = (bf16[3520,128]{1,0:T(8,128)(2,1)S(1)}, bf16[3520,128]{1,0:T(8,128)(2,1)}, u32[]{:S(2)}, u32[]{:S(2)}) collective-permute-start(bf16[3520,128]{1,0:T(8,128)(2,1)S(1)} %broadcast_select_fusion.3), channel_id=1, source_target_pairs={{0,4},{1,5},{2,6},{3,7},{4,0},{5,1},{6,2},{7,3},{8,12},{9,13},{10,... | collective-permute-start | bytes 2703368 | tf_op jit(solution)/shard_map/ppermute | solution.py:188
  28.9 21.6 %collective-permute-start.3 = (bf16[3520,128]{1,0:T(8,128)(2,1)S(1)}, bf16[3520,128]{1,0:T(8,128)(2,1)}, u32[]{:S(2)}, u32[]{:S(2)}) collective-permute-start(bf16[3520,128]{1,0:T(8,128)(2,1)S(1)} %broadcast_select_fusion.1), channel_id=1, source_target_pairs={{0,2},{1,3},{2,0},{3,1},{4,6},{5,7},{6,4},{7,5},{8,10},{9,11},{10,... | collective-permute-start | bytes 2703368 | tf_op jit(solution)/shard_map/ppermute | solution.py:188
  29.7 24.5 %collective-permute-start.6 = (bf16[3520,128]{1,0:T(8,128)(2,1)S(1)}, bf16[3520,128]{1,0:T(8,128)(2,1)S(1)}, u32[]{:S(2)}, u32[]{:S(2)}) collective-permute-start(bf16[3520,128]{1,0:T(8,128)(2,1)S(1)} %collective-permute-done.rest_2_.refs_8_), channel_id=1, source_target_pairs={{0,1},{1,0},{2,3},{3,2},{4,5},{5,4},{6,7},{7,6},{8,9},{9,8},{10,11... | collective-permute-start | bytes 2703368 | tf_op jit(solution)/shard_map/ppermute | solution.py:188
  30.7 26.6 %collective-permute-start.7 = (bf16[3520,128]{1,0:T(8,128)(2,1)}, bf16[3520,128]{1,0:T(8,128)(2,1)S(1)}, u32[]{:S(2)}, u32[]{:S(2)}) collective-permute-start(bf16[3520,128]{1,0:T(8,128)(2,1)} %collective-permute-done.1.rest_3_.refs_9_), channel_id=1, source_target_pairs={{0,1},{1,0},{2,3},{3,2},{4,5},{5,4},{6,7},{7,6},{8,9},{9,8},{10,11... | collective-permute-start | bytes 2703368 | tf_op jit(solution)/shard_map/ppermute | solution.py:188
  47.9 9.4 %collective-permute-start.8 = (bf16[3520,128]{1,0:T(8,128)(2,1)}, bf16[3520,128]{1,0:T(8,128)(2,1)}, u32[]{:S(2)}, u32[]{:S(2)}) collective-permute-start(bf16[3520,128]{1,0:T(8,128)(2,1)} %collective-permute-done.2.rest_4_.refs_10_), channel_id=1, source_target_pairs={{0,1},{1,0},{2,3},{3,2},{4,5},{5,4},{6,7},{7,6},{8,9},{9,8},{10,11... | collective-permute-start | bytes 2703368 | tf_op jit(solution)/shard_map/ppermute | solution.py:188
  50.5 6.8 %collective-permute-start.9 = (bf16[3520,128]{1,0:T(8,128)(2,1)}, bf16[3520,128]{1,0:T(8,128)(2,1)}, u32[]{:S(2)}, u32[]{:S(2)}) collective-permute-start(bf16[3520,128]{1,0:T(8,128)(2,1)} %collective-permute-done.3.rest_5_.refs_11_), channel_id=1, source_target_pairs={{0,1},{1,0},{2,3},{3,2},{4,5},{5,4},{6,7},{7,6},{8,9},{9,8},{10,11... | collective-permute-start | bytes 2703368 | tf_op jit(solution)/shard_map/ppermute | solution.py:188
  52.7 26.4 %collective-permute-start.10 = (bf16[3520,128]{1,0:T(8,128)(2,1)}, bf16[3520,128]{1,0:T(8,128)(2,1)S(1)}, u32[]{:S(2)}, u32[]{:S(2)}) collective-permute-start(bf16[3520,128]{1,0:T(8,128)(2,1)} %broadcast_select_fusion.2), channel_id=1, source_target_pairs={{0,4},{1,5},{2,6},{3,7},{4,0},{5,1},{6,2},{7,3},{8,12},{9,13},{10,... | collective-permute-start | bytes 2703368 | tf_op jit(solution)/shard_map/ppermute | solution.py:188
  55.2 23.9 %collective-permute-start.11 = (bf16[3520,128]{1,0:T(8,128)(2,1)}, bf16[3520,128]{1,0:T(8,128)(2,1)S(1)}, u32[]{:S(2)}, u32[]{:S(2)}) collective-permute-start(bf16[3520,128]{1,0:T(8,128)(2,1)} %broadcast_select_fusion), channel_id=1, source_target_pairs={{0,2},{1,3},{2,0},{3,1},{4,6},{5,7},{6,4},{7,5},{8,10},{9,11},{10,... | collective-permute-start | bytes 2703368 | tf_op jit(solution)/shard_map/ppermute | solution.py:188
  79.1 3.0 collective-permute-start.12
  79.2 3.9 %collective-permute-start.13 = (bf16[3520,128]{1,0:T(8,128)(2,1)S(1)}, bf16[3520,128]{1,0:T(8,128)(2,1)}, u32[]{:S(2)}, u32[]{:S(2)}) collective-permute-start(bf16[3520,128]{1,0:T(8,128)(2,1)S(1)} %collective-permute-done.11.refs_13_), channel_id=1, source_target_pairs={{0,1},{1,0},{2,3},{3,2},{4,5},{5,4},{6,7},{7,6},{8,9},{9,8},{10,11... | collective-permute-start | bytes 2703368 | tf_op jit(solution)/shard_map/ppermute | solution.py:188
  163.4 9.3 %collective-permute-start.14 = (bf16[3,7040,128]{2,1,0:T(8,128)(2,1)}, bf16[3,7040,128]{2,1,0:T(8,128)(2,1)}, u32[]{:S(2)}, u32[]{:S(2)}) collective-permute-start(bf16[3,7040,128]{2,1,0:T(8,128)(2,1)} %get-tuple-element.133), channel_id=1, source_target_pairs={{0,1},{1,0},{2,3},{3,2},{4,5},{5,4},{6,7},{7,6},{8,9},{9,8},{10,11... | collective-permute-start | bytes 16220168 | tf_op jit(solution)/shard_map/ppermute | solution.py:188
  176.1 18.9 %collective-permute-start.15 = (bf16[1760,128]{1,0:T(8,128)(2,1)}, bf16[1760,128]{1,0:T(8,128)(2,1)S(1)}, u32[]{:S(2)}, u32[]{:S(2)}) collective-permute-start(bf16[1760,128]{1,0:T(8,128)(2,1)} %get-tuple-element.144), channel_id=1, source_target_pairs={{0,4},{1,5},{2,6},{3,7},{4,0},{5,1},{6,2},{7,3},{8,12},{9,13},{10,... | collective-permute-start | bytes 1351688 | tf_op jit(solution)/shard_map/ppermute | solution.py:188
  176.5 18.5 %collective-permute-start.16 = (bf16[1760,128]{1,0:T(8,128)(2,1)}, bf16[1760,128]{1,0:T(8,128)(2,1)S(1)}, u32[]{:S(2)}, u32[]{:S(2)}) collective-permute-start(bf16[1760,128]{1,0:T(8,128)(2,1)} %get-tuple-element.155), channel_id=1, source_target_pairs={{0,2},{1,3},{2,0},{3,1},{4,6},{5,7},{6,4},{7,5},{8,10},{9,11},{10,... | collective-permute-start | bytes 1351688 | tf_op jit(solution)/shard_map/ppermute | solution.py:188
  195.0 4.0 %collective-permute-start.17 = (bf16[1,7040,128]{2,1,0:T(8,128)(2,1)}, bf16[1,7040,128]{2,1,0:T(8,128)(2,1)S(1)}, u32[]{:S(2)}, u32[]{:S(2)}) collective-permute-start(bf16[1,7040,128]{2,1,0:T(8,128)(2,1)} %get-tuple-element.157), channel_id=1, source_target_pairs={{0,1},{1,0},{2,3},{3,2},{4,5},{5,4},{6,7},{7,6},{8,9},{9,8},{10,11... | collective-permute-start | bytes 5406728 | tf_op jit(solution)/shard_map/ppermute | solution.py:188
  195.1 13.4 %collective-permute-start.18 = (bf16[1760,128]{1,0:T(8,128)(2,1)}, bf16[1760,128]{1,0:T(8,128)(2,1)S(1)}, u32[]{:S(2)}, u32[]{:S(2)}) collective-permute-start(bf16[1760,128]{1,0:T(8,128)(2,1)} %get-tuple-element.159), channel_id=1, source_target_pairs={{0,4},{1,5},{2,6},{3,7},{4,0},{5,1},{6,2},{7,3},{8,12},{9,13},{10,... | collective-permute-start | bytes 1351688 | tf_op jit(solution)/shard_map/ppermute | solution.py:188
  196.7 13.4 %collective-permute-start.19 = (bf16[1760,128]{1,0:T(8,128)(2,1)}, bf16[1760,128]{1,0:T(8,128)(2,1)S(1)}, u32[]{:S(2)}, u32[]{:S(2)}) collective-permute-start(bf16[1760,128]{1,0:T(8,128)(2,1)} %get-tuple-element.160), channel_id=1, source_target_pairs={{0,2},{1,3},{2,0},{3,1},{4,6},{5,7},{6,4},{7,5},{8,10},{9,11},{10,... | collective-permute-start | bytes 1351688 | tf_op jit(solution)/shard_map/ppermute | solution.py:188
  203.6 16.8 %collective-permute-start.20 = (bf16[1760,128]{1,0:T(8,128)(2,1)}, bf16[1760,128]{1,0:T(8,128)(2,1)S(1)}, u32[]{:S(2)}, u32[]{:S(2)}) collective-permute-start(bf16[1760,128]{1,0:T(8,128)(2,1)} %get-tuple-element.158), channel_id=1, source_target_pairs={{0,4},{1,5},{2,6},{3,7},{4,0},{5,1},{6,2},{7,3},{8,12},{9,13},{10,... | collective-permute-start | bytes 1351688 | tf_op jit(solution)/shard_map/ppermute | solution.py:188
  205.2 15.3 %collective-permute-start.21 = (bf16[1760,128]{1,0:T(8,128)(2,1)}, bf16[1760,128]{1,0:T(8,128)(2,1)S(1)}, u32[]{:S(2)}, u32[]{:S(2)}) collective-permute-start(bf16[1760,128]{1,0:T(8,128)(2,1)} %get-tuple-element.167), channel_id=1, source_target_pairs={{0,2},{1,3},{2,0},{3,1},{4,6},{5,7},{6,4},{7,5},{8,10},{9,11},{10,... | collective-permute-start | bytes 1351688 | tf_op jit(solution)/shard_map/ppermute | solution.py:188
  210.1 20.7 %collective-permute-start.26 = (bf16[1760,128]{1,0:T(8,128)(2,1)}, bf16[1760,128]{1,0:T(8,128)(2,1)S(1)}, u32[]{:S(2)}, u32[]{:S(2)}) collective-permute-start(bf16[1760,128]{1,0:T(8,128)(2,1)} %get-tuple-element.180), channel_id=1, source_target_pairs={{0,4},{1,5},{2,6},{3,7},{4,0},{5,1},{6,2},{7,3},{8,12},{9,13},{10,... | collective-permute-start | bytes 1351688 | tf_op jit(solution)/shard_map/ppermute | solution.py:188
  210.6 20.2 %collective-permute-start.27 = (bf16[1760,128]{1,0:T(8,128)(2,1)}, bf16[1760,128]{1,0:T(8,128)(2,1)S(1)}, u32[]{:S(2)}, u32[]{:S(2)}) collective-permute-start(bf16[1760,128]{1,0:T(8,128)(2,1)} %get-tuple-element.181), channel_id=1, source_target_pairs={{0,2},{1,3},{2,0},{3,1},{4,6},{5,7},{6,4},{7,5},{8,10},{9,11},{10,... | collective-permute-start | bytes 1351688 | tf_op jit(solution)/shard_map/ppermute | solution.py:188
  224.8 14.3 %collective-permute-start.22 = (bf16[1760,128]{1,0:T(8,128)(2,1)}, bf16[1760,128]{1,0:T(8,128)(2,1)S(1)}, u32[]{:S(2)}, u32[]{:S(2)}) collective-permute-start(bf16[1760,128]{1,0:T(8,128)(2,1)} %get-tuple-element.170), channel_id=1, source_target_pairs={{0,2},{1,3},{2,0},{3,1},{4,6},{5,7},{6,4},{7,5},{8,10},{9,11},{10,... | collective-permute-start | bytes 1351688 | tf_op jit(solution)/shard_map/ppermute | solution.py:188
  226.5 14.4 %collective-permute-start.24 = (bf16[1760,128]{1,0:T(8,128)(2,1)}, bf16[1760,128]{1,0:T(8,128)(2,1)S(1)}, u32[]{:S(2)}, u32[]{:S(2)}) collective-permute-start(bf16[1760,128]{1,0:T(8,128)(2,1)} %get-tuple-element.177), channel_id=1, source_target_pairs={{0,4},{1,5},{2,6},{3,7},{4,0},{5,1},{6,2},{7,3},{8,12},{9,13},{10,... | collective-permute-start | bytes 1351688 | tf_op jit(solution)/shard_map/ppermute | solution.py:188
  234.5 13.4 %collective-permute-start.28 = (bf16[1760,128]{1,0:T(8,128)(2,1)}, bf16[1760,128]{1,0:T(8,128)(2,1)S(1)}, u32[]{:S(2)}, u32[]{:S(2)}) collective-permute-start(bf16[1760,128]{1,0:T(8,128)(2,1)} %get-tuple-element.189), channel_id=1, source_target_pairs={{0,2},{1,3},{2,0},{3,1},{4,6},{5,7},{6,4},{7,5},{8,10},{9,11},{10,... | collective-permute-start | bytes 1351688 | tf_op jit(solution)/shard_map/ppermute | solution.py:188
  235.1 13.9 %collective-permute-start.29 = (bf16[1760,128]{1,0:T(8,128)(2,1)}, bf16[1760,128]{1,0:T(8,128)(2,1)S(1)}, u32[]{:S(2)}, u32[]{:S(2)}) collective-permute-start(bf16[1760,128]{1,0:T(8,128)(2,1)} %get-tuple-element.191), channel_id=1, source_target_pairs={{0,4},{1,5},{2,6},{3,7},{4,0},{5,1},{6,2},{7,3},{8,12},{9,13},{10,... | collective-permute-start | bytes 1351688 | tf_op jit(solution)/shard_map/ppermute | solution.py:188
  239.2 11.0 %collective-permute-start.23 = (bf16[880,128]{1,0:T(8,128)(2,1)S(1)}, bf16[880,128]{1,0:T(8,128)(2,1)S(1)}, u32[]{:S(2)}, u32[]{:S(2)}) collective-permute-start(bf16[880,128]{1,0:T(8,128)(2,1)S(1)} %dynamic-slice_bitcast_fusion.3), channel_id=1, source_target_pairs={{0,8},{8,0},{16,24},{24,16},{1,9},{9,1},{17,25},{25,17},{2,10},{10... | collective-permute-start | bytes 675848 | tf_op jit(solution)/shard_map/ppermute | solution.py:1096
  241.0 11.6 %collective-permute-start.25 = (bf16[880,128]{1,0:T(8,128)(2,1)S(1)}, bf16[880,128]{1,0:T(8,128)(2,1)S(1)}, u32[]{:S(2)}, u32[]{:S(2)}) collective-permute-start(bf16[880,128]{1,0:T(8,128)(2,1)S(1)} %dynamic-slice_bitcast_fusion.2), channel_id=1, source_target_pairs={{0,16},{8,24},{16,0},{24,8},{1,17},{9,25},{17,1},{25,9},{2,18},{10... | collective-permute-start | bytes 675848 | tf_op jit(solution)/shard_map/ppermute | solution.py:1096
  252.6 20.9 %collective-permute-start.30 = (bf16[880,128]{1,0:T(8,128)(2,1)S(1)}, bf16[880,128]{1,0:T(8,128)(2,1)S(1)}, u32[]{:S(2)}, u32[]{:S(2)}) collective-permute-start(bf16[880,128]{1,0:T(8,128)(2,1)S(1)} %dynamic-slice_bitcast_fusion.1), channel_id=1, source_target_pairs={{0,8},{8,0},{16,24},{24,16},{1,9},{9,1},{17,25},{25,17},{2,10},{10... | collective-permute-start | bytes 675848 | tf_op jit(solution)/shard_map/ppermute | solution.py:1096
  252.7 46.4 %copy-start.1 = (f32[900608]{0:T(1024)S(1)}, f32[900608]{0:T(1024)}, u32[]{:S(2)}) copy-start(f32[900608]{0:T(1024)} %param.19) | copy-start | bytes 10807300
  252.8 20.8 %collective-permute-start.31 = (bf16[880,128]{1,0:T(8,128)(2,1)S(1)}, bf16[880,128]{1,0:T(8,128)(2,1)S(1)}, u32[]{:S(2)}, u32[]{:S(2)}) collective-permute-start(bf16[880,128]{1,0:T(8,128)(2,1)S(1)} %dynamic-slice_bitcast_fusion), channel_id=1, source_target_pairs={{0,16},{8,24},{16,0},{24,8},{1,17},{9,25},{17,1},{25,9},{2,18},{10... | collective-permute-start | bytes 675848 | tf_op jit(solution)/shard_map/ppermute | solution.py:1096
  255.8 14.1 %collective-permute-start.38 = (bf16[440,128]{1,0:T(8,128)(2,1)S(1)}, bf16[440,128]{1,0:T(8,128)(2,1)S(1)}, u32[]{:S(2)}, u32[]{:S(2)}) collective-permute-start(bf16[440,128]{1,0:T(8,128)(2,1)S(1)} %dynamic-slice_bitcast_fusion.5), channel_id=1, source_target_pairs={{0,16},{8,24},{16,0},{24,8},{1,17},{9,25},{17,1},{25,9},{2,18},{10... | collective-permute-start | bytes 337928 | tf_op jit(solution)/shard_map/ppermute | solution.py:1096
  255.9 14.1 %collective-permute-start.41 = (bf16[440,128]{1,0:T(8,128)(2,1)S(1)}, bf16[440,128]{1,0:T(8,128)(2,1)S(1)}, u32[]{:S(2)}, u32[]{:S(2)}) collective-permute-start(bf16[440,128]{1,0:T(8,128)(2,1)S(1)} %dynamic-slice_bitcast_fusion.4), channel_id=1, source_target_pairs={{0,8},{8,0},{16,24},{24,16},{1,9},{9,1},{17,25},{25,17},{2,10},{10... | collective-permute-start | bytes 337928 | tf_op jit(solution)/shard_map/ppermute | solution.py:1096
  270.0 8.8 %collective-permute-start.39 = (bf16[440,128]{1,0:T(8,128)(2,1)S(1)}, bf16[440,128]{1,0:T(8,128)(2,1)S(1)}, u32[]{:S(2)}, u32[]{:S(2)}) collective-permute-start(bf16[440,128]{1,0:T(8,128)(2,1)S(1)} %bitcast_add_fusion.5), channel_id=1, source_target_pairs={{0,16},{8,24},{16,0},{24,8},{1,17},{9,25},{17,1},{25,9},{2,18},{10... | collective-permute-start | bytes 337928 | tf_op jit(solution)/shard_map/ppermute | solution.py:1096
  270.1 11.5 %collective-permute-start.42 = (bf16[440,128]{1,0:T(8,128)(2,1)S(1)}, bf16[440,128]{1,0:T(8,128)(2,1)S(1)}, u32[]{:S(2)}, u32[]{:S(2)}) collective-permute-start(bf16[440,128]{1,0:T(8,128)(2,1)S(1)} %bitcast_add_fusion.4), channel_id=1, source_target_pairs={{0,8},{8,0},{16,24},{24,16},{1,9},{9,1},{17,25},{25,17},{2,10},{10... | collective-permute-start | bytes 337928 | tf_op jit(solution)/shard_map/ppermute | solution.py:1096
  273.5 25.6 %copy-start = (f32[900608]{0:T(1024)S(1)}, f32[900608]{0:T(1024)}, u32[]{:S(2)}) copy-start(f32[900608]{0:T(1024)} %param.18) | copy-start | bytes 10807300
  273.6 8.8 %collective-permute-start.32 = (bf16[440,128]{1,0:T(8,128)(2,1)S(1)}, bf16[440,128]{1,0:T(8,128)(2,1)S(1)}, u32[]{:S(2)}, u32[]{:S(2)}) collective-permute-start(bf16[440,128]{1,0:T(8,128)(2,1)S(1)} %dynamic-slice_bitcast_fusion.7), channel_id=1, source_target_pairs={{0,16},{8,24},{16,0},{24,8},{1,17},{9,25},{17,1},{25,9},{2,18},{10... | collective-permute-start | bytes 337928 | tf_op jit(solution)/shard_map/ppermute | solution.py:1096
  273.7 14.0 %collective-permute-start.35 = (bf16[440,128]{1,0:T(8,128)(2,1)S(1)}, bf16[440,128]{1,0:T(8,128)(2,1)S(1)}, u32[]{:S(2)}, u32[]{:S(2)}) collective-permute-start(bf16[440,128]{1,0:T(8,128)(2,1)S(1)} %dynamic-slice_bitcast_fusion.6), channel_id=1, source_target_pairs={{0,8},{8,0},{16,24},{24,16},{1,9},{9,1},{17,25},{25,17},{2,10},{10... | collective-permute-start | bytes 337928 | tf_op jit(solution)/shard_map/ppermute | solution.py:1096
  278.8 20.3 %collective-permute-start.40 = (bf16[880,128]{1,0:T(8,128)(2,1)S(1)}, bf16[880,128]{1,0:T(8,128)(2,1)S(1)}, u32[]{:S(2)}, u32[]{:S(2)}) collective-permute-start(bf16[880,128]{1,0:T(8,128)(2,1)S(1)} %maximum_select_fusion.2.one), channel_id=1, source_target_pairs={{0,8},{8,0},{16,24},{24,16},{1,9},{9,1},{17,25},{25,17},{2,10},{10... | collective-permute-start | bytes 675848 | tf_op jit(solution)/shard_map/ppermute | solution.py:1096
  281.7 17.4 %collective-permute-start.43 = (bf16[880,128]{1,0:T(8,128)(2,1)S(1)}, bf16[880,128]{1,0:T(8,128)(2,1)S(1)}, u32[]{:S(2)}, u32[]{:S(2)}) collective-permute-start(bf16[880,128]{1,0:T(8,128)(2,1)S(1)} %maximum_select_fusion.3.two), channel_id=1, source_target_pairs={{0,16},{8,24},{16,0},{24,8},{1,17},{9,25},{17,1},{25,9},{2,18},{10... | collective-permute-start | bytes 675848 | tf_op jit(solution)/shard_map/ppermute | solution.py:1096
  282.4 13.9 %collective-permute-start.33 = (bf16[440,128]{1,0:T(8,128)(2,1)S(1)}, bf16[440,128]{1,0:T(8,128)(2,1)S(1)}, u32[]{:S(2)}, u32[]{:S(2)}) collective-permute-start(bf16[440,128]{1,0:T(8,128)(2,1)S(1)} %bitcast_add_fusion.7), channel_id=1, source_target_pairs={{0,16},{8,24},{16,0},{24,8},{1,17},{9,25},{17,1},{25,9},{2,18},{10... | collective-permute-start | bytes 337928 | tf_op jit(solution)/shard_map/ppermute | solution.py:1096
  287.7 11.2 %collective-permute-start.36 = (bf16[440,128]{1,0:T(8,128)(2,1)S(1)}, bf16[440,128]{1,0:T(8,128)(2,1)S(1)}, u32[]{:S(2)}, u32[]{:S(2)}) collective-permute-start(bf16[440,128]{1,0:T(8,128)(2,1)S(1)} %bitcast_add_fusion.6), channel_id=1, source_target_pairs={{0,8},{8,0},{16,24},{24,16},{1,9},{9,1},{17,25},{25,17},{2,10},{10... | collective-permute-start | bytes 337928 | tf_op jit(solution)/shard_map/ppermute | solution.py:1096
  296.4 6.0 %collective-permute-start.34 = (bf16[880,128]{1,0:T(8,128)(2,1)S(1)}, bf16[880,128]{1,0:T(8,128)(2,1)S(1)}, u32[]{:S(2)}, u32[]{:S(2)}) collective-permute-start(bf16[880,128]{1,0:T(8,128)(2,1)S(1)} %maximum_select_fusion.one), channel_id=1, source_target_pairs={{0,8},{8,0},{16,24},{24,16},{1,9},{9,1},{17,25},{25,17},{2,10},{10... | collective-permute-start | bytes 675848 | tf_op jit(solution)/shard_map/ppermute | solution.py:1096
  299.0 8.7 %collective-permute-start.37 = (bf16[880,128]{1,0:T(8,128)(2,1)S(1)}, bf16[880,128]{1,0:T(8,128)(2,1)S(1)}, u32[]{:S(2)}, u32[]{:S(2)}) collective-permute-start(bf16[880,128]{1,0:T(8,128)(2,1)S(1)} %maximum_select_fusion.1.two), channel_id=1, source_target_pairs={{0,16},{8,24},{16,0},{24,8},{1,17},{9,25},{17,1},{25,9},{2,18},{10... | collective-permute-start | bytes 675848 | tf_op jit(solution)/shard_map/ppermute | solution.py:1096
  (24 other events, 197.9 us)

commit v8 on v7

--- a/solution.py
+++ b/solution.py
@@ -202,8 +202,7 @@
         flat[pl.ds(place + half * n + done, real - done), :] = src[done : done + CHUNK, :].astype(F32)[: real - done]
 
 
-def unpack_first_kernel(shard_rows, me_ref, *rest):
-    pieces, (wqkv, bq, flat, buf, sems) = rest[:12], rest[12:]
+def unpack_first(shard_rows, me_ref, pieces, wqkv, bq, flat, buf, sems):
     chip, core = me_ref[0] >> 1, me_ref[0] & 1
     picks = []
     for side in range(2):
@@ -230,24 +229,6 @@
 
 
 SM = pl.BlockSpec(memory_space=pltpu.SMEM)
-
-
-def unpack_first(me, shard_rows, *pieces):
-    n = pieces[0].shape[0]
-    return pl.pallas_call(
-        functools.partial(unpack_first_kernel, shard_rows),
-        in_specs=[SM] + [ANY] * len(pieces),
-        out_specs=[VM] * 2,
-        out_shape=FIRST,
-        scratch_shapes=[
-            pltpu.VMEM((2 * shard_rows + 16, LANE), F32),
-            pltpu.VMEM((4, n, LANE), BF),
-            pltpu.SemaphoreType.DMA((4,)),
-        ],
-        compiler_params=params_of(),
-        cost_estimate=TINY,
-        name="unpack_first",
-    )(me, *pieces)
 
 
 SLOTS = 8
@@ -351,7 +332,7 @@
     last = (swap(jnp.where(x == 1, held[0], close[0]), 4), swap(jnp.where(y == 1, held[1], close[1]), 2))
     early = own + near + far
     early_c = tuple(swap(v, 1) for v in early)
-    first = unpack_first(me.reshape(1), shard_rows, *early, *early_c)
+    first = (me.reshape(1), *early, *early_c)
 
     def finish(after):
         late, _ = lax.optimization_barrier((last, after))
@@ -377,7 +358,7 @@
     return jnp.where(lane < 64, v[:n], v[n:])
 
 
-def attend_kernel(x_ref, segc_ref, segr_ref, wq_ref, wk_ref, wv_ref, bq_ref, q_ref, k_ref, v_ref, p_ref, att_ref, bias):
+def attend_kernel(x_ref, segc_ref, segr_ref, weights_of, bq_ref, q_ref, k_ref, v_ref, p_ref, att_ref, bias):
     step, row = pl.program_id(0), pl.program_id(1)
 
     @pl.when(step == 0)
@@ -387,9 +368,9 @@
             for h in range(2):
                 bias[row, h * QB : (h + 1) * QB, OFFSETS[i] : OFFSETS[i] + hi - lo] = here
 
-    for n, (w_ref, out_ref) in enumerate(((wq_ref, q_ref), (wk_ref, k_ref), (wv_ref, v_ref))):
+    for n, out_ref in enumerate((q_ref, k_ref, v_ref)):
         cols = at(step + n * (D // 256), 256)
-        out_ref[0] = ((dot(x_ref[row], w_ref[...]) + bq_ref[0:1, cols]) * bq_ref[1:2, cols]).astype(BF)
+        out_ref[0] = ((dot(x_ref[row], weights_of(n)) + bq_ref[0:1, cols]) * bq_ref[1:2, cols]).astype(BF)
 
     blocks = [
         (p, slice(p * LANE, (p + 1) * LANE), i, lo, hi, slice(OFFSETS[i], OFFSETS[i] + hi - lo))
@@ -412,23 +393,65 @@
     return pl.BlockSpec((1, *shape), lambda r: (r,) + (0,) * len(shape))
 
 
-def attend(x, segc, segr, wqkv, bq):
+def attend(x, segc, segr, given, shard_rows=None):
     rows = x.shape[0]
+    steps = D // 256
     tall = pl.BlockSpec((1, LEN, 256), lambda g, r: (r, 0, g))
-    weights = [pl.BlockSpec((D, 256), lambda g, r, n=n: (0, g + n * (D // 256))) for n in range(3)]
     probs = pl.BlockSpec((1, 2, 2 * QB, WIDE), lambda g, r: (r, g, 0, 0))
     token = SDS((rows, LEN, D), BF)
+    out_specs = [tall, tall, tall, probs, tall]
+    out_shape = [token, token, token, SDS((rows, PAIRS, 2 * QB, WIDE), BF), token]
+    scratch = [pltpu.VMEM((rows, 2 * QB, WIDE), F32)]
+    if shard_rows is None:
+        weights = [pl.BlockSpec((D, 256), lambda g, r, n=n: (0, g + n * steps)) for n in range(3)]
+        specs = weights + [once(8, 3 * D)]
+        given = (given[0], given[0], given[0], given[1])
+
+        def kernel(x_ref, segc_ref, segr_ref, wq_ref, wk_ref, wv_ref, bq_ref, *rest):
+            attend_kernel(x_ref, segc_ref, segr_ref, lambda n: (wq_ref, wk_ref, wv_ref)[n][...], bq_ref, *rest)
+
+    else:
+        specs = [SM] + [ANY] * (len(given) - 1)
+        out_specs = out_specs + [ANY]
+        out_shape = out_shape + [FIRST[0]]
+        scratch += [
+            pltpu.VMEM(FIRST[0].shape, BF),
+            pltpu.VMEM(FIRST[1].shape, F32),
+            pltpu.VMEM((2 * shard_rows + 16, LANE), F32),
+            pltpu.VMEM((4, *given[1].shape), BF),
+            pltpu.SemaphoreType.DMA((4,)),
+            pltpu.SemaphoreType.DMA((1,)),
+        ]
+
+        def kernel(x_ref, segc_ref, segr_ref, me_ref, *rest):
+            pieces, (*outs, w_out, bias, wqkv, bq, flat, buf, sems, out_sem) = rest[:12], rest[12:]
+            step, row = pl.program_id(0), pl.program_id(1)
+            put = pltpu.make_async_copy(wqkv, w_out, out_sem.at[0])
+
+            @pl.when((step == 0) & (row == 0))
+            def _():
+                unpack_first(shard_rows, me_ref, pieces, wqkv, bq, flat, buf, sems)
+                put.start()
+
+            attend_kernel(
+                x_ref, segc_ref, segr_ref, lambda n: wqkv[:, at(step + n * steps, 256)], bq, *outs, bias
+            )
+
+            @pl.when((step == steps - 1) & (row == rows - 1))
+            def _():
+                put.wait()
+
     return pl.pallas_call(
-        attend_kernel,
-        grid=(D // 256, rows),
-        in_specs=[once(*v.shape) for v in (x, segc, segr)] + weights + [once(8, 3 * D)],
-        out_specs=[tall, tall, tall, probs, tall],
-        out_shape=[token, token, token, SDS((rows, PAIRS, 2 * QB, WIDE), BF), token],
-        scratch_shapes=[pltpu.VMEM((rows, 2 * QB, WIDE), F32)],
+        kernel,
+        grid=(steps, rows),
+        in_specs=[once(*v.shape) for v in (x, segc, segr)] + specs,
+        out_specs=out_specs,
+        out_shape=out_shape,
+        scratch_shapes=scratch,
         compiler_params=params_of(),
         cost_estimate=TINY,
         name="attend",
-    )(x, segc, segr, wqkv, wqkv, wqkv, bq)
+    )(x, segc, segr, *given)
 
 
 TB = 512
@@ -1151,8 +1174,11 @@
         mine = jnp.pad(params.reshape(shard_rows, LANE).astype(BF), ((0, padded - shard_rows), (0, 0)))
         both = unpack(lax.all_gather(mine, "fsdp", axis=0, tiled=False), shard_rows)
         first, finish = both[:2], lambda after: both[2:]
-    wqkv, bq = first
-    q, k, v, probs, att = attend(inputs, segc, segr, wqkv, bq)
+    if count == 8:
+        q, k, v, probs, att, wqkv = attend(inputs, segc, segr, first, shard_rows)
+    else:
+        wqkv = first[0]
+        q, k, v, probs, att = attend(inputs, segc, segr, first)
     if count == 8:
         owners, pieces = finish(att)
         results = middle(inputs, att, segc, hot, out_cotangent, (owners,), pieces, shard_rows)

time: 312 us -> 309 us (level)
    pallas_call x2 -> x1, Pallas kernels: 20.7 us -> 18.8 us  [attend(): pl.pallas_call(kernel, grid=(steps, rows), in_specs=[once(*v.shape) for v...]
  transfers between devices with their start and end apart: 44 -> 44, of which waited for: 21 -> 23; matrix products, arithmetic and copies ran while one was open for 3% -> 3% of each run, Pallas kernels for 23% -> 23%
where the time goes in v8:
time: 309 us
  Pallas kernels  158 us (51%)
  waiting for transfers between devices  90.8 us (29%)
  starting transfers between devices  40.9 us (13%)
  other arithmetic  10 us (3%)
  local copies, waits for them, and re-layouts  8.31 us (3%)
    pallas_call x1, Pallas kernels, middle(): pl.pallas_call(kernel, grid=(rows,), in_specs=[row_spec(LEN, D), row_spec...  55.6 us
    ppermute x28, waiting for transfers between devices, swap(): return lax.ppermute(v, 'fsdp', [(d, d ^ bit) for d in range(8)])  50 us
    ppermute x16, waiting for transfers between devices, sum_replicas(): lax.ppermute(v, 'rep', [(i, i ^ bit) for i in range(4)])  40.8 us
    pallas_call x1, Pallas kernels, late_pairs(): pl.pallas_call(functools.partial(late_pair_kernel, shard_rows), in_specs=...  24.7 us
    ppermute x28, starting transfers between devices, swap(): return lax.ppermute(v, 'fsdp', [(d, d ^ bit) for d in range(8)])  24.2 us
    pallas_call x1, Pallas kernels, attend(): pl.pallas_call(kernel, grid=(steps, rows), in_specs=[once(*v.shape) for v...  18.8 us
    pallas_call x6, Pallas kernels, combine(): pl.pallas_call(functools.partial(combine_kernel, plan, len(extras)), in_s...  17.8 us
    ppermute x16, starting transfers between devices, sum_replicas(): lax.ppermute(v, 'rep', [(i, i ^ bit) for i in range(4)])  16.7 us
  transfers between devices with their start and end apart: 44, of which 23 were waited for; matrix products, arithmetic and copies ran while one was open for 3% of the time, Pallas kernels for 23%

profile of v8, /device:TPU:0, one launch (start us, length us, event | category | flops | bytes accessed | tf_op | source)
XLA Modules:
  0.0 308.8 jit_solution(15316582665518135238)
XLA Ops:
  0.6 2.2 convert.4
  3.1 3.0 collective-permute-start
  7.8 18.2 %collective-permute-done.rest_2_.refs_8_ = bf16[3520,128]{1,0:T(8,128)(2,1)S(1)} collective-permute-done((bf16[3520,128]{1,0:T(8,128)(2,1)S(1)}, bf16[3520,128]{1,0:T(8,128)(2,1)S(1)}, u32[]{:S(2)}, u32[]{:S(2)}) %collective-permute-start) | collective-permute-done | bytes 901152 | tf_op jit(solution)/shard_map/ppermute | solution.py:188
  26.2 1.8 collective-permute-start.2
  31.2 16.7 %collective-permute-done.2.rest_4_.refs_10_ = bf16[3520,128]{1,0:T(8,128)(2,1)} collective-permute-done((bf16[3520,128]{1,0:T(8,128)(2,1)S(1)}, bf16[3520,128]{1,0:T(8,128)(2,1)}, u32[]{:S(2)}, u32[]{:S(2)}) %collective-permute-start.2) | collective-permute-done | bytes 901152 | tf_op jit(solution)/shard_map/ppermute | solution.py:188
  47.9 2.6 collective-permute-done.3.rest_5_.refs_11_
  50.5 2.2 broadcast_select_fusion
  52.7 1.5 collective-permute-start.10
  58.3 18.8 %attend.1 = (bf16[2,512,768]{2,1,0:T(8,128)(2,1)}, bf16[2,512,768]{2,1,0:T(8,128)(2,1)}, bf16[2,512,768]{2,1,0:T(8,128)(2,1)}, bf16[2,6,256,1280]{3,2,1,0:T(8,12...) custom-call(bf16[2,512,768]{2,1,0:T(8,128)(2,1)} %refs_0_.1, s32[2,512,1]{2,1,0:T(8,128)} %copy.26.segc_ref.refs_2_, ...), custom_call_target="tpu_custom_call" | custom-call | flops 1 | bytes 1 | tf_op jit(solution)/shard_map/attend/pallas_call | solution.py:444
  79.5 1.7 collective-permute-done.12.refs_20_
  82.1 55.6 %middle.1 = (bf16[2,512,768]{2,1,0:T(8,128)(2,1)}, bf16[2,512,768]{2,1,0:T(8,128)(2,1)}, bf16[2,512,3072]{2,1,0:T(8,128)(2,1)}, bf16[2,512,768]{2,1,0:T(8,128)(2...) custom-call(bf16[2,512,768]{2,1,0:T(8,128)(2,1)} %refs_0_.1, ...), custom_call_target="tpu_custom_call" | custom-call | flops 1 | bytes 1 | tf_op jit(solution)/shard_map/middle/pallas_call | solution.py:701
  137.7 24.7 %late_grads.1 = (bf16[3,7040,128]{2,1,0:T(8,128)(2,1)}, bf16[3,7040,128]{2,1,0:T(8,128)(2,1)}, f32[240,128]{1,0:T(8,128)}) custom-call(s32[1]{0:T(128)} %bitcast.1.me_ref, bf16[1024,768]{1,0:T(8,128)(2,1)} %bitcast.74, bf16[1024,768]{1,0:T(8,128)(2,1)} %bitcast.89, bf16[1024,768]{1,0:T(8,128)(2,1)} %bitcast.87, bf16[1024,3072]{1,0:T(8,128)(2,1)} %bitcast.73, ...), custom_call_target="tpu_custom_call" | custom-call | flops 1 | bytes 1 | tf_op jit(solution)/shard_map/late_grads/pallas_call | solution.py:1023
  162.5 7.8 %retreat.2 = (bf16[2,512,768]{2,1,0:T(8,128)(2,1)}, bf16[2,512,768]{2,1,0:T(8,128)(2,1)}, bf16[2,512,768]{2,1,0:T(8,128)(2,1)}, f32[8,768]{1,0:T(8,128)}) custom-call(bf16[2,512,768]{2,1,0:T(8,128)(2,1)} %get-tuple-element.115.refs_0_, bf16[2,512,768]{2,1,0:T(8,128)(2,1)} %get-tuple-element.116.refs_1_, bf16[2,512,768]{2,1,0:T(8,128)(2,1)} %get-tuple-element.117.refs_2_, ...), custom_call_target="tpu_custom_call" | custom-call | flops 1 | bytes 1 | tf_op jit(solution)/shard_map/retreat/pallas_call | solution.py:786
  171.7 3.3 %combine_one.1 = (bf16[1760,128]{1,0:T(8,128)(2,1)}, bf16[1760,128]{1,0:T(8,128)(2,1)}, bf16[1760,128]{1,0:T(8,128)(2,1)}, bf16[1760,128]{1,0:T(8,128)(2,1)}) custom-call(s32[1]{0:T(128)} %bitcast.1.me_ref, bf16[3,7040,128]{2,1,0:T(8,128)(2,1)} %get-tuple-element.139.refs_0_.refs_2_, bf16[3,7040,128]{2,1,0:T(8,128)(2,1)} %collective-permute-done.14.refs_1_.refs_3_, ...), custom_call_target="tpu_custom_call" | custom-call | flops 1 | bytes 1 | tf_op jit(solution)/shard_map/combine_one/pallas_call | solution.py:1096
  176.1 7.9 %retreat.3 = (bf16[2,512,768]{2,1,0:T(8,128)(2,1)}, bf16[2,512,768]{2,1,0:T(8,128)(2,1)}, bf16[2,512,768]{2,1,0:T(8,128)(2,1)}, f32[8,768]{1,0:T(8,128)}) custom-call(bf16[2,512,768]{2,1,0:T(8,128)(2,1)} %get-tuple-element.115.refs_0_, bf16[2,512,768]{2,1,0:T(8,128)(2,1)} %get-tuple-element.116.refs_1_, ...), custom_call_target="tpu_custom_call", output_to_operand_aliasing={{0}: (5, {}), {1}: (6, {}), {2}: (7, {})} | custom-call | flops 1 | bytes 1 | tf_op jit(solution)/shard_map/retreat/pallas_call | solution.py:786
  184.0 8.8 %early_grads.1 = (bf16[1,7040,128]{2,1,0:T(8,128)(2,1)}, bf16[1,7040,128]{2,1,0:T(8,128)(2,1)}) custom-call(s32[1]{0:T(128)} %bitcast.1.me_ref, bf16[1024,768]{1,0:T(8,128)(2,1)} %bitcast.71, bf16[1024,768]{1,0:T(8,128)(2,1)} %bitcast.68, bf16[1024,768]{1,0:T(8,128)(2,1)} %bitcast.69, bf16[1024,768]{1,0:T(8,128)(2,1)} %bitcast.70, ...), custom_call_target="tpu_custom_call" | custom-call | flops 1 | bytes 1 | tf_op jit(solution)/shard_map/early_grads/pallas_call | solution.py:1045
  192.9 1.6 collective-permute-start.18
  194.5 1.5 collective-permute-start.19
  198.1 3.3 %combine_two.1 = (bf16[1760,128]{1,0:T(8,128)(2,1)}, bf16[1760,128]{1,0:T(8,128)(2,1)}, bf16[1760,128]{1,0:T(8,128)(2,1)}, bf16[1760,128]{1,0:T(8,128)(2,1)}) custom-call(s32[1]{0:T(128)} %bitcast.1.me_ref, bf16[3,7040,128]{2,1,0:T(8,128)(2,1)} %get-tuple-element.139.refs_0_.refs_2_, bf16[3,7040,128]{2,1,0:T(8,128)(2,1)} %collective-permute-done.14.refs_1_.refs_3_, ...), custom_call_target="tpu_custom_call" | custom-call | flops 1 | bytes 1 | tf_op jit(solution)/shard_map/combine_two/pallas_call | solution.py:1096
  201.4 1.6 collective-permute-start.20
  203.0 1.5 collective-permute-start.21
  204.5 1.8 collective-permute-done.18.refs_4_
  206.4 1.6 collective-permute-done.19.refs_5_
  208.4 1.5 collective-permute-start.27
  210.0 9.5 %project_back.1 = bf16[2,512,768]{2,1,0:T(8,128)(2,1)} custom-call(bf16[2,512,768]{2,1,0:T(8,128)(2,1)} %get-tuple-element.158.dq_ref, bf16[2,512,768]{2,1,0:T(8,128)(2,1)} %get-tuple-element.159.dk_ref, bf16[2,512,768]{2,1,0:T(8,128)(2,1)} %get-tuple-element.160.dv_ref, f32[2,512,768]{2,1,0:T(8,128)} %get-tuple-element.161.dh1_ref, ...), custom_call_target="tpu_custom_call" | custom-call | flops 1 | bytes 1 | tf_op jit(solution)/shard_map/project_back/pallas_call | solution.py:814
  221.0 2.8 combine_three.2
  225.9 2.8 combine_own.2
  229.6 2.8 combine_three.3
  232.4 1.6 collective-permute-start.28
  234.5 2.8 collective-permute-done.22
  237.5 1.6 collective-permute-start.23
  239.3 2.6 collective-permute-start.25
  242.0 2.8 combine_own.3
  248.1 1.9 collective-permute-done.25
  250.3 2.8 collective-permute-start.31
  253.5 1.8 collective-permute-start.41
  255.3 12.2 %collective-permute-done.38 = bf16[440,128]{1,0:T(8,128)(2,1)S(1)} collective-permute-done((bf16[440,128]{1,0:T(8,128)(2,1)S(1)}, bf16[440,128]{1,0:T(8,128)(2,1)S(1)}, u32[]{:S(2)}, u32[]{:S(2)}) %collective-permute-start.38) | collective-permute-done | bytes 112672 | tf_op jit(solution)/shard_map/ppermute | solution.py:1119
  267.7 3.2 %collective-permute-start.42 = (bf16[440,128]{1,0:T(8,128)(2,1)S(1)}, bf16[440,128]{1,0:T(8,128)(2,1)S(1)}, u32[]{:S(2)}, u32[]{:S(2)}) collective-permute-start(bf16[440,128]{1,0:T(8,128)(2,1)S(1)} %bitcast_add_fusion.4), channel_id=1, source_target_pairs={{0,8},{8,0},{16,24},{24,16},{1,9},{9,1},{17,25},{25,17},{2,10},{10... | collective-permute-start | bytes 337928 | tf_op jit(solution)/shard_map/ppermute | solution.py:1119
  271.2 1.8 collective-permute-start.35
  272.9 3.5 %collective-permute-done.39 = bf16[440,128]{1,0:T(8,128)(2,1)S(1)} collective-permute-done((bf16[440,128]{1,0:T(8,128)(2,1)S(1)}, bf16[440,128]{1,0:T(8,128)(2,1)S(1)}, u32[]{:S(2)}, u32[]{:S(2)}) %collective-permute-start.39) | collective-permute-done | bytes 112672 | tf_op jit(solution)/shard_map/ppermute | solution.py:1119
  276.6 2.0 collective-permute-done.42
  280.1 1.7 collective-permute-start.33
  281.8 3.4 %collective-permute-done.35 = bf16[440,128]{1,0:T(8,128)(2,1)S(1)} collective-permute-done((bf16[440,128]{1,0:T(8,128)(2,1)S(1)}, bf16[440,128]{1,0:T(8,128)(2,1)S(1)}, u32[]{:S(2)}, u32[]{:S(2)}) %collective-permute-start.35) | collective-permute-done | bytes 112672 | tf_op jit(solution)/shard_map/ppermute | solution.py:1119
  285.3 8.4 %collective-permute-done.33 = bf16[440,128]{1,0:T(8,128)(2,1)S(1)} collective-permute-done((bf16[440,128]{1,0:T(8,128)(2,1)S(1)}, bf16[440,128]{1,0:T(8,128)(2,1)S(1)}, u32[]{:S(2)}, u32[]{:S(2)}) %collective-permute-start.33) | collective-permute-done | bytes 112672 | tf_op jit(solution)/shard_map/ppermute | solution.py:1119
  293.8 2.6 collective-permute-done.36
  296.6 3.3 %adam.2 = (f32[7036,128]{1,0:T(8,128)}, f32[7036,128]{1,0:T(8,128)}, f32[7036,128]{1,0:T(8,128)}) custom-call(s32[1]{0:T(128)} %bitcast.16.z_ref, bf16[880,128]{1,0:T(8,128)(2,1)S(1)} %maximum_select_fusion.2.one, bf16[880,128]{1,0:T(8,128)(2,1)S(1)} %collective-permute-done.40.one_other, bf16[880,128]{1,0:T(8,128)(2,1)S(1)} %maximum_select_fusion.3.two, ...), custom_call_target="tpu_custom_call" | custom-call | flops 1 | bytes 1 | tf_op jit(solution)/shard_map/adam/pallas_call | solution.py:1148
  299.9 5.4 %collective-permute-done.37.two_other = bf16[880,128]{1,0:T(8,128)(2,1)S(1)} collective-permute-done((bf16[880,128]{1,0:T(8,128)(2,1)S(1)}, bf16[880,128]{1,0:T(8,128)(2,1)S(1)}, u32[]{:S(2)}, u32[]{:S(2)}) %collective-permute-start.37) | collective-permute-done | bytes 225312 | tf_op jit(solution)/shard_map/ppermute | solution.py:1119
  305.4 3.4 %adam.3 = (f32[7036,128]{1,0:T(8,128)}, f32[7036,128]{1,0:T(8,128)}, f32[7036,128]{1,0:T(8,128)}) custom-call(s32[1]{0:T(128)} %bitcast.16.z_ref, bf16[880,128]{1,0:T(8,128)(2,1)S(1)} %maximum_select_fusion.one, bf16[880,128]{1,0:T(8,128)(2,1)S(1)} %collective-permute-done.34.one_other, ...), custom_call_target="tpu_custom_call", output_to_operand_aliasing={{0}: (7, {}), {1}: (8, {}), {2}: (9, {})} | custom-call | flops 1 | bytes 1 | tf_op jit(solution)/shard_map/adam/pallas_call | solution.py:1148
  (148 shorter events, 29.4 us)
Async XLA Ops:
  2.9 26.8 %copy-start.3 = (bf16[3520,128]{1,0:T(8,128)(2,1)}, bf16[3520,128]{1,0:T(8,128)(2,1)S(1)}, u32[]{:S(2)}) copy-start(bf16[3520,128]{1,0:T(8,128)(2,1)S(1)} %slice_bitcast_fusion.1.rest_0_.refs_6_) | copy-start | bytes 2703364
  3.0 47.4 %copy-start.4 = (bf16[3520,128]{1,0:T(8,128)(2,1)}, bf16[3520,128]{1,0:T(8,128)(2,1)S(1)}, u32[]{:S(2)}) copy-start(bf16[3520,128]{1,0:T(8,128)(2,1)S(1)} %pad.4.rest_1_.refs_7_) | copy-start | bytes 2703364
  3.1 23.0 %collective-permute-start = (bf16[3520,128]{1,0:T(8,128)(2,1)S(1)}, bf16[3520,128]{1,0:T(8,128)(2,1)S(1)}, u32[]{:S(2)}, u32[]{:S(2)}) collective-permute-start(bf16[3520,128]{1,0:T(8,128)(2,1)S(1)} %slice_bitcast_fusion.1.rest_0_.refs_6_), channel_id=1, source_target_pairs={{0,2},{1,3},{2,0},{3,1},{4,6},{5,7},{6,4},{7,5},{8,10},{9,11},{10,... | collective-permute-start | bytes 2703368 | tf_op jit(solution)/shard_map/ppermute | solution.py:188
  6.1 24.6 %collective-permute-start.4 = (bf16[3520,128]{1,0:T(8,128)(2,1)S(1)}, bf16[3520,128]{1,0:T(8,128)(2,1)}, u32[]{:S(2)}, u32[]{:S(2)}) collective-permute-start(bf16[3520,128]{1,0:T(8,128)(2,1)S(1)} %slice_bitcast_fusion.1.rest_0_.refs_6_), channel_id=1, source_target_pairs={{0,1},{1,0},{2,3},{3,2},{4,5},{5,4},{6,7},{7,6},{8,9},{9,8},{10,11... | collective-permute-start | bytes 2703368 | tf_op jit(solution)/shard_map/ppermute | solution.py:188
  6.1 22.7 %collective-permute-start.1 = (bf16[3520,128]{1,0:T(8,128)(2,1)S(1)}, bf16[3520,128]{1,0:T(8,128)(2,1)}, u32[]{:S(2)}, u32[]{:S(2)}) collective-permute-start(bf16[3520,128]{1,0:T(8,128)(2,1)S(1)} %pad.4.rest_1_.refs_7_), channel_id=1, source_target_pairs={{0,4},{1,5},{2,6},{3,7},{4,0},{5,1},{6,2},{7,3},{8,12},{9,13},{10,... | collective-permute-start | bytes 2703368 | tf_op jit(solution)/shard_map/ppermute | solution.py:188
  7.6 45.1 %collective-permute-start.5 = (bf16[3520,128]{1,0:T(8,128)(2,1)S(1)}, bf16[3520,128]{1,0:T(8,128)(2,1)}, u32[]{:S(2)}, u32[]{:S(2)}) collective-permute-start(bf16[3520,128]{1,0:T(8,128)(2,1)S(1)} %pad.4.rest_1_.refs_7_), channel_id=1, source_target_pairs={{0,1},{1,0},{2,3},{3,2},{4,5},{5,4},{6,7},{7,6},{8,9},{9,8},{10,11... | collective-permute-start | bytes 2703368 | tf_op jit(solution)/shard_map/ppermute | solution.py:188
  26.2 21.7 %collective-permute-start.2 = (bf16[3520,128]{1,0:T(8,128)(2,1)S(1)}, bf16[3520,128]{1,0:T(8,128)(2,1)}, u32[]{:S(2)}, u32[]{:S(2)}) collective-permute-start(bf16[3520,128]{1,0:T(8,128)(2,1)S(1)} %broadcast_select_fusion.3), channel_id=1, source_target_pairs={{0,4},{1,5},{2,6},{3,7},{4,0},{5,1},{6,2},{7,3},{8,12},{9,13},{10,... | collective-permute-start | bytes 2703368 | tf_op jit(solution)/shard_map/ppermute | solution.py:188
  28.9 21.6 %collective-permute-start.3 = (bf16[3520,128]{1,0:T(8,128)(2,1)S(1)}, bf16[3520,128]{1,0:T(8,128)(2,1)}, u32[]{:S(2)}, u32[]{:S(2)}) collective-permute-start(bf16[3520,128]{1,0:T(8,128)(2,1)S(1)} %broadcast_select_fusion.1), channel_id=1, source_target_pairs={{0,2},{1,3},{2,0},{3,1},{4,6},{5,7},{6,4},{7,5},{8,10},{9,11},{10,... | collective-permute-start | bytes 2703368 | tf_op jit(solution)/shard_map/ppermute | solution.py:188
  29.7 24.5 %collective-permute-start.6 = (bf16[3520,128]{1,0:T(8,128)(2,1)S(1)}, bf16[3520,128]{1,0:T(8,128)(2,1)S(1)}, u32[]{:S(2)}, u32[]{:S(2)}) collective-permute-start(bf16[3520,128]{1,0:T(8,128)(2,1)S(1)} %collective-permute-done.rest_2_.refs_8_), channel_id=1, source_target_pairs={{0,1},{1,0},{2,3},{3,2},{4,5},{5,4},{6,7},{7,6},{8,9},{9,8},{10,11... | collective-permute-start | bytes 2703368 | tf_op jit(solution)/shard_map/ppermute | solution.py:188
  30.7 26.6 %collective-permute-start.7 = (bf16[3520,128]{1,0:T(8,128)(2,1)}, bf16[3520,128]{1,0:T(8,128)(2,1)S(1)}, u32[]{:S(2)}, u32[]{:S(2)}) collective-permute-start(bf16[3520,128]{1,0:T(8,128)(2,1)} %collective-permute-done.1.rest_3_.refs_9_), channel_id=1, source_target_pairs={{0,1},{1,0},{2,3},{3,2},{4,5},{5,4},{6,7},{7,6},{8,9},{9,8},{10,11... | collective-permute-start | bytes 2703368 | tf_op jit(solution)/shard_map/ppermute | solution.py:188
  47.9 9.4 %collective-permute-start.8 = (bf16[3520,128]{1,0:T(8,128)(2,1)}, bf16[3520,128]{1,0:T(8,128)(2,1)}, u32[]{:S(2)}, u32[]{:S(2)}) collective-permute-start(bf16[3520,128]{1,0:T(8,128)(2,1)} %collective-permute-done.2.rest_4_.refs_10_), channel_id=1, source_target_pairs={{0,1},{1,0},{2,3},{3,2},{4,5},{5,4},{6,7},{7,6},{8,9},{9,8},{10,11... | collective-permute-start | bytes 2703368 | tf_op jit(solution)/shard_map/ppermute | solution.py:188
  50.5 6.8 %collective-permute-start.9 = (bf16[3520,128]{1,0:T(8,128)(2,1)}, bf16[3520,128]{1,0:T(8,128)(2,1)}, u32[]{:S(2)}, u32[]{:S(2)}) collective-permute-start(bf16[3520,128]{1,0:T(8,128)(2,1)} %collective-permute-done.3.rest_5_.refs_11_), channel_id=1, source_target_pairs={{0,1},{1,0},{2,3},{3,2},{4,5},{5,4},{6,7},{7,6},{8,9},{9,8},{10,11... | collective-permute-start | bytes 2703368 | tf_op jit(solution)/shard_map/ppermute | solution.py:188
  52.7 24.4 %collective-permute-start.10 = (bf16[3520,128]{1,0:T(8,128)(2,1)}, bf16[3520,128]{1,0:T(8,128)(2,1)S(1)}, u32[]{:S(2)}, u32[]{:S(2)}) collective-permute-start(bf16[3520,128]{1,0:T(8,128)(2,1)} %broadcast_select_fusion.2), channel_id=1, source_target_pairs={{0,4},{1,5},{2,6},{3,7},{4,0},{5,1},{6,2},{7,3},{8,12},{9,13},{10,... | collective-permute-start | bytes 2703368 | tf_op jit(solution)/shard_map/ppermute | solution.py:188
  55.2 22.3 %collective-permute-start.11 = (bf16[3520,128]{1,0:T(8,128)(2,1)}, bf16[3520,128]{1,0:T(8,128)(2,1)S(1)}, u32[]{:S(2)}, u32[]{:S(2)}) collective-permute-start(bf16[3520,128]{1,0:T(8,128)(2,1)} %broadcast_select_fusion), channel_id=1, source_target_pairs={{0,2},{1,3},{2,0},{3,1},{4,6},{5,7},{6,4},{7,5},{8,10},{9,11},{10,... | collective-permute-start | bytes 2703368 | tf_op jit(solution)/shard_map/ppermute | solution.py:188
  77.5 3.7 %collective-permute-start.12 = (bf16[3520,128]{1,0:T(8,128)(2,1)S(1)}, bf16[3520,128]{1,0:T(8,128)(2,1)S(1)}, u32[]{:S(2)}, u32[]{:S(2)}) collective-permute-start(bf16[3520,128]{1,0:T(8,128)(2,1)S(1)} %collective-permute-done.10.refs_12_), channel_id=1, source_target_pairs={{0,1},{1,0},{2,3},{3,2},{4,5},{5,4},{6,7},{7,6},{8,9},{9,8},{10,11... | collective-permute-start | bytes 2703368 | tf_op jit(solution)/shard_map/ppermute | solution.py:188
  77.5 3.9 %collective-permute-start.13 = (bf16[3520,128]{1,0:T(8,128)(2,1)S(1)}, bf16[3520,128]{1,0:T(8,128)(2,1)}, u32[]{:S(2)}, u32[]{:S(2)}) collective-permute-start(bf16[3520,128]{1,0:T(8,128)(2,1)S(1)} %collective-permute-done.11.refs_13_), channel_id=1, source_target_pairs={{0,1},{1,0},{2,3},{3,2},{4,5},{5,4},{6,7},{7,6},{8,9},{9,8},{10,11... | collective-permute-start | bytes 2703368 | tf_op jit(solution)/shard_map/ppermute | solution.py:188
  162.4 9.3 %collective-permute-start.14 = (bf16[3,7040,128]{2,1,0:T(8,128)(2,1)}, bf16[3,7040,128]{2,1,0:T(8,128)(2,1)}, u32[]{:S(2)}, u32[]{:S(2)}) collective-permute-start(bf16[3,7040,128]{2,1,0:T(8,128)(2,1)} %get-tuple-element.130), channel_id=1, source_target_pairs={{0,1},{1,0},{2,3},{3,2},{4,5},{5,4},{6,7},{7,6},{8,9},{9,8},{10,11... | collective-permute-start | bytes 16220168 | tf_op jit(solution)/shard_map/ppermute | solution.py:188
  175.0 17.8 %collective-permute-start.15 = (bf16[1760,128]{1,0:T(8,128)(2,1)}, bf16[1760,128]{1,0:T(8,128)(2,1)S(1)}, u32[]{:S(2)}, u32[]{:S(2)}) collective-permute-start(bf16[1760,128]{1,0:T(8,128)(2,1)} %get-tuple-element.141), channel_id=1, source_target_pairs={{0,4},{1,5},{2,6},{3,7},{4,0},{5,1},{6,2},{7,3},{8,12},{9,13},{10,... | collective-permute-start | bytes 1351688 | tf_op jit(solution)/shard_map/ppermute | solution.py:188
  175.6 17.2 %collective-permute-start.16 = (bf16[1760,128]{1,0:T(8,128)(2,1)}, bf16[1760,128]{1,0:T(8,128)(2,1)S(1)}, u32[]{:S(2)}, u32[]{:S(2)}) collective-permute-start(bf16[1760,128]{1,0:T(8,128)(2,1)} %get-tuple-element.152), channel_id=1, source_target_pairs={{0,2},{1,3},{2,0},{3,1},{4,6},{5,7},{6,4},{7,5},{8,10},{9,11},{10,... | collective-permute-start | bytes 1351688 | tf_op jit(solution)/shard_map/ppermute | solution.py:188
  192.9 4.0 %collective-permute-start.17 = (bf16[1,7040,128]{2,1,0:T(8,128)(2,1)}, bf16[1,7040,128]{2,1,0:T(8,128)(2,1)S(1)}, u32[]{:S(2)}, u32[]{:S(2)}) collective-permute-start(bf16[1,7040,128]{2,1,0:T(8,128)(2,1)} %get-tuple-element.154), channel_id=1, source_target_pairs={{0,1},{1,0},{2,3},{3,2},{4,5},{5,4},{6,7},{7,6},{8,9},{9,8},{10,11... | collective-permute-start | bytes 5406728 | tf_op jit(solution)/shard_map/ppermute | solution.py:188
  192.9 13.4 %collective-permute-start.18 = (bf16[1760,128]{1,0:T(8,128)(2,1)}, bf16[1760,128]{1,0:T(8,128)(2,1)S(1)}, u32[]{:S(2)}, u32[]{:S(2)}) collective-permute-start(bf16[1760,128]{1,0:T(8,128)(2,1)} %get-tuple-element.156), channel_id=1, source_target_pairs={{0,4},{1,5},{2,6},{3,7},{4,0},{5,1},{6,2},{7,3},{8,12},{9,13},{10,... | collective-permute-start | bytes 1351688 | tf_op jit(solution)/shard_map/ppermute | solution.py:188
  194.5 13.4 %collective-permute-start.19 = (bf16[1760,128]{1,0:T(8,128)(2,1)}, bf16[1760,128]{1,0:T(8,128)(2,1)S(1)}, u32[]{:S(2)}, u32[]{:S(2)}) collective-permute-start(bf16[1760,128]{1,0:T(8,128)(2,1)} %get-tuple-element.157), channel_id=1, source_target_pairs={{0,2},{1,3},{2,0},{3,1},{4,6},{5,7},{6,4},{7,5},{8,10},{9,11},{10,... | collective-permute-start | bytes 1351688 | tf_op jit(solution)/shard_map/ppermute | solution.py:188
  201.4 18.0 %collective-permute-start.20 = (bf16[1760,128]{1,0:T(8,128)(2,1)}, bf16[1760,128]{1,0:T(8,128)(2,1)S(1)}, u32[]{:S(2)}, u32[]{:S(2)}) collective-permute-start(bf16[1760,128]{1,0:T(8,128)(2,1)} %get-tuple-element.155), channel_id=1, source_target_pairs={{0,4},{1,5},{2,6},{3,7},{4,0},{5,1},{6,2},{7,3},{8,12},{9,13},{10,... | collective-permute-start | bytes 1351688 | tf_op jit(solution)/shard_map/ppermute | solution.py:188
  203.0 16.4 %collective-permute-start.21 = (bf16[1760,128]{1,0:T(8,128)(2,1)}, bf16[1760,128]{1,0:T(8,128)(2,1)S(1)}, u32[]{:S(2)}, u32[]{:S(2)}) collective-permute-start(bf16[1760,128]{1,0:T(8,128)(2,1)} %get-tuple-element.165), channel_id=1, source_target_pairs={{0,2},{1,3},{2,0},{3,1},{4,6},{5,7},{6,4},{7,5},{8,10},{9,11},{10,... | collective-permute-start | bytes 1351688 | tf_op jit(solution)/shard_map/ppermute | solution.py:188
  207.9 20.7 %collective-permute-start.26 = (bf16[1760,128]{1,0:T(8,128)(2,1)}, bf16[1760,128]{1,0:T(8,128)(2,1)S(1)}, u32[]{:S(2)}, u32[]{:S(2)}) collective-permute-start(bf16[1760,128]{1,0:T(8,128)(2,1)} %get-tuple-element.178), channel_id=1, source_target_pairs={{0,4},{1,5},{2,6},{3,7},{4,0},{5,1},{6,2},{7,3},{8,12},{9,13},{10,... | collective-permute-start | bytes 1351688 | tf_op jit(solution)/shard_map/ppermute | solution.py:188
  208.4 20.2 %collective-permute-start.27 = (bf16[1760,128]{1,0:T(8,128)(2,1)}, bf16[1760,128]{1,0:T(8,128)(2,1)S(1)}, u32[]{:S(2)}, u32[]{:S(2)}) collective-permute-start(bf16[1760,128]{1,0:T(8,128)(2,1)} %get-tuple-element.179), channel_id=1, source_target_pairs={{0,2},{1,3},{2,0},{3,1},{4,6},{5,7},{6,4},{7,5},{8,10},{9,11},{10,... | collective-permute-start | bytes 1351688 | tf_op jit(solution)/shard_map/ppermute | solution.py:188
  223.8 13.6 %collective-permute-start.22 = (bf16[1760,128]{1,0:T(8,128)(2,1)}, bf16[1760,128]{1,0:T(8,128)(2,1)S(1)}, u32[]{:S(2)}, u32[]{:S(2)}) collective-permute-start(bf16[1760,128]{1,0:T(8,128)(2,1)} %get-tuple-element.168), channel_id=1, source_target_pairs={{0,2},{1,3},{2,0},{3,1},{4,6},{5,7},{6,4},{7,5},{8,10},{9,11},{10,... | collective-permute-start | bytes 1351688 | tf_op jit(solution)/shard_map/ppermute | solution.py:188
  224.4 14.8 %collective-permute-start.24 = (bf16[1760,128]{1,0:T(8,128)(2,1)}, bf16[1760,128]{1,0:T(8,128)(2,1)S(1)}, u32[]{:S(2)}, u32[]{:S(2)}) collective-permute-start(bf16[1760,128]{1,0:T(8,128)(2,1)} %get-tuple-element.175), channel_id=1, source_target_pairs={{0,4},{1,5},{2,6},{3,7},{4,0},{5,1},{6,2},{7,3},{8,12},{9,13},{10,... | collective-permute-start | bytes 1351688 | tf_op jit(solution)/shard_map/ppermute | solution.py:188
  232.4 13.3 %collective-permute-start.28 = (bf16[1760,128]{1,0:T(8,128)(2,1)}, bf16[1760,128]{1,0:T(8,128)(2,1)S(1)}, u32[]{:S(2)}, u32[]{:S(2)}) collective-permute-start(bf16[1760,128]{1,0:T(8,128)(2,1)} %get-tuple-element.187), channel_id=1, source_target_pairs={{0,2},{1,3},{2,0},{3,1},{4,6},{5,7},{6,4},{7,5},{8,10},{9,11},{10,... | collective-permute-start | bytes 1351688 | tf_op jit(solution)/shard_map/ppermute | solution.py:188
  234.0 12.9 %collective-permute-start.29 = (bf16[1760,128]{1,0:T(8,128)(2,1)}, bf16[1760,128]{1,0:T(8,128)(2,1)S(1)}, u32[]{:S(2)}, u32[]{:S(2)}) collective-permute-start(bf16[1760,128]{1,0:T(8,128)(2,1)} %get-tuple-element.189), channel_id=1, source_target_pairs={{0,4},{1,5},{2,6},{3,7},{4,0},{5,1},{6,2},{7,3},{8,12},{9,13},{10,... | collective-permute-start | bytes 1351688 | tf_op jit(solution)/shard_map/ppermute | solution.py:188
  237.5 10.6 %collective-permute-start.23 = (bf16[880,128]{1,0:T(8,128)(2,1)S(1)}, bf16[880,128]{1,0:T(8,128)(2,1)S(1)}, u32[]{:S(2)}, u32[]{:S(2)}) collective-permute-start(bf16[880,128]{1,0:T(8,128)(2,1)S(1)} %dynamic-slice_bitcast_fusion.3), channel_id=1, source_target_pairs={{0,8},{8,0},{16,24},{24,16},{1,9},{9,1},{17,25},{25,17},{2,10},{10... | collective-permute-start | bytes 675848 | tf_op jit(solution)/shard_map/ppermute | solution.py:1119
  239.3 10.6 %collective-permute-start.25 = (bf16[880,128]{1,0:T(8,128)(2,1)S(1)}, bf16[880,128]{1,0:T(8,128)(2,1)S(1)}, u32[]{:S(2)}, u32[]{:S(2)}) collective-permute-start(bf16[880,128]{1,0:T(8,128)(2,1)S(1)} %dynamic-slice_bitcast_fusion.2), channel_id=1, source_target_pairs={{0,16},{8,24},{16,0},{24,8},{1,17},{9,25},{17,1},{25,9},{2,18},{10... | collective-permute-start | bytes 675848 | tf_op jit(solution)/shard_map/ppermute | solution.py:1119
  250.0 21.0 %collective-permute-start.30 = (bf16[880,128]{1,0:T(8,128)(2,1)S(1)}, bf16[880,128]{1,0:T(8,128)(2,1)S(1)}, u32[]{:S(2)}, u32[]{:S(2)}) collective-permute-start(bf16[880,128]{1,0:T(8,128)(2,1)S(1)} %dynamic-slice_bitcast_fusion.1), channel_id=1, source_target_pairs={{0,8},{8,0},{16,24},{24,16},{1,9},{9,1},{17,25},{25,17},{2,10},{10... | collective-permute-start | bytes 675848 | tf_op jit(solution)/shard_map/ppermute | solution.py:1119
  250.3 46.3 %copy-start.1 = (f32[900608]{0:T(1024)S(1)}, f32[900608]{0:T(1024)}, u32[]{:S(2)}) copy-start(f32[900608]{0:T(1024)} %param.19) | copy-start | bytes 10807300
  250.3 20.6 %collective-permute-start.31 = (bf16[880,128]{1,0:T(8,128)(2,1)S(1)}, bf16[880,128]{1,0:T(8,128)(2,1)S(1)}, u32[]{:S(2)}, u32[]{:S(2)}) collective-permute-start(bf16[880,128]{1,0:T(8,128)(2,1)S(1)} %dynamic-slice_bitcast_fusion), channel_id=1, source_target_pairs={{0,16},{8,24},{16,0},{24,8},{1,17},{9,25},{17,1},{25,9},{2,18},{10... | collective-permute-start | bytes 675848 | tf_op jit(solution)/shard_map/ppermute | solution.py:1119
  253.2 14.3 %collective-permute-start.38 = (bf16[440,128]{1,0:T(8,128)(2,1)S(1)}, bf16[440,128]{1,0:T(8,128)(2,1)S(1)}, u32[]{:S(2)}, u32[]{:S(2)}) collective-permute-start(bf16[440,128]{1,0:T(8,128)(2,1)S(1)} %dynamic-slice_bitcast_fusion.5), channel_id=1, source_target_pairs={{0,16},{8,24},{16,0},{24,8},{1,17},{9,25},{17,1},{25,9},{2,18},{10... | collective-permute-start | bytes 337928 | tf_op jit(solution)/shard_map/ppermute | solution.py:1119
  253.5 14.2 %collective-permute-start.41 = (bf16[440,128]{1,0:T(8,128)(2,1)S(1)}, bf16[440,128]{1,0:T(8,128)(2,1)S(1)}, u32[]{:S(2)}, u32[]{:S(2)}) collective-permute-start(bf16[440,128]{1,0:T(8,128)(2,1)S(1)} %dynamic-slice_bitcast_fusion.4), channel_id=1, source_target_pairs={{0,8},{8,0},{16,24},{24,16},{1,9},{9,1},{17,25},{25,17},{2,10},{10... | collective-permute-start | bytes 337928 | tf_op jit(solution)/shard_map/ppermute | solution.py:1119
  267.6 8.9 %collective-permute-start.39 = (bf16[440,128]{1,0:T(8,128)(2,1)S(1)}, bf16[440,128]{1,0:T(8,128)(2,1)S(1)}, u32[]{:S(2)}, u32[]{:S(2)}) collective-permute-start(bf16[440,128]{1,0:T(8,128)(2,1)S(1)} %bitcast_add_fusion.5), channel_id=1, source_target_pairs={{0,16},{8,24},{16,0},{24,8},{1,17},{9,25},{17,1},{25,9},{2,18},{10... | collective-permute-start | bytes 337928 | tf_op jit(solution)/shard_map/ppermute | solution.py:1119
  267.7 10.9 %collective-permute-start.42 = (bf16[440,128]{1,0:T(8,128)(2,1)S(1)}, bf16[440,128]{1,0:T(8,128)(2,1)S(1)}, u32[]{:S(2)}, u32[]{:S(2)}) collective-permute-start(bf16[440,128]{1,0:T(8,128)(2,1)S(1)} %bitcast_add_fusion.4), channel_id=1, source_target_pairs={{0,8},{8,0},{16,24},{24,16},{1,9},{9,1},{17,25},{25,17},{2,10},{10... | collective-permute-start | bytes 337928 | tf_op jit(solution)/shard_map/ppermute | solution.py:1119
  271.0 25.6 %copy-start = (f32[900608]{0:T(1024)S(1)}, f32[900608]{0:T(1024)}, u32[]{:S(2)}) copy-start(f32[900608]{0:T(1024)} %param.18) | copy-start | bytes 10807300
  271.0 9.0 %collective-permute-start.32 = (bf16[440,128]{1,0:T(8,128)(2,1)S(1)}, bf16[440,128]{1,0:T(8,128)(2,1)S(1)}, u32[]{:S(2)}, u32[]{:S(2)}) collective-permute-start(bf16[440,128]{1,0:T(8,128)(2,1)S(1)} %dynamic-slice_bitcast_fusion.7), channel_id=1, source_target_pairs={{0,16},{8,24},{16,0},{24,8},{1,17},{9,25},{17,1},{25,9},{2,18},{10... | collective-permute-start | bytes 337928 | tf_op jit(solution)/shard_map/ppermute | solution.py:1119
  271.2 14.0 %collective-permute-start.35 = (bf16[440,128]{1,0:T(8,128)(2,1)S(1)}, bf16[440,128]{1,0:T(8,128)(2,1)S(1)}, u32[]{:S(2)}, u32[]{:S(2)}) collective-permute-start(bf16[440,128]{1,0:T(8,128)(2,1)S(1)} %dynamic-slice_bitcast_fusion.6), channel_id=1, source_target_pairs={{0,8},{8,0},{16,24},{24,16},{1,9},{9,1},{17,25},{25,17},{2,10},{10... | collective-permute-start | bytes 337928 | tf_op jit(solution)/shard_map/ppermute | solution.py:1119
  276.5 20.1 %collective-permute-start.40 = (bf16[880,128]{1,0:T(8,128)(2,1)S(1)}, bf16[880,128]{1,0:T(8,128)(2,1)S(1)}, u32[]{:S(2)}, u32[]{:S(2)}) collective-permute-start(bf16[880,128]{1,0:T(8,128)(2,1)S(1)} %maximum_select_fusion.2.one), channel_id=1, source_target_pairs={{0,8},{8,0},{16,24},{24,16},{1,9},{9,1},{17,25},{25,17},{2,10},{10... | collective-permute-start | bytes 675848 | tf_op jit(solution)/shard_map/ppermute | solution.py:1119
  278.7 17.9 %collective-permute-start.43 = (bf16[880,128]{1,0:T(8,128)(2,1)S(1)}, bf16[880,128]{1,0:T(8,128)(2,1)S(1)}, u32[]{:S(2)}, u32[]{:S(2)}) collective-permute-start(bf16[880,128]{1,0:T(8,128)(2,1)S(1)} %maximum_select_fusion.3.two), channel_id=1, source_target_pairs={{0,16},{8,24},{16,0},{24,8},{1,17},{9,25},{17,1},{25,9},{2,18},{10... | collective-permute-start | bytes 675848 | tf_op jit(solution)/shard_map/ppermute | solution.py:1119
  280.1 13.5 %collective-permute-start.33 = (bf16[440,128]{1,0:T(8,128)(2,1)S(1)}, bf16[440,128]{1,0:T(8,128)(2,1)S(1)}, u32[]{:S(2)}, u32[]{:S(2)}) collective-permute-start(bf16[440,128]{1,0:T(8,128)(2,1)S(1)} %bitcast_add_fusion.7), channel_id=1, source_target_pairs={{0,16},{8,24},{16,0},{24,8},{1,17},{9,25},{17,1},{25,9},{2,18},{10... | collective-permute-start | bytes 337928 | tf_op jit(solution)/shard_map/ppermute | solution.py:1119
  285.2 11.2 %collective-permute-start.36 = (bf16[440,128]{1,0:T(8,128)(2,1)S(1)}, bf16[440,128]{1,0:T(8,128)(2,1)S(1)}, u32[]{:S(2)}, u32[]{:S(2)}) collective-permute-start(bf16[440,128]{1,0:T(8,128)(2,1)S(1)} %bitcast_add_fusion.6), channel_id=1, source_target_pairs={{0,8},{8,0},{16,24},{24,16},{1,9},{9,1},{17,25},{25,17},{2,10},{10... | collective-permute-start | bytes 337928 | tf_op jit(solution)/shard_map/ppermute | solution.py:1119
  293.7 6.2 %collective-permute-start.34 = (bf16[880,128]{1,0:T(8,128)(2,1)S(1)}, bf16[880,128]{1,0:T(8,128)(2,1)S(1)}, u32[]{:S(2)}, u32[]{:S(2)}) collective-permute-start(bf16[880,128]{1,0:T(8,128)(2,1)S(1)} %maximum_select_fusion.one), channel_id=1, source_target_pairs={{0,8},{8,0},{16,24},{24,16},{1,9},{9,1},{17,25},{25,17},{2,10},{10... | collective-permute-start | bytes 675848 | tf_op jit(solution)/shard_map/ppermute | solution.py:1119
  296.5 8.9 %collective-permute-start.37 = (bf16[880,128]{1,0:T(8,128)(2,1)S(1)}, bf16[880,128]{1,0:T(8,128)(2,1)S(1)}, u32[]{:S(2)}, u32[]{:S(2)}) collective-permute-start(bf16[880,128]{1,0:T(8,128)(2,1)S(1)} %maximum_select_fusion.1.two), channel_id=1, source_target_pairs={{0,16},{8,24},{16,0},{24,8},{1,17},{9,25},{17,1},{25,9},{2,18},{10... | collective-permute-start | bytes 675848 | tf_op jit(solution)/shard_map/ppermute | solution.py:1119
  (24 other events, 219.6 us)

commit v9 on v8

--- a/solution.py
+++ b/solution.py
@@ -485,11 +485,11 @@
         pl.when(r > 0)(lambda: copy(n, r - 1).wait())
 
     def first(t, _):
-        cols = at(t, 384)
+        cols = at(t, D)
         hid[:, cols] = x_ref[0, :, cols].astype(F32) + (dot(att_ref[0], wout[:, cols]) + vec[0:1, cols])
         return 0
 
-    lax.fori_loop(0, D // 384, first, 0)
+    lax.fori_loop(0, D // D, first, 0)
 
     def norm_one(b, _):
         rows = at(b, TB)
@@ -586,11 +586,11 @@
     sg_ref[3:4, :] += jnp.sum(dl, axis=0, keepdims=True)
 
     def spread(t, _):
-        cols = at(t, 384)
+        cols = at(t, D)
         hid[:, cols] = cot_ref[0, :, cols].astype(F32) + dot(dstu_ref[0], wstu[cols, :], NT)
         return 0
 
-    lax.fori_loop(0, D // 384, spread, 0)
+    lax.fori_loop(0, D // D, spread, 0)
 
     def back_two(b, _):
         rows = at(b, TB)

time: 309 us -> 308 us (level)
  no operation moved by 1% of the time
where the time goes in v9:
time: 308 us
  Pallas kernels  156 us (51%)
  waiting for transfers between devices  90.7 us (29%)
  starting transfers between devices  41 us (13%)
  other arithmetic  10 us (3%)
  local copies, waits for them, and re-layouts  8.31 us (3%)
    pallas_call x1, Pallas kernels, middle(): pl.pallas_call(kernel, grid=(rows,), in_specs=[row_spec(LEN, D), row_spec...  54.4 us
    ppermute x28, waiting for transfers between devices, swap(): return lax.ppermute(v, 'fsdp', [(d, d ^ bit) for d in range(8)])  50 us
    ppermute x16, waiting for transfers between devices, sum_replicas(): lax.ppermute(v, 'rep', [(i, i ^ bit) for i in range(4)])  40.6 us
    pallas_call x1, Pallas kernels, late_pairs(): pl.pallas_call(functools.partial(late_pair_kernel, shard_rows), in_specs=...  24.7 us
    ppermute x28, starting transfers between devices, swap(): return lax.ppermute(v, 'fsdp', [(d, d ^ bit) for d in range(8)])  24.1 us
    pallas_call x1, Pallas kernels, attend(): pl.pallas_call(kernel, grid=(steps, rows), in_specs=[once(*v.shape) for v...  18.8 us
    pallas_call x6, Pallas kernels, combine(): pl.pallas_call(functools.partial(combine_kernel, plan, len(extras)), in_s...  17.8 us
    ppermute x16, starting transfers between devices, sum_replicas(): lax.ppermute(v, 'rep', [(i, i ^ bit) for i in range(4)])  16.8 us
  transfers between devices with their start and end apart: 44, of which 23 were waited for; matrix products, arithmetic and copies ran while one was open for 3% of the time, Pallas kernels for 23%

profile of v9, /device:TPU:0, one launch (start us, length us, event | category | flops | bytes accessed | tf_op | source)
XLA Modules:
  0.0 307.6 jit_solution(5509341370766532151)
XLA Ops:
  0.6 2.2 convert.4
  3.1 3.0 collective-permute-start
  6.1 1.5 collective-permute-start.1
  7.8 18.2 %collective-permute-done.rest_2_.refs_8_ = bf16[3520,128]{1,0:T(8,128)(2,1)S(1)} collective-permute-done((bf16[3520,128]{1,0:T(8,128)(2,1)S(1)}, bf16[3520,128]{1,0:T(8,128)(2,1)S(1)}, u32[]{:S(2)}, u32[]{:S(2)}) %collective-permute-start) | collective-permute-done | bytes 901152 | tf_op jit(solution)/shard_map/ppermute | solution.py:188
  26.2 1.8 collective-permute-start.2
  31.2 16.7 %collective-permute-done.2.rest_4_.refs_10_ = bf16[3520,128]{1,0:T(8,128)(2,1)} collective-permute-done((bf16[3520,128]{1,0:T(8,128)(2,1)S(1)}, bf16[3520,128]{1,0:T(8,128)(2,1)}, u32[]{:S(2)}, u32[]{:S(2)}) %collective-permute-start.2) | collective-permute-done | bytes 901152 | tf_op jit(solution)/shard_map/ppermute | solution.py:188
  47.9 2.6 collective-permute-done.3.rest_5_.refs_11_
  50.5 2.2 broadcast_select_fusion
  52.7 1.5 collective-permute-start.10
  58.3 18.8 %attend.1 = (bf16[2,512,768]{2,1,0:T(8,128)(2,1)}, bf16[2,512,768]{2,1,0:T(8,128)(2,1)}, bf16[2,512,768]{2,1,0:T(8,128)(2,1)}, bf16[2,6,256,1280]{3,2,1,0:T(8,12...) custom-call(bf16[2,512,768]{2,1,0:T(8,128)(2,1)} %refs_0_.1, s32[2,512,1]{2,1,0:T(8,128)} %copy.26.segc_ref.refs_2_, ...), custom_call_target="tpu_custom_call" | custom-call | flops 1 | bytes 1 | tf_op jit(solution)/shard_map/attend/pallas_call | solution.py:444
  79.5 1.7 collective-permute-done.12.refs_20_
  82.1 54.4 %middle.1 = (bf16[2,512,768]{2,1,0:T(8,128)(2,1)}, bf16[2,512,768]{2,1,0:T(8,128)(2,1)}, bf16[2,512,3072]{2,1,0:T(8,128)(2,1)}, bf16[2,512,768]{2,1,0:T(8,128)(2...) custom-call(bf16[2,512,768]{2,1,0:T(8,128)(2,1)} %refs_0_.1, ...), custom_call_target="tpu_custom_call" | custom-call | flops 1 | bytes 1 | tf_op jit(solution)/shard_map/middle/pallas_call | solution.py:701
  136.6 24.7 %late_grads.1 = (bf16[3,7040,128]{2,1,0:T(8,128)(2,1)}, bf16[3,7040,128]{2,1,0:T(8,128)(2,1)}, f32[240,128]{1,0:T(8,128)}) custom-call(s32[1]{0:T(128)} %bitcast.1.me_ref, bf16[1024,768]{1,0:T(8,128)(2,1)} %bitcast.74, bf16[1024,768]{1,0:T(8,128)(2,1)} %bitcast.89, bf16[1024,768]{1,0:T(8,128)(2,1)} %bitcast.87, bf16[1024,3072]{1,0:T(8,128)(2,1)} %bitcast.73, ...), custom_call_target="tpu_custom_call" | custom-call | flops 1 | bytes 1 | tf_op jit(solution)/shard_map/late_grads/pallas_call | solution.py:1023
  161.4 7.8 %retreat.2 = (bf16[2,512,768]{2,1,0:T(8,128)(2,1)}, bf16[2,512,768]{2,1,0:T(8,128)(2,1)}, bf16[2,512,768]{2,1,0:T(8,128)(2,1)}, f32[8,768]{1,0:T(8,128)}) custom-call(bf16[2,512,768]{2,1,0:T(8,128)(2,1)} %get-tuple-element.115.refs_0_, bf16[2,512,768]{2,1,0:T(8,128)(2,1)} %get-tuple-element.116.refs_1_, bf16[2,512,768]{2,1,0:T(8,128)(2,1)} %get-tuple-element.117.refs_2_, ...), custom_call_target="tpu_custom_call" | custom-call | flops 1 | bytes 1 | tf_op jit(solution)/shard_map/retreat/pallas_call | solution.py:786
  170.6 3.3 %combine_one.1 = (bf16[1760,128]{1,0:T(8,128)(2,1)}, bf16[1760,128]{1,0:T(8,128)(2,1)}, bf16[1760,128]{1,0:T(8,128)(2,1)}, bf16[1760,128]{1,0:T(8,128)(2,1)}) custom-call(s32[1]{0:T(128)} %bitcast.1.me_ref, bf16[3,7040,128]{2,1,0:T(8,128)(2,1)} %get-tuple-element.139.refs_0_.refs_2_, bf16[3,7040,128]{2,1,0:T(8,128)(2,1)} %collective-permute-done.14.refs_1_.refs_3_, ...), custom_call_target="tpu_custom_call" | custom-call | flops 1 | bytes 1 | tf_op jit(solution)/shard_map/combine_one/pallas_call | solution.py:1096
  175.0 7.9 %retreat.3 = (bf16[2,512,768]{2,1,0:T(8,128)(2,1)}, bf16[2,512,768]{2,1,0:T(8,128)(2,1)}, bf16[2,512,768]{2,1,0:T(8,128)(2,1)}, f32[8,768]{1,0:T(8,128)}) custom-call(bf16[2,512,768]{2,1,0:T(8,128)(2,1)} %get-tuple-element.115.refs_0_, bf16[2,512,768]{2,1,0:T(8,128)(2,1)} %get-tuple-element.116.refs_1_, ...), custom_call_target="tpu_custom_call", output_to_operand_aliasing={{0}: (5, {}), {1}: (6, {}), {2}: (7, {})} | custom-call | flops 1 | bytes 1 | tf_op jit(solution)/shard_map/retreat/pallas_call | solution.py:786
  182.9 8.8 %early_grads.1 = (bf16[1,7040,128]{2,1,0:T(8,128)(2,1)}, bf16[1,7040,128]{2,1,0:T(8,128)(2,1)}) custom-call(s32[1]{0:T(128)} %bitcast.1.me_ref, bf16[1024,768]{1,0:T(8,128)(2,1)} %bitcast.71, bf16[1024,768]{1,0:T(8,128)(2,1)} %bitcast.68, bf16[1024,768]{1,0:T(8,128)(2,1)} %bitcast.69, bf16[1024,768]{1,0:T(8,128)(2,1)} %bitcast.70, ...), custom_call_target="tpu_custom_call" | custom-call | flops 1 | bytes 1 | tf_op jit(solution)/shard_map/early_grads/pallas_call | solution.py:1045
  191.8 1.6 collective-permute-start.18
  193.4 1.5 collective-permute-start.19
  197.0 3.3 %combine_two.1 = (bf16[1760,128]{1,0:T(8,128)(2,1)}, bf16[1760,128]{1,0:T(8,128)(2,1)}, bf16[1760,128]{1,0:T(8,128)(2,1)}, bf16[1760,128]{1,0:T(8,128)(2,1)}) custom-call(s32[1]{0:T(128)} %bitcast.1.me_ref, bf16[3,7040,128]{2,1,0:T(8,128)(2,1)} %get-tuple-element.139.refs_0_.refs_2_, bf16[3,7040,128]{2,1,0:T(8,128)(2,1)} %collective-permute-done.14.refs_1_.refs_3_, ...), custom_call_target="tpu_custom_call" | custom-call | flops 1 | bytes 1 | tf_op jit(solution)/shard_map/combine_two/pallas_call | solution.py:1096
  200.3 1.6 collective-permute-start.20
  201.9 1.5 collective-permute-start.21
  203.4 1.8 collective-permute-done.18.refs_4_
  205.2 1.6 collective-permute-done.19.refs_5_
  208.8 9.5 %project_back.1 = bf16[2,512,768]{2,1,0:T(8,128)(2,1)} custom-call(bf16[2,512,768]{2,1,0:T(8,128)(2,1)} %get-tuple-element.158.dq_ref, bf16[2,512,768]{2,1,0:T(8,128)(2,1)} %get-tuple-element.159.dk_ref, bf16[2,512,768]{2,1,0:T(8,128)(2,1)} %get-tuple-element.160.dv_ref, f32[2,512,768]{2,1,0:T(8,128)} %get-tuple-element.161.dh1_ref, ...), custom_call_target="tpu_custom_call" | custom-call | flops 1 | bytes 1 | tf_op jit(solution)/shard_map/project_back/pallas_call | solution.py:814
  219.8 2.8 combine_three.2
  224.7 2.8 combine_own.2
  228.4 2.8 combine_three.3
  231.3 1.6 collective-permute-start.28
  233.4 2.8 collective-permute-done.22
  236.4 1.6 collective-permute-start.23
  238.2 2.7 collective-permute-start.25
  240.8 2.8 combine_own.3
  246.9 1.9 collective-permute-done.25
  249.2 2.8 collective-permute-start.31
  252.3 1.8 collective-permute-start.41
  254.2 12.2 %collective-permute-done.38 = bf16[440,128]{1,0:T(8,128)(2,1)S(1)} collective-permute-done((bf16[440,128]{1,0:T(8,128)(2,1)S(1)}, bf16[440,128]{1,0:T(8,128)(2,1)S(1)}, u32[]{:S(2)}, u32[]{:S(2)}) %collective-permute-start.38) | collective-permute-done | bytes 112672 | tf_op jit(solution)/shard_map/ppermute | solution.py:1119
  266.5 3.3 %collective-permute-start.42 = (bf16[440,128]{1,0:T(8,128)(2,1)S(1)}, bf16[440,128]{1,0:T(8,128)(2,1)S(1)}, u32[]{:S(2)}, u32[]{:S(2)}) collective-permute-start(bf16[440,128]{1,0:T(8,128)(2,1)S(1)} %bitcast_add_fusion.4), channel_id=1, source_target_pairs={{0,8},{8,0},{16,24},{24,16},{1,9},{9,1},{17,25},{25,17},{2,10},{10... | collective-permute-start | bytes 337928 | tf_op jit(solution)/shard_map/ppermute | solution.py:1119
  270.0 1.8 collective-permute-start.35
  271.8 3.5 %collective-permute-done.39 = bf16[440,128]{1,0:T(8,128)(2,1)S(1)} collective-permute-done((bf16[440,128]{1,0:T(8,128)(2,1)S(1)}, bf16[440,128]{1,0:T(8,128)(2,1)S(1)}, u32[]{:S(2)}, u32[]{:S(2)}) %collective-permute-start.39) | collective-permute-done | bytes 112672 | tf_op jit(solution)/shard_map/ppermute | solution.py:1119
  275.4 2.1 collective-permute-done.42
  278.9 1.8 collective-permute-start.33
  280.6 3.5 %collective-permute-done.35 = bf16[440,128]{1,0:T(8,128)(2,1)S(1)} collective-permute-done((bf16[440,128]{1,0:T(8,128)(2,1)S(1)}, bf16[440,128]{1,0:T(8,128)(2,1)S(1)}, u32[]{:S(2)}, u32[]{:S(2)}) %collective-permute-start.35) | collective-permute-done | bytes 112672 | tf_op jit(solution)/shard_map/ppermute | solution.py:1119
  284.2 8.3 %collective-permute-done.33 = bf16[440,128]{1,0:T(8,128)(2,1)S(1)} collective-permute-done((bf16[440,128]{1,0:T(8,128)(2,1)S(1)}, bf16[440,128]{1,0:T(8,128)(2,1)S(1)}, u32[]{:S(2)}, u32[]{:S(2)}) %collective-permute-start.33) | collective-permute-done | bytes 112672 | tf_op jit(solution)/shard_map/ppermute | solution.py:1119
  292.6 2.6 collective-permute-done.36
  295.4 3.3 %adam.2 = (f32[7036,128]{1,0:T(8,128)}, f32[7036,128]{1,0:T(8,128)}, f32[7036,128]{1,0:T(8,128)}) custom-call(s32[1]{0:T(128)} %bitcast.16.z_ref, bf16[880,128]{1,0:T(8,128)(2,1)S(1)} %maximum_select_fusion.2.one, bf16[880,128]{1,0:T(8,128)(2,1)S(1)} %collective-permute-done.40.one_other, bf16[880,128]{1,0:T(8,128)(2,1)S(1)} %maximum_select_fusion.3.two, ...), custom_call_target="tpu_custom_call" | custom-call | flops 1 | bytes 1 | tf_op jit(solution)/shard_map/adam/pallas_call | solution.py:1148
  298.7 5.4 %collective-permute-done.37.two_other = bf16[880,128]{1,0:T(8,128)(2,1)S(1)} collective-permute-done((bf16[880,128]{1,0:T(8,128)(2,1)S(1)}, bf16[880,128]{1,0:T(8,128)(2,1)S(1)}, u32[]{:S(2)}, u32[]{:S(2)}) %collective-permute-start.37) | collective-permute-done | bytes 225312 | tf_op jit(solution)/shard_map/ppermute | solution.py:1119
  304.2 3.4 %adam.3 = (f32[7036,128]{1,0:T(8,128)}, f32[7036,128]{1,0:T(8,128)}, f32[7036,128]{1,0:T(8,128)}) custom-call(s32[1]{0:T(128)} %bitcast.16.z_ref, bf16[880,128]{1,0:T(8,128)(2,1)S(1)} %maximum_select_fusion.one, bf16[880,128]{1,0:T(8,128)(2,1)S(1)} %collective-permute-done.34.one_other, ...), custom_call_target="tpu_custom_call", output_to_operand_aliasing={{0}: (7, {}), {1}: (8, {}), {2}: (9, {})} | custom-call | flops 1 | bytes 1 | tf_op jit(solution)/shard_map/adam/pallas_call | solution.py:1148
  (148 shorter events, 29.3 us)
Async XLA Ops:
  2.9 26.8 %copy-start.3 = (bf16[3520,128]{1,0:T(8,128)(2,1)}, bf16[3520,128]{1,0:T(8,128)(2,1)S(1)}, u32[]{:S(2)}) copy-start(bf16[3520,128]{1,0:T(8,128)(2,1)S(1)} %slice_bitcast_fusion.1.rest_0_.refs_6_) | copy-start | bytes 2703364
  3.0 47.4 %copy-start.4 = (bf16[3520,128]{1,0:T(8,128)(2,1)}, bf16[3520,128]{1,0:T(8,128)(2,1)S(1)}, u32[]{:S(2)}) copy-start(bf16[3520,128]{1,0:T(8,128)(2,1)S(1)} %pad.4.rest_1_.refs_7_) | copy-start | bytes 2703364
  3.1 23.0 %collective-permute-start = (bf16[3520,128]{1,0:T(8,128)(2,1)S(1)}, bf16[3520,128]{1,0:T(8,128)(2,1)S(1)}, u32[]{:S(2)}, u32[]{:S(2)}) collective-permute-start(bf16[3520,128]{1,0:T(8,128)(2,1)S(1)} %slice_bitcast_fusion.1.rest_0_.refs_6_), channel_id=1, source_target_pairs={{0,2},{1,3},{2,0},{3,1},{4,6},{5,7},{6,4},{7,5},{8,10},{9,11},{10,... | collective-permute-start | bytes 2703368 | tf_op jit(solution)/shard_map/ppermute | solution.py:188
  6.1 24.6 %collective-permute-start.4 = (bf16[3520,128]{1,0:T(8,128)(2,1)S(1)}, bf16[3520,128]{1,0:T(8,128)(2,1)}, u32[]{:S(2)}, u32[]{:S(2)}) collective-permute-start(bf16[3520,128]{1,0:T(8,128)(2,1)S(1)} %slice_bitcast_fusion.1.rest_0_.refs_6_), channel_id=1, source_target_pairs={{0,1},{1,0},{2,3},{3,2},{4,5},{5,4},{6,7},{7,6},{8,9},{9,8},{10,11... | collective-permute-start | bytes 2703368 | tf_op jit(solution)/shard_map/ppermute | solution.py:188
  6.1 22.7 %collective-permute-start.1 = (bf16[3520,128]{1,0:T(8,128)(2,1)S(1)}, bf16[3520,128]{1,0:T(8,128)(2,1)}, u32[]{:S(2)}, u32[]{:S(2)}) collective-permute-start(bf16[3520,128]{1,0:T(8,128)(2,1)S(1)} %pad.4.rest_1_.refs_7_), channel_id=1, source_target_pairs={{0,4},{1,5},{2,6},{3,7},{4,0},{5,1},{6,2},{7,3},{8,12},{9,13},{10,... | collective-permute-start | bytes 2703368 | tf_op jit(solution)/shard_map/ppermute | solution.py:188
  7.6 45.1 %collective-permute-start.5 = (bf16[3520,128]{1,0:T(8,128)(2,1)S(1)}, bf16[3520,128]{1,0:T(8,128)(2,1)}, u32[]{:S(2)}, u32[]{:S(2)}) collective-permute-start(bf16[3520,128]{1,0:T(8,128)(2,1)S(1)} %pad.4.rest_1_.refs_7_), channel_id=1, source_target_pairs={{0,1},{1,0},{2,3},{3,2},{4,5},{5,4},{6,7},{7,6},{8,9},{9,8},{10,11... | collective-permute-start | bytes 2703368 | tf_op jit(solution)/shard_map/ppermute | solution.py:188
  26.2 21.7 %collective-permute-start.2 = (bf16[3520,128]{1,0:T(8,128)(2,1)S(1)}, bf16[3520,128]{1,0:T(8,128)(2,1)}, u32[]{:S(2)}, u32[]{:S(2)}) collective-permute-start(bf16[3520,128]{1,0:T(8,128)(2,1)S(1)} %broadcast_select_fusion.3), channel_id=1, source_target_pairs={{0,4},{1,5},{2,6},{3,7},{4,0},{5,1},{6,2},{7,3},{8,12},{9,13},{10,... | collective-permute-start | bytes 2703368 | tf_op jit(solution)/shard_map/ppermute | solution.py:188
  28.9 21.6 %collective-permute-start.3 = (bf16[3520,128]{1,0:T(8,128)(2,1)S(1)}, bf16[3520,128]{1,0:T(8,128)(2,1)}, u32[]{:S(2)}, u32[]{:S(2)}) collective-permute-start(bf16[3520,128]{1,0:T(8,128)(2,1)S(1)} %broadcast_select_fusion.1), channel_id=1, source_target_pairs={{0,2},{1,3},{2,0},{3,1},{4,6},{5,7},{6,4},{7,5},{8,10},{9,11},{10,... | collective-permute-start | bytes 2703368 | tf_op jit(solution)/shard_map/ppermute | solution.py:188
  29.7 24.5 %collective-permute-start.6 = (bf16[3520,128]{1,0:T(8,128)(2,1)S(1)}, bf16[3520,128]{1,0:T(8,128)(2,1)S(1)}, u32[]{:S(2)}, u32[]{:S(2)}) collective-permute-start(bf16[3520,128]{1,0:T(8,128)(2,1)S(1)} %collective-permute-done.rest_2_.refs_8_), channel_id=1, source_target_pairs={{0,1},{1,0},{2,3},{3,2},{4,5},{5,4},{6,7},{7,6},{8,9},{9,8},{10,11... | collective-permute-start | bytes 2703368 | tf_op jit(solution)/shard_map/ppermute | solution.py:188
  30.7 26.6 %collective-permute-start.7 = (bf16[3520,128]{1,0:T(8,128)(2,1)}, bf16[3520,128]{1,0:T(8,128)(2,1)S(1)}, u32[]{:S(2)}, u32[]{:S(2)}) collective-permute-start(bf16[3520,128]{1,0:T(8,128)(2,1)} %collective-permute-done.1.rest_3_.refs_9_), channel_id=1, source_target_pairs={{0,1},{1,0},{2,3},{3,2},{4,5},{5,4},{6,7},{7,6},{8,9},{9,8},{10,11... | collective-permute-start | bytes 2703368 | tf_op jit(solution)/shard_map/ppermute | solution.py:188
  47.9 9.4 %collective-permute-start.8 = (bf16[3520,128]{1,0:T(8,128)(2,1)}, bf16[3520,128]{1,0:T(8,128)(2,1)}, u32[]{:S(2)}, u32[]{:S(2)}) collective-permute-start(bf16[3520,128]{1,0:T(8,128)(2,1)} %collective-permute-done.2.rest_4_.refs_10_), channel_id=1, source_target_pairs={{0,1},{1,0},{2,3},{3,2},{4,5},{5,4},{6,7},{7,6},{8,9},{9,8},{10,11... | collective-permute-start | bytes 2703368 | tf_op jit(solution)/shard_map/ppermute | solution.py:188
  50.5 6.8 %collective-permute-start.9 = (bf16[3520,128]{1,0:T(8,128)(2,1)}, bf16[3520,128]{1,0:T(8,128)(2,1)}, u32[]{:S(2)}, u32[]{:S(2)}) collective-permute-start(bf16[3520,128]{1,0:T(8,128)(2,1)} %collective-permute-done.3.rest_5_.refs_11_), channel_id=1, source_target_pairs={{0,1},{1,0},{2,3},{3,2},{4,5},{5,4},{6,7},{7,6},{8,9},{9,8},{10,11... | collective-permute-start | bytes 2703368 | tf_op jit(solution)/shard_map/ppermute | solution.py:188
  52.7 24.4 %collective-permute-start.10 = (bf16[3520,128]{1,0:T(8,128)(2,1)}, bf16[3520,128]{1,0:T(8,128)(2,1)S(1)}, u32[]{:S(2)}, u32[]{:S(2)}) collective-permute-start(bf16[3520,128]{1,0:T(8,128)(2,1)} %broadcast_select_fusion.2), channel_id=1, source_target_pairs={{0,4},{1,5},{2,6},{3,7},{4,0},{5,1},{6,2},{7,3},{8,12},{9,13},{10,... | collective-permute-start | bytes 2703368 | tf_op jit(solution)/shard_map/ppermute | solution.py:188
  55.2 22.3 %collective-permute-start.11 = (bf16[3520,128]{1,0:T(8,128)(2,1)}, bf16[3520,128]{1,0:T(8,128)(2,1)S(1)}, u32[]{:S(2)}, u32[]{:S(2)}) collective-permute-start(bf16[3520,128]{1,0:T(8,128)(2,1)} %broadcast_select_fusion), channel_id=1, source_target_pairs={{0,2},{1,3},{2,0},{3,1},{4,6},{5,7},{6,4},{7,5},{8,10},{9,11},{10,... | collective-permute-start | bytes 2703368 | tf_op jit(solution)/shard_map/ppermute | solution.py:188
  77.5 3.7 %collective-permute-start.12 = (bf16[3520,128]{1,0:T(8,128)(2,1)S(1)}, bf16[3520,128]{1,0:T(8,128)(2,1)S(1)}, u32[]{:S(2)}, u32[]{:S(2)}) collective-permute-start(bf16[3520,128]{1,0:T(8,128)(2,1)S(1)} %collective-permute-done.10.refs_12_), channel_id=1, source_target_pairs={{0,1},{1,0},{2,3},{3,2},{4,5},{5,4},{6,7},{7,6},{8,9},{9,8},{10,11... | collective-permute-start | bytes 2703368 | tf_op jit(solution)/shard_map/ppermute | solution.py:188
  77.5 3.9 %collective-permute-start.13 = (bf16[3520,128]{1,0:T(8,128)(2,1)S(1)}, bf16[3520,128]{1,0:T(8,128)(2,1)}, u32[]{:S(2)}, u32[]{:S(2)}) collective-permute-start(bf16[3520,128]{1,0:T(8,128)(2,1)S(1)} %collective-permute-done.11.refs_13_), channel_id=1, source_target_pairs={{0,1},{1,0},{2,3},{3,2},{4,5},{5,4},{6,7},{7,6},{8,9},{9,8},{10,11... | collective-permute-start | bytes 2703368 | tf_op jit(solution)/shard_map/ppermute | solution.py:188
  161.3 9.3 %collective-permute-start.14 = (bf16[3,7040,128]{2,1,0:T(8,128)(2,1)}, bf16[3,7040,128]{2,1,0:T(8,128)(2,1)}, u32[]{:S(2)}, u32[]{:S(2)}) collective-permute-start(bf16[3,7040,128]{2,1,0:T(8,128)(2,1)} %get-tuple-element.130), channel_id=1, source_target_pairs={{0,1},{1,0},{2,3},{3,2},{4,5},{5,4},{6,7},{7,6},{8,9},{9,8},{10,11... | collective-permute-start | bytes 16220168 | tf_op jit(solution)/shard_map/ppermute | solution.py:188
  173.9 17.8 %collective-permute-start.15 = (bf16[1760,128]{1,0:T(8,128)(2,1)}, bf16[1760,128]{1,0:T(8,128)(2,1)S(1)}, u32[]{:S(2)}, u32[]{:S(2)}) collective-permute-start(bf16[1760,128]{1,0:T(8,128)(2,1)} %get-tuple-element.141), channel_id=1, source_target_pairs={{0,4},{1,5},{2,6},{3,7},{4,0},{5,1},{6,2},{7,3},{8,12},{9,13},{10,... | collective-permute-start | bytes 1351688 | tf_op jit(solution)/shard_map/ppermute | solution.py:188
  174.5 17.3 %collective-permute-start.16 = (bf16[1760,128]{1,0:T(8,128)(2,1)}, bf16[1760,128]{1,0:T(8,128)(2,1)S(1)}, u32[]{:S(2)}, u32[]{:S(2)}) collective-permute-start(bf16[1760,128]{1,0:T(8,128)(2,1)} %get-tuple-element.152), channel_id=1, source_target_pairs={{0,2},{1,3},{2,0},{3,1},{4,6},{5,7},{6,4},{7,5},{8,10},{9,11},{10,... | collective-permute-start | bytes 1351688 | tf_op jit(solution)/shard_map/ppermute | solution.py:188
  191.7 4.0 %collective-permute-start.17 = (bf16[1,7040,128]{2,1,0:T(8,128)(2,1)}, bf16[1,7040,128]{2,1,0:T(8,128)(2,1)S(1)}, u32[]{:S(2)}, u32[]{:S(2)}) collective-permute-start(bf16[1,7040,128]{2,1,0:T(8,128)(2,1)} %get-tuple-element.154), channel_id=1, source_target_pairs={{0,1},{1,0},{2,3},{3,2},{4,5},{5,4},{6,7},{7,6},{8,9},{9,8},{10,11... | collective-permute-start | bytes 5406728 | tf_op jit(solution)/shard_map/ppermute | solution.py:188
  191.8 13.4 %collective-permute-start.18 = (bf16[1760,128]{1,0:T(8,128)(2,1)}, bf16[1760,128]{1,0:T(8,128)(2,1)S(1)}, u32[]{:S(2)}, u32[]{:S(2)}) collective-permute-start(bf16[1760,128]{1,0:T(8,128)(2,1)} %get-tuple-element.156), channel_id=1, source_target_pairs={{0,4},{1,5},{2,6},{3,7},{4,0},{5,1},{6,2},{7,3},{8,12},{9,13},{10,... | collective-permute-start | bytes 1351688 | tf_op jit(solution)/shard_map/ppermute | solution.py:188
  193.4 13.4 %collective-permute-start.19 = (bf16[1760,128]{1,0:T(8,128)(2,1)}, bf16[1760,128]{1,0:T(8,128)(2,1)S(1)}, u32[]{:S(2)}, u32[]{:S(2)}) collective-permute-start(bf16[1760,128]{1,0:T(8,128)(2,1)} %get-tuple-element.157), channel_id=1, source_target_pairs={{0,2},{1,3},{2,0},{3,1},{4,6},{5,7},{6,4},{7,5},{8,10},{9,11},{10,... | collective-permute-start | bytes 1351688 | tf_op jit(solution)/shard_map/ppermute | solution.py:188
  200.3 18.0 %collective-permute-start.20 = (bf16[1760,128]{1,0:T(8,128)(2,1)}, bf16[1760,128]{1,0:T(8,128)(2,1)S(1)}, u32[]{:S(2)}, u32[]{:S(2)}) collective-permute-start(bf16[1760,128]{1,0:T(8,128)(2,1)} %get-tuple-element.155), channel_id=1, source_target_pairs={{0,4},{1,5},{2,6},{3,7},{4,0},{5,1},{6,2},{7,3},{8,12},{9,13},{10,... | collective-permute-start | bytes 1351688 | tf_op jit(solution)/shard_map/ppermute | solution.py:188
  201.9 16.4 %collective-permute-start.21 = (bf16[1760,128]{1,0:T(8,128)(2,1)}, bf16[1760,128]{1,0:T(8,128)(2,1)S(1)}, u32[]{:S(2)}, u32[]{:S(2)}) collective-permute-start(bf16[1760,128]{1,0:T(8,128)(2,1)} %get-tuple-element.165), channel_id=1, source_target_pairs={{0,2},{1,3},{2,0},{3,1},{4,6},{5,7},{6,4},{7,5},{8,10},{9,11},{10,... | collective-permute-start | bytes 1351688 | tf_op jit(solution)/shard_map/ppermute | solution.py:188
  206.8 20.7 %collective-permute-start.26 = (bf16[1760,128]{1,0:T(8,128)(2,1)}, bf16[1760,128]{1,0:T(8,128)(2,1)S(1)}, u32[]{:S(2)}, u32[]{:S(2)}) collective-permute-start(bf16[1760,128]{1,0:T(8,128)(2,1)} %get-tuple-element.178), channel_id=1, source_target_pairs={{0,4},{1,5},{2,6},{3,7},{4,0},{5,1},{6,2},{7,3},{8,12},{9,13},{10,... | collective-permute-start | bytes 1351688 | tf_op jit(solution)/shard_map/ppermute | solution.py:188
  207.3 20.2 %collective-permute-start.27 = (bf16[1760,128]{1,0:T(8,128)(2,1)}, bf16[1760,128]{1,0:T(8,128)(2,1)S(1)}, u32[]{:S(2)}, u32[]{:S(2)}) collective-permute-start(bf16[1760,128]{1,0:T(8,128)(2,1)} %get-tuple-element.179), channel_id=1, source_target_pairs={{0,2},{1,3},{2,0},{3,1},{4,6},{5,7},{6,4},{7,5},{8,10},{9,11},{10,... | collective-permute-start | bytes 1351688 | tf_op jit(solution)/shard_map/ppermute | solution.py:188
  222.6 13.6 %collective-permute-start.22 = (bf16[1760,128]{1,0:T(8,128)(2,1)}, bf16[1760,128]{1,0:T(8,128)(2,1)S(1)}, u32[]{:S(2)}, u32[]{:S(2)}) collective-permute-start(bf16[1760,128]{1,0:T(8,128)(2,1)} %get-tuple-element.168), channel_id=1, source_target_pairs={{0,2},{1,3},{2,0},{3,1},{4,6},{5,7},{6,4},{7,5},{8,10},{9,11},{10,... | collective-permute-start | bytes 1351688 | tf_op jit(solution)/shard_map/ppermute | solution.py:188
  223.2 14.8 %collective-permute-start.24 = (bf16[1760,128]{1,0:T(8,128)(2,1)}, bf16[1760,128]{1,0:T(8,128)(2,1)S(1)}, u32[]{:S(2)}, u32[]{:S(2)}) collective-permute-start(bf16[1760,128]{1,0:T(8,128)(2,1)} %get-tuple-element.175), channel_id=1, source_target_pairs={{0,4},{1,5},{2,6},{3,7},{4,0},{5,1},{6,2},{7,3},{8,12},{9,13},{10,... | collective-permute-start | bytes 1351688 | tf_op jit(solution)/shard_map/ppermute | solution.py:188
  231.3 13.3 %collective-permute-start.28 = (bf16[1760,128]{1,0:T(8,128)(2,1)}, bf16[1760,128]{1,0:T(8,128)(2,1)S(1)}, u32[]{:S(2)}, u32[]{:S(2)}) collective-permute-start(bf16[1760,128]{1,0:T(8,128)(2,1)} %get-tuple-element.187), channel_id=1, source_target_pairs={{0,2},{1,3},{2,0},{3,1},{4,6},{5,7},{6,4},{7,5},{8,10},{9,11},{10,... | collective-permute-start | bytes 1351688 | tf_op jit(solution)/shard_map/ppermute | solution.py:188
  232.9 12.9 %collective-permute-start.29 = (bf16[1760,128]{1,0:T(8,128)(2,1)}, bf16[1760,128]{1,0:T(8,128)(2,1)S(1)}, u32[]{:S(2)}, u32[]{:S(2)}) collective-permute-start(bf16[1760,128]{1,0:T(8,128)(2,1)} %get-tuple-element.189), channel_id=1, source_target_pairs={{0,4},{1,5},{2,6},{3,7},{4,0},{5,1},{6,2},{7,3},{8,12},{9,13},{10,... | collective-permute-start | bytes 1351688 | tf_op jit(solution)/shard_map/ppermute | solution.py:188
  236.4 10.6 %collective-permute-start.23 = (bf16[880,128]{1,0:T(8,128)(2,1)S(1)}, bf16[880,128]{1,0:T(8,128)(2,1)S(1)}, u32[]{:S(2)}, u32[]{:S(2)}) collective-permute-start(bf16[880,128]{1,0:T(8,128)(2,1)S(1)} %dynamic-slice_bitcast_fusion.3), channel_id=1, source_target_pairs={{0,8},{8,0},{16,24},{24,16},{1,9},{9,1},{17,25},{25,17},{2,10},{10... | collective-permute-start | bytes 675848 | tf_op jit(solution)/shard_map/ppermute | solution.py:1119
  238.2 10.6 %collective-permute-start.25 = (bf16[880,128]{1,0:T(8,128)(2,1)S(1)}, bf16[880,128]{1,0:T(8,128)(2,1)S(1)}, u32[]{:S(2)}, u32[]{:S(2)}) collective-permute-start(bf16[880,128]{1,0:T(8,128)(2,1)S(1)} %dynamic-slice_bitcast_fusion.2), channel_id=1, source_target_pairs={{0,16},{8,24},{16,0},{24,8},{1,17},{9,25},{17,1},{25,9},{2,18},{10... | collective-permute-start | bytes 675848 | tf_op jit(solution)/shard_map/ppermute | solution.py:1119
  248.8 21.0 %collective-permute-start.30 = (bf16[880,128]{1,0:T(8,128)(2,1)S(1)}, bf16[880,128]{1,0:T(8,128)(2,1)S(1)}, u32[]{:S(2)}, u32[]{:S(2)}) collective-permute-start(bf16[880,128]{1,0:T(8,128)(2,1)S(1)} %dynamic-slice_bitcast_fusion.1), channel_id=1, source_target_pairs={{0,8},{8,0},{16,24},{24,16},{1,9},{9,1},{17,25},{25,17},{2,10},{10... | collective-permute-start | bytes 675848 | tf_op jit(solution)/shard_map/ppermute | solution.py:1119
  249.2 46.2 %copy-start.1 = (f32[900608]{0:T(1024)S(1)}, f32[900608]{0:T(1024)}, u32[]{:S(2)}) copy-start(f32[900608]{0:T(1024)} %param.19) | copy-start | bytes 10807300
  249.2 20.6 %collective-permute-start.31 = (bf16[880,128]{1,0:T(8,128)(2,1)S(1)}, bf16[880,128]{1,0:T(8,128)(2,1)S(1)}, u32[]{:S(2)}, u32[]{:S(2)}) collective-permute-start(bf16[880,128]{1,0:T(8,128)(2,1)S(1)} %dynamic-slice_bitcast_fusion), channel_id=1, source_target_pairs={{0,16},{8,24},{16,0},{24,8},{1,17},{9,25},{17,1},{25,9},{2,18},{10... | collective-permute-start | bytes 675848 | tf_op jit(solution)/shard_map/ppermute | solution.py:1119
  252.1 14.3 %collective-permute-start.38 = (bf16[440,128]{1,0:T(8,128)(2,1)S(1)}, bf16[440,128]{1,0:T(8,128)(2,1)S(1)}, u32[]{:S(2)}, u32[]{:S(2)}) collective-permute-start(bf16[440,128]{1,0:T(8,128)(2,1)S(1)} %dynamic-slice_bitcast_fusion.5), channel_id=1, source_target_pairs={{0,16},{8,24},{16,0},{24,8},{1,17},{9,25},{17,1},{25,9},{2,18},{10... | collective-permute-start | bytes 337928 | tf_op jit(solution)/shard_map/ppermute | solution.py:1119
  252.3 14.1 %collective-permute-start.41 = (bf16[440,128]{1,0:T(8,128)(2,1)S(1)}, bf16[440,128]{1,0:T(8,128)(2,1)S(1)}, u32[]{:S(2)}, u32[]{:S(2)}) collective-permute-start(bf16[440,128]{1,0:T(8,128)(2,1)S(1)} %dynamic-slice_bitcast_fusion.4), channel_id=1, source_target_pairs={{0,8},{8,0},{16,24},{24,16},{1,9},{9,1},{17,25},{25,17},{2,10},{10... | collective-permute-start | bytes 337928 | tf_op jit(solution)/shard_map/ppermute | solution.py:1119
  266.4 8.8 %collective-permute-start.39 = (bf16[440,128]{1,0:T(8,128)(2,1)S(1)}, bf16[440,128]{1,0:T(8,128)(2,1)S(1)}, u32[]{:S(2)}, u32[]{:S(2)}) collective-permute-start(bf16[440,128]{1,0:T(8,128)(2,1)S(1)} %bitcast_add_fusion.5), channel_id=1, source_target_pairs={{0,16},{8,24},{16,0},{24,8},{1,17},{9,25},{17,1},{25,9},{2,18},{10... | collective-permute-start | bytes 337928 | tf_op jit(solution)/shard_map/ppermute | solution.py:1119
  266.5 10.9 %collective-permute-start.42 = (bf16[440,128]{1,0:T(8,128)(2,1)S(1)}, bf16[440,128]{1,0:T(8,128)(2,1)S(1)}, u32[]{:S(2)}, u32[]{:S(2)}) collective-permute-start(bf16[440,128]{1,0:T(8,128)(2,1)S(1)} %bitcast_add_fusion.4), channel_id=1, source_target_pairs={{0,8},{8,0},{16,24},{24,16},{1,9},{9,1},{17,25},{25,17},{2,10},{10... | collective-permute-start | bytes 337928 | tf_op jit(solution)/shard_map/ppermute | solution.py:1119
  269.8 25.5 %copy-start = (f32[900608]{0:T(1024)S(1)}, f32[900608]{0:T(1024)}, u32[]{:S(2)}) copy-start(f32[900608]{0:T(1024)} %param.18) | copy-start | bytes 10807300
  269.9 9.0 %collective-permute-start.32 = (bf16[440,128]{1,0:T(8,128)(2,1)S(1)}, bf16[440,128]{1,0:T(8,128)(2,1)S(1)}, u32[]{:S(2)}, u32[]{:S(2)}) collective-permute-start(bf16[440,128]{1,0:T(8,128)(2,1)S(1)} %dynamic-slice_bitcast_fusion.7), channel_id=1, source_target_pairs={{0,16},{8,24},{16,0},{24,8},{1,17},{9,25},{17,1},{25,9},{2,18},{10... | collective-permute-start | bytes 337928 | tf_op jit(solution)/shard_map/ppermute | solution.py:1119
  270.0 14.1 %collective-permute-start.35 = (bf16[440,128]{1,0:T(8,128)(2,1)S(1)}, bf16[440,128]{1,0:T(8,128)(2,1)S(1)}, u32[]{:S(2)}, u32[]{:S(2)}) collective-permute-start(bf16[440,128]{1,0:T(8,128)(2,1)S(1)} %dynamic-slice_bitcast_fusion.6), channel_id=1, source_target_pairs={{0,8},{8,0},{16,24},{24,16},{1,9},{9,1},{17,25},{25,17},{2,10},{10... | collective-permute-start | bytes 337928 | tf_op jit(solution)/shard_map/ppermute | solution.py:1119
  275.3 20.0 %collective-permute-start.40 = (bf16[880,128]{1,0:T(8,128)(2,1)S(1)}, bf16[880,128]{1,0:T(8,128)(2,1)S(1)}, u32[]{:S(2)}, u32[]{:S(2)}) collective-permute-start(bf16[880,128]{1,0:T(8,128)(2,1)S(1)} %maximum_select_fusion.2.one), channel_id=1, source_target_pairs={{0,8},{8,0},{16,24},{24,16},{1,9},{9,1},{17,25},{25,17},{2,10},{10... | collective-permute-start | bytes 675848 | tf_op jit(solution)/shard_map/ppermute | solution.py:1119
  277.5 17.8 %collective-permute-start.43 = (bf16[880,128]{1,0:T(8,128)(2,1)S(1)}, bf16[880,128]{1,0:T(8,128)(2,1)S(1)}, u32[]{:S(2)}, u32[]{:S(2)}) collective-permute-start(bf16[880,128]{1,0:T(8,128)(2,1)S(1)} %maximum_select_fusion.3.two), channel_id=1, source_target_pairs={{0,16},{8,24},{16,0},{24,8},{1,17},{9,25},{17,1},{25,9},{2,18},{10... | collective-permute-start | bytes 675848 | tf_op jit(solution)/shard_map/ppermute | solution.py:1119
  278.9 13.6 %collective-permute-start.33 = (bf16[440,128]{1,0:T(8,128)(2,1)S(1)}, bf16[440,128]{1,0:T(8,128)(2,1)S(1)}, u32[]{:S(2)}, u32[]{:S(2)}) collective-permute-start(bf16[440,128]{1,0:T(8,128)(2,1)S(1)} %bitcast_add_fusion.7), channel_id=1, source_target_pairs={{0,16},{8,24},{16,0},{24,8},{1,17},{9,25},{17,1},{25,9},{2,18},{10... | collective-permute-start | bytes 337928 | tf_op jit(solution)/shard_map/ppermute | solution.py:1119
  284.1 11.1 %collective-permute-start.36 = (bf16[440,128]{1,0:T(8,128)(2,1)S(1)}, bf16[440,128]{1,0:T(8,128)(2,1)S(1)}, u32[]{:S(2)}, u32[]{:S(2)}) collective-permute-start(bf16[440,128]{1,0:T(8,128)(2,1)S(1)} %bitcast_add_fusion.6), channel_id=1, source_target_pairs={{0,8},{8,0},{16,24},{24,16},{1,9},{9,1},{17,25},{25,17},{2,10},{10... | collective-permute-start | bytes 337928 | tf_op jit(solution)/shard_map/ppermute | solution.py:1119
  292.6 6.2 %collective-permute-start.34 = (bf16[880,128]{1,0:T(8,128)(2,1)S(1)}, bf16[880,128]{1,0:T(8,128)(2,1)S(1)}, u32[]{:S(2)}, u32[]{:S(2)}) collective-permute-start(bf16[880,128]{1,0:T(8,128)(2,1)S(1)} %maximum_select_fusion.one), channel_id=1, source_target_pairs={{0,8},{8,0},{16,24},{24,16},{1,9},{9,1},{17,25},{25,17},{2,10},{10... | collective-permute-start | bytes 675848 | tf_op jit(solution)/shard_map/ppermute | solution.py:1119
  295.3 8.9 %collective-permute-start.37 = (bf16[880,128]{1,0:T(8,128)(2,1)S(1)}, bf16[880,128]{1,0:T(8,128)(2,1)S(1)}, u32[]{:S(2)}, u32[]{:S(2)}) collective-permute-start(bf16[880,128]{1,0:T(8,128)(2,1)S(1)} %maximum_select_fusion.1.two), channel_id=1, source_target_pairs={{0,16},{8,24},{16,0},{24,8},{1,17},{9,25},{17,1},{25,9},{2,18},{10... | collective-permute-start | bytes 675848 | tf_op jit(solution)/shard_map/ppermute | solution.py:1119
  (24 other events, 219.6 us)
